TPU v7x, 32 devices: a whole 2x2x4 slice. The times are simulated.
32 devices in a mesh: rep: 8 (over y, x, core), shard: 4 (over z).
Axes of the slice: x: 2, y: 2, z: 4, core: 2. Of those that a mesh axis runs over, the one named last changes fastest.
Arguments:
- tokens: bfloat16 [4096, 768], P(('rep', 'shard')), may hold values from -6 to 6
- segment_ids: int32 [4096], P(('rep', 'shard')), may hold values from -1 to 4095, as said below
- cotangent: bfloat16 [4096, 768], P(('rep', 'shard')), may hold values from -6 to 6
- params: float32 [7090176], P('shard')
- moment_one: float32 [7090176], P(('shard', 'rep')), may hold values from -1.8 to 1.8
- moment_two: float32 [7090176], P(('shard', 'rep')), may hold values from 0.05 to 1
Outputs:
- output: float32 [4096, 768], P(('rep', 'shard'))
- grad_input: float32 [4096, 768], P(('rep', 'shard'))
- grad_params: float32 [7090176], P('shard')
- new_params: float32 [7090176], P('shard')
- new_moment_one: float32 [7090176], P(('shard', 'rep'))
- new_moment_two: float32 [7090176], P(('shard', 'rep'))
Inputs may be any that keep to these rules, and one draw needn't show every extreme that they name: `segment_ids`: on each device's 128 slots the live slots come first and hold whole sequences, each slot marked by the global index of its sequence's first slot; the rest are padding, marked -1. Every device has at least 2/5 of its slots live; the last device is full and its last slot starts a sequence of one slot; the other devices are not full.
All inputs are finite; a program needn't handle non-finite values.
Results may differ from a plain program's by a relative error of at most 0.012.
Values may be sent and summed in bfloat16 or wider, within the bound.
No kernel may reach another device: no remote copies, remote signals or barrier semaphores. Data moves between devices by JAX's collectives and lax.ppermute only.
A program may use at most 192 MiB of HBM per device.

v0:
```python
import math

import jax
import jax.numpy as jnp
from jax import lax
from jax.sharding import PartitionSpec as P

D = 768
HEADS = 12
HD = 64
ROT = 16
FF = 3072


EPS_NORM = 1e-05
ROPE_BASE = 10000.0
NEG_BIG = -1e30
BETA_ONE = 0.9
BETA_TWO = 0.95
ADAM_STEP = 3.0
LEARN_RATE = 0.05
DECAY = 0.01
ADAM_EPS = 1e-08
INV_ROOT_TWO = 0.7071067811865476
INV_ROOT_TWO_PI = 0.3989422804014327


def layout_offsets():
    q_width = HEADS * HD
    o_wqkv = 2 * D
    o_bqkv = o_wqkv + 3 * q_width * D
    o_wout = o_bqkv + 3 * q_width
    o_bout = o_wout + q_width * D
    o_gain2 = o_bout + D
    o_shift2 = o_gain2 + D
    o_win = o_shift2 + D
    o_bin = o_win + D * FF
    o_wout2 = o_bin + FF
    o_bout2 = o_wout2 + FF * D
    return (
        o_wqkv,
        o_bqkv,
        o_wout,
        o_bout,
        o_gain2,
        o_shift2,
        o_win,
        o_bin,
        o_wout2,
        o_bout2,
        o_bout2 + D,
    )


def split_params(flat16):
    q_width = HEADS * HD
    o_wqkv, o_bqkv, o_wout, o_bout, o_gain2, o_shift2, o_win, o_bin, o_wout2, o_bout2, o_end = (
        layout_offsets()
    )
    return (
        flat16[0:D],
        flat16[D:o_wqkv],
        flat16[o_wqkv:o_bqkv].reshape(D, 3 * q_width),
        flat16[o_bqkv:o_wout],
        flat16[o_wout:o_bout].reshape(q_width, D),
        flat16[o_bout:o_gain2],
        flat16[o_gain2:o_shift2],
        flat16[o_shift2:o_win],
        flat16[o_win:o_bin].reshape(D, FF),
        flat16[o_bin:o_wout2],
        flat16[o_wout2:o_bout2].reshape(FF, D),
        flat16[o_bout2:o_end],
    )


def positions_of(segments):
    count = segments.shape[0]
    slot_ids = jnp.arange(count, dtype=jnp.int32)
    before = jnp.concatenate([jnp.full((1,), -2, jnp.int32), segments[:-1]])
    begins = segments != before
    first_slot = lax.cummax(jnp.where(begins, slot_ids, 0), axis=0)
    return slot_ids - first_slot


def rotary_tables(positions):
    half = ROT // 2
    steps_j = jnp.arange(half, dtype=jnp.float32)
    freqs = jnp.power(jnp.float32(ROPE_BASE), -2.0 * steps_j / ROT)
    angle = positions.astype(jnp.float32)[:, None] * freqs[None, :]
    return (jnp.cos(angle)[:, None, :], jnp.sin(angle)[:, None, :])


def rotate(values, cosine, sine, sign):
    half = cosine.shape[-1]
    lower = values[..., :half]
    upper = values[..., half : 2 * half]
    rest = values[..., 2 * half :]
    return jnp.concatenate(
        [lower * cosine - sign * upper * sine, upper * cosine + sign * lower * sine, rest], axis=-1
    )


def gelu_exact(value):
    return value * 0.5 * (1.0 + lax.erf(value * INV_ROOT_TWO))


def gelu_slope(value):
    return (
        0.5 * (1.0 + lax.erf(value * INV_ROOT_TWO))
        + value * jnp.exp(-0.5 * value * value) * INV_ROOT_TWO_PI
    )


def masked_scores(q_blk, keys, seg_rows, seg_cols, begin_row):
    scale = q_blk.shape[-1] ** (-0.5)
    raw_scores = jnp.einsum("qhd,khd->hqk", q_blk, keys, preferred_element_type=jnp.float32) * scale
    row_ids = begin_row + jnp.arange(q_blk.shape[0], dtype=jnp.int32)
    col_ids = jnp.arange(keys.shape[0], dtype=jnp.int32)
    allowed = (seg_rows[:, None] == seg_cols[None, :]) & (col_ids[None, :] <= row_ids[:, None])
    return jnp.where(allowed[None], raw_scores, NEG_BIG)


def attend_forward(query16, key16, value16, segments):
    scores = masked_scores(query16, key16, segments, segments, 0)
    row_max = jnp.max(scores, axis=-1, keepdims=True)
    expd = jnp.exp(scores - row_max)
    row_total = jnp.sum(expd, axis=-1, keepdims=True)
    probs16 = (expd / row_total).astype(jnp.bfloat16)
    attn_blk = jnp.einsum("hqk,khd->qhd", probs16, value16, preferred_element_type=jnp.float32)
    pieces_out = attn_blk.astype(jnp.bfloat16)
    lse_list = [row_max + jnp.log(row_total)]
    return (pieces_out, lse_list)


def attend_backward(query16, key16, value16, attn16, lse_list, segments, grad_attn16):
    count = query16.shape[0]
    block = min(512, count)
    scale = query16.shape[-1] ** (-0.5)
    grad_query = []
    grad_key = jnp.zeros(key16.shape, jnp.float32)
    grad_value = jnp.zeros(value16.shape, jnp.float32)
    for turn, begin_row in enumerate(range(0, count, block)):
        stop_row = begin_row + block
        scores = masked_scores(query16, key16, segments, segments, begin_row)
        chances = jnp.exp(scores - lse_list[turn])
        chances16 = chances.astype(jnp.bfloat16)
        grad_value = grad_value.at[:stop_row].add(
            jnp.einsum("hqk,qhd->khd", chances16, grad_attn16, preferred_element_type=jnp.float32)
        )
        grad_chance = jnp.einsum(
            "qhd,khd->hqk", grad_attn16, value16, preferred_element_type=jnp.float32
        )
        delta = jnp.sum(grad_attn16.astype(jnp.float32) * attn16.astype(jnp.float32), axis=-1)
        grad_scores = (chances * (grad_chance - jnp.transpose(delta)[:, :, None]) * scale).astype(
            jnp.bfloat16
        )
        grad_query.append(
            jnp.einsum("hqk,khd->qhd", grad_scores, key16, preferred_element_type=jnp.float32)
        )
        grad_key = grad_key.at[:stop_row].add(
            jnp.einsum("hqk,qhd->khd", grad_scores, query16, preferred_element_type=jnp.float32)
        )
    return (grad_query[0], grad_key, grad_value)


def norm_back(grad_act, normed, inv_std, gain):
    grad_gain = jnp.sum(grad_act * normed, axis=0)
    grad_shift = jnp.sum(grad_act, axis=0)
    grad_norm = grad_act * gain.astype(jnp.float32)
    grad_x = inv_std * (
        grad_norm
        - jnp.mean(grad_norm, axis=1, keepdims=True)
        - normed * jnp.mean(grad_norm * normed, axis=1, keepdims=True)
    )
    return (grad_gain, grad_shift, grad_x)


def layer_forward(tokens, segments, pieces):
    (
        gain_one,
        shift_one,
        w_qkv,
        b_qkv,
        w_out,
        b_out,
        gain_two,
        shift_two,
        w_in,
        b_in,
        w_out2,
        b_out2,
    ) = pieces
    count = tokens.shape[0]
    x_wide = tokens.astype(jnp.float32)
    row_mean = jnp.mean(x_wide, axis=1, keepdims=True)
    centered = x_wide - row_mean
    variance = jnp.mean(centered * centered, axis=1, keepdims=True)
    inv_std = lax.rsqrt(variance + EPS_NORM)
    normed = centered * inv_std
    act_one = (normed * gain_one.astype(jnp.float32) + shift_one.astype(jnp.float32)).astype(
        jnp.bfloat16
    )
    act_two = (normed * gain_two.astype(jnp.float32) + shift_two.astype(jnp.float32)).astype(
        jnp.bfloat16
    )
    mixed = jnp.dot(act_one, w_qkv, preferred_element_type=jnp.float32) + b_qkv.astype(jnp.float32)
    mixed = mixed.reshape(count, 3, HEADS, HD)
    cosine, sine = rotary_tables(positions_of(segments))
    query16 = rotate(mixed[:, 0], cosine, sine, 1.0).astype(jnp.bfloat16)
    key16 = rotate(mixed[:, 1], cosine, sine, 1.0).astype(jnp.bfloat16)
    value16 = mixed[:, 2].astype(jnp.bfloat16)
    attn16, lse_list = attend_forward(query16, key16, value16, segments)
    proj = jnp.dot(
        attn16.reshape(count, HEADS * HD), w_out, preferred_element_type=jnp.float32
    ) + b_out.astype(jnp.float32)
    pre = jnp.dot(act_two, w_in, preferred_element_type=jnp.float32) + b_in.astype(jnp.float32)
    hidden16 = gelu_exact(pre).astype(jnp.bfloat16)
    feed = jnp.dot(hidden16, w_out2, preferred_element_type=jnp.float32) + b_out2.astype(
        jnp.float32
    )
    output = x_wide + proj + feed
    saved = (
        normed,
        inv_std,
        act_one,
        act_two,
        query16,
        key16,
        value16,
        attn16,
        lse_list,
        cosine,
        sine,
        pre,
        hidden16,
    )
    return (output, saved)


def layer_backward(cotangent, segments, pieces, saved, total_len):
    (
        gain_one,
        shift_one,
        w_qkv,
        b_qkv,
        w_out,
        b_out,
        gain_two,
        shift_two,
        w_in,
        b_in,
        w_out2,
        b_out2,
    ) = pieces
    (
        normed,
        inv_std,
        act_one,
        act_two,
        query16,
        key16,
        value16,
        attn16,
        lse_list,
        cosine,
        sine,
        pre,
        hidden16,
    ) = saved
    count = cotangent.shape[0]
    contract_rows = (((0,), (0,)), ((), ()))
    contract_cols = (((1,), (1,)), ((), ()))
    live_rows = (segments >= 0).astype(jnp.float32)[:, None]
    grad_y = cotangent.astype(jnp.float32) * live_rows
    grad_y16 = grad_y.astype(jnp.bfloat16)
    grad_b_out = jnp.sum(grad_y, axis=0)
    attn_flat = attn16.reshape(count, HEADS * HD)
    grad_w_out = lax.dot_general(
        attn_flat, grad_y16, contract_rows, preferred_element_type=jnp.float32
    )
    grad_w_out2 = lax.dot_general(
        hidden16, grad_y16, contract_rows, preferred_element_type=jnp.float32
    )
    grad_hidden = lax.dot_general(
        grad_y16, w_out2, contract_cols, preferred_element_type=jnp.float32
    )
    grad_pre = grad_hidden * gelu_slope(pre)
    grad_b_in = jnp.sum(grad_pre, axis=0)
    grad_pre16 = grad_pre.astype(jnp.bfloat16)
    grad_w_in = lax.dot_general(
        act_two, grad_pre16, contract_rows, preferred_element_type=jnp.float32
    )
    grad_act_two = lax.dot_general(
        grad_pre16, w_in, contract_cols, preferred_element_type=jnp.float32
    )
    grad_attn16 = (
        lax.dot_general(grad_y16, w_out, contract_cols, preferred_element_type=jnp.float32)
        .astype(jnp.bfloat16)
        .reshape(count, HEADS, HD)
    )
    grad_query, grad_key, grad_value = attend_backward(
        query16, key16, value16, attn16, lse_list, segments, grad_attn16
    )
    grad_query = rotate(grad_query, cosine, sine, -1.0)
    grad_key = rotate(grad_key, cosine, sine, -1.0)
    grad_mixed = jnp.stack([grad_query, grad_key, grad_value], axis=1).reshape(
        count, 3 * HEADS * HD
    )
    grad_b_qkv = jnp.sum(grad_mixed, axis=0)
    grad_mixed16 = grad_mixed.astype(jnp.bfloat16)
    grad_w_qkv = lax.dot_general(
        act_one, grad_mixed16, contract_rows, preferred_element_type=jnp.float32
    )
    grad_act_one = lax.dot_general(
        grad_mixed16, w_qkv, contract_cols, preferred_element_type=jnp.float32
    )
    gain_grad_one, shift_grad_one, grad_x_one = norm_back(grad_act_one, normed, inv_std, gain_one)
    gain_grad_two, shift_grad_two, grad_x_two = norm_back(grad_act_two, normed, inv_std, gain_two)
    grad_in = grad_y + grad_x_one + grad_x_two
    flat_parts = [
        gain_grad_one,
        shift_grad_one,
        grad_w_qkv.reshape(-1),
        grad_b_qkv,
        grad_w_out.reshape(-1),
        grad_b_out,
        gain_grad_two,
        shift_grad_two,
        grad_w_in.reshape(-1),
        grad_b_in,
        grad_w_out2.reshape(-1),
        grad_b_out,
    ]
    used = layout_offsets()[-1]
    rounded = [part.astype(jnp.bfloat16) for part in flat_parts]
    flat_grad = jnp.concatenate(rounded + [jnp.zeros((total_len - used,), jnp.bfloat16)])
    return (grad_in, flat_grad)


def adam_update(weights, first_moment, second_moment, gradient):
    new_first = BETA_ONE * first_moment + (1.0 - BETA_ONE) * gradient
    new_second = BETA_TWO * second_moment + (1.0 - BETA_TWO) * gradient * gradient
    unbiased_first = new_first / (1.0 - BETA_ONE**ADAM_STEP)
    unbiased_second = new_second / (1.0 - BETA_TWO**ADAM_STEP)
    new_weights = weights - LEARN_RATE * (
        unbiased_first / (jnp.sqrt(unbiased_second) + ADAM_EPS) + DECAY * weights
    )
    return (new_weights, new_first, new_second)


def on_device(tokens, segment_ids, cotangent, params, moment_one, moment_two):
    gathered = lax.all_gather(params.astype(jnp.bfloat16), "shard", axis=0, tiled=True)
    total_len = gathered.shape[0]
    pieces = split_params(gathered)
    output, saved = layer_forward(tokens, segment_ids, pieces)
    grad_input, local_grad = layer_backward(cotangent, segment_ids, pieces, saved, total_len)
    owned = lax.psum_scatter(local_grad, "shard", scatter_dimension=0, tiled=True).astype(
        jnp.float32
    )
    tokens_all = tokens.shape[0] * lax.axis_size("rep") * lax.axis_size("shard")
    factor = 1.0 / math.sqrt(tokens_all)
    width = moment_one.shape[0]
    begin = lax.axis_index("rep") * width
    param_share = lax.dynamic_slice_in_dim(params, begin, width)
    share = lax.psum_scatter(owned, "rep", scatter_dimension=0, tiled=True)
    grad_share = share * factor
    upd_params, upd_first, upd_second = adam_update(param_share, moment_one, moment_two, grad_share)
    grad_params, new_params = (
        lax.all_gather(grad_share, "rep", axis=0, tiled=True),
        lax.all_gather(upd_params, "rep", axis=0, tiled=True),
    )
    return (output, grad_input, grad_params, new_params, upd_first, upd_second)


def solution(mesh):
    in_specs = (
        P(("rep", "shard"), None),
        P(("rep", "shard")),
        P(("rep", "shard"), None),
        P("shard"),
        P(("shard", "rep")),
        P(("shard", "rep")),
    )
    out_specs = (
        P(("rep", "shard"), None),
        P(("rep", "shard"), None),
        P("shard"),
        P("shard"),
        P(("shard", "rep")),
        P(("shard", "rep")),
    )
    return jax.shard_map(
        on_device, mesh=mesh, in_specs=in_specs, out_specs=out_specs, check_vma=False
    )
```

profile of v0, /device:TPU:0, one launch (start us, length us, event | category | flops | bytes accessed | tf_op | source)
XLA Modules:
  0.0 1184.8 jit_solution(15967616981541426107)
XLA Ops:
  7.2 4.5 convert_element_type.156
  13.4 245.5 %all-gather.6.cloned.1.call-done = bf16[7090176]{0:T(1024)(128)(2,1)} async-done(((bf16[1772544]{0:T(1024)(128)(2,1)}), bf16[7090176]{0:T(1024)(128)(2,1)}) %all-gather.6.cloned.1.call-update) | async-done | bytes 14180368 | tf_op jit(solution)/shard_map/all_gather | solution.py:352
  262.2 3.7 slice.188
  265.9 7.6 reshape.305
  275.6 3.7 convolution_add_fusion
  285.9 8.2 fusion.63
  294.2 9.2 slice.178
  303.4 8.2 slice.175
  312.5 3.6 convolution_add_fusion.1
  320.2 3.7 fusion
  323.9 3.6 convolution_convert_fusion
  327.5 3.0 convolution_convert_fusion.2
  330.5 2.7 fusion.37
  335.5 7.7 convert_element_type.187
  347.1 3.3 convert_element_type.191
  350.4 5.9 copy.43
  356.3 9.2 convert_element_type.199
  368.4 54.7 %dynamic-update-slice.6 = bf16[7090176]{0:T(1024)(128)(2,1)} dynamic-update-slice(bf16[7090176]{0:T(1024)(128)(2,1)} %dynamic-update-slice.5, bf16[1769472]{0:T(1024)(128)(2,1)} %convert_element_type.187, s32[]{} %constant.158) | dynamic-update-slice | bytes 7077892
  424.6 19.2 %dynamic-update-slice.8 = bf16[7090176]{0:T(1024)(128)(2,1)} dynamic-update-slice(bf16[7090176]{0:T(1024)(128)(2,1)} %dynamic-update-slice.7, bf16[589824]{0:T(1024)(128)(2,1)} %convert_element_type.191, s32[]{} %constant.160) | dynamic-update-slice | bytes 2359300
  450.2 5.5 constant_dynamic-update-slice_fusion.1
  456.2 5.4 constant_dynamic-update-slice_fusion
  466.4 474.5 %all-reduce.5.cloned.1.call-done = bf16[7090176]{0:T(1024)(128)(2,1)} async-done(((bf16[7090176]{0:T(1024)(128)(2,1)}), bf16[7090176]{0:T(1024)(128)(2,1)}) %all-reduce.5.cloned.1.call-update) | async-done | bytes 14180368
  940.9 4.7 dynamic-slice_convert_fusion
  947.5 110.6 %all-reduce.7.cloned.1.call-done = f32[1772544]{0:T(1024)} async-done(((f32[1772544]{0:T(1024)}), f32[1772544]{0:T(1024)}) %all-reduce.7.cloned.1.call-update) | async-done | bytes 7090192
  1058.1 4.6 multiply_subtract_fusion
  1062.7 4.9 reshape.311
  1067.6 5.0 reshape.313
  1072.7 3.6 convolution_add_fusion.3
  1077.5 39.1 %all-gather.8.cloned.1.call-done = f32[8,1,221568]{2,1,0:T(1,128)} async-done(((f32[1,1,221568]{2,1,0:T(1,128)}), f32[8,1,221568]{2,1,0:T(1,128)}) %all-gather.8.cloned.1.call-update) | async-done | bytes 7090192 | tf_op jit(solution)/shard_map/all_gather | solution.py:369
  1116.6 50.8 %all-gather.10.cloned.1.call-done = f32[8,1,221568]{2,1,0:T(1,128)} async-done(((f32[1,1,221568]{2,1,0:T(1,128)}), f32[8,1,221568]{2,1,0:T(1,128)}) %all-gather.10.cloned.1.call-update) | async-done | bytes 7090192 | tf_op jit(solution)/shard_map/all_gather | solution.py:370
  1167.5 6.0 copy.61
  1175.1 3.2 copy.62
  (121 shorter events, 43.9 us)
Async XLA Ops:
  7.2 251.7 %all-gather.6.cloned.1.call-start = ((), (), s32[]{:S(2)}) async-start(), calls=%async_computation | async-start | bytes 17725440 | tf_op jit(solution)/shard_map/all_gather | solution.py:352
  11.7 0.7 copy-start.17
  11.7 1.1 copy-start.1
  11.7 249.8 %copy-start.4 = (bf16[128,768]{1,0:T(8,128)(2,1)S(1)}, bf16[128,768]{1,0:T(8,128)(2,1)}, u32[]{:S(2)}) copy-start(bf16[128,768]{1,0:T(8,128)(2,1)} %param.16) | copy-start | bytes 589828
  11.7 929.2 %all-reduce.5.cloned.1.call-start = ((), (), s32[]{:S(2)}) async-start(), calls=%async_computation.3 | async-start | bytes 28360704
  13.0 299.5 %copy-start.7 = (f32[128]{0:T(128)}, f32[128]{0:T(128)S(1)}, u32[]{:S(2)}) copy-start(f32[128]{0:T(128)S(1)} %broadcast_multiply_fusion.5) | copy-start | bytes 1540
  13.2 302.9 %copy-start.14 = (f32[128]{0:T(128)}, f32[128]{0:T(128)S(1)}, u32[]{:S(2)}) copy-start(f32[128]{0:T(128)S(1)} %compare_convert_fusion) | copy-start | bytes 1540
  13.2 299.3 %copy-start.10 = (f32[128]{0:T(128)}, f32[128]{0:T(128)S(1)}, u32[]{:S(2)}) copy-start(f32[128]{0:T(128)S(1)} %add_rsqrt_fusion) | copy-start | bytes 1540
  311.6 4.5 copy-start
  312.5 6.0 slice-start
  316.1 2.4 slice-start.1
  318.5 1.7 copy-start.8
  318.5 1.7 copy-start.11
  320.2 3.7 copy-start.15
  323.9 3.6 copy-start.5
  327.5 3.0 copy-start.2
  335.5 9.1 copy-start.16
  356.3 9.2 copy-start.19
  368.4 75.5 %copy-start.9 = (f32[128]{0:T(128)S(1)}, f32[128]{0:T(128)}, u32[]{:S(2)}) copy-start(f32[128]{0:T(128)} %copy-done.7) | copy-start | bytes 1540
  450.2 5.5 copy-start.18
  464.5 0.7 copy-start.21
  464.5 593.6 %all-reduce.7.cloned.1.call-start = ((), (), s32[]{:S(2)}) async-start(), calls=%async_computation.4 | async-start | bytes 14180352
  945.6 0.7 copy-start.20
  945.6 171.0 %all-gather.8.cloned.1.call-start = ((), (), s32[]{:S(2)}) async-start(), calls=%async_computation.1 | async-start | bytes 7976448 | tf_op jit(solution)/shard_map/all_gather | solution.py:369
  1062.7 10.0 copy-start.13
  1067.6 99.9 %all-gather.10.cloned.1.call-start = ((), (), s32[]{:S(2)}) async-start(), calls=%async_computation.2 | async-start | bytes 7976448 | tf_op jit(solution)/shard_map/all_gather | solution.py:370
  1072.7 3.7 copy-start.6
  1072.7 3.7 copy-start.12
  1167.5 7.6 copy-start.3
Sparse Core Ops, SparseCore 0:
  11.8 247.0 all-gather.5
  464.6 476.2 all-reduce.4
  945.7 112.3 all-reduce.6
  1067.7 48.8 all-gather.7
  1118.5 48.8 all-gather.9
where the time goes:
time: 1190 us; the launch traced here: 1180 us
  waiting for transfers between devices  921 us (77%)
  local copies, waits for them, and re-layouts  190 us (16%)
  matrix products  34.8 us (3%)
  other arithmetic  24 us (2%)
  between operations  15.5 us (1%)
    unnamed x7, waiting for transfers between devices  585 us
    all_gather x1, waiting for transfers between devices, on_device(): lax.all_gather(params.astype(jnp.bfloat16), 'shard', axis=0, tiled=True)  245 us
    unnamed x67, local copies, waits for them, and re-layouts  125 us
    all_gather x1, waiting for transfers between devices, on_device(): lax.all_gather(upd_params, 'rep', axis=0, tiled=True)  50.8 us
    all_gather x1, waiting for transfers between devices, on_device(): lax.all_gather(grad_share, 'rep', axis=0, tiled=True)  39.1 us
  transfers between devices with their start and end apart: 5, of which 5 were waited for; matrix products, arithmetic and copies ran while one was open for 1% of the time, Pallas kernels for 0%

commit v1 on v0

--- a/solution.py
+++ b/solution.py
@@ -1,8 +1,11 @@
+import functools
 import math
 
 import jax
 import jax.numpy as jnp
 from jax import lax
+from jax.experimental import pallas as pl
+from jax.experimental.pallas import tpu as pltpu
 from jax.sharding import PartitionSpec as P
 
 D = 768
@@ -237,7 +240,7 @@
     return (output, saved)
 
 
-def layer_backward(cotangent, segments, pieces, saved, total_len):
+def layer_backward(cotangent, segments, pieces, saved):
     (
         gain_one,
         shift_one,
@@ -317,24 +320,29 @@
     gain_grad_one, shift_grad_one, grad_x_one = norm_back(grad_act_one, normed, inv_std, gain_one)
     gain_grad_two, shift_grad_two, grad_x_two = norm_back(grad_act_two, normed, inv_std, gain_two)
     grad_in = grad_y + grad_x_one + grad_x_two
-    flat_parts = [
-        gain_grad_one,
-        shift_grad_one,
-        grad_w_qkv.reshape(-1),
-        grad_b_qkv,
-        grad_w_out.reshape(-1),
-        grad_b_out,
-        gain_grad_two,
-        shift_grad_two,
-        grad_w_in.reshape(-1),
-        grad_b_in,
-        grad_w_out2.reshape(-1),
-        grad_b_out,
-    ]
+    return (
+        grad_in,
+        [
+            gain_grad_one,
+            shift_grad_one,
+            grad_w_qkv,
+            grad_b_qkv,
+            grad_w_out,
+            grad_b_out,
+            gain_grad_two,
+            shift_grad_two,
+            grad_w_in,
+            grad_b_in,
+            grad_w_out2,
+            grad_b_out,
+        ],
+    )
+
+
+def flatten_grads(parts, total_len):
     used = layout_offsets()[-1]
-    rounded = [part.astype(jnp.bfloat16) for part in flat_parts]
-    flat_grad = jnp.concatenate(rounded + [jnp.zeros((total_len - used,), jnp.bfloat16)])
-    return (grad_in, flat_grad)
+    rounded = [part.astype(jnp.bfloat16).reshape(-1) for part in parts]
+    return jnp.concatenate(rounded + [jnp.zeros((total_len - used,), jnp.bfloat16)])
 
 
 def adam_update(weights, first_moment, second_moment, gradient):
@@ -353,7 +361,8 @@
     total_len = gathered.shape[0]
     pieces = split_params(gathered)
     output, saved = layer_forward(tokens, segment_ids, pieces)
-    grad_input, local_grad = layer_backward(cotangent, segment_ids, pieces, saved, total_len)
+    grad_input, parts = layer_backward(cotangent, segment_ids, pieces, saved)
+    local_grad = flatten_grads(parts, total_len)
     owned = lax.psum_scatter(local_grad, "shard", scatter_dimension=0, tiled=True).astype(
         jnp.float32
     )
@@ -372,6 +381,208 @@
     return (output, grad_input, grad_params, new_params, upd_first, upd_second)
 
 
+LANES = 128
+REPS = 8
+SHARDS = 4
+PIECE = 288
+FLAT_ROWS = 13848
+MOVED = PIECE * D // LANES
+
+
+PARTS = (
+    ((12, 1728, 96, 3, 0),),
+    ((6, 576, 96, 1, 0), (4632, 1152, 48, 4, 96)),
+    ((0, 1152, 48, 4, 0), (9240, 576, 96, 1, 192)),
+    ((0, 1728, 288, 1, 0),),
+)
+VECTOR_ROWS = ((0, 1, 2306, 2307), (0, 769, 770, 771), (1536, 1537, 1538, 1539), (2304, 2305, 2306, 2307))
+
+
+def pack_kernel(where, flat_ref, out_ref, held, sems):
+    shard = where[0]
+    rep = where[1]
+    for z in range(SHARDS):
+
+        @pl.when(shard == z)
+        def _(z=z):
+            copies = []
+            at = 0
+            for turn, (first, step, _, _, _) in enumerate(PARTS[z]):
+                lead = first % 8
+                count = step + (8 if lead else 0)
+                begin = pl.multiple_of(first - lead + step * rep, 8)
+                copies.append(
+                    pltpu.make_async_copy(
+                        flat_ref.at[pl.ds(begin, count)], held.at[pl.ds(at, count)], sems.at[turn]
+                    )
+                )
+                at += count
+            for copy in copies:
+                copy.start()
+            at = 0
+            for copy, (first, step, rows, blocks, place) in zip(copies, PARTS[z]):
+                copy.wait()
+                lead = first % 8
+                stride = 6 * blocks
+                for block in range(blocks):
+                    for col in range(6):
+                        got = held[pl.ds(at + lead + 6 * block + col, rows, stride=stride), :]
+                        out_ref[
+                            place + rows * block : place + rows * (block + 1),
+                            LANES * col : LANES * (col + 1),
+                        ] = got.astype(jnp.bfloat16)
+                at += step + (8 if lead else 0)
+
+
+def pack_piece(params, shard, rep):
+    return pl.pallas_call(
+        pack_kernel,
+        grid_spec=pltpu.PrefetchScalarGridSpec(
+            num_scalar_prefetch=1,
+            in_specs=[pl.BlockSpec(memory_space=pltpu.HBM)],
+            out_specs=pl.BlockSpec(memory_space=pltpu.VMEM),
+            scratch_shapes=[
+                pltpu.VMEM((MOVED + 16, LANES), jnp.float32),
+                pltpu.SemaphoreType.DMA((2,)),
+            ],
+        ),
+        out_shape=jax.ShapeDtypeStruct((PIECE, D), jnp.bfloat16),
+    )(jnp.stack([shard, rep]), params.reshape(FLAT_ROWS, LANES))
+
+
+def unpack_kernel(factor, where, grad_ref, vec_ref, out_ref):
+    shard = where[0]
+    for z in range(SHARDS):
+
+        @pl.when(shard == z)
+        def _(z=z):
+            for slot, row in enumerate(VECTOR_ROWS[z]):
+                for col in range(6):
+                    out_ref[6 * row + col : 6 * row + col + 1, :] = (
+                        vec_ref[slot : slot + 1, LANES * col : LANES * (col + 1)] * factor
+                    )
+            for rep in range(REPS):
+                for first, step, rows, blocks, place in PARTS[z]:
+                    for block in range(blocks):
+                        for col in range(6):
+                            got = grad_ref[
+                                rep,
+                                place + rows * block : place + rows * (block + 1),
+                                LANES * col : LANES * (col + 1),
+                            ]
+                            out_ref[
+                                pl.ds(
+                                    first + step * rep + 6 * block + col, rows, stride=6 * blocks
+                                ),
+                                :,
+                            ] = got.astype(jnp.float32) * factor
+
+
+def unpack_grads(grads, vectors, shard, factor):
+    return pl.pallas_call(
+        functools.partial(unpack_kernel, factor),
+        grid_spec=pltpu.PrefetchScalarGridSpec(
+            num_scalar_prefetch=1,
+            in_specs=[pl.BlockSpec(memory_space=pltpu.VMEM)] * 2,
+            out_specs=pl.BlockSpec(memory_space=pltpu.VMEM),
+        ),
+        out_shape=jax.ShapeDtypeStruct((FLAT_ROWS, LANES), jnp.float32),
+        compiler_params=pltpu.CompilerParams(vmem_limit_bytes=32 * 2**20),
+    )(jnp.stack([shard]), grads, vectors)
+
+
+def shard_vectors(params, shard):
+    rows = jnp.asarray(VECTOR_ROWS, jnp.int32)[shard]
+    return jnp.stack([lax.dynamic_slice_in_dim(params, rows[i] * D, D) for i in range(4)])
+
+
+def pieces_of(gathered, vectors):
+    first, second, third, fourth = (gathered[z] for z in range(SHARDS))
+    w_qkv = jnp.concatenate(
+        [first[:, 96 * j : 96 * (j + 1)].reshape(D, D) for j in range(3)], axis=1
+    )
+    w_out = second[:, 0:96].reshape(D, D)
+    w_in = jnp.concatenate(
+        [
+            jnp.concatenate(
+                [
+                    second[:, 96 + 48 * j : 144 + 48 * j].reshape(D // 2, D),
+                    third[:, 48 * j : 48 * (j + 1)].reshape(D // 2, D),
+                ],
+                axis=0,
+            )
+            for j in range(4)
+        ],
+        axis=1,
+    )
+    w_out2 = jnp.concatenate([third[:, 192:288].reshape(D, D), fourth.reshape(3 * D, D)], axis=0)
+    return (
+        vectors[0, 0],
+        vectors[0, 1],
+        w_qkv,
+        jnp.concatenate([vectors[0, 2], vectors[0, 3], vectors[1, 0]]),
+        w_out,
+        vectors[1, 1],
+        vectors[1, 2],
+        vectors[1, 3],
+        w_in,
+        vectors[2].reshape(-1),
+        w_out2,
+        vectors[3, 0],
+    )
+
+
+def grads_by_owner(parts):
+    w_qkv, w_out, w_in, w_out2 = (part.astype(jnp.bfloat16) for part in parts)
+    col = lambda w, j: w[:, D * j : D * (j + 1)]
+    first = [col(w_qkv, j).reshape(REPS, 96, D) for j in range(3)]
+    second = [w_out.reshape(REPS, 96, D)] + [
+        col(w_in, j)[: D // 2].reshape(REPS, 48, D) for j in range(4)
+    ]
+    third = [col(w_in, j)[D // 2 :].reshape(REPS, 48, D) for j in range(4)] + [
+        w_out2[:D].reshape(REPS, 96, D)
+    ]
+    fourth = [w_out2[D:].reshape(REPS, PIECE, D)]
+    return jnp.stack(
+        [jnp.concatenate(group, axis=1) for group in (first, second, third, fourth)]
+    )
+
+
+def on_device_rows(tokens, segment_ids, cotangent, params, moment_one, moment_two):
+    shard = lax.axis_index("shard")
+    rep = lax.axis_index("rep")
+    piece = pack_piece(params, shard, rep)
+    vectors = lax.all_gather(shard_vectors(params, shard).astype(jnp.bfloat16), "shard", axis=0)
+    gathered = lax.all_gather(piece, ("shard", "rep"), axis=0, tiled=True)
+    gathered = gathered.reshape(SHARDS, REPS, PIECE, D)
+    pieces = pieces_of(gathered, vectors)
+    output, saved = layer_forward(tokens, segment_ids, pieces)
+    grad_input, parts = layer_backward(cotangent, segment_ids, pieces, saved)
+    (g1, s1, gw_qkv, gb_qkv, gw_out, gb_out, g2, s2, gw_in, gb_in, gw_out2, gb_out2) = parts
+    owned = lax.psum_scatter(
+        grads_by_owner((gw_qkv, gw_out, gw_in, gw_out2)).reshape(SHARDS * REPS * PIECE, D),
+        ("shard", "rep"),
+        scatter_dimension=0,
+        tiled=True,
+    )
+    zero = jnp.zeros((3 * D,), jnp.float32)
+    vec_grads = jnp.concatenate([g1, s1, gb_qkv, gb_out, g2, s2, gb_in, gb_out2, zero])
+    vec_grads = lax.psum(
+        vec_grads.astype(jnp.bfloat16).astype(jnp.float32), ("shard", "rep")
+    ).reshape(SHARDS, 4, D)
+    own_vectors = lax.dynamic_index_in_dim(vec_grads, shard, 0, keepdims=False)
+    grads = lax.all_gather(owned, "rep", axis=0, tiled=True).reshape(REPS, PIECE, D)
+    tokens_all = tokens.shape[0] * lax.axis_size("rep") * lax.axis_size("shard")
+    grad_params = unpack_grads(grads, own_vectors, shard, 1.0 / math.sqrt(tokens_all)).reshape(-1)
+    width = moment_one.shape[0]
+    begin = rep * width
+    param_share = lax.dynamic_slice_in_dim(params, begin, width)
+    grad_share = lax.dynamic_slice_in_dim(grad_params, begin, width)
+    upd_params, upd_first, upd_second = adam_update(param_share, moment_one, moment_two, grad_share)
+    new_params = lax.all_gather(upd_params, "rep", axis=0, tiled=True)
+    return (output, grad_input, grad_params, new_params, upd_first, upd_second)
+
+
 def solution(mesh):
     in_specs = (
         P(("rep", "shard"), None),
@@ -389,6 +600,7 @@
         P(("shard", "rep")),
         P(("shard", "rep")),
     )
+    in_rows = mesh.shape["rep"] == REPS and mesh.shape["shard"] == SHARDS
     return jax.shard_map(
-        on_device, mesh=mesh, in_specs=in_specs, out_specs=out_specs, check_vma=False
-    )
+        on_device_rows if in_rows else on_device, mesh=mesh, in_specs=in_specs, out_specs=out_specs, check_vma=False
+    )

time: 1190 us -> 511 us (0.43)
  waiting for transfers between devices: 921 us -> 288 us
  local copies, waits for them, and re-layouts: 190 us -> 55.7 us
  blocking collectives: 0 us -> 54.9 us
  other arithmetic: 24 us -> 52.9 us
    unnamed x7 -> x4, waiting for transfers between devices: 585 us -> 0.07 us
    all_gather x3, waiting for transfers between devices: 335 us -> 127 us  [the longest x1 82.8 us: on_device_rows(): gathered = lax.all_gather(piece, ('shard', 'rep'), axis=0, tiled=True)]
    reduce_scatter x0 -> x1, waiting for transfers between devices: none -> 161 us  [on_device_rows(): lax.psum_scatter(grads_by_owner((gw_qkv, gw_out, gw_in, gw_out2)).reshape...]
    unnamed x67 -> x150, local copies, waits for them, and re-layouts: 125 us -> 32.5 us
    psum x0 -> x1, blocking collectives: none -> 39.9 us  [on_device_rows(): lax.psum(vec_grads.astype(jnp.bfloat16).astype(jnp.float32), ('shard', 'r...]
    concatenate x0 -> x1, other arithmetic: none -> 33.3 us  [pieces_of(): jnp.concatenate([jnp.concatenate([second[:, 96 + 48 * j:144 + 48 * j].res...]
    convert_element_type x4 -> x1, local copies, waits for them, and re-layouts: 21.6 us -> 0.61 us  [layer_forward(): b_in.astype(jnp.float32)]
    slice x6 -> x14, local copies, waits for them, and re-layouts: 32 us -> 15.6 us  [the longest x1 7.38 us: pieces_of(): first, second, third, fourth = (gathered[z] for z in range(SHARDS))]
  transfers between devices with their start and end apart: 5 -> 4, of which waited for: 5 -> 3; matrix products, arithmetic and copies ran while one was open for 1% -> 8% of each run, Pallas kernels for 0% -> 0%
where the time goes in v1:
time: 511 us; the launch traced here: 505 us
  waiting for transfers between devices  288 us (56%)
  local copies, waits for them, and re-layouts  55.7 us (11%)
  blocking collectives  54.9 us (11%)
  other arithmetic  52.9 us (10%)
  matrix products  28.9 us (6%)
  between operations  18 us (4%)
  Pallas kernels  6.35 us (1%)
    reduce_scatter x1, waiting for transfers between devices, on_device_rows(): lax.psum_scatter(grads_by_owner((gw_qkv, gw_out, gw_in, gw_out2)).reshape...  161 us
    all_gather x1, waiting for transfers between devices, on_device_rows(): gathered = lax.all_gather(piece, ('shard', 'rep'), axis=0, tiled=True)  82.8 us
    all_gather x1, waiting for transfers between devices, on_device_rows(): new_params = lax.all_gather(upd_params, 'rep', axis=0, tiled=True)  44.2 us
    psum x1, blocking collectives, on_device_rows(): lax.psum(vec_grads.astype(jnp.bfloat16).astype(jnp.float32), ('shard', 'r...  39.9 us
    concatenate x1, other arithmetic, pieces_of(): jnp.concatenate([jnp.concatenate([second[:, 96 + 48 * j:144 + 48 * j].res...  33.3 us
    unnamed x150, local copies, waits for them, and re-layouts  32.5 us
    all_gather x1, blocking collectives, on_device_rows(): lax.all_gather(shard_vectors(params, shard).astype(jnp.bfloat16), 'shard'...  14.9 us
  transfers between devices with their start and end apart: 4, of which 3 were waited for; matrix products, arithmetic and copies ran while one was open for 8% of the time, Pallas kernels for 0%

profile of v1, /device:TPU:0, one launch (start us, length us, event | category | flops | bytes accessed | tf_op | source)
XLA Modules:
  0.0 504.8 jit_solution(17649494349353487721)
XLA Ops:
  7.8 2.8 shard_map.128
  15.6 14.9 %all_gather.13 = bf16[4,4,768]{2,1,0:T(4,128)(2,1)S(1)} all-gather(bf16[1,4,768]{2,1,0:T(4,128)(2,1)S(1)} %pad_maximum_fusion.16), channel_id=1, replica_groups=mesh['rep'=8,'shard'=4] {'shard'}, dimensions={0}, use_global_device_ids=true | all-gather | bytes 30720 | tf_op jit(solution)/shard_map/all_gather | solution.py:555
  34.6 82.8 %all-gather.5.cloned.1.call-done = bf16[9216,768]{1,0:T(8,128)(2,1)} async-done(((bf16[288,768]{1,0:T(8,128)(2,1)}), bf16[9216,768]{1,0:T(8,128)(2,1)}) %all-gather.5.cloned.1.call-update) | async-done | bytes 14155792 | tf_op jit(solution)/shard_map/all_gather | solution.py:556
  117.4 7.4 %fusion.77 = (bf16[2304,768]{1,0:T(8,128)(2,1)S(1)}, bf16[2304,768]{1,0:T(8,128)(2,1)}, bf16[2304,768]{1,0:T(8,128)(2,1)S(1)}, bf16[2304,768]{1,0:T(8,128)(2,1)S(1)}) fusion(bf16[9216,768]{1,0:T(8,128)(2,1)} %all-gather.5.cloned.1.call-done), kind=kLoop, calls=%fused_computation.163 | loop fusion | bytes 28311552 | tf_op jit(solution)/shard_map/slice | solution.py:500
  125.9 1.4 fusion.83
  127.4 1.5 fusion.82
  130.9 1.7 convolution_add_fusion
  132.7 1.7 copy.31
  137.5 1.4 multiply_reduce_fusion
  141.5 33.3 %maximum_maximum_fusion = bf16[768,3072]{1,0:T(8,128)(2,1)S(1)} fusion(bf16[384,768]{1,0:T(8,128)(2,1)S(1)} %bitcast.119, bf16[384,768]{1,0:T(8,128)(2,1)S(1)} %bitcast.123, bf16[384,768]{1,0:T(8,128)(2,1)S(1)} %bitcast.120, bf16[384,768]{1,0:T(8,128)(2,1)S(1)} %bitcast.124, bf16[384,768]{1,0:T(8,128)(2,1)S(1)} %bitcast.121, ...), kind=kLoop, calls=%fused_computation.4 | loop fusion | flops 37748736 | bytes 9437184 | tf_op jit(solution)/shard_map/concatenate | solution.py:505
  175.8 1.5 convolution_convert_fusion
  177.3 2.2 copy-done.2
  183.9 1.7 copy-done.5
  186.0 3.9 fusion.86
  189.8 1.5 convolution_convert_fusion.1
  193.4 1.7 slice-done.1
  195.1 5.2 %pad_maximum_fusion = bf16[4,8,288,768]{3,2,1,0:T(8,128)(2,1)} fusion(bf16[1,8,288,768]{3,2,1,0:T(8,128)(2,1)S(1)} %bitcast.97, bf16[1,8,288,768]{3,2,1,0:T(8,128)(2,1)S(1)} %bitcast.110, bf16[1,8,288,768]{3,2,1,0:T(8,128)(2,1)S(1)} %bitcast.109, bf16[1,8,288,768]{3,2,1,0:T(8,128)(2,1)S(1)} %maximum_bitcast_fusion), kind=kLoop, calls=%fused_computation | loop fusion | flops 21233664 | bytes 28311552 | tf_op jit(solution)/shard_map/stack | solution.py:546
  200.4 160.9 %reduce-scatter.2.cloned.1.call-done = bf16[288,768]{1,0:T(8,128)(2,1)} async-done(((bf16[9216,768]{1,0:T(8,128)(2,1)}), bf16[288,768]{1,0:T(8,128)(2,1)}) %reduce-scatter.2.cloned.1.call-update) | async-done | bytes 442384 | tf_op jit(solution)/shard_map/reduce_scatter | solution.py:562
  361.4 1.5 fusion.14
  363.6 4.4 fusion.45
  368.1 3.5 fusion.40
  371.6 1.7 dynamic-update-slice.4
  374.7 1.4 dynamic-update-slice.6
  378.8 2.1 fusion.48
  390.0 39.9 %psum.7 = f32[4,4,768]{2,1,0:T(4,128)S(1)} all-reduce(f32[4,4,768]{2,1,0:T(4,128)S(1)} %reshape.541), channel_id=1, replica_groups=mesh['rep'=8,'shard'=4] {'shard','rep'}, use_global_device_ids=true, to_apply=%region_18.19 | all-reduce | flops 12288 | bytes 98304 | tf_op jit(solution)/shard_map/psum | solution.py:570
  429.9 2.0 copy-done
  431.9 3.5 shard_map.129
  435.5 3.6 multiply_subtract_fusion
  439.1 4.9 reshape.550
  444.0 3.3 fusion.12
  448.5 44.2 %all-gather.9.cloned.1.call-done = f32[8,1,221568]{2,1,0:T(1,128)} async-done(((f32[1,1,221568]{2,1,0:T(1,128)}), f32[8,1,221568]{2,1,0:T(1,128)}) %all-gather.9.cloned.1.call-update) | async-done | bytes 7090192 | tf_op jit(solution)/shard_map/all_gather | solution.py:582
  492.6 5.2 %copy.62 = f32[1772544]{0:T(1024)} copy(f32[1772544]{0:T(1024)} %bitcast.108) | data formatting | bytes 14180352
  (224 shorter events, 38.0 us)
Async XLA Ops:
  7.2 110.2 %all-gather.5.cloned.1.call-start = ((), (), s32[]{:S(2)}) async-start(), calls=%async_computation.1 | async-start | bytes 14598144 | tf_op jit(solution)/shard_map/all_gather | solution.py:556
  7.8 23.3 %copy-start.64 = (s32[128]{0:T(128)S(1)}, s32[128]{0:T(128)}, u32[]{:S(2)}) copy-start(s32[128]{0:T(128)} %param.16) | copy-start | bytes 1540
  7.8 24.5 %copy-start.3 = (bf16[128,768]{1,0:T(8,128)(2,1)S(1)}, bf16[128,768]{1,0:T(8,128)(2,1)}, u32[]{:S(2)}) copy-start(bf16[128,768]{1,0:T(8,128)(2,1)} %param.15) | copy-start | bytes 589828
  10.7 350.6 %reduce-scatter.2.cloned.1.call-start = ((), (), s32[]{:S(2)}) async-start(), calls=%async_computation.2 | async-start | bytes 14598144 | tf_op jit(solution)/shard_map/reduce_scatter | solution.py:562
  32.3 96.9 %copy-start.49 = (f32[768]{0:T(1024)}, f32[768]{0:T(1024)S(1)}, u32[]{:S(2)}) copy-start(f32[768]{0:T(1024)S(1)} %get-tuple-element.63) | copy-start | bytes 9220
  32.3 96.9 %copy-start.58 = (f32[768]{0:T(1024)}, f32[768]{0:T(1024)S(1)}, u32[]{:S(2)}) copy-start(f32[768]{0:T(1024)S(1)} %get-tuple-element.62) | copy-start | bytes 9220
  32.4 96.8 %copy-start.53 = (f32[128]{0:T(128)}, f32[128]{0:T(128)S(1)}, u32[]{:S(2)}) copy-start(f32[128]{0:T(128)S(1)} %broadcast_multiply_fusion.5) | copy-start | bytes 1540
  33.2 96.0 %copy-start.60 = (f32[128]{0:T(128)}, f32[128]{0:T(128)S(1)}, u32[]{:S(2)}) copy-start(f32[128]{0:T(128)S(1)} %add_rsqrt_fusion) | copy-start | bytes 1540
  34.0 100.5 %copy-start.47 = (f32[128,8]{0,1:T(8,128)}, f32[128,8]{0,1:T(8,128)S(1)}, u32[]{:S(2)}) copy-start(f32[128,8]{0,1:T(8,128)S(1)} %get-tuple-element.118) | copy-start | bytes 12292
  137.4 4.0 copy-start.10
  137.4 4.0 copy-start.11
  137.4 4.0 copy-start.12
  137.4 4.0 copy-start.13
  137.5 4.0 copy-start.14
  137.5 4.0 copy-start.15
  137.5 4.0 copy-start.16
  139.0 40.6 %copy-start.31 = (bf16[12,64,128]{2,1,0:T(8,128)(2,1)}, bf16[12,64,128]{2,1,0:T(8,128)(2,1)S(1)}, u32[]{:S(2)}) copy-start(bf16[12,64,128]{2,1,0:T(8,128)(2,1)S(1)} %get-tuple-element.126) | copy-start | bytes 589828
  141.1 38.4 %copy-start.20 = (f32[128,12,64]{0,2,1:T(8,128)}, f32[128,12,64]{0,2,1:T(8,128)S(1)}, u32[]{:S(2)}) copy-start(f32[128,12,64]{0,2,1:T(8,128)S(1)} %convolution_bitcast_fusion.1) | copy-start | bytes 1179652
  141.4 38.1 %copy-start.21 = (f32[128,12,64]{0,2,1:T(8,128)}, f32[128,12,64]{0,2,1:T(8,128)S(1)}, u32[]{:S(2)}) copy-start(f32[128,12,64]{0,2,1:T(8,128)S(1)} %convolution_bitcast_fusion.2) | copy-start | bytes 1179652
  141.5 33.4 %copy-start.37 = (f32[768]{0:T(1024)S(1)}, f32[768]{0:T(1024)}, u32[]{:S(2)}) copy-start(f32[768]{0:T(1024)} %get-tuple-element.60) | copy-start | bytes 9220
  141.5 33.4 %copy-start.46 = (f32[3072]{0:T(1024)S(1)}, f32[3072]{0:T(1024)}, u32[]{:S(2)}) copy-start(f32[3072]{0:T(1024)} %reshape.548) | copy-start | bytes 36868
  141.5 33.4 %copy-start.54 = (f32[128]{0:T(128)S(1)}, f32[128]{0:T(128)}, u32[]{:S(2)}) copy-start(f32[128]{0:T(128)} %copy-done.53) | copy-start | bytes 1540
  141.5 33.4 %copy-start.61 = (f32[128]{0:T(128)S(1)}, f32[128]{0:T(128)}, u32[]{:S(2)}) copy-start(f32[128]{0:T(128)} %copy-done.60) | copy-start | bytes 1540
  200.3 229.6 %all-gather.7.cloned.1.call-start = ((), (), s32[]{:S(2)}) async-start(), calls=%async_computation.3 | async-start | bytes 3981312 | tf_op jit(solution)/shard_map/all_gather | solution.py:574
  361.3 131.3 %all-gather.9.cloned.1.call-start = ((), (), s32[]{:S(2)}) async-start(), calls=%async_computation.4 | async-start | bytes 7976448 | tf_op jit(solution)/shard_map/all_gather | solution.py:582
  363.6 4.4 copy-start.19
  363.6 4.4 copy-start.23
  363.6 4.4 copy-start.25
  363.6 4.4 copy-start.27
  368.0 6.6 %copy-start.52 = (bf16[2304]{0:T(1024)(128)(2,1)S(1)}, bf16[2304]{0:T(1024)(128)(2,1)}, u32[]{:S(2)}) copy-start(bf16[2304]{0:T(1024)(128)(2,1)} %reduce_sum.148) | copy-start | bytes 13828
  368.1 10.7 %copy-start.51 = (f32[768]{0:T(1024)S(1)}, f32[768]{0:T(1024)}, u32[]{:S(2)}) copy-start(f32[768]{0:T(1024)} %copy-done.49) | copy-start | bytes 9220
  435.5 8.5 %copy-start.65 = (f32[768]{0:T(1024)S(1)}, f32[768]{0:T(1024)}, u32[]{:S(2)}) copy-start(f32[768]{0:T(1024)} %get-tuple-element.59) | copy-start | bytes 9220
  (42 other events, 97.3 us)
Sparse Core Ops, SparseCore 0:
  11.5 105.8 all-gather.4
  200.5 160.8 reduce-scatter.1
  363.2 32.8 all-gather.6
  444.1 48.4 all-gather.8

commit v2 on v1

--- a/solution.py
+++ b/solution.py
@@ -6,6 +6,7 @@
 from jax import lax
 from jax.experimental import pallas as pl
 from jax.experimental.pallas import tpu as pltpu
+from jax.sharding import Mesh
 from jax.sharding import PartitionSpec as P
 
 D = 768
@@ -398,43 +399,98 @@
 VECTOR_ROWS = ((0, 1, 2306, 2307), (0, 769, 770, 771), (1536, 1537, 1538, 1539), (2304, 2305, 2306, 2307))
 
 
+PLANE = ("y", "x", "core")
+EVERY = PLANE + ("z",)
+HOPS = (1, 2, 3, 0)
+
+
+def plane_permute(value, flips):
+    return lax.ppermute(value, PLANE, [(i, i ^ flips[i % 2]) for i in range(REPS)])
+
+
+def first_cross(value):
+    return plane_permute(value, (2, 4))
+
+
+def second_cross(value):
+    return plane_permute(value, (4, 2))
+
+
+def core_cross(value):
+    return plane_permute(value, (1, 1))
+
+
+def ring_step(value):
+    return lax.ppermute(value, "z", [(i, (i + 1) % SHARDS) for i in range(SHARDS)])
+
+
+def flips_of(rep):
+    core = rep % 2
+    first = 2 + 2 * core
+    return (0, first, 6 - first, 6)
+
+
+def spread_in_plane(piece):
+    first = first_cross(piece)
+    second = second_cross(piece)
+    both = second_cross(first)
+    mine = [piece, first, second, both]
+    return mine + [core_cross(value) for value in mine]
+
+
+def spread_ids(rep):
+    other = rep ^ 1
+    return [rep ^ flip for flip in flips_of(rep)] + [other ^ flip for flip in flips_of(other)]
+
+
 def pack_kernel(where, flat_ref, out_ref, held, sems):
     shard = where[0]
-    rep = where[1]
     for z in range(SHARDS):
 
         @pl.when(shard == z)
         def _(z=z):
-            copies = []
-            at = 0
-            for turn, (first, step, _, _, _) in enumerate(PARTS[z]):
-                lead = first % 8
-                count = step + (8 if lead else 0)
-                begin = pl.multiple_of(first - lead + step * rep, 8)
-                copies.append(
-                    pltpu.make_async_copy(
-                        flat_ref.at[pl.ds(begin, count)], held.at[pl.ds(at, count)], sems.at[turn]
+            def start(turn, slot):
+                copies = []
+                at = 0
+                rep = where[1 + turn]
+                for part, (first, step, _, _, _) in enumerate(PARTS[z]):
+                    lead = first % 8
+                    count = step + (8 if lead else 0)
+                    begin = pl.multiple_of(first - lead + step * rep, 8)
+                    copy = pltpu.make_async_copy(
+                        flat_ref.at[pl.ds(begin, count)],
+                        held.at[slot, pl.ds(at, count)],
+                        sems.at[slot, part],
                     )
-                )
-                at += count
-            for copy in copies:
-                copy.start()
-            at = 0
-            for copy, (first, step, rows, blocks, place) in zip(copies, PARTS[z]):
-                copy.wait()
-                lead = first % 8
-                stride = 6 * blocks
-                for block in range(blocks):
-                    for col in range(6):
-                        got = held[pl.ds(at + lead + 6 * block + col, rows, stride=stride), :]
-                        out_ref[
-                            place + rows * block : place + rows * (block + 1),
-                            LANES * col : LANES * (col + 1),
-                        ] = got.astype(jnp.bfloat16)
-                at += step + (8 if lead else 0)
-
-
-def pack_piece(params, shard, rep):
+                    copy.start()
+                    copies.append(copy)
+                    at += count
+                return copies
+
+            turns = out_ref.shape[0]
+            running = start(0, 0)
+            for turn in range(turns):
+                slot = turn % 2
+                following = start(turn + 1, 1 - slot) if turn + 1 < turns else None
+                rep = where[1 + turn] if turns > 1 else 0
+                at = 0
+                for copy, (first, step, rows, blocks, place) in zip(running, PARTS[z]):
+                    copy.wait()
+                    lead = first % 8
+                    for block in range(blocks):
+                        for col in range(6):
+                            begin = at + lead + 6 * block + col
+                            got = held[slot, pl.ds(begin, rows, stride=6 * blocks), :]
+                            out_ref[
+                                rep,
+                                place + rows * block : place + rows * (block + 1),
+                                LANES * col : LANES * (col + 1),
+                            ] = got.astype(jnp.bfloat16)
+                    at += step + (8 if lead else 0)
+                running = following
+
+
+def pack_pieces(params, shard, reps):
     return pl.pallas_call(
         pack_kernel,
         grid_spec=pltpu.PrefetchScalarGridSpec(
@@ -442,15 +498,75 @@
             in_specs=[pl.BlockSpec(memory_space=pltpu.HBM)],
             out_specs=pl.BlockSpec(memory_space=pltpu.VMEM),
             scratch_shapes=[
-                pltpu.VMEM((MOVED + 16, LANES), jnp.float32),
-                pltpu.SemaphoreType.DMA((2,)),
+                pltpu.VMEM((2, MOVED + 16, LANES), jnp.float32),
+                pltpu.SemaphoreType.DMA((2, 2)),
             ],
         ),
-        out_shape=jax.ShapeDtypeStruct((PIECE, D), jnp.bfloat16),
-    )(jnp.stack([shard, rep]), params.reshape(FLAT_ROWS, LANES))
-
-
-def unpack_kernel(factor, where, grad_ref, vec_ref, out_ref):
+        out_shape=jax.ShapeDtypeStruct((len(reps), PIECE, D), jnp.bfloat16),
+        compiler_params=pltpu.CompilerParams(vmem_limit_bytes=16 * 2**20),
+    )(jnp.stack([shard] + reps), params.reshape(FLAT_ROWS, LANES))
+
+
+def place_kernel(where, *refs):
+    out_ref, sem = refs[-2:]
+    copies = []
+    for turn, ref in enumerate(refs[:-2]):
+        copies.append(pltpu.make_async_copy(ref, out_ref.at[where[turn]], sem.at[turn]))
+    for copy in copies:
+        copy.start()
+    for copy in copies:
+        copy.wait()
+
+
+def place_pieces(blocks, ids, slots):
+    return pl.pallas_call(
+        place_kernel,
+        grid_spec=pltpu.PrefetchScalarGridSpec(
+            num_scalar_prefetch=1,
+            in_specs=[pl.BlockSpec(memory_space=pltpu.HBM)] * len(blocks),
+            out_specs=pl.BlockSpec(memory_space=pltpu.HBM),
+            scratch_shapes=[pltpu.SemaphoreType.DMA((len(blocks),))],
+        ),
+        out_shape=jax.ShapeDtypeStruct((slots,) + blocks[0].shape, blocks[0].dtype),
+    )(jnp.stack(ids), *blocks)
+
+
+def order_kernel(where, in_ref, out_ref, sem):
+    copies = []
+    for turn in range(out_ref.shape[0]):
+        copies.append(
+            pltpu.make_async_copy(in_ref.at[where[turn]], out_ref.at[turn], sem.at[turn])
+        )
+    for copy in copies:
+        copy.start()
+    for copy in copies:
+        copy.wait()
+
+
+def order_pieces(pieces, ids):
+    return pl.pallas_call(
+        order_kernel,
+        grid_spec=pltpu.PrefetchScalarGridSpec(
+            num_scalar_prefetch=1,
+            in_specs=[pl.BlockSpec(memory_space=pltpu.HBM)],
+            out_specs=pl.BlockSpec(memory_space=pltpu.HBM),
+            scratch_shapes=[pltpu.SemaphoreType.DMA((len(ids),))],
+        ),
+        out_shape=jax.ShapeDtypeStruct((len(ids),) + pieces.shape[1:], pieces.dtype),
+    )(jnp.stack(ids), pieces)
+
+
+def unpack_kernel(factor, where, *refs):
+    vec_ref, out_ref, held, sems = refs[REPS:]
+    copies = []
+    for turn in range(REPS):
+        copies.append(
+            pltpu.make_async_copy(refs[turn], held.at[where[1 + turn]], sems.at[turn])
+        )
+    for copy in copies:
+        copy.start()
+    for copy in copies:
+        copy.wait()
     shard = where[0]
     for z in range(SHARDS):
 
@@ -461,34 +577,78 @@
                     out_ref[6 * row + col : 6 * row + col + 1, :] = (
                         vec_ref[slot : slot + 1, LANES * col : LANES * (col + 1)] * factor
                     )
-            for rep in range(REPS):
+
+            @pl.loop(0, REPS)
+            def _(rep):
                 for first, step, rows, blocks, place in PARTS[z]:
                     for block in range(blocks):
                         for col in range(6):
-                            got = grad_ref[
+                            got = held[
                                 rep,
                                 place + rows * block : place + rows * (block + 1),
                                 LANES * col : LANES * (col + 1),
                             ]
-                            out_ref[
-                                pl.ds(
-                                    first + step * rep + 6 * block + col, rows, stride=6 * blocks
-                                ),
-                                :,
-                            ] = got.astype(jnp.float32) * factor
-
-
-def unpack_grads(grads, vectors, shard, factor):
+                            begin = first + step * rep + 6 * block + col
+                            out_ref[pl.ds(begin, rows, stride=6 * blocks), :] = (
+                                got.astype(jnp.float32) * factor
+                            )
+
+
+def unpack_grads(blocks, ids, vectors, shard, factor):
     return pl.pallas_call(
         functools.partial(unpack_kernel, factor),
         grid_spec=pltpu.PrefetchScalarGridSpec(
             num_scalar_prefetch=1,
-            in_specs=[pl.BlockSpec(memory_space=pltpu.VMEM)] * 2,
+            in_specs=[pl.BlockSpec(memory_space=pltpu.HBM)] * REPS
+            + [pl.BlockSpec(memory_space=pltpu.VMEM)],
             out_specs=pl.BlockSpec(memory_space=pltpu.VMEM),
+            scratch_shapes=[
+                pltpu.VMEM((REPS, PIECE, D), jnp.bfloat16),
+                pltpu.SemaphoreType.DMA((REPS,)),
+            ],
         ),
         out_shape=jax.ShapeDtypeStruct((FLAT_ROWS, LANES), jnp.float32),
         compiler_params=pltpu.CompilerParams(vmem_limit_bytes=32 * 2**20),
-    )(jnp.stack([shard]), grads, vectors)
+    )(jnp.stack([shard] + ids), *blocks, vectors)
+
+
+def gather_matrices(params, shard, rep):
+    piece = pack_pieces(params, shard, [rep])[0]
+    own = pack_pieces(params, shard, [rep * 0 + turn for turn in range(REPS)])
+    reps = spread_ids(rep)
+    blocks, ids = [], []
+    for hop in range(1, SHARDS):
+        piece = ring_step(piece)
+        owner = (shard + SHARDS - hop) % SHARDS
+        blocks += spread_in_plane(piece)
+        ids += [owner * REPS + which for which in reps]
+    blocks += [own[turn] for turn in range(REPS)]
+    ids += [shard * REPS + turn for turn in range(REPS)]
+    return place_pieces(blocks, ids, SHARDS * REPS)
+
+
+def slots_of(shard, rep):
+    ids = []
+    for base in (rep ^ 1, rep):
+        own, first, second, both = (base ^ flip for flip in flips_of(base))
+        for hop in HOPS:
+            owner = (shard + SHARDS - hop) % SHARDS
+            ids += [owner * REPS + which for which in (first, both, own, second)]
+    return ids
+
+
+def scatter_sums(ordered):
+    sent, kept = ordered[0], ordered[1]
+    carried = None
+    for turn in range(SHARDS):
+        chip = kept[turn] + core_cross(sent[turn])
+        pair = chip[2:4] + first_cross(chip[0:2])
+        total = pair[0] + second_cross(pair[1])
+        if carried is not None:
+            total = total + carried
+        if turn < SHARDS - 1:
+            carried = ring_step(total)
+    return total
 
 
 def shard_vectors(params, shard):
@@ -549,58 +709,47 @@
 
 
 def on_device_rows(tokens, segment_ids, cotangent, params, moment_one, moment_two):
-    shard = lax.axis_index("shard")
-    rep = lax.axis_index("rep")
-    piece = pack_piece(params, shard, rep)
-    vectors = lax.all_gather(shard_vectors(params, shard).astype(jnp.bfloat16), "shard", axis=0)
-    gathered = lax.all_gather(piece, ("shard", "rep"), axis=0, tiled=True)
-    gathered = gathered.reshape(SHARDS, REPS, PIECE, D)
+    shard = lax.axis_index("z")
+    rep = lax.axis_index(PLANE)
+    vectors = lax.all_gather(shard_vectors(params, shard).astype(jnp.bfloat16), "z", axis=0)
+    gathered = gather_matrices(params, shard, rep).reshape(SHARDS, REPS, PIECE, D)
     pieces = pieces_of(gathered, vectors)
     output, saved = layer_forward(tokens, segment_ids, pieces)
     grad_input, parts = layer_backward(cotangent, segment_ids, pieces, saved)
     (g1, s1, gw_qkv, gb_qkv, gw_out, gb_out, g2, s2, gw_in, gb_in, gw_out2, gb_out2) = parts
-    owned = lax.psum_scatter(
-        grads_by_owner((gw_qkv, gw_out, gw_in, gw_out2)).reshape(SHARDS * REPS * PIECE, D),
-        ("shard", "rep"),
-        scatter_dimension=0,
-        tiled=True,
-    )
+    by_owner = grads_by_owner((gw_qkv, gw_out, gw_in, gw_out2))
+    ordered = order_pieces(by_owner.reshape(SHARDS * REPS, PIECE, D), slots_of(shard, rep))
+    owned = scatter_sums(ordered.reshape(2, SHARDS, 4, PIECE, D))
     zero = jnp.zeros((3 * D,), jnp.float32)
     vec_grads = jnp.concatenate([g1, s1, gb_qkv, gb_out, g2, s2, gb_in, gb_out2, zero])
-    vec_grads = lax.psum(
-        vec_grads.astype(jnp.bfloat16).astype(jnp.float32), ("shard", "rep")
-    ).reshape(SHARDS, 4, D)
-    own_vectors = lax.dynamic_index_in_dim(vec_grads, shard, 0, keepdims=False)
-    grads = lax.all_gather(owned, "rep", axis=0, tiled=True).reshape(REPS, PIECE, D)
-    tokens_all = tokens.shape[0] * lax.axis_size("rep") * lax.axis_size("shard")
-    grad_params = unpack_grads(grads, own_vectors, shard, 1.0 / math.sqrt(tokens_all)).reshape(-1)
+    vec_grads = lax.psum(vec_grads.astype(jnp.bfloat16).astype(jnp.float32), EVERY)
+    own_vectors = lax.dynamic_index_in_dim(
+        vec_grads.reshape(SHARDS, 4, D), shard, 0, keepdims=False
+    )
+    tokens_all = tokens.shape[0] * lax.axis_size(EVERY)
+    grad_params = unpack_grads(
+        spread_in_plane(owned), spread_ids(rep), own_vectors, shard, 1.0 / math.sqrt(tokens_all)
+    ).reshape(-1)
     width = moment_one.shape[0]
     begin = rep * width
     param_share = lax.dynamic_slice_in_dim(params, begin, width)
     grad_share = lax.dynamic_slice_in_dim(grad_params, begin, width)
     upd_params, upd_first, upd_second = adam_update(param_share, moment_one, moment_two, grad_share)
-    new_params = lax.all_gather(upd_params, "rep", axis=0, tiled=True)
+    new_params = lax.all_gather(upd_params, PLANE, axis=0, tiled=True)
     return (output, grad_input, grad_params, new_params, upd_first, upd_second)
 
 
 def solution(mesh):
-    in_specs = (
-        P(("rep", "shard"), None),
-        P(("rep", "shard")),
-        P(("rep", "shard"), None),
-        P("shard"),
-        P(("shard", "rep")),
-        P(("shard", "rep")),
-    )
-    out_specs = (
-        P(("rep", "shard"), None),
-        P(("rep", "shard"), None),
-        P("shard"),
-        P("shard"),
-        P(("shard", "rep")),
-        P(("shard", "rep")),
-    )
     in_rows = mesh.shape["rep"] == REPS and mesh.shape["shard"] == SHARDS
-    return jax.shard_map(
-        on_device_rows if in_rows else on_device, mesh=mesh, in_specs=in_specs, out_specs=out_specs, check_vma=False
-    )
+    if in_rows:
+        rep, shard = PLANE, "z"
+        mesh = Mesh(mesh.devices.reshape(2, 2, 2, SHARDS), EVERY)
+        body = on_device_rows
+    else:
+        rep, shard = ("rep",), "shard"
+        body = on_device
+    rows = rep + (shard,)
+    owner = (shard,) + rep
+    in_specs = (P(rows, None), P(rows), P(rows, None), P(shard), P(owner), P(owner))
+    out_specs = (P(rows, None), P(rows, None), P(shard), P(shard), P(owner), P(owner))
+    return jax.shard_map(body, mesh=mesh, in_specs=in_specs, out_specs=out_specs, check_vma=False)

time: 511 us -> 1300 us (2.54)
  Pallas kernels: 6.35 us -> 872 us
  waiting for transfers between devices: 288 us -> 165 us
  starting transfers between devices: 0.16 us -> 29.6 us
    pallas_call x1 -> x4, Pallas kernels: 2.83 us -> 866 us  [the longest x1 431 us: place_pieces(): pl.pallas_call(place_kernel, grid_spec=pltpu.PrefetchScalarGridSpec(num_s...]
    reduce_scatter x1 -> x0, waiting for transfers between devices: 161 us -> none  [on_device_rows(): lax.psum_scatter(grads_by_owner((gw_qkv, gw_out, gw_in, gw_out2)).reshape...]
    ppermute x0 -> x46, waiting for transfers between devices: none -> 120 us  [the longest x40 91 us: plane_permute(): lax.ppermute(value, PLANE, [(i, i ^ flips[i % 2]) for i in range(REPS)])]
    all_gather x3 -> x1, waiting for transfers between devices: 127 us -> 45.9 us  [on_device_rows(): new_params = lax.all_gather(upd_params, PLANE, axis=0, tiled=True)]
    ppermute x0 -> x46, starting transfers between devices: none -> 29.5 us  [the longest x40 25.5 us: plane_permute(): lax.ppermute(value, PLANE, [(i, i ^ flips[i % 2]) for i in range(REPS)])]
    unnamed x150 -> x172, local copies, waits for them, and re-layouts: 32.5 us -> 31.2 us
  transfers between devices with their start and end apart: 4 -> 47, of which waited for: 3 -> 21; matrix products, arithmetic and copies ran while one was open for 8% -> 3% of each run, Pallas kernels for 0% -> 0%
where the time goes in v2:
time: 1300 us; the launch traced here: 1290 us
  Pallas kernels  872 us (67%)
  waiting for transfers between devices  165 us (13%)
  local copies, waits for them, and re-layouts  63.6 us (5%)
  other arithmetic  62.1 us (5%)
  blocking collectives  52.3 us (4%)
  starting transfers between devices  29.6 us (2%)
  matrix products  27.8 us (2%)
  between operations  18.5 us (1%)
    pallas_call x1, Pallas kernels, place_pieces(): pl.pallas_call(place_kernel, grid_spec=pltpu.PrefetchScalarGridSpec(num_s...  431 us
    pallas_call x1, Pallas kernels, order_pieces(): pl.pallas_call(order_kernel, grid_spec=pltpu.PrefetchScalarGridSpec(num_s...  431 us
    ppermute x40, waiting for transfers between devices, plane_permute(): lax.ppermute(value, PLANE, [(i, i ^ flips[i % 2]) for i in range(REPS)])  91 us
    all_gather x1, waiting for transfers between devices, on_device_rows(): new_params = lax.all_gather(upd_params, PLANE, axis=0, tiled=True)  45.9 us
    psum x1, blocking collectives, on_device_rows(): lax.psum(vec_grads.astype(jnp.bfloat16).astype(jnp.float32), EVERY)  37.8 us
    concatenate x1, other arithmetic, pieces_of(): jnp.concatenate([jnp.concatenate([second[:, 96 + 48 * j:144 + 48 * j].res...  33.5 us
    unnamed x172, local copies, waits for them, and re-layouts  31.2 us
    ppermute x6, waiting for transfers between devices, ring_step(): lax.ppermute(value, 'z', [(i, (i + 1) % SHARDS) for i in range(SHARDS)])  28.6 us
  transfers between devices with their start and end apart: 47, of which 21 were waited for; matrix products, arithmetic and copies ran while one was open for 3% of the time, Pallas kernels for 0%

profile of v2, /device:TPU:0, one launch (start us, length us, event | category | flops | bytes accessed | tf_op | source)
XLA Modules:
  0.0 1291.2 jit_solution(671077759230174225)
XLA Ops:
  19.2 14.5 %all_gather.7 = bf16[4,4,768]{2,1,0:T(4,128)(2,1)S(1)} all-gather(bf16[1,4,768]{2,1,0:T(4,128)(2,1)S(1)} %pad_maximum_fusion.16), channel_id=1, replica_groups=mesh['y'=2,'x'=2,'core'=2,'z'=4] {'z'}, dimensions={0}, use_global_device_ids=true | all-gather | bytes 30720 | tf_op jit(solution)/shard_map/all_gather | solution.py:714
  39.0 7.3 collective-permute-done.8.refs_8_
  50.1 6.7 collective-permute-done.16.refs_16_
  64.6 3.2 collective-permute-done.3.refs_3_
  68.7 5.2 collective-permute-done.17.refs_17_
  79.4 4.7 collective-permute-done.19.refs_19_
  95.1 430.9 %shard_map.130 = bf16[32,288,768]{2,1,0:T(8,128)(2,1)} custom-call(s32[32]{0:T(128)} %stack.265.where, bf16[288,768]{1,0:T(8,128)(2,1)} %copy-done.40, bf16[288,768]{1,0:T(8,128)(2,1)} %copy-done.44, bf16[288,768]{1,0:T(8,128)(2,1)} %copy-done.43, bf16[288,768]{1,0:T(8,128)(2,1)} %collective-permute-done.3.refs_3_, bf16[288,768]{1,0:T(8,128)(2,1)} %copy-done.42, ...), custom_call_target="tpu_custom_call" | custom-call | tf_op jit(solution)/shard_map/pallas_call | solution.py:522
  526.0 4.0 slice.496
  530.0 4.2 fusion.85
  534.2 4.7 fusion.84
  540.8 3.3 convolution_add_fusion
  549.6 33.5 %maximum_maximum_fusion = bf16[768,3072]{1,0:T(8,128)(2,1)S(1)} fusion(bf16[384,768]{1,0:T(8,128)(2,1)S(1)} %bitcast.208, bf16[384,768]{1,0:T(8,128)(2,1)S(1)} %bitcast.209, bf16[384,768]{1,0:T(8,128)(2,1)S(1)} %bitcast.210, bf16[384,768]{1,0:T(8,128)(2,1)S(1)} %bitcast.211, bf16[384,768]{1,0:T(8,128)(2,1)S(1)} %bitcast.212, ...), kind=kLoop, calls=%fused_computation.4 | loop fusion | flops 37748736 | bytes 9437184 | tf_op jit(solution)/shard_map/concatenate | solution.py:665
  592.6 3.9 fusion.91
  601.8 5.3 pad_maximum_fusion
  607.0 430.9 %shard_map.131 = bf16[32,288,768]{2,1,0:T(8,128)(2,1)} custom-call(s32[32]{0:T(128)} %stack.290.where, bf16[32,288,768]{2,1,0:T(8,128)(2,1)} %bitcast.188), custom_call_target="tpu_custom_call" | custom-call | tf_op jit(solution)/shard_map/pallas_call | solution.py:547
  1040.0 3.3 collective-permute-done.24
  1043.4 3.5 slice_add_fusion.3
  1055.7 5.0 slice_add_fusion.2
  1066.8 4.3 fusion.52
  1078.7 11.7 collective-permute-done.31
  1092.1 22.0 %collective-permute-done.28 = bf16[2,288,768]{2,1,0:T(8,128)(2,1)S(1)} collective-permute-done((bf16[2,288,768]{2,1,0:T(8,128)(2,1)S(1)}, bf16[2,288,768]{2,1,0:T(8,128)(2,1)S(1)}, u32[]{:S(2)}, u32[]{:S(2)}) %collective-permute-start.28) | collective-permute-done | bytes 884768 | tf_op jit(solution)/shard_map/ppermute | solution.py:408
  1116.8 5.9 collective-permute-done.29
  1122.7 5.9 collective-permute-done.37
  1132.2 8.7 collective-permute-done.38
  1143.2 10.9 collective-permute-done.39.refs_1_
  1154.8 7.6 collective-permute-done.41.refs_3_
  1175.1 37.8 %psum.7 = f32[4,4,768]{2,1,0:T(4,128)} all-reduce(f32[4,4,768]{2,1,0:T(4,128)} %reshape.559), channel_id=1, replica_groups=mesh['y'=2,'x'=2,'core'=2,'z'=4] {'y','x','core','z'}, use_global_device_ids=true, to_apply=%region_17.18 | all-reduce | flops 12288 | bytes 98304 | tf_op jit(solution)/shard_map/psum | solution.py:725
  1213.6 6.2 shard_map.132
  1219.9 3.8 multiply_subtract_fusion
  1223.7 5.1 reshape.568
  1233.0 45.9 %all-gather.3.cloned.1.call-done = f32[8,1,221568]{2,1,0:T(1,128)} async-done(((f32[1,1,221568]{2,1,0:T(1,128)}), f32[8,1,221568]{2,1,0:T(1,128)}) %all-gather.3.cloned.1.call-update) | async-done | bytes 7090192 | tf_op jit(solution)/shard_map/all_gather | solution.py:738
  1278.9 5.2 copy.62
  (353 shorter events, 117.7 us)
Async XLA Ops:
  7.2 1271.8 %all-gather.3.cloned.1.call-start = ((), (), s32[]{:S(2)}) async-start(), calls=%async_computation | async-start | bytes 7976448 | tf_op jit(solution)/shard_map/all_gather | solution.py:738
  11.2 23.8 %collective-permute-start = (bf16[288,768]{1,0:T(8,128)(2,1)S(1)}, bf16[288,768]{1,0:T(8,128)(2,1)S(1)}, u32[]{:S(2)}, u32[]{:S(2)}) collective-permute-start(bf16[288,768]{1,0:T(8,128)(2,1)S(1)} %bitcast.187), channel_id=1, source_target_pairs={{0,1},{1,2},{2,3},{3,0},{4,5},{5,6},{6,7},{7,4},{8,9},{9,10},{10,1... | collective-permute-start | bytes 1327112 | tf_op jit(solution)/shard_map/ppermute | solution.py:424
  35.1 12.6 collective-permute-start.2
  37.4 12.6 collective-permute-start.1
  46.3 11.4 collective-permute-start.12
  46.4 12.8 collective-permute-start.10
  47.7 13.1 %collective-permute-start.9 = (bf16[288,768]{1,0:T(8,128)(2,1)S(1)}, bf16[288,768]{1,0:T(8,128)(2,1)S(1)}, u32[]{:S(2)}, u32[]{:S(2)}) collective-permute-start(bf16[288,768]{1,0:T(8,128)(2,1)S(1)} %collective-permute-done.8.refs_8_), channel_id=1, source_target_pairs={{0,8},{4,20},{8,0},{12,28},{16,24},{20,4},{24,16},{28,12},{1,9},{5... | collective-permute-start | bytes 1327112 | tf_op jit(solution)/shard_map/ppermute | solution.py:408
  50.1 14.6 %collective-permute-start.5 = (bf16[288,768]{1,0:T(8,128)(2,1)S(1)}, bf16[288,768]{1,0:T(8,128)(2,1)S(1)}, u32[]{:S(2)}, u32[]{:S(2)}) collective-permute-start(bf16[288,768]{1,0:T(8,128)(2,1)S(1)} %collective-permute-done.1.refs_1_), channel_id=1, source_target_pairs={{0,4},{4,0},{8,12},{12,8},{16,20},{20,16},{24,28},{28,24},{1,5},{5... | collective-permute-start | bytes 1327112 | tf_op jit(solution)/shard_map/ppermute | solution.py:408
  60.8 13.1 %collective-permute-start.17 = (bf16[288,768]{1,0:T(8,128)(2,1)S(1)}, bf16[288,768]{1,0:T(8,128)(2,1)}, u32[]{:S(2)}, u32[]{:S(2)}) collective-permute-start(bf16[288,768]{1,0:T(8,128)(2,1)S(1)} %collective-permute-done.16.refs_16_), channel_id=1, source_target_pairs={{0,8},{4,20},{8,0},{12,28},{16,24},{20,4},{24,16},{28,12},{1,9},{5... | collective-permute-start | bytes 1327112 | tf_op jit(solution)/shard_map/ppermute | solution.py:408
  63.1 13.2 %collective-permute-start.18 = (bf16[288,768]{1,0:T(8,128)(2,1)S(1)}, bf16[288,768]{1,0:T(8,128)(2,1)}, u32[]{:S(2)}, u32[]{:S(2)}) collective-permute-start(bf16[288,768]{1,0:T(8,128)(2,1)S(1)} %collective-permute-done.16.refs_16_), channel_id=1, source_target_pairs={{0,16},{4,12},{8,24},{12,4},{16,0},{20,28},{24,8},{28,20},{1,17},{... | collective-permute-start | bytes 1327112 | tf_op jit(solution)/shard_map/ppermute | solution.py:408
  64.6 12.2 collective-permute-start.13
  67.8 11.5 collective-permute-start.11
  76.3 18.8 %collective-permute-start.7 = (bf16[288,768]{1,0:T(8,128)(2,1)}, bf16[288,768]{1,0:T(8,128)(2,1)}, u32[]{:S(2)}, u32[]{:S(2)}) collective-permute-start(bf16[288,768]{1,0:T(8,128)(2,1)} %collective-permute-done.3.refs_3_), channel_id=1, source_target_pairs={{0,4},{4,0},{8,12},{12,8},{16,20},{20,16},{24,28},{28,24},{1,5},{5... | collective-permute-start | bytes 1327112 | tf_op jit(solution)/shard_map/ppermute | solution.py:408
  76.3 18.8 %collective-permute-start.21 = (bf16[288,768]{1,0:T(8,128)(2,1)}, bf16[288,768]{1,0:T(8,128)(2,1)}, u32[]{:S(2)}, u32[]{:S(2)}) collective-permute-start(bf16[288,768]{1,0:T(8,128)(2,1)} %collective-permute-done.17.refs_17_), channel_id=1, source_target_pairs={{0,4},{4,0},{8,12},{12,8},{16,20},{20,16},{24,28},{28,24},{1,5},{5... | collective-permute-start | bytes 1327112 | tf_op jit(solution)/shard_map/ppermute | solution.py:408
  76.8 18.3 %collective-permute-start.22 = (bf16[288,768]{1,0:T(8,128)(2,1)}, bf16[288,768]{1,0:T(8,128)(2,1)}, u32[]{:S(2)}, u32[]{:S(2)}) collective-permute-start(bf16[288,768]{1,0:T(8,128)(2,1)} %collective-permute-done.18.refs_18_), channel_id=1, source_target_pairs={{0,4},{4,0},{8,12},{12,8},{16,20},{20,16},{24,28},{28,24},{1,5},{5... | collective-permute-start | bytes 1327112 | tf_op jit(solution)/shard_map/ppermute | solution.py:408
  79.3 15.7 %collective-permute-start.15 = (bf16[288,768]{1,0:T(8,128)(2,1)}, bf16[288,768]{1,0:T(8,128)(2,1)}, u32[]{:S(2)}, u32[]{:S(2)}) collective-permute-start(bf16[288,768]{1,0:T(8,128)(2,1)} %collective-permute-done.11.refs_11_), channel_id=1, source_target_pairs={{0,4},{4,0},{8,12},{12,8},{16,20},{20,16},{24,28},{28,24},{1,5},{5... | collective-permute-start | bytes 1327112 | tf_op jit(solution)/shard_map/ppermute | solution.py:408
  1062.9 13.4 %collective-permute-start.34 = (bf16[2,288,768]{2,1,0:T(8,128)(2,1)}, bf16[2,288,768]{2,1,0:T(8,128)(2,1)}, u32[]{:S(2)}, u32[]{:S(2)}) collective-permute-start(bf16[2,288,768]{2,1,0:T(8,128)(2,1)} %slice.538), channel_id=1, source_target_pairs={{0,8},{4,20},{8,0},{12,28},{16,24},{20,4},{24,16},{28,12},{1,9},{5... | collective-permute-start | bytes 2654216 | tf_op jit(solution)/shard_map/ppermute | solution.py:408
  1065.7 24.7 %collective-permute-start.31 = (bf16[2,288,768]{2,1,0:T(8,128)(2,1)S(1)}, bf16[2,288,768]{2,1,0:T(8,128)(2,1)S(1)}, u32[]{:S(2)}, u32[]{:S(2)}) collective-permute-start(bf16[2,288,768]{2,1,0:T(8,128)(2,1)S(1)} %slice.532), channel_id=1, source_target_pairs={{0,8},{4,20},{8,0},{12,28},{16,24},{20,4},{24,16},{28,12},{1,9},{5... | collective-permute-start | bytes 2654216 | tf_op jit(solution)/shard_map/ppermute | solution.py:408
  1071.2 44.7 %collective-permute-start.25 = (bf16[2,288,768]{2,1,0:T(8,128)(2,1)S(1)}, bf16[2,288,768]{2,1,0:T(8,128)(2,1)S(1)}, u32[]{:S(2)}, u32[]{:S(2)}) collective-permute-start(bf16[2,288,768]{2,1,0:T(8,128)(2,1)S(1)} %slice.520), channel_id=1, source_target_pairs={{0,8},{4,20},{8,0},{12,28},{16,24},{20,4},{24,16},{28,12},{1,9},{5... | collective-permute-start | bytes 2654216 | tf_op jit(solution)/shard_map/ppermute | solution.py:408
  1072.3 41.8 %collective-permute-start.28 = (bf16[2,288,768]{2,1,0:T(8,128)(2,1)S(1)}, bf16[2,288,768]{2,1,0:T(8,128)(2,1)S(1)}, u32[]{:S(2)}, u32[]{:S(2)}) collective-permute-start(bf16[2,288,768]{2,1,0:T(8,128)(2,1)S(1)} %slice.526), channel_id=1, source_target_pairs={{0,8},{4,20},{8,0},{12,28},{16,24},{20,4},{24,16},{28,12},{1,9},{5... | collective-permute-start | bytes 2654216 | tf_op jit(solution)/shard_map/ppermute | solution.py:408
  1077.6 14.1 %collective-permute-start.35 = (bf16[288,768]{1,0:T(8,128)(2,1)S(1)}, bf16[288,768]{1,0:T(8,128)(2,1)S(1)}, u32[]{:S(2)}, u32[]{:S(2)}) collective-permute-start(bf16[288,768]{1,0:T(8,128)(2,1)S(1)} %slice_bitcast_fusion), channel_id=1, source_target_pairs={{0,16},{4,12},{8,24},{12,4},{16,0},{20,28},{24,8},{28,20},{1,17},{... | collective-permute-start | bytes 1327112 | tf_op jit(solution)/shard_map/ppermute | solution.py:408
  1090.6 24.8 %collective-permute-start.32 = (bf16[288,768]{1,0:T(8,128)(2,1)S(1)}, bf16[288,768]{1,0:T(8,128)(2,1)S(1)}, u32[]{:S(2)}, u32[]{:S(2)}) collective-permute-start(bf16[288,768]{1,0:T(8,128)(2,1)S(1)} %slice_bitcast_fusion.2), channel_id=1, source_target_pairs={{0,16},{4,12},{8,24},{12,4},{16,0},{20,28},{24,8},{28,20},{1,17},{... | collective-permute-start | bytes 1327112 | tf_op jit(solution)/shard_map/ppermute | solution.py:408
  1091.7 23.7 %collective-permute-start.36 = (bf16[288,768]{1,0:T(8,128)(2,1)S(1)}, bf16[288,768]{1,0:T(8,128)(2,1)S(1)}, u32[]{:S(2)}, u32[]{:S(2)}) collective-permute-start(bf16[288,768]{1,0:T(8,128)(2,1)S(1)} %fusion.28), channel_id=1, source_target_pairs={{0,1},{1,2},{2,3},{3,0},{4,5},{5,6},{6,7},{7,4},{8,9},{9,10},{10,1... | collective-permute-start | bytes 1327112 | tf_op jit(solution)/shard_map/ppermute | solution.py:424
  1115.5 13.1 %collective-permute-start.37 = (bf16[288,768]{1,0:T(8,128)(2,1)S(1)}, bf16[288,768]{1,0:T(8,128)(2,1)S(1)}, u32[]{:S(2)}, u32[]{:S(2)}) collective-permute-start(bf16[288,768]{1,0:T(8,128)(2,1)S(1)} %fusion.30), channel_id=1, source_target_pairs={{0,1},{1,2},{2,3},{3,0},{4,5},{5,6},{6,7},{7,4},{8,9},{9,10},{10,1... | collective-permute-start | bytes 1327112 | tf_op jit(solution)/shard_map/ppermute | solution.py:424
  1116.0 16.2 %collective-permute-start.26 = (bf16[288,768]{1,0:T(8,128)(2,1)S(1)}, bf16[288,768]{1,0:T(8,128)(2,1)S(1)}, u32[]{:S(2)}, u32[]{:S(2)}) collective-permute-start(bf16[288,768]{1,0:T(8,128)(2,1)S(1)} %slice_bitcast_fusion.6), channel_id=1, source_target_pairs={{0,16},{4,12},{8,24},{12,4},{16,0},{20,28},{24,8},{28,20},{1,17},{... | collective-permute-start | bytes 1327112 | tf_op jit(solution)/shard_map/ppermute | solution.py:408
  1128.7 12.2 collective-permute-start.38
  1141.0 13.1 %collective-permute-start.39 = (bf16[288,768]{1,0:T(8,128)(2,1)S(1)}, bf16[288,768]{1,0:T(8,128)(2,1)S(1)}, u32[]{:S(2)}, u32[]{:S(2)}) collective-permute-start(bf16[288,768]{1,0:T(8,128)(2,1)S(1)} %fusion.34.refs_0_), channel_id=1, source_target_pairs={{0,8},{4,20},{8,0},{12,28},{16,24},{20,4},{24,16},{28,12},{1,9},{5... | collective-permute-start | bytes 1327112 | tf_op jit(solution)/shard_map/ppermute | solution.py:408
  1141.6 13.1 %collective-permute-start.40 = (bf16[288,768]{1,0:T(8,128)(2,1)S(1)}, bf16[288,768]{1,0:T(8,128)(2,1)S(1)}, u32[]{:S(2)}, u32[]{:S(2)}) collective-permute-start(bf16[288,768]{1,0:T(8,128)(2,1)S(1)} %fusion.34.refs_0_), channel_id=1, source_target_pairs={{0,16},{4,12},{8,24},{12,4},{16,0},{20,28},{24,8},{28,20},{1,17},{... | collective-permute-start | bytes 1327112 | tf_op jit(solution)/shard_map/ppermute | solution.py:408
  1154.1 59.5 %collective-permute-start.42 = (bf16[288,768]{1,0:T(8,128)(2,1)S(1)}, bf16[288,768]{1,0:T(8,128)(2,1)S(1)}, u32[]{:S(2)}, u32[]{:S(2)}) collective-permute-start(bf16[288,768]{1,0:T(8,128)(2,1)S(1)} %fusion.34.refs_0_), channel_id=1, source_target_pairs={{0,4},{4,0},{8,12},{12,8},{16,20},{20,16},{24,28},{28,24},{1,5},{5... | collective-permute-start | bytes 1327112 | tf_op jit(solution)/shard_map/ppermute | solution.py:408
  1154.2 59.4 %collective-permute-start.43 = (bf16[288,768]{1,0:T(8,128)(2,1)S(1)}, bf16[288,768]{1,0:T(8,128)(2,1)S(1)}, u32[]{:S(2)}, u32[]{:S(2)}) collective-permute-start(bf16[288,768]{1,0:T(8,128)(2,1)S(1)} %collective-permute-done.39.refs_1_), channel_id=1, source_target_pairs={{0,4},{4,0},{8,12},{12,8},{16,20},{20,16},{24,28},{28,24},{1,5},{5... | collective-permute-start | bytes 1327112 | tf_op jit(solution)/shard_map/ppermute | solution.py:408
  1154.7 58.9 %collective-permute-start.44 = (bf16[288,768]{1,0:T(8,128)(2,1)S(1)}, bf16[288,768]{1,0:T(8,128)(2,1)S(1)}, u32[]{:S(2)}, u32[]{:S(2)}) collective-permute-start(bf16[288,768]{1,0:T(8,128)(2,1)S(1)} %collective-permute-done.40.refs_2_), channel_id=1, source_target_pairs={{0,4},{4,0},{8,12},{12,8},{16,20},{20,16},{24,28},{28,24},{1,5},{5... | collective-permute-start | bytes 1327112 | tf_op jit(solution)/shard_map/ppermute | solution.py:408
  1162.4 51.2 %collective-permute-start.45 = (bf16[288,768]{1,0:T(8,128)(2,1)S(1)}, bf16[288,768]{1,0:T(8,128)(2,1)S(1)}, u32[]{:S(2)}, u32[]{:S(2)}) collective-permute-start(bf16[288,768]{1,0:T(8,128)(2,1)S(1)} %collective-permute-done.41.refs_3_), channel_id=1, source_target_pairs={{0,4},{4,0},{8,12},{12,8},{16,20},{20,16},{24,28},{28,24},{1,5},{5... | collective-permute-start | bytes 1327112 | tf_op jit(solution)/shard_map/ppermute | solution.py:408
  (96 other events, 1248.9 us)
Sparse Core Ops, SparseCore 0:
  1228.9 49.9 all-gather.2

commit v3 on v2

--- a/solution.py
+++ b/solution.py
@@ -14,6 +14,7 @@
 HD = 64
 ROT = 16
 FF = 3072
+TOK_DEV = 128
 
 
 EPS_NORM = 1e-05
@@ -445,36 +446,43 @@
 
 def pack_kernel(where, flat_ref, out_ref, held, sems):
     shard = where[0]
+    turns = out_ref.shape[0]
     for z in range(SHARDS):
 
         @pl.when(shard == z)
         def _(z=z):
-            def start(turn, slot):
+            def copies_of(turn):
+                slot = turn % 2
+                rep = where[1 + turn]
                 copies = []
                 at = 0
-                rep = where[1 + turn]
                 for part, (first, step, _, _, _) in enumerate(PARTS[z]):
                     lead = first % 8
                     count = step + (8 if lead else 0)
                     begin = pl.multiple_of(first - lead + step * rep, 8)
-                    copy = pltpu.make_async_copy(
-                        flat_ref.at[pl.ds(begin, count)],
-                        held.at[slot, pl.ds(at, count)],
-                        sems.at[slot, part],
+                    copies.append(
+                        pltpu.make_async_copy(
+                            flat_ref.at[pl.ds(begin, count)],
+                            held.at[slot, pl.ds(at, count)],
+                            sems.at[slot, part],
+                        )
                     )
-                    copy.start()
-                    copies.append(copy)
                     at += count
                 return copies
 
-            turns = out_ref.shape[0]
-            running = start(0, 0)
-            for turn in range(turns):
+            for copy in copies_of(0):
+                copy.start()
+
+            @pl.loop(0, turns)
+            def _(turn):
+                @pl.when(turn + 1 < turns)
+                def _():
+                    for copy in copies_of(turn + 1):
+                        copy.start()
+
                 slot = turn % 2
-                following = start(turn + 1, 1 - slot) if turn + 1 < turns else None
-                rep = where[1 + turn] if turns > 1 else 0
                 at = 0
-                for copy, (first, step, rows, blocks, place) in zip(running, PARTS[z]):
+                for copy, (first, step, rows, blocks, place) in zip(copies_of(turn), PARTS[z]):
                     copy.wait()
                     lead = first % 8
                     for block in range(blocks):
@@ -482,12 +490,11 @@
                             begin = at + lead + 6 * block + col
                             got = held[slot, pl.ds(begin, rows, stride=6 * blocks), :]
                             out_ref[
-                                rep,
+                                turn,
                                 place + rows * block : place + rows * (block + 1),
                                 LANES * col : LANES * (col + 1),
                             ] = got.astype(jnp.bfloat16)
                     at += step + (8 if lead else 0)
-                running = following
 
 
 def pack_pieces(params, shard, reps):
@@ -507,53 +514,274 @@
     )(jnp.stack([shard] + reps), params.reshape(FLAT_ROWS, LANES))
 
 
-def place_kernel(where, *refs):
-    out_ref, sem = refs[-2:]
+PIECES = SHARDS * REPS
+ALL_ROWS = PIECES * PIECE
+
+
+def fetch_pieces(ids, blocks, own, shard, held, sems):
     copies = []
-    for turn, ref in enumerate(refs[:-2]):
-        copies.append(pltpu.make_async_copy(ref, out_ref.at[where[turn]], sem.at[turn]))
+    for turn, block in enumerate(blocks):
+        row = pl.multiple_of(ids[turn] * PIECE, 16)
+        copies.append(pltpu.make_async_copy(block, held.at[pl.ds(row, PIECE)], sems.at[turn]))
+    row = pl.multiple_of(shard * (REPS * PIECE), 16)
+    copies.append(
+        pltpu.make_async_copy(own, held.at[pl.ds(row, REPS * PIECE)], sems.at[len(blocks)])
+    )
+    for copy in copies:
+        copy.start()
+    return copies
+
+
+def rows_of(held, shard, begin, rows):
+    return jnp.concatenate(
+        [held[pl.ds((shard * REPS + r) * PIECE + begin, rows), :] for r in range(REPS)], axis=0
+    )
+
+
+def w_qkv_of(held, j):
+    return rows_of(held, 0, 96 * j, 96)
+
+
+def w_out_of(held):
+    return rows_of(held, 1, 0, 96)
+
+
+def w_in_of(held, j):
+    return jnp.concatenate([rows_of(held, 1, 96 + 48 * j, 48), rows_of(held, 2, 48 * j, 48)], axis=0)
+
+
+def w_out2_of(held, j):
+    if j == 0:
+        return rows_of(held, 2, 192, 96)
+    return held[pl.ds(3 * REPS * PIECE + D * (j - 1), D), :]
+
+
+def dot32(a, b):
+    return jnp.dot(a, b, preferred_element_type=jnp.float32)
+
+
+def gradient_kernel(where, *refs):
+    count = PIECES - REPS
+    blocks, own = refs[:count], refs[count]
+    (act_one, act_two, grad_y, vecs, rot_cos, rot_up, rot_down, bias) = refs[count + 1 : count + 9]
+    outs = refs[count + 9 : count + 9 + 13]
+    sent, kept = outs[0:4], outs[4:8]
+    attn_out, hidden_out, pre_out, mixed_out, sums_out = outs[8:13]
+    held, grads, query, key, value, grad_attn, sems, out_sems = refs[count + 22 :]
+    shard = where[0]
+    for copy in fetch_pieces([where[1 + t] for t in range(count)], blocks, own, shard, held, sems):
+        copy.wait()
+    slot_row = lambda z, r: pl.multiple_of(where[1 + count + z * REPS + r] * PIECE, 16)
+
+    def keep_rows(z, begin, rows, part):
+        for r in range(part.shape[0] // rows):
+            grads[pl.ds(slot_row(z, r) + begin, rows), :] = part[rows * r : rows * (r + 1), :]
+
+    act1 = act_one[...]
+    for j, out in enumerate((query, key, value)):
+        got = dot32(act1, w_qkv_of(held, j)) + vecs[2 + j : 3 + j, :]
+        if j < 2:
+            for p in range(6):
+                lanes = slice(LANES * p, LANES * (p + 1))
+                part = got[:, lanes]
+                part = (
+                    part * rot_cos[...]
+                    + pltpu.roll(part, LANES - 8, 1) * rot_up[...]
+                    + pltpu.roll(part, 8, 1) * rot_down[...]
+                )
+                out[:, lanes] = part.astype(jnp.bfloat16)
+        else:
+            out[...] = got.astype(jnp.bfloat16)
+    gy_t = grad_y[...].T
+    grad_attn[...] = dot32(w_out_of(held), gy_t).T.astype(jnp.bfloat16)
+
+    low = lax.broadcasted_iota(jnp.int32, (LANES, LANES), 1) < HD
+    scale = HD ** (-0.5)
+    for p in range(6):
+        lanes = slice(LANES * p, LANES * (p + 1))
+        q2, k2, v2, g2 = (ref[:, lanes] for ref in (query, key, value, grad_attn))
+        k2_t, v2_t = k2.T, v2.T
+        attn_parts, value_parts, query_parts, key_parts = [], [], [], []
+        for half in range(2):
+            here = low if half == 0 else ~low
+            zero = jnp.zeros_like(q2)
+            scores = dot32(jnp.where(here, q2, zero), k2_t) * scale
+            scores = jnp.where(bias[...] > 0.5, scores, NEG_BIG)
+            expd = jnp.exp(scores - jnp.max(scores, axis=1, keepdims=True))
+            chances = expd / jnp.sum(expd, axis=1, keepdims=True)
+            chances16 = chances.astype(jnp.bfloat16)
+            attn = dot32(chances16, v2)
+            attn16 = attn.astype(jnp.bfloat16)
+            masked = jnp.where(here, g2, zero)
+            delta = jnp.sum(
+                masked.astype(jnp.float32) * attn16.astype(jnp.float32), axis=1, keepdims=True
+            )
+            grad_chance = dot32(masked, v2_t)
+            slope = (chances * (grad_chance - delta) * scale).astype(jnp.bfloat16)
+            attn_parts.append(attn16)
+            value_parts.append(dot32(chances16.T, g2))
+            query_parts.append(dot32(slope, k2))
+            key_parts.append(dot32(slope.T, q2))
+        attn_out[:, lanes] = jnp.where(low, *attn_parts)
+        for j, parts in enumerate((query_parts, key_parts, value_parts)):
+            part = jnp.where(low, *parts)
+            if j < 2:
+                part = (
+                    part * rot_cos[...]
+                    - pltpu.roll(part, LANES - 8, 1) * rot_up[...]
+                    - pltpu.roll(part, 8, 1) * rot_down[...]
+                )
+            wide = slice(D * j + LANES * p, D * j + LANES * (p + 1))
+            sums_out[2 + j : 3 + j, lanes] = jnp.sum(part, axis=0, keepdims=True)
+            mixed_out[:, wide] = part.astype(jnp.bfloat16)
+
+    gy = grad_y[...]
+    act1_t = act1.T
+    for j in range(3):
+        keep_rows(
+            0, 96 * j, 96, dot32(act1_t, mixed_out[:, D * j : D * (j + 1)]).astype(jnp.bfloat16)
+        )
+    keep_rows(1, 0, 96, dot32(attn_out[...].T, gy).astype(jnp.bfloat16))
+
+    act2 = act_two[...]
+    act2_t = act2.T
+    for j in range(4):
+        wide = slice(D * j, D * (j + 1))
+        pre = dot32(act2, w_in_of(held, j)) + vecs[8 + j : 9 + j, :]
+        bell = 0.5 * (1.0 + lax.erf(pre * INV_ROOT_TWO))
+        hidden = (pre * bell).astype(jnp.bfloat16)
+        hidden_out[:, wide] = hidden
+        grad_hidden = dot32(w_out2_of(held, j), gy_t).T
+        grad_pre = grad_hidden * (bell + pre * jnp.exp(-0.5 * pre * pre) * INV_ROOT_TWO_PI)
+        sums_out[8 + j : 9 + j, :] = jnp.sum(grad_pre, axis=0, keepdims=True)
+        grad_pre16 = grad_pre.astype(jnp.bfloat16)
+        pre_out[:, wide] = grad_pre16
+        w2 = dot32(hidden.T, gy).astype(jnp.bfloat16)
+        if j == 0:
+            keep_rows(2, 192, 96, w2)
+        else:
+            at = D * (j - 1)
+            while at < D * j:
+                r, begin = divmod(at, PIECE)
+                rows = min(PIECE - begin, D * j - at)
+                grads[pl.ds(slot_row(3, r) + begin, rows), :] = w2[
+                    at - D * (j - 1) : at - D * (j - 1) + rows, :
+                ]
+                at += rows
+        w1 = dot32(act2_t, grad_pre16).astype(jnp.bfloat16)
+        keep_rows(1, 96 + 48 * j, 48, w1[: D // 2])
+        keep_rows(2, 48 * j, 48, w1[D // 2 :])
+    copies = []
+    for turn, out in enumerate(sent + kept):
+        for p in range(4):
+            copies.append(
+                pltpu.make_async_copy(
+                    grads.at[pl.ds((turn * 4 + p) * PIECE, PIECE)],
+                    out.at[p],
+                    out_sems.at[turn * 4 + p],
+                )
+            )
     for copy in copies:
         copy.start()
     for copy in copies:
         copy.wait()
 
 
-def place_pieces(blocks, ids, slots):
+def weight_gradients(scalars, blocks, own, small):
+    hbm = pl.BlockSpec(memory_space=pltpu.HBM)
+    vmem = pl.BlockSpec(memory_space=pltpu.VMEM)
+    bf16 = jnp.bfloat16
+    group = jax.ShapeDtypeStruct((4, PIECE, D), bf16)
     return pl.pallas_call(
-        place_kernel,
+        gradient_kernel,
         grid_spec=pltpu.PrefetchScalarGridSpec(
             num_scalar_prefetch=1,
-            in_specs=[pl.BlockSpec(memory_space=pltpu.HBM)] * len(blocks),
-            out_specs=pl.BlockSpec(memory_space=pltpu.HBM),
-            scratch_shapes=[pltpu.SemaphoreType.DMA((len(blocks),))],
+            in_specs=[hbm] * (len(blocks) + 1) + [vmem] * len(small),
+            out_specs=[hbm] * 8 + [vmem] * 5,
+            scratch_shapes=[
+                pltpu.VMEM((ALL_ROWS, D), bf16),
+                pltpu.VMEM((ALL_ROWS, D), bf16),
+                pltpu.VMEM((TOK_DEV, D), bf16),
+                pltpu.VMEM((TOK_DEV, D), bf16),
+                pltpu.VMEM((TOK_DEV, D), bf16),
+                pltpu.VMEM((TOK_DEV, D), bf16),
+                pltpu.SemaphoreType.DMA((PIECES,)),
+                pltpu.SemaphoreType.DMA((PIECES,)),
+            ],
         ),
-        out_shape=jax.ShapeDtypeStruct((slots,) + blocks[0].shape, blocks[0].dtype),
-    )(jnp.stack(ids), *blocks)
-
-
-def order_kernel(where, in_ref, out_ref, sem):
-    copies = []
-    for turn in range(out_ref.shape[0]):
-        copies.append(
-            pltpu.make_async_copy(in_ref.at[where[turn]], out_ref.at[turn], sem.at[turn])
+        out_shape=[group] * 8
+        + [
+            jax.ShapeDtypeStruct((TOK_DEV, D), bf16),
+            jax.ShapeDtypeStruct((TOK_DEV, FF), bf16),
+            jax.ShapeDtypeStruct((TOK_DEV, FF), bf16),
+            jax.ShapeDtypeStruct((TOK_DEV, 3 * D), bf16),
+            jax.ShapeDtypeStruct((16, D), jnp.float32),
+        ],
+        compiler_params=pltpu.CompilerParams(vmem_limit_bytes=56 * 2**20),
+    )(scalars, *blocks, own, *small)
+
+
+def result_kernel(where, *refs):
+    count = PIECES - REPS
+    blocks, own = refs[:count], refs[count]
+    (tokens, normed, inv_std, grad_y, vecs, attn, hidden, grad_pre, grad_mixed, sums) = refs[
+        count + 1 : count + 11
+    ]
+    output, grad_input, vec_out, held, sems = refs[count + 11 :]
+    shard = where[0]
+    for copy in fetch_pieces([where[1 + t] for t in range(count)], blocks, own, shard, held, sems):
+        copy.wait()
+    total = dot32(attn[...], w_out_of(held)) + vecs[5:6, :]
+    for j in range(4):
+        total = total + dot32(hidden[:, D * j : D * (j + 1)], w_out2_of(held, j))
+    output[...] = tokens[...].astype(jnp.float32) + (total + vecs[12:13, :])
+    vec_out[...] = sums[...]
+    gy = grad_y[...].astype(jnp.float32)
+    total = gy
+    for norm, (parts, width, weights) in enumerate(
+        ((grad_mixed, 3, w_qkv_of), (grad_pre, 4, w_in_of))
+    ):
+        back = None
+        for j in range(width):
+            part = dot32(weights(held, j), parts[:, D * j : D * (j + 1)].T)
+            back = part if back is None else back + part
+        grad_act = back.T
+        gain_row = 0 if norm == 0 else 6
+        unit = normed[...]
+        vec_out[gain_row : gain_row + 1, :] = jnp.sum(grad_act * unit, axis=0, keepdims=True)
+        vec_out[gain_row + 1 : gain_row + 2, :] = jnp.sum(grad_act, axis=0, keepdims=True)
+        grad_norm = grad_act * vecs[gain_row : gain_row + 1, :]
+        total = total + inv_std[...] * (
+            grad_norm
+            - jnp.mean(grad_norm, axis=1, keepdims=True)
+            - unit * jnp.mean(grad_norm * unit, axis=1, keepdims=True)
         )
-    for copy in copies:
-        copy.start()
-    for copy in copies:
-        copy.wait()
-
-
-def order_pieces(pieces, ids):
+    grad_input[...] = total
+    bottom = jnp.sum(gy, axis=0, keepdims=True)
+    vec_out[5:6, :] = bottom
+    vec_out[12:13, :] = bottom
+    vec_out[13:16, :] = jnp.zeros((3, D), jnp.float32)
+    vec_out[...] = vec_out[...].astype(jnp.bfloat16).astype(jnp.float32)
+
+
+def layer_results(scalars, blocks, own, small):
+    hbm = pl.BlockSpec(memory_space=pltpu.HBM)
+    vmem = pl.BlockSpec(memory_space=pltpu.VMEM)
+    rows = jax.ShapeDtypeStruct((TOK_DEV, D), jnp.float32)
     return pl.pallas_call(
-        order_kernel,
+        result_kernel,
         grid_spec=pltpu.PrefetchScalarGridSpec(
             num_scalar_prefetch=1,
-            in_specs=[pl.BlockSpec(memory_space=pltpu.HBM)],
-            out_specs=pl.BlockSpec(memory_space=pltpu.HBM),
-            scratch_shapes=[pltpu.SemaphoreType.DMA((len(ids),))],
+            in_specs=[hbm] * (len(blocks) + 1) + [vmem] * len(small),
+            out_specs=[vmem] * 3,
+            scratch_shapes=[
+                pltpu.VMEM((ALL_ROWS, D), jnp.bfloat16),
+                pltpu.SemaphoreType.DMA((PIECES,)),
+            ],
         ),
-        out_shape=jax.ShapeDtypeStruct((len(ids),) + pieces.shape[1:], pieces.dtype),
-    )(jnp.stack(ids), pieces)
+        out_shape=[rows, rows, jax.ShapeDtypeStruct((16, D), jnp.float32)],
+        compiler_params=pltpu.CompilerParams(vmem_limit_bytes=40 * 2**20),
+    )(scalars, *blocks, own, *small)
 
 
 def unpack_kernel(factor, where, *refs):
@@ -622,23 +850,47 @@
         owner = (shard + SHARDS - hop) % SHARDS
         blocks += spread_in_plane(piece)
         ids += [owner * REPS + which for which in reps]
-    blocks += [own[turn] for turn in range(REPS)]
-    ids += [shard * REPS + turn for turn in range(REPS)]
-    return place_pieces(blocks, ids, SHARDS * REPS)
-
-
-def slots_of(shard, rep):
-    ids = []
-    for base in (rep ^ 1, rep):
-        own, first, second, both = (base ^ flip for flip in flips_of(base))
-        for hop in HOPS:
-            owner = (shard + SHARDS - hop) % SHARDS
-            ids += [owner * REPS + which for which in (first, both, own, second)]
-    return ids
-
-
-def scatter_sums(ordered):
-    sent, kept = ordered[0], ordered[1]
+    return blocks, own.reshape(REPS * PIECE, D), ids
+
+
+def gather_vectors(params, shard):
+    mine = shard_vectors(params, shard)
+    held = [mine.astype(jnp.bfloat16)]
+    for _ in range(1, SHARDS):
+        held.append(ring_step(held[-1]))
+    turned = jnp.stack(held).astype(jnp.float32)
+    order = (shard + SHARDS - jnp.arange(SHARDS)) % SHARDS
+    return jnp.take(turned, order, axis=0).reshape(16, D)
+
+
+def sum_everywhere(value):
+    for flips in ((1, 1), (2, 2), (4, 4)):
+        value = value + plane_permute(value, flips)
+    total, moving = value, value
+    for _ in range(1, SHARDS):
+        moving = ring_step(moving)
+        total = total + moving
+    return total
+
+
+def slots_by_piece(shard, rep):
+    slots = []
+    for owner in range(SHARDS):
+        hop = (shard + SHARDS - owner + 3) % SHARDS
+        for which in range(REPS):
+            apart = rep ^ which
+            kept = 1 - apart % 2
+            core = which % 2
+            across = apart & 6
+            first = 2 + 2 * core
+            place = jnp.where(
+                across == 0, 2, jnp.where(across == 6, 1, jnp.where(across == first, 0, 3))
+            )
+            slots.append((kept * SHARDS + hop) * 4 + place)
+    return slots
+
+
+def scatter_sums(sent, kept):
     carried = None
     for turn in range(SHARDS):
         chip = kept[turn] + core_cross(sent[turn])
@@ -656,73 +908,41 @@
     return jnp.stack([lax.dynamic_slice_in_dim(params, rows[i] * D, D) for i in range(4)])
 
 
-def pieces_of(gathered, vectors):
-    first, second, third, fourth = (gathered[z] for z in range(SHARDS))
-    w_qkv = jnp.concatenate(
-        [first[:, 96 * j : 96 * (j + 1)].reshape(D, D) for j in range(3)], axis=1
-    )
-    w_out = second[:, 0:96].reshape(D, D)
-    w_in = jnp.concatenate(
-        [
-            jnp.concatenate(
-                [
-                    second[:, 96 + 48 * j : 144 + 48 * j].reshape(D // 2, D),
-                    third[:, 48 * j : 48 * (j + 1)].reshape(D // 2, D),
-                ],
-                axis=0,
-            )
-            for j in range(4)
-        ],
-        axis=1,
-    )
-    w_out2 = jnp.concatenate([third[:, 192:288].reshape(D, D), fourth.reshape(3 * D, D)], axis=0)
-    return (
-        vectors[0, 0],
-        vectors[0, 1],
-        w_qkv,
-        jnp.concatenate([vectors[0, 2], vectors[0, 3], vectors[1, 0]]),
-        w_out,
-        vectors[1, 1],
-        vectors[1, 2],
-        vectors[1, 3],
-        w_in,
-        vectors[2].reshape(-1),
-        w_out2,
-        vectors[3, 0],
-    )
-
-
-def grads_by_owner(parts):
-    w_qkv, w_out, w_in, w_out2 = (part.astype(jnp.bfloat16) for part in parts)
-    col = lambda w, j: w[:, D * j : D * (j + 1)]
-    first = [col(w_qkv, j).reshape(REPS, 96, D) for j in range(3)]
-    second = [w_out.reshape(REPS, 96, D)] + [
-        col(w_in, j)[: D // 2].reshape(REPS, 48, D) for j in range(4)
-    ]
-    third = [col(w_in, j)[D // 2 :].reshape(REPS, 48, D) for j in range(4)] + [
-        w_out2[:D].reshape(REPS, 96, D)
-    ]
-    fourth = [w_out2[D:].reshape(REPS, PIECE, D)]
-    return jnp.stack(
-        [jnp.concatenate(group, axis=1) for group in (first, second, third, fourth)]
-    )
-
-
 def on_device_rows(tokens, segment_ids, cotangent, params, moment_one, moment_two):
     shard = lax.axis_index("z")
     rep = lax.axis_index(PLANE)
-    vectors = lax.all_gather(shard_vectors(params, shard).astype(jnp.bfloat16), "z", axis=0)
-    gathered = gather_matrices(params, shard, rep).reshape(SHARDS, REPS, PIECE, D)
-    pieces = pieces_of(gathered, vectors)
-    output, saved = layer_forward(tokens, segment_ids, pieces)
-    grad_input, parts = layer_backward(cotangent, segment_ids, pieces, saved)
-    (g1, s1, gw_qkv, gb_qkv, gw_out, gb_out, g2, s2, gw_in, gb_in, gw_out2, gb_out2) = parts
-    by_owner = grads_by_owner((gw_qkv, gw_out, gw_in, gw_out2))
-    ordered = order_pieces(by_owner.reshape(SHARDS * REPS, PIECE, D), slots_of(shard, rep))
-    owned = scatter_sums(ordered.reshape(2, SHARDS, 4, PIECE, D))
-    zero = jnp.zeros((3 * D,), jnp.float32)
-    vec_grads = jnp.concatenate([g1, s1, gb_qkv, gb_out, g2, s2, gb_in, gb_out2, zero])
-    vec_grads = lax.psum(vec_grads.astype(jnp.bfloat16).astype(jnp.float32), EVERY)
+    vecs = gather_vectors(params, shard)
+    blocks, own, ids = gather_matrices(params, shard, rep)
+    x_wide = tokens.astype(jnp.float32)
+    centered = x_wide - jnp.mean(x_wide, axis=1, keepdims=True)
+    variance = jnp.mean(centered * centered, axis=1, keepdims=True)
+    inv_std = lax.rsqrt(variance + EPS_NORM)
+    normed = centered * inv_std
+    act_one = (normed * vecs[0] + vecs[1]).astype(jnp.bfloat16)
+    act_two = (normed * vecs[6] + vecs[7]).astype(jnp.bfloat16)
+    live_rows = (segment_ids >= 0)[:, None]
+    grad_y = jnp.where(live_rows, cotangent, jnp.zeros_like(cotangent))
+    cosine, sine = rotary_tables(positions_of(segment_ids))
+    cosine, sine = cosine[:, 0], sine[:, 0]
+    rest = jnp.ones((TOK_DEV, HD - ROT), jnp.float32)
+    none = jnp.zeros_like(rest)
+    gap = jnp.zeros_like(sine)
+    rot_cos = jnp.concatenate([cosine, cosine, rest] * 2, axis=1)
+    rot_up = jnp.concatenate([-sine, gap, none] * 2, axis=1)
+    rot_down = jnp.concatenate([gap, sine, none] * 2, axis=1)
+    slot_ids = jnp.arange(TOK_DEV, dtype=jnp.int32)
+    allowed = (segment_ids[:, None] == segment_ids[None, :]) & (
+        slot_ids[None, :] <= slot_ids[:, None]
+    )
+    scalars = jnp.stack([shard] + ids + slots_by_piece(shard, rep))
+    small = (act_one, act_two, grad_y, vecs, rot_cos, rot_up, rot_down, allowed.astype(jnp.float32))
+    made = weight_gradients(scalars, blocks, own, small)
+    sent, kept = made[0:4], made[4:8]
+    attn, hidden, grad_pre, grad_mixed, sums = made[8:]
+    owned = scatter_sums(sent, kept)
+    small = (tokens, normed, inv_std, grad_y, vecs, attn, hidden, grad_pre, grad_mixed, sums)
+    output, grad_input, vec_grads = layer_results(scalars, blocks, own, small)
+    vec_grads = sum_everywhere(vec_grads)
     own_vectors = lax.dynamic_index_in_dim(
         vec_grads.reshape(SHARDS, 4, D), shard, 0, keepdims=False
     )

time: 1300 us -> 359 us (0.28)
  Pallas kernels: 872 us -> 49.3 us
  blocking collectives: 52.3 us -> 0 us
  other arithmetic: 62.1 us -> 12.3 us
  waiting for transfers between devices: 165 us -> 196 us
  matrix products: 27.8 us -> 0 us
  local copies, waits for them, and re-layouts: 63.6 us -> 44.1 us
    pallas_call x2, Pallas kernels: 862 us -> 39.8 us  [the longest x1 28.3 us: weight_gradients(): pl.pallas_call(gradient_kernel, grid_spec=pltpu.PrefetchScalarGridSpec(nu...]
    psum x1 -> x0, blocking collectives: 37.8 us -> none  [on_device_rows(): lax.psum(vec_grads.astype(jnp.bfloat16).astype(jnp.float32), EVERY)]
    concatenate x1 -> x0, other arithmetic: 33.5 us -> none  [pieces_of(): jnp.concatenate([jnp.concatenate([second[:, 96 + 48 * j:144 + 48 * j].res...]
    dot_general x18 -> x0, matrix products: 27.8 us -> none  [the longest x1 4.26 us: layer_backward(): lax.dot_general(grad_pre16, w_in, contract_cols, preferred_element_type=j...]
    ppermute x6 -> x12, waiting for transfers between devices: 28.6 us -> 55.9 us  [ring_step(): lax.ppermute(value, 'z', [(i, (i + 1) % SHARDS) for i in range(SHARDS)])]
    slice x17 -> x1, local copies, waits for them, and re-layouts: 18.1 us -> 0.03 us  [on_device_rows(): act_two = (normed * vecs[6] + vecs[7]).astype(jnp.bfloat16)]
    all_gather x1 -> x0, blocking collectives: 14.5 us -> none  [on_device_rows(): lax.all_gather(shard_vectors(params, shard).astype(jnp.bfloat16), 'z', ax...]
    unnamed x172 -> x114, local copies, waits for them, and re-layouts: 31.2 us -> 36.6 us
  transfers between devices with their start and end apart: 47 -> 56, of which waited for: 21 -> 26; matrix products, arithmetic and copies ran while one was open for 3% -> 4% of each run, Pallas kernels for 0% -> 4%
where the time goes in v3:
time: 359 us; the launch traced here: 358 us
  waiting for transfers between devices  196 us (55%)
  Pallas kernels  49.3 us (14%)
  local copies, waits for them, and re-layouts  44.1 us (12%)
  starting transfers between devices  38.5 us (11%)
  between operations  17.8 us (5%)
  other arithmetic  12.3 us (3%)
    ppermute x43, waiting for transfers between devices, plane_permute(): lax.ppermute(value, PLANE, [(i, i ^ flips[i % 2]) for i in range(REPS)])  93.4 us
    ppermute x12, waiting for transfers between devices, ring_step(): lax.ppermute(value, 'z', [(i, (i + 1) % SHARDS) for i in range(SHARDS)])  55.9 us
    all_gather x1, waiting for transfers between devices, on_device_rows(): new_params = lax.all_gather(upd_params, PLANE, axis=0, tiled=True)  47 us
    unnamed x114, local copies, waits for them, and re-layouts  36.6 us
    ppermute x43, starting transfers between devices, plane_permute(): lax.ppermute(value, PLANE, [(i, i ^ flips[i % 2]) for i in range(REPS)])  30.4 us
    pallas_call x1, Pallas kernels, weight_gradients(): pl.pallas_call(gradient_kernel, grid_spec=pltpu.PrefetchScalarGridSpec(nu...  28.3 us
    pallas_call x1, Pallas kernels, layer_results(): pl.pallas_call(result_kernel, grid_spec=pltpu.PrefetchScalarGridSpec(num_...  11.5 us
    ppermute x12, starting transfers between devices, ring_step(): lax.ppermute(value, 'z', [(i, (i + 1) % SHARDS) for i in range(SHARDS)])  8.1 us
  transfers between devices with their start and end apart: 56, of which 26 were waited for; matrix products, arithmetic and copies ran while one was open for 4% of the time, Pallas kernels for 4%

profile of v3, /device:TPU:0, one launch (start us, length us, event | category | flops | bytes accessed | tf_op | source)
XLA Modules:
  0.0 358.2 jit_solution(1693423899045266985)
XLA Ops:
  12.1 3.1 collective-permute-start.24
  15.2 3.0 copy-done
  21.5 11.1 %collective-permute-done.refs_0_ = bf16[288,768]{1,0:T(8,128)(2,1)S(1)} collective-permute-done((bf16[288,768]{1,0:T(8,128)(2,1)S(1)}, bf16[288,768]{1,0:T(8,128)(2,1)S(1)}, u32[]{:S(2)}, u32[]{:S(2)}) %collective-permute-start) | collective-permute-done | bytes 442400 | tf_op jit(solution)/shard_map/ppermute | solution.py:425
  36.3 9.0 %collective-permute-done.25 = bf16[4,768]{1,0:T(4,128)(2,1)S(1)} collective-permute-done((bf16[4,768]{1,0:T(4,128)(2,1)S(1)}, bf16[4,768]{1,0:T(4,128)(2,1)S(1)}, u32[]{:S(2)}, u32[]{:S(2)}) %collective-permute-start.25) | collective-permute-done | bytes 6176 | tf_op jit(solution)/shard_map/ppermute | solution.py:425
  47.0 3.0 copy-done.1
  50.1 2.8 shard_map.119
  60.2 7.7 %collective-permute-done.1.refs_1_ = bf16[288,768]{1,0:T(8,128)(2,1)S(1)} collective-permute-done((bf16[288,768]{1,0:T(8,128)(2,1)S(1)}, bf16[288,768]{1,0:T(8,128)(2,1)S(1)}, u32[]{:S(2)}, u32[]{:S(2)}) %collective-permute-start.1) | collective-permute-done | bytes 442400 | tf_op jit(solution)/shard_map/ppermute | solution.py:409
  70.8 5.3 %collective-permute-done.9.refs_9_ = bf16[288,768]{1,0:T(8,128)(2,1)} collective-permute-done((bf16[288,768]{1,0:T(8,128)(2,1)S(1)}, bf16[288,768]{1,0:T(8,128)(2,1)}, u32[]{:S(2)}, u32[]{:S(2)}) %collective-permute-start.9) | collective-permute-done | bytes 442400 | tf_op jit(solution)/shard_map/ppermute | solution.py:409
  80.7 8.6 %collective-permute-done.17.refs_17_ = bf16[288,768]{1,0:T(8,128)(2,1)} collective-permute-done((bf16[288,768]{1,0:T(8,128)(2,1)S(1)}, bf16[288,768]{1,0:T(8,128)(2,1)}, u32[]{:S(2)}, u32[]{:S(2)}) %collective-permute-start.17) | collective-permute-done | bytes 442400 | tf_op jit(solution)/shard_map/ppermute | solution.py:409
  93.4 4.5 %collective-permute-done.19.refs_19_ = bf16[288,768]{1,0:T(8,128)(2,1)} collective-permute-done((bf16[288,768]{1,0:T(8,128)(2,1)}, bf16[288,768]{1,0:T(8,128)(2,1)}, u32[]{:S(2)}, u32[]{:S(2)}) %collective-permute-start.19) | collective-permute-done | bytes 442400 | tf_op jit(solution)/shard_map/ppermute | solution.py:409
  100.7 28.3 %shard_map.120 = (bf16[4,288,768]{2,1,0:T(8,128)(2,1)}, bf16[4,288,768]{2,1,0:T(8,128)(2,1)}, bf16[4,288,768]{2,1,0:T(8,128)(2,1)}, bf16[4,288,768]{2,1,0:T(8,12...) custom-call(s32[57]{0:T(128)} %stack.311.where, ...), custom_call_target="tpu_custom_call" | custom-call | tf_op jit(solution)/shard_map/pallas_call | solution.py:695
  130.1 2.9 collective-permute-done.36
  142.4 5.6 %collective-permute-done.37 = bf16[2,288,768]{2,1,0:T(8,128)(2,1)S(1)} collective-permute-done((bf16[2,288,768]{2,1,0:T(8,128)(2,1)S(1)}, bf16[2,288,768]{2,1,0:T(8,128)(2,1)S(1)}, u32[]{:S(2)}, u32[]{:S(2)}) %collective-permute-start.37) | collective-permute-done | bytes 884768 | tf_op jit(solution)/shard_map/ppermute | solution.py:409
  149.8 12.5 %collective-permute-done.34 = bf16[2,288,768]{2,1,0:T(8,128)(2,1)S(1)} collective-permute-done((bf16[2,288,768]{2,1,0:T(8,128)(2,1)S(1)}, bf16[2,288,768]{2,1,0:T(8,128)(2,1)S(1)}, u32[]{:S(2)}, u32[]{:S(2)}) %collective-permute-start.34) | collective-permute-done | bytes 884768 | tf_op jit(solution)/shard_map/ppermute | solution.py:409
  164.8 21.1 %collective-permute-done.31 = bf16[2,288,768]{2,1,0:T(8,128)(2,1)S(1)} collective-permute-done((bf16[2,288,768]{2,1,0:T(8,128)(2,1)S(1)}, bf16[2,288,768]{2,1,0:T(8,128)(2,1)S(1)}, u32[]{:S(2)}, u32[]{:S(2)}) %collective-permute-start.31) | collective-permute-done | bytes 884768 | tf_op jit(solution)/shard_map/ppermute | solution.py:409
  189.4 5.1 %collective-permute-done.32 = bf16[288,768]{1,0:T(8,128)(2,1)S(1)} collective-permute-done((bf16[288,768]{1,0:T(8,128)(2,1)S(1)}, bf16[288,768]{1,0:T(8,128)(2,1)S(1)}, u32[]{:S(2)}, u32[]{:S(2)}) %collective-permute-start.32) | collective-permute-done | bytes 442400 | tf_op jit(solution)/shard_map/ppermute | solution.py:409
  194.5 6.3 %collective-permute-done.40 = bf16[288,768]{1,0:T(8,128)(2,1)S(1)} collective-permute-done((bf16[288,768]{1,0:T(8,128)(2,1)S(1)}, bf16[288,768]{1,0:T(8,128)(2,1)S(1)}, u32[]{:S(2)}, u32[]{:S(2)}) %collective-permute-start.40) | collective-permute-done | bytes 442400 | tf_op jit(solution)/shard_map/ppermute | solution.py:425
  200.9 12.0 %collective-permute-done.41 = bf16[288,768]{1,0:T(8,128)(2,1)S(1)} collective-permute-done((bf16[288,768]{1,0:T(8,128)(2,1)S(1)}, bf16[288,768]{1,0:T(8,128)(2,1)S(1)}, u32[]{:S(2)}, u32[]{:S(2)}) %collective-permute-start.41) | collective-permute-done | bytes 442400 | tf_op jit(solution)/shard_map/ppermute | solution.py:425
  214.1 2.5 collective-permute-start.43
  216.7 10.5 %collective-permute-done.42.refs_1_ = bf16[288,768]{1,0:T(8,128)(2,1)} collective-permute-done((bf16[288,768]{1,0:T(8,128)(2,1)}, bf16[288,768]{1,0:T(8,128)(2,1)}, u32[]{:S(2)}, u32[]{:S(2)}) %collective-permute-start.42) | collective-permute-done | bytes 442400 | tf_op jit(solution)/shard_map/ppermute | solution.py:409
  244.0 11.5 %shard_map.121 = (f32[128,768]{1,0:T(8,128)}, f32[128,768]{1,0:T(8,128)}, f32[16,768]{1,0:T(8,128)S(1)}) custom-call(s32[57]{0:T(128)S(1)} %copy-done.48, bf16[288,768]{1,0:T(8,128)(2,1)S(1)} %copy-done.6, bf16[288,768]{1,0:T(8,128)(2,1)S(1)} %copy-done.14, bf16[288,768]{1,0:T(8,128)(2,1)S(1)} %copy-done.12, bf16[288,768]{1,0:T(8,128)(2,1)S(1)} %copy-done.22, ...), custom_call_target="tpu_custom_call" | custom-call | tf_op jit(solution)/shard_map/pallas_call | solution.py:771
  257.2 3.8 %collective-permute-done.50 = f32[16,768]{1,0:T(8,128)S(1)} collective-permute-done((f32[16,768]{1,0:T(8,128)S(1)}, f32[16,768]{1,0:T(8,128)S(1)}, u32[]{:S(2)}, u32[]{:S(2)}) %collective-permute-start.50) | collective-permute-done | bytes 49184 | tf_op jit(solution)/shard_map/ppermute | solution.py:409
  261.0 2.1 collective-permute-start.51
  263.0 2.1 collective-permute-done.51
  266.3 4.8 %collective-permute-done.52 = f32[16,768]{1,0:T(8,128)S(1)} collective-permute-done((f32[16,768]{1,0:T(8,128)S(1)}, f32[16,768]{1,0:T(8,128)S(1)}, u32[]{:S(2)}, u32[]{:S(2)}) %collective-permute-start.52) | collective-permute-done | bytes 49184 | tf_op jit(solution)/shard_map/ppermute | solution.py:425
  271.1 5.9 %collective-permute-done.53 = f32[16,768]{1,0:T(8,128)S(1)} collective-permute-done((f32[16,768]{1,0:T(8,128)S(1)}, f32[16,768]{1,0:T(8,128)S(1)}, u32[]{:S(2)}, u32[]{:S(2)}) %collective-permute-start.53) | collective-permute-done | bytes 49184 | tf_op jit(solution)/shard_map/ppermute | solution.py:425
  277.0 5.8 %collective-permute-done.54 = f32[16,768]{1,0:T(8,128)S(1)} collective-permute-done((f32[16,768]{1,0:T(8,128)S(1)}, f32[16,768]{1,0:T(8,128)S(1)}, u32[]{:S(2)}, u32[]{:S(2)}) %collective-permute-start.54) | collective-permute-done | bytes 49184 | tf_op jit(solution)/shard_map/ppermute | solution.py:425
  284.7 5.8 %shard_map.122 = f32[13848,128]{1,0:T(8,128)} custom-call(s32[9]{0:T(128)S(1)} %stack.336.where, bf16[288,768]{1,0:T(8,128)(2,1)} %fusion.9.refs_0_, bf16[288,768]{1,0:T(8,128)(2,1)} %collective-permute-done.42.refs_1_, bf16[288,768]{1,0:T(8,128)(2,1)} %collective-permute-done.43.refs_2_, bf16[288,768]{1,0:T(8,128)(2,1)} %collective-permute-done.44.refs_3_, ...), custom_call_target="tpu_custom_call" | custom-call | tf_op jit(solution)/shard_map/pallas_call | solution.py:826
  290.6 3.6 %multiply_subtract_fusion = (f32[221568]{0:T(1024)S(1)}, f32[221568]{0:T(1024)}, f32[221568]{0:T(1024)}) fusion(f32[1772544]{0:T(1024)} %param.10, s32[]{:T(128)S(6)} %select_n.383, f32[1772544]{0:T(1024)} %bitcast.121, f32[221568]{0:T(1024)S(1)} %copy-done.52, f32[221568]{0:T(1024)S(1)} %copy-done.53), kind=kLoop, calls=%fused_computation.3 | loop fusion | flops 3323520 | bytes 6203908 | tf_op jit(solution)/shard_map/sub | solution.py:355
  294.2 4.9 %reshape.236 = f32[1,1,221568]{2,1,0:T(1,128)} reshape(f32[221568]{0:T(1024)S(1)} %get-tuple-element.42) | data formatting | bytes 1772544
  299.1 47.0 %all-gather.3.cloned.1.call-done = f32[8,1,221568]{2,1,0:T(1,128)} async-done(((f32[1,1,221568]{2,1,0:T(1,128)}), f32[8,1,221568]{2,1,0:T(1,128)}) %all-gather.3.cloned.1.call-update) | async-done | bytes 7090192 | tf_op jit(solution)/shard_map/all_gather | solution.py:958
  346.2 5.2 %copy.23 = f32[1772544]{0:T(1024)} copy(f32[1772544]{0:T(1024)} %bitcast.123) | data formatting | bytes 14180352
  (275 shorter events, 72.9 us)
Async XLA Ops:
  7.2 339.0 %all-gather.3.cloned.1.call-start = ((), (), s32[]{:S(2)}) async-start(), calls=%async_computation | async-start | bytes 7976448 | tf_op jit(solution)/shard_map/all_gather | solution.py:958
  12.1 22.6 %collective-permute-start.24 = (bf16[4,768]{1,0:T(4,128)(2,1)S(1)}, bf16[4,768]{1,0:T(4,128)(2,1)S(1)}, u32[]{:S(2)}, u32[]{:S(2)}) collective-permute-start(bf16[4,768]{1,0:T(4,128)(2,1)S(1)} %pad_maximum_fusion), channel_id=1, source_target_pairs={{0,1},{1,2},{2,3},{3,0},{4,5},{5,6},{6,7},{7,4},{8,9},{9,10},{10,1... | collective-permute-start | bytes 18440 | tf_op jit(solution)/shard_map/ppermute | solution.py:425
  19.1 13.5 %collective-permute-start = (bf16[288,768]{1,0:T(8,128)(2,1)S(1)}, bf16[288,768]{1,0:T(8,128)(2,1)S(1)}, u32[]{:S(2)}, u32[]{:S(2)}) collective-permute-start(bf16[288,768]{1,0:T(8,128)(2,1)S(1)} %bitcast.120), channel_id=1, source_target_pairs={{0,1},{1,2},{2,3},{3,0},{4,5},{5,6},{6,7},{7,4},{8,9},{9,10},{10,1... | collective-permute-start | bytes 1327112 | tf_op jit(solution)/shard_map/ppermute | solution.py:425
  32.6 25.1 %collective-permute-start.8 = (bf16[288,768]{1,0:T(8,128)(2,1)S(1)}, bf16[288,768]{1,0:T(8,128)(2,1)S(1)}, u32[]{:S(2)}, u32[]{:S(2)}) collective-permute-start(bf16[288,768]{1,0:T(8,128)(2,1)S(1)} %collective-permute-done.refs_0_), channel_id=1, source_target_pairs={{0,1},{1,2},{2,3},{3,0},{4,5},{5,6},{6,7},{7,4},{8,9},{9,10},{10,1... | collective-permute-start | bytes 1327112 | tf_op jit(solution)/shard_map/ppermute | solution.py:425
  32.6 25.2 %collective-permute-start.4 = (bf16[288,768]{1,0:T(8,128)(2,1)S(1)}, bf16[288,768]{1,0:T(8,128)(2,1)S(1)}, u32[]{:S(2)}, u32[]{:S(2)}) collective-permute-start(bf16[288,768]{1,0:T(8,128)(2,1)S(1)} %collective-permute-done.refs_0_), channel_id=1, source_target_pairs={{0,4},{4,0},{8,12},{12,8},{16,20},{20,16},{24,28},{28,24},{1,5},{5... | collective-permute-start | bytes 1327112 | tf_op jit(solution)/shard_map/ppermute | solution.py:409
  32.6 26.8 %collective-permute-start.2 = (bf16[288,768]{1,0:T(8,128)(2,1)S(1)}, bf16[288,768]{1,0:T(8,128)(2,1)S(1)}, u32[]{:S(2)}, u32[]{:S(2)}) collective-permute-start(bf16[288,768]{1,0:T(8,128)(2,1)S(1)} %collective-permute-done.refs_0_), channel_id=1, source_target_pairs={{0,16},{4,12},{8,24},{12,4},{16,0},{20,28},{24,8},{28,20},{1,17},{... | collective-permute-start | bytes 1327112 | tf_op jit(solution)/shard_map/ppermute | solution.py:409
  45.2 12.6 %collective-permute-start.26 = (bf16[4,768]{1,0:T(4,128)(2,1)S(1)}, bf16[4,768]{1,0:T(4,128)(2,1)S(1)}, u32[]{:S(2)}, u32[]{:S(2)}) collective-permute-start(bf16[4,768]{1,0:T(4,128)(2,1)S(1)} %collective-permute-done.25), channel_id=1, source_target_pairs={{0,1},{1,2},{2,3},{3,0},{4,5},{5,6},{6,7},{7,4},{8,9},{9,10},{10,1... | collective-permute-start | bytes 18440 | tf_op jit(solution)/shard_map/ppermute | solution.py:425
  56.1 11.8 %collective-permute-start.1 = (bf16[288,768]{1,0:T(8,128)(2,1)S(1)}, bf16[288,768]{1,0:T(8,128)(2,1)S(1)}, u32[]{:S(2)}, u32[]{:S(2)}) collective-permute-start(bf16[288,768]{1,0:T(8,128)(2,1)S(1)} %collective-permute-done.refs_0_), channel_id=1, source_target_pairs={{0,8},{4,20},{8,0},{12,28},{16,24},{20,4},{24,16},{28,12},{1,9},{5... | collective-permute-start | bytes 1327112 | tf_op jit(solution)/shard_map/ppermute | solution.py:409
  57.8 12.9 %collective-permute-start.10 = (bf16[288,768]{1,0:T(8,128)(2,1)S(1)}, bf16[288,768]{1,0:T(8,128)(2,1)}, u32[]{:S(2)}, u32[]{:S(2)}) collective-permute-start(bf16[288,768]{1,0:T(8,128)(2,1)S(1)} %collective-permute-done.8.refs_8_), channel_id=1, source_target_pairs={{0,16},{4,12},{8,24},{12,4},{16,0},{20,28},{24,8},{28,20},{1,17},{... | collective-permute-start | bytes 1327112 | tf_op jit(solution)/shard_map/ppermute | solution.py:409
  59.4 16.7 %collective-permute-start.9 = (bf16[288,768]{1,0:T(8,128)(2,1)S(1)}, bf16[288,768]{1,0:T(8,128)(2,1)}, u32[]{:S(2)}, u32[]{:S(2)}) collective-permute-start(bf16[288,768]{1,0:T(8,128)(2,1)S(1)} %collective-permute-done.8.refs_8_), channel_id=1, source_target_pairs={{0,8},{4,20},{8,0},{12,28},{16,24},{20,4},{24,16},{28,12},{1,9},{5... | collective-permute-start | bytes 1327112 | tf_op jit(solution)/shard_map/ppermute | solution.py:409
  76.1 13.2 %collective-permute-start.17 = (bf16[288,768]{1,0:T(8,128)(2,1)S(1)}, bf16[288,768]{1,0:T(8,128)(2,1)}, u32[]{:S(2)}, u32[]{:S(2)}) collective-permute-start(bf16[288,768]{1,0:T(8,128)(2,1)S(1)} %collective-permute-done.16.refs_16_), channel_id=1, source_target_pairs={{0,8},{4,20},{8,0},{12,28},{16,24},{20,4},{24,16},{28,12},{1,9},{5... | collective-permute-start | bytes 1327112 | tf_op jit(solution)/shard_map/ppermute | solution.py:409
  78.1 14.2 %collective-permute-start.18 = (bf16[288,768]{1,0:T(8,128)(2,1)S(1)}, bf16[288,768]{1,0:T(8,128)(2,1)}, u32[]{:S(2)}, u32[]{:S(2)}) collective-permute-start(bf16[288,768]{1,0:T(8,128)(2,1)S(1)} %collective-permute-done.16.refs_16_), channel_id=1, source_target_pairs={{0,16},{4,12},{8,24},{12,4},{16,0},{20,28},{24,8},{28,20},{1,17},{... | collective-permute-start | bytes 1327112 | tf_op jit(solution)/shard_map/ppermute | solution.py:409
  79.6 13.3 %collective-permute-start.13 = (bf16[288,768]{1,0:T(8,128)(2,1)}, bf16[288,768]{1,0:T(8,128)(2,1)}, u32[]{:S(2)}, u32[]{:S(2)}) collective-permute-start(bf16[288,768]{1,0:T(8,128)(2,1)} %collective-permute-done.9.refs_9_), channel_id=1, source_target_pairs={{0,4},{4,0},{8,12},{12,8},{16,20},{20,16},{24,28},{28,24},{1,5},{5... | collective-permute-start | bytes 1327112 | tf_op jit(solution)/shard_map/ppermute | solution.py:409
  80.6 12.3 %collective-permute-start.11 = (bf16[288,768]{1,0:T(8,128)(2,1)}, bf16[288,768]{1,0:T(8,128)(2,1)}, u32[]{:S(2)}, u32[]{:S(2)}) collective-permute-start(bf16[288,768]{1,0:T(8,128)(2,1)} %collective-permute-done.9.refs_9_), channel_id=1, source_target_pairs={{0,16},{4,12},{8,24},{12,4},{16,0},{20,28},{24,8},{28,20},{1,17},{... | collective-permute-start | bytes 1327112 | tf_op jit(solution)/shard_map/ppermute | solution.py:409
  80.7 11.7 %collective-permute-start.14 = (bf16[288,768]{1,0:T(8,128)(2,1)}, bf16[288,768]{1,0:T(8,128)(2,1)}, u32[]{:S(2)}, u32[]{:S(2)}) collective-permute-start(bf16[288,768]{1,0:T(8,128)(2,1)} %collective-permute-done.10.refs_10_), channel_id=1, source_target_pairs={{0,4},{4,0},{8,12},{12,8},{16,20},{20,16},{24,28},{28,24},{1,5},{5... | collective-permute-start | bytes 1327112 | tf_op jit(solution)/shard_map/ppermute | solution.py:409
  134.9 13.1 %collective-permute-start.37 = (bf16[2,288,768]{2,1,0:T(8,128)(2,1)S(1)}, bf16[2,288,768]{2,1,0:T(8,128)(2,1)S(1)}, u32[]{:S(2)}, u32[]{:S(2)}) collective-permute-start(bf16[2,288,768]{2,1,0:T(8,128)(2,1)S(1)} %slice.123), channel_id=1, source_target_pairs={{0,8},{4,20},{8,0},{12,28},{16,24},{20,4},{24,16},{28,12},{1,9},{5... | collective-permute-start | bytes 2654216 | tf_op jit(solution)/shard_map/ppermute | solution.py:409
  136.9 25.4 %collective-permute-start.34 = (bf16[2,288,768]{2,1,0:T(8,128)(2,1)S(1)}, bf16[2,288,768]{2,1,0:T(8,128)(2,1)S(1)}, u32[]{:S(2)}, u32[]{:S(2)}) collective-permute-start(bf16[2,288,768]{2,1,0:T(8,128)(2,1)S(1)} %slice.119), channel_id=1, source_target_pairs={{0,8},{4,20},{8,0},{12,28},{16,24},{20,4},{24,16},{28,12},{1,9},{5... | collective-permute-start | bytes 2654216 | tf_op jit(solution)/shard_map/ppermute | solution.py:409
  138.8 49.7 %collective-permute-start.28 = (bf16[2,288,768]{2,1,0:T(8,128)(2,1)S(1)}, bf16[2,288,768]{2,1,0:T(8,128)(2,1)S(1)}, u32[]{:S(2)}, u32[]{:S(2)}) collective-permute-start(bf16[2,288,768]{2,1,0:T(8,128)(2,1)S(1)} %slice.111), channel_id=1, source_target_pairs={{0,8},{4,20},{8,0},{12,28},{16,24},{20,4},{24,16},{28,12},{1,9},{5... | collective-permute-start | bytes 2654216 | tf_op jit(solution)/shard_map/ppermute | solution.py:409
  141.1 44.9 %collective-permute-start.31 = (bf16[2,288,768]{2,1,0:T(8,128)(2,1)S(1)}, bf16[2,288,768]{2,1,0:T(8,128)(2,1)S(1)}, u32[]{:S(2)}, u32[]{:S(2)}) collective-permute-start(bf16[2,288,768]{2,1,0:T(8,128)(2,1)S(1)} %slice.115), channel_id=1, source_target_pairs={{0,8},{4,20},{8,0},{12,28},{16,24},{20,4},{24,16},{28,12},{1,9},{5... | collective-permute-start | bytes 2654216 | tf_op jit(solution)/shard_map/ppermute | solution.py:409
  148.2 15.8 %collective-permute-start.38 = (bf16[288,768]{1,0:T(8,128)(2,1)S(1)}, bf16[288,768]{1,0:T(8,128)(2,1)S(1)}, u32[]{:S(2)}, u32[]{:S(2)}) collective-permute-start(bf16[288,768]{1,0:T(8,128)(2,1)S(1)} %slice_bitcast_fusion), channel_id=1, source_target_pairs={{0,16},{4,12},{8,24},{12,4},{16,0},{20,28},{24,8},{28,20},{1,17},{... | collective-permute-start | bytes 1327112 | tf_op jit(solution)/shard_map/ppermute | solution.py:409
  162.4 25.3 %collective-permute-start.35 = (bf16[288,768]{1,0:T(8,128)(2,1)S(1)}, bf16[288,768]{1,0:T(8,128)(2,1)S(1)}, u32[]{:S(2)}, u32[]{:S(2)}) collective-permute-start(bf16[288,768]{1,0:T(8,128)(2,1)S(1)} %slice_bitcast_fusion.2), channel_id=1, source_target_pairs={{0,16},{4,12},{8,24},{12,4},{16,0},{20,28},{24,8},{28,20},{1,17},{... | collective-permute-start | bytes 1327112 | tf_op jit(solution)/shard_map/ppermute | solution.py:409
  164.0 23.6 %collective-permute-start.39 = (bf16[288,768]{1,0:T(8,128)(2,1)S(1)}, bf16[288,768]{1,0:T(8,128)(2,1)S(1)}, u32[]{:S(2)}, u32[]{:S(2)}) collective-permute-start(bf16[288,768]{1,0:T(8,128)(2,1)S(1)} %fusion.3), channel_id=1, source_target_pairs={{0,1},{1,2},{2,3},{3,0},{4,5},{5,6},{6,7},{7,4},{8,9},{9,10},{10,1... | collective-permute-start | bytes 1327112 | tf_op jit(solution)/shard_map/ppermute | solution.py:425
  187.8 13.0 %collective-permute-start.40 = (bf16[288,768]{1,0:T(8,128)(2,1)S(1)}, bf16[288,768]{1,0:T(8,128)(2,1)S(1)}, u32[]{:S(2)}, u32[]{:S(2)}) collective-permute-start(bf16[288,768]{1,0:T(8,128)(2,1)S(1)} %fusion.5), channel_id=1, source_target_pairs={{0,1},{1,2},{2,3},{3,0},{4,5},{5,6},{6,7},{7,4},{8,9},{9,10},{10,1... | collective-permute-start | bytes 1327112 | tf_op jit(solution)/shard_map/ppermute | solution.py:425
  188.8 12.1 %collective-permute-start.29 = (bf16[288,768]{1,0:T(8,128)(2,1)S(1)}, bf16[288,768]{1,0:T(8,128)(2,1)S(1)}, u32[]{:S(2)}, u32[]{:S(2)}) collective-permute-start(bf16[288,768]{1,0:T(8,128)(2,1)S(1)} %slice_bitcast_fusion.6), channel_id=1, source_target_pairs={{0,16},{4,12},{8,24},{12,4},{16,0},{20,28},{24,8},{28,20},{1,17},{... | collective-permute-start | bytes 1327112 | tf_op jit(solution)/shard_map/ppermute | solution.py:409
  200.8 12.1 %collective-permute-start.41 = (bf16[288,768]{1,0:T(8,128)(2,1)S(1)}, bf16[288,768]{1,0:T(8,128)(2,1)S(1)}, u32[]{:S(2)}, u32[]{:S(2)}) collective-permute-start(bf16[288,768]{1,0:T(8,128)(2,1)S(1)} %fusion.7), channel_id=1, source_target_pairs={{0,1},{1,2},{2,3},{3,0},{4,5},{5,6},{6,7},{7,4},{8,9},{9,10},{10,1... | collective-permute-start | bytes 1327112 | tf_op jit(solution)/shard_map/ppermute | solution.py:425
  213.8 13.4 %collective-permute-start.42 = (bf16[288,768]{1,0:T(8,128)(2,1)}, bf16[288,768]{1,0:T(8,128)(2,1)}, u32[]{:S(2)}, u32[]{:S(2)}) collective-permute-start(bf16[288,768]{1,0:T(8,128)(2,1)} %fusion.9.refs_0_), channel_id=1, source_target_pairs={{0,8},{4,20},{8,0},{12,28},{16,24},{20,4},{24,16},{28,12},{1,9},{5... | collective-permute-start | bytes 1327112 | tf_op jit(solution)/shard_map/ppermute | solution.py:409
  214.1 51.6 %collective-permute-start.43 = (bf16[288,768]{1,0:T(8,128)(2,1)}, bf16[288,768]{1,0:T(8,128)(2,1)}, u32[]{:S(2)}, u32[]{:S(2)}) collective-permute-start(bf16[288,768]{1,0:T(8,128)(2,1)} %fusion.9.refs_0_), channel_id=1, source_target_pairs={{0,16},{4,12},{8,24},{12,4},{16,0},{20,28},{24,8},{28,20},{1,17},{... | collective-permute-start | bytes 1327112 | tf_op jit(solution)/shard_map/ppermute | solution.py:409
  227.1 38.7 %collective-permute-start.44 = (bf16[288,768]{1,0:T(8,128)(2,1)}, bf16[288,768]{1,0:T(8,128)(2,1)}, u32[]{:S(2)}, u32[]{:S(2)}) collective-permute-start(bf16[288,768]{1,0:T(8,128)(2,1)} %collective-permute-done.42.refs_1_), channel_id=1, source_target_pairs={{0,16},{4,12},{8,24},{12,4},{16,0},{20,28},{24,8},{28,20},{1,17},{... | collective-permute-start | bytes 1327112 | tf_op jit(solution)/shard_map/ppermute | solution.py:409
  265.2 17.7 %collective-permute-start.45 = (bf16[288,768]{1,0:T(8,128)(2,1)}, bf16[288,768]{1,0:T(8,128)(2,1)S(1)}, u32[]{:S(2)}, u32[]{:S(2)}) collective-permute-start(bf16[288,768]{1,0:T(8,128)(2,1)} %fusion.9.refs_0_), channel_id=1, source_target_pairs={{0,4},{4,0},{8,12},{12,8},{16,20},{20,16},{24,28},{28,24},{1,5},{5... | collective-permute-start | bytes 1327112 | tf_op jit(solution)/shard_map/ppermute | solution.py:409
  265.3 17.7 %collective-permute-start.46 = (bf16[288,768]{1,0:T(8,128)(2,1)}, bf16[288,768]{1,0:T(8,128)(2,1)S(1)}, u32[]{:S(2)}, u32[]{:S(2)}) collective-permute-start(bf16[288,768]{1,0:T(8,128)(2,1)} %collective-permute-done.42.refs_1_), channel_id=1, source_target_pairs={{0,4},{4,0},{8,12},{12,8},{16,20},{20,16},{24,28},{28,24},{1,5},{5... | collective-permute-start | bytes 1327112 | tf_op jit(solution)/shard_map/ppermute | solution.py:409
  265.8 17.1 %collective-permute-start.47 = (bf16[288,768]{1,0:T(8,128)(2,1)}, bf16[288,768]{1,0:T(8,128)(2,1)S(1)}, u32[]{:S(2)}, u32[]{:S(2)}) collective-permute-start(bf16[288,768]{1,0:T(8,128)(2,1)} %collective-permute-done.43.refs_2_), channel_id=1, source_target_pairs={{0,4},{4,0},{8,12},{12,8},{16,20},{20,16},{24,28},{28,24},{1,5},{5... | collective-permute-start | bytes 1327112 | tf_op jit(solution)/shard_map/ppermute | solution.py:409
  265.8 17.1 %collective-permute-start.48 = (bf16[288,768]{1,0:T(8,128)(2,1)}, bf16[288,768]{1,0:T(8,128)(2,1)S(1)}, u32[]{:S(2)}, u32[]{:S(2)}) collective-permute-start(bf16[288,768]{1,0:T(8,128)(2,1)} %collective-permute-done.44.refs_3_), channel_id=1, source_target_pairs={{0,4},{4,0},{8,12},{12,8},{16,20},{20,16},{24,28},{28,24},{1,5},{5... | collective-permute-start | bytes 1327112 | tf_op jit(solution)/shard_map/ppermute | solution.py:409
  (80 other events, 958.8 us)
Sparse Core Ops, SparseCore 0:
  299.2 46.8 all-gather.2

commit v4 on v3

--- a/solution.py
+++ b/solution.py
@@ -515,21 +515,28 @@
 
 
 PIECES = SHARDS * REPS
+GROUPS = 9
 ALL_ROWS = PIECES * PIECE
 
 
 def fetch_pieces(ids, blocks, own, shard, held, sems):
-    copies = []
-    for turn, block in enumerate(blocks):
-        row = pl.multiple_of(ids[turn] * PIECE, 16)
-        copies.append(pltpu.make_async_copy(block, held.at[pl.ds(row, PIECE)], sems.at[turn]))
-    row = pl.multiple_of(shard * (REPS * PIECE), 16)
-    copies.append(
-        pltpu.make_async_copy(own, held.at[pl.ds(row, REPS * PIECE)], sems.at[len(blocks)])
-    )
-    for copy in copies:
-        copy.start()
-    return copies
+    views = []
+    for block in blocks:
+        views += [block.at[p] for p in range(4)] if len(block.shape) == 3 else [block]
+    ids = ids + [shard * REPS + r for r in range(REPS)]
+    views += [own.at[pl.ds(r * PIECE, PIECE)] for r in range(REPS)]
+    for which, view in zip(ids, views):
+        row = pl.multiple_of(which * PIECE, 16)
+        pltpu.make_async_copy(view, held.at[pl.ds(row, PIECE)], sems.at[which]).start()
+
+    def arrive(owner):
+        for r in range(REPS):
+            at = owner * REPS + r
+            pltpu.make_async_copy(
+                own.at[pl.ds(0, PIECE)], held.at[pl.ds(at * PIECE, PIECE)], sems.at[at]
+            ).wait()
+
+    return arrive
 
 
 def rows_of(held, shard, begin, rows):
@@ -562,21 +569,21 @@
 
 def gradient_kernel(where, *refs):
     count = PIECES - REPS
-    blocks, own = refs[:count], refs[count]
-    (act_one, act_two, grad_y, vecs, rot_cos, rot_up, rot_down, bias) = refs[count + 1 : count + 9]
-    outs = refs[count + 9 : count + 9 + 13]
+    blocks, own = refs[:GROUPS], refs[GROUPS]
+    (act_one, act_two, grad_y, vecs, rot_cos, rot_up, rot_down, bias) = refs[GROUPS + 1 : GROUPS + 9]
+    outs = refs[GROUPS + 9 : GROUPS + 9 + 14]
     sent, kept = outs[0:4], outs[4:8]
-    attn_out, hidden_out, pre_out, mixed_out, sums_out = outs[8:13]
-    held, grads, query, key, value, grad_attn, sems, out_sems = refs[count + 22 :]
+    matrices, attn_out, hidden_out, pre_out, mixed_out, sums_out = outs[8:14]
+    held, grads, query, key, value, grad_attn, sems, out_sems = refs[GROUPS + 23 :]
     shard = where[0]
-    for copy in fetch_pieces([where[1 + t] for t in range(count)], blocks, own, shard, held, sems):
-        copy.wait()
+    arrive = fetch_pieces([where[1 + t] for t in range(count)], blocks, own, shard, held, sems)
     slot_row = lambda z, r: pl.multiple_of(where[1 + count + z * REPS + r] * PIECE, 16)
 
     def keep_rows(z, begin, rows, part):
         for r in range(part.shape[0] // rows):
             grads[pl.ds(slot_row(z, r) + begin, rows), :] = part[rows * r : rows * (r + 1), :]
 
+    arrive(0)
     act1 = act_one[...]
     for j, out in enumerate((query, key, value)):
         got = dot32(act1, w_qkv_of(held, j)) + vecs[2 + j : 3 + j, :]
@@ -593,8 +600,13 @@
         else:
             out[...] = got.astype(jnp.bfloat16)
     gy_t = grad_y[...].T
+    arrive(1)
     grad_attn[...] = dot32(w_out_of(held), gy_t).T.astype(jnp.bfloat16)
 
+    arrive(2)
+    arrive(3)
+    saving = pltpu.make_async_copy(held, matrices, out_sems.at[PIECES])
+    saving.start()
     low = lax.broadcasted_iota(jnp.int32, (LANES, LANES), 1) < HD
     scale = HD ** (-0.5)
     for p in range(6):
@@ -685,10 +697,11 @@
         copy.start()
     for copy in copies:
         copy.wait()
+    saving.wait()
 
 
 def weight_gradients(scalars, blocks, own, small):
-    hbm = pl.BlockSpec(memory_space=pltpu.HBM)
+    hbm = pl.BlockSpec(memory_space=pl.ANY)
     vmem = pl.BlockSpec(memory_space=pltpu.VMEM)
     bf16 = jnp.bfloat16
     group = jax.ShapeDtypeStruct((4, PIECE, D), bf16)
@@ -697,7 +710,7 @@
         grid_spec=pltpu.PrefetchScalarGridSpec(
             num_scalar_prefetch=1,
             in_specs=[hbm] * (len(blocks) + 1) + [vmem] * len(small),
-            out_specs=[hbm] * 8 + [vmem] * 5,
+            out_specs=[hbm] * 9 + [vmem] * 5,
             scratch_shapes=[
                 pltpu.VMEM((ALL_ROWS, D), bf16),
                 pltpu.VMEM((ALL_ROWS, D), bf16),
@@ -706,11 +719,12 @@
                 pltpu.VMEM((TOK_DEV, D), bf16),
                 pltpu.VMEM((TOK_DEV, D), bf16),
                 pltpu.SemaphoreType.DMA((PIECES,)),
-                pltpu.SemaphoreType.DMA((PIECES,)),
+                pltpu.SemaphoreType.DMA((PIECES + 1,)),
             ],
         ),
         out_shape=[group] * 8
         + [
+            jax.ShapeDtypeStruct((ALL_ROWS, D), bf16),
             jax.ShapeDtypeStruct((TOK_DEV, D), bf16),
             jax.ShapeDtypeStruct((TOK_DEV, FF), bf16),
             jax.ShapeDtypeStruct((TOK_DEV, FF), bf16),
@@ -721,15 +735,16 @@
     )(scalars, *blocks, own, *small)
 
 
-def result_kernel(where, *refs):
-    count = PIECES - REPS
-    blocks, own = refs[:count], refs[count]
-    (tokens, normed, inv_std, grad_y, vecs, attn, hidden, grad_pre, grad_mixed, sums) = refs[
-        count + 1 : count + 11
-    ]
-    output, grad_input, vec_out, held, sems = refs[count + 11 :]
-    shard = where[0]
-    for copy in fetch_pieces([where[1 + t] for t in range(count)], blocks, own, shard, held, sems):
+def result_kernel(matrices, *refs):
+    (tokens, normed, inv_std, grad_y, vecs, attn, hidden, grad_pre, grad_mixed, sums) = refs[:10]
+    output, grad_input, vec_out, held, sems = refs[10:]
+    copies = []
+    for z in range(SHARDS):
+        rows = pl.ds(z * REPS * PIECE, REPS * PIECE)
+        copies.append(pltpu.make_async_copy(matrices.at[rows], held.at[rows], sems.at[z]))
+    for copy in copies:
+        copy.start()
+    for copy in copies:
         copy.wait()
     total = dot32(attn[...], w_out_of(held)) + vecs[5:6, :]
     for j in range(4):
@@ -764,36 +779,70 @@
     vec_out[...] = vec_out[...].astype(jnp.bfloat16).astype(jnp.float32)
 
 
-def layer_results(scalars, blocks, own, small):
-    hbm = pl.BlockSpec(memory_space=pltpu.HBM)
+def layer_results(matrices, small):
+    hbm = pl.BlockSpec(memory_space=pl.ANY)
     vmem = pl.BlockSpec(memory_space=pltpu.VMEM)
     rows = jax.ShapeDtypeStruct((TOK_DEV, D), jnp.float32)
     return pl.pallas_call(
         result_kernel,
+        in_specs=[hbm] + [vmem] * len(small),
+        out_specs=[vmem] * 3,
+        scratch_shapes=[
+            pltpu.VMEM((ALL_ROWS, D), jnp.bfloat16),
+            pltpu.SemaphoreType.DMA((SHARDS,)),
+        ],
+        out_shape=[rows, rows, jax.ShapeDtypeStruct((16, D), jnp.float32)],
+        compiler_params=pltpu.CompilerParams(vmem_limit_bytes=40 * 2**20),
+    )(matrices, *small)
+
+
+SHARE = FLAT_ROWS // REPS
+BEGINS = tuple(SHARE * r // 16 * 16 for r in range(REPS)) + (FLAT_ROWS,)
+SHARE_ROWS = 1760
+STEP = 288
+
+
+def align_kernel(where, one_ref, two_ref, out_ref, held):
+    for r in range(REPS):
+
+        @pl.when(where[0] == r)
+        def _(r=r):
+            lead = SHARE * r - BEGINS[r]
+            for turn, ref in enumerate((one_ref, two_ref)):
+                held[0:16, :] = jnp.zeros((16, LANES), jnp.float32)
+                held[SHARE_ROWS - 32 :, :] = jnp.zeros((32, LANES), jnp.float32)
+                held[lead : lead + SHARE, :] = ref[...]
+                out_ref[turn] = held[...].astype(jnp.bfloat16)
+
+
+def align_moments(moment_one, moment_two, rep):
+    return pl.pallas_call(
+        align_kernel,
         grid_spec=pltpu.PrefetchScalarGridSpec(
             num_scalar_prefetch=1,
-            in_specs=[hbm] * (len(blocks) + 1) + [vmem] * len(small),
-            out_specs=[vmem] * 3,
-            scratch_shapes=[
-                pltpu.VMEM((ALL_ROWS, D), jnp.bfloat16),
-                pltpu.SemaphoreType.DMA((PIECES,)),
-            ],
+            in_specs=[pl.BlockSpec(memory_space=pltpu.VMEM)] * 2,
+            out_specs=pl.BlockSpec(memory_space=pltpu.VMEM),
+            scratch_shapes=[pltpu.VMEM((SHARE_ROWS, LANES), jnp.float32)],
         ),
-        out_shape=[rows, rows, jax.ShapeDtypeStruct((16, D), jnp.float32)],
-        compiler_params=pltpu.CompilerParams(vmem_limit_bytes=40 * 2**20),
-    )(scalars, *blocks, own, *small)
-
-
-def unpack_kernel(factor, where, *refs):
-    vec_ref, out_ref, held, sems = refs[REPS:]
+        out_shape=jax.ShapeDtypeStruct((2, SHARE_ROWS, LANES), jnp.bfloat16),
+        compiler_params=pltpu.CompilerParams(vmem_limit_bytes=16 * 2**20),
+    )(jnp.stack([rep]), moment_one.reshape(SHARE, LANES), moment_two.reshape(SHARE, LANES))
+
+
+def update_kernel(factor, where, *refs):
+    blocks = refs[:REPS]
+    vec_ref, params, moments, grad_out, params_out = refs[REPS : REPS + 5]
+    held, grad, weight, moment, sems, out_sems = refs[REPS + 5 :]
     copies = []
     for turn in range(REPS):
         copies.append(
-            pltpu.make_async_copy(refs[turn], held.at[where[1 + turn]], sems.at[turn])
+            pltpu.make_async_copy(blocks[turn], held.at[where[1 + turn]], sems.at[turn])
         )
+    copies.append(pltpu.make_async_copy(moments, moment, sems.at[REPS]))
+    copies.append(pltpu.make_async_copy(params, weight, sems.at[REPS + 1]))
     for copy in copies:
         copy.start()
-    for copy in copies:
+    for copy in copies[:REPS]:
         copy.wait()
     shard = where[0]
     for z in range(SHARDS):
@@ -802,7 +851,7 @@
         def _(z=z):
             for slot, row in enumerate(VECTOR_ROWS[z]):
                 for col in range(6):
-                    out_ref[6 * row + col : 6 * row + col + 1, :] = (
+                    grad[6 * row + col : 6 * row + col + 1, :] = (
                         vec_ref[slot : slot + 1, LANES * col : LANES * (col + 1)] * factor
                     )
 
@@ -817,27 +866,68 @@
                                 LANES * col : LANES * (col + 1),
                             ]
                             begin = first + step * rep + 6 * block + col
-                            out_ref[pl.ds(begin, rows, stride=6 * blocks), :] = (
+                            grad[pl.ds(begin, rows, stride=6 * blocks), :] = (
                                 got.astype(jnp.float32) * factor
                             )
 
-
-def unpack_grads(blocks, ids, vectors, shard, factor):
+    saving = [pltpu.make_async_copy(grad, grad_out, out_sems.at[REPS])]
+    saving[0].start()
+    for copy in copies[REPS:]:
+        copy.wait()
+    for r in range(REPS):
+        base = BEGINS[r]
+        length = BEGINS[r + 1] - base
+        if r > 0:
+            tail = base - BEGINS[r - 1]
+            moment[r, :, 0:16, :] = moment[r, :, 0:16, :] + moment[r - 1, :, tail : tail + 16, :]
+
+        def renew(at, rows, r=r, base=base):
+            here = pl.ds(pl.multiple_of(base + at, 8), rows)
+            there = pl.ds(pl.multiple_of(at, 16), rows)
+            updated, _, _ = adam_update(
+                weight[here, :],
+                moment[r, 0, there, :].astype(jnp.float32),
+                moment[r, 1, there, :].astype(jnp.float32),
+                grad[here, :],
+            )
+            weight[here, :] = updated
+
+        @pl.loop(0, length // STEP)
+        def _(turn):
+            renew(turn * STEP, STEP)
+
+        if length % STEP:
+            renew(length // STEP * STEP, length % STEP)
+        rows = pl.ds(base, length)
+        saving.append(
+            pltpu.make_async_copy(weight.at[rows], params_out.at[rows], out_sems.at[r])
+        )
+        saving[-1].start()
+    for copy in saving:
+        copy.wait()
+
+
+def update_shard(blocks, ids, vectors, params, moments, shard, factor):
+    anywhere = pl.BlockSpec(memory_space=pl.ANY)
+    flat = jax.ShapeDtypeStruct((FLAT_ROWS, LANES), jnp.float32)
     return pl.pallas_call(
-        functools.partial(unpack_kernel, factor),
+        functools.partial(update_kernel, factor),
         grid_spec=pltpu.PrefetchScalarGridSpec(
             num_scalar_prefetch=1,
-            in_specs=[pl.BlockSpec(memory_space=pltpu.HBM)] * REPS
-            + [pl.BlockSpec(memory_space=pltpu.VMEM)],
-            out_specs=pl.BlockSpec(memory_space=pltpu.VMEM),
+            in_specs=[anywhere] * REPS + [pl.BlockSpec(memory_space=pltpu.VMEM)] + [anywhere] * 2,
+            out_specs=[anywhere] * 2,
             scratch_shapes=[
                 pltpu.VMEM((REPS, PIECE, D), jnp.bfloat16),
-                pltpu.SemaphoreType.DMA((REPS,)),
+                pltpu.VMEM((FLAT_ROWS, LANES), jnp.float32),
+                pltpu.VMEM((FLAT_ROWS, LANES), jnp.float32),
+                pltpu.VMEM((REPS, 2, SHARE_ROWS, LANES), jnp.bfloat16),
+                pltpu.SemaphoreType.DMA((REPS + 2,)),
+                pltpu.SemaphoreType.DMA((REPS + 1,)),
             ],
         ),
-        out_shape=jax.ShapeDtypeStruct((FLAT_ROWS, LANES), jnp.float32),
-        compiler_params=pltpu.CompilerParams(vmem_limit_bytes=32 * 2**20),
-    )(jnp.stack([shard] + ids), *blocks, vectors)
+        out_shape=[flat, flat],
+        compiler_params=pltpu.CompilerParams(vmem_limit_bytes=40 * 2**20),
+    )(jnp.stack([shard] + ids), *blocks, vectors, params.reshape(FLAT_ROWS, LANES), moments)
 
 
 def gather_matrices(params, shard, rep):
@@ -848,29 +938,37 @@
     for hop in range(1, SHARDS):
         piece = ring_step(piece)
         owner = (shard + SHARDS - hop) % SHARDS
-        blocks += spread_in_plane(piece)
+        if hop < SHARDS - 1:
+            first = first_cross(piece)
+            mine = jnp.stack([piece, first, second_cross(piece), second_cross(first)])
+            blocks += [mine, core_cross(mine)]
+        else:
+            blocks += spread_in_plane(piece)
         ids += [owner * REPS + which for which in reps]
-    return blocks, own.reshape(REPS * PIECE, D), ids
+    mine = jnp.stack(blocks[4:8])
+    return blocks[:4] + [mine] + blocks[8:], own.reshape(REPS * PIECE, D), ids
+
+
+def ring_shift(value, hop):
+    return lax.ppermute(value, "z", [(i, (i + hop) % SHARDS) for i in range(SHARDS)])
 
 
 def gather_vectors(params, shard):
-    mine = shard_vectors(params, shard)
-    held = [mine.astype(jnp.bfloat16)]
-    for _ in range(1, SHARDS):
-        held.append(ring_step(held[-1]))
+    mine = shard_vectors(params, shard).astype(jnp.bfloat16)
+    held = [mine] + [ring_shift(mine, hop) for hop in range(1, SHARDS)]
     turned = jnp.stack(held).astype(jnp.float32)
     order = (shard + SHARDS - jnp.arange(SHARDS)) % SHARDS
     return jnp.take(turned, order, axis=0).reshape(16, D)
 
 
-def sum_everywhere(value):
+def sum_in_plane(value):
     for flips in ((1, 1), (2, 2), (4, 4)):
         value = value + plane_permute(value, flips)
-    total, moving = value, value
-    for _ in range(1, SHARDS):
-        moving = ring_step(moving)
-        total = total + moving
-    return total
+    return value
+
+
+def sum_over_shards(value):
+    return value + ring_shift(value, 1) + ring_shift(value, 2) + ring_shift(value, 3)
 
 
 def slots_by_piece(shard, rep):
@@ -890,17 +988,28 @@
     return slots
 
 
-def scatter_sums(sent, kept):
+def scatter_sums(sent, kept, small, results):
     carried = None
     for turn in range(SHARDS):
         chip = kept[turn] + core_cross(sent[turn])
         pair = chip[2:4] + first_cross(chip[0:2])
+        if turn == 0:
+            pair, small = lax.optimization_barrier((pair, small))
+            output, grad_input, vectors = results(small)
+        elif turn == 1:
+            pair, vectors = lax.optimization_barrier((pair, vectors))
+            vectors = sum_in_plane(vectors)
+        elif turn == 2:
+            pair, vectors = lax.optimization_barrier((pair, vectors))
+            vectors = sum_over_shards(vectors)
+        else:
+            pair, vectors = lax.optimization_barrier((pair, vectors))
         total = pair[0] + second_cross(pair[1])
         if carried is not None:
             total = total + carried
         if turn < SHARDS - 1:
             carried = ring_step(total)
-    return total
+    return total, output, grad_input, vectors
 
 
 def shard_vectors(params, shard):
@@ -936,27 +1045,34 @@
     )
     scalars = jnp.stack([shard] + ids + slots_by_piece(shard, rep))
     small = (act_one, act_two, grad_y, vecs, rot_cos, rot_up, rot_down, allowed.astype(jnp.float32))
+    moments = align_moments(moment_one, moment_two, rep).reshape(2 * SHARE_ROWS, LANES)
+    moments, blocks[-1] = lax.optimization_barrier((moments, blocks[-1]))
+    moments = lax.all_gather(moments, PLANE, axis=0, tiled=True)
     made = weight_gradients(scalars, blocks, own, small)
     sent, kept = made[0:4], made[4:8]
-    attn, hidden, grad_pre, grad_mixed, sums = made[8:]
-    owned = scatter_sums(sent, kept)
-    small = (tokens, normed, inv_std, grad_y, vecs, attn, hidden, grad_pre, grad_mixed, sums)
-    output, grad_input, vec_grads = layer_results(scalars, blocks, own, small)
-    vec_grads = sum_everywhere(vec_grads)
+    matrices = made[8]
+    small = (tokens, normed, inv_std, grad_y, vecs) + tuple(made[9:])
+    owned, output, grad_input, vec_grads = scatter_sums(
+        sent, kept, small, lambda small: layer_results(matrices, small)
+    )
     own_vectors = lax.dynamic_index_in_dim(
         vec_grads.reshape(SHARDS, 4, D), shard, 0, keepdims=False
     )
     tokens_all = tokens.shape[0] * lax.axis_size(EVERY)
-    grad_params = unpack_grads(
-        spread_in_plane(owned), spread_ids(rep), own_vectors, shard, 1.0 / math.sqrt(tokens_all)
-    ).reshape(-1)
+    grad_params, new_params = update_shard(
+        spread_in_plane(owned),
+        spread_ids(rep),
+        own_vectors,
+        params,
+        moments.reshape(REPS, 2, SHARE_ROWS, LANES),
+        shard,
+        1.0 / math.sqrt(tokens_all),
+    )
+    grad_params = grad_params.reshape(-1)
     width = moment_one.shape[0]
-    begin = rep * width
-    param_share = lax.dynamic_slice_in_dim(params, begin, width)
-    grad_share = lax.dynamic_slice_in_dim(grad_params, begin, width)
-    upd_params, upd_first, upd_second = adam_update(param_share, moment_one, moment_two, grad_share)
-    new_params = lax.all_gather(upd_params, PLANE, axis=0, tiled=True)
-    return (output, grad_input, grad_params, new_params, upd_first, upd_second)
+    grad_share = lax.dynamic_slice_in_dim(grad_params, rep * width, width)
+    _, upd_first, upd_second = adam_update(moment_one, moment_one, moment_two, grad_share)
+    return (output, grad_input, grad_params, new_params.reshape(-1), upd_first, upd_second)
 
 
 def solution(mesh):

time: 359 us -> 352 us (0.981)
  waiting for transfers between devices: 196 us -> 176 us
  local copies, waits for them, and re-layouts: 44.1 us -> 29.4 us
  Pallas kernels: 49.3 us -> 61.2 us
  other arithmetic: 12.3 us -> 22.4 us
  starting transfers between devices: 38.5 us -> 44 us
    all_gather x1, waiting for transfers between devices: 47 us -> 0.02 us  [on_device_rows(): moments = lax.all_gather(moments, PLANE, axis=0, tiled=True)]
    unnamed x114 -> x66, local copies, waits for them, and re-layouts: 36.6 us -> 17.1 us
    ppermute x43 -> x37, waiting for transfers between devices: 93.4 us -> 112 us  [plane_permute(): lax.ppermute(value, PLANE, [(i, i ^ flips[i % 2]) for i in range(REPS)])]
    ppermute x0 -> x6, waiting for transfers between devices: none -> 10.9 us  [ring_shift(): lax.ppermute(value, 'z', [(i, (i + hop) % SHARDS) for i in range(SHARDS)])]
    ppermute x0 -> x6, starting transfers between devices: none -> 7.38 us  [ring_shift(): lax.ppermute(value, 'z', [(i, (i + hop) % SHARDS) for i in range(SHARDS)])]
    pallas_call x2 -> x3, Pallas kernels: 17.4 us -> 24.6 us  [the longest x1 14.1 us: update_shard(): pl.pallas_call(functools.partial(update_kernel, factor), grid_spec=pltpu....]
    another operation x3 -> x6, other arithmetic: 0.35 us -> 7.14 us  [the longest x2 4.08 us: gather_matrices(): mine = jnp.stack([piece, first, second_cross(piece), second_cross(first)])]
    add x4, other arithmetic: 0.4 us -> 4.97 us  [scatter_sums(): pair = chip[2:4] + first_cross(chip[0:2])]
  transfers between devices with their start and end apart: 56 -> 50, of which waited for: 26 -> 23; matrix products, arithmetic and copies ran while one was open for 4% -> 9% of each run, Pallas kernels for 4% -> 13%
where the time goes in v4:
time: 352 us; the launch traced here: 351 us
  waiting for transfers between devices  176 us (50%)
  Pallas kernels  61.2 us (17%)
  starting transfers between devices  44 us (12%)
  local copies, waits for them, and re-layouts  29.4 us (8%)
  other arithmetic  22.4 us (6%)
  between operations  17.7 us (5%)
    ppermute x37, waiting for transfers between devices, plane_permute(): lax.ppermute(value, PLANE, [(i, i ^ flips[i % 2]) for i in range(REPS)])  112 us
    ppermute x6, waiting for transfers between devices, ring_step(): lax.ppermute(value, 'z', [(i, (i + 1) % SHARDS) for i in range(SHARDS)])  53 us
    pallas_call x1, Pallas kernels, weight_gradients(): pl.pallas_call(gradient_kernel, grid_spec=pltpu.PrefetchScalarGridSpec(nu...  32.7 us
    ppermute x37, starting transfers between devices, plane_permute(): lax.ppermute(value, PLANE, [(i, i ^ flips[i % 2]) for i in range(REPS)])  27 us
    unnamed x66, local copies, waits for them, and re-layouts  17.1 us
    pallas_call x1, Pallas kernels, update_shard(): pl.pallas_call(functools.partial(update_kernel, factor), grid_spec=pltpu....  14.1 us
    ppermute x6, waiting for transfers between devices, ring_shift(): lax.ppermute(value, 'z', [(i, (i + hop) % SHARDS) for i in range(SHARDS)])  10.9 us
    ppermute x6, starting transfers between devices, ring_step(): lax.ppermute(value, 'z', [(i, (i + 1) % SHARDS) for i in range(SHARDS)])  9.58 us
  transfers between devices with their start and end apart: 50, of which 23 were waited for; matrix products, arithmetic and copies ran while one was open for 9% of the time, Pallas kernels for 13%

profile of v4, /device:TPU:0, one launch (start us, length us, event | category | flops | bytes accessed | tf_op | source)
XLA Modules:
  0.0 350.8 jit_solution(3404588008188133722)
XLA Ops:
  7.3 3.0 copy-done
  11.2 3.1 collective-permute-start
  14.3 12.2 %collective-permute-done = bf16[288,768]{1,0:T(8,128)(2,1)} collective-permute-done((bf16[288,768]{1,0:T(8,128)(2,1)S(1)}, bf16[288,768]{1,0:T(8,128)(2,1)}, u32[]{:S(2)}, u32[]{:S(2)}) %collective-permute-start) | collective-permute-done | bytes 442400 | tf_op jit(solution)/shard_map/ppermute | solution.py:425
  26.6 13.4 %collective-permute-done.5 = bf16[288,768]{1,0:T(8,128)(2,1)S(1)} collective-permute-done((bf16[288,768]{1,0:T(8,128)(2,1)}, bf16[288,768]{1,0:T(8,128)(2,1)S(1)}, u32[]{:S(2)}, u32[]{:S(2)}) %collective-permute-start.5) | collective-permute-done | bytes 442400 | tf_op jit(solution)/shard_map/ppermute | solution.py:425
  39.9 12.2 %collective-permute-done.10 = bf16[288,768]{1,0:T(8,128)(2,1)S(1)} collective-permute-done((bf16[288,768]{1,0:T(8,128)(2,1)S(1)}, bf16[288,768]{1,0:T(8,128)(2,1)S(1)}, u32[]{:S(2)}, u32[]{:S(2)}) %collective-permute-start.10) | collective-permute-done | bytes 442400 | tf_op jit(solution)/shard_map/ppermute | solution.py:425
  53.1 7.9 %collective-permute-done.11 = bf16[288,768]{1,0:T(8,128)(2,1)} collective-permute-done((bf16[288,768]{1,0:T(8,128)(2,1)S(1)}, bf16[288,768]{1,0:T(8,128)(2,1)}, u32[]{:S(2)}, u32[]{:S(2)}) %collective-permute-start.11) | collective-permute-done | bytes 442400 | tf_op jit(solution)/shard_map/ppermute | solution.py:409
  62.3 7.3 %collective-permute-done.13 = bf16[288,768]{1,0:T(8,128)(2,1)S(1)} collective-permute-done((bf16[288,768]{1,0:T(8,128)(2,1)}, bf16[288,768]{1,0:T(8,128)(2,1)S(1)}, u32[]{:S(2)}, u32[]{:S(2)}) %collective-permute-start.13) | collective-permute-done | bytes 442400 | tf_op jit(solution)/shard_map/ppermute | solution.py:409
  81.7 17.4 %collective-permute-done.1 = bf16[288,768]{1,0:T(8,128)(2,1)} collective-permute-done((bf16[288,768]{1,0:T(8,128)(2,1)}, bf16[288,768]{1,0:T(8,128)(2,1)}, u32[]{:S(2)}, u32[]{:S(2)}) %collective-permute-start.1) | collective-permute-done | bytes 442400 | tf_op jit(solution)/shard_map/ppermute | solution.py:409
  101.2 8.6 %collective-permute-done.6 = bf16[288,768]{1,0:T(8,128)(2,1)S(1)} collective-permute-done((bf16[288,768]{1,0:T(8,128)(2,1)S(1)}, bf16[288,768]{1,0:T(8,128)(2,1)S(1)}, u32[]{:S(2)}, u32[]{:S(2)}) %collective-permute-start.6) | collective-permute-done | bytes 442400 | tf_op jit(solution)/shard_map/ppermute | solution.py:409
  112.6 2.6 pad_maximum_fusion.refs_0_
  115.1 11.5 %collective-permute-done.7 = bf16[288,768]{1,0:T(8,128)(2,1)S(1)} collective-permute-done((bf16[288,768]{1,0:T(8,128)(2,1)S(1)}, bf16[288,768]{1,0:T(8,128)(2,1)S(1)}, u32[]{:S(2)}, u32[]{:S(2)}) %collective-permute-start.7) | collective-permute-done | bytes 442400 | tf_op jit(solution)/shard_map/ppermute | solution.py:409
  126.7 10.9 %collective-permute-done.8 = bf16[288,768]{1,0:T(8,128)(2,1)S(1)} collective-permute-done((bf16[288,768]{1,0:T(8,128)(2,1)S(1)}, bf16[288,768]{1,0:T(8,128)(2,1)S(1)}, u32[]{:S(2)}, u32[]{:S(2)}) %collective-permute-start.8) | collective-permute-done | bytes 442400 | tf_op jit(solution)/shard_map/ppermute | solution.py:409
  142.9 3.4 collective-permute-start.20
  146.4 3.0 copy-done.1
  149.4 3.0 shard_map.120
  159.6 2.7 pad_maximum_fusion.2.refs_4_
  163.4 32.7 %shard_map.121 = (bf16[4,288,768]{2,1,0:T(8,128)(2,1)}, bf16[4,288,768]{2,1,0:T(8,128)(2,1)}, bf16[4,288,768]{2,1,0:T(8,128)(2,1)}, bf16[4,288,768]{2,1,0:T(8,12...) custom-call(s32[57]{0:T(128)} %stack.357.where, ...), custom_call_target="tpu_custom_call" | custom-call | tf_op jit(solution)/shard_map/pallas_call | solution.py:708
  197.5 2.9 collective-permute-done.21
  200.4 1.9 add.671
  212.5 3.0 collective-permute-done.22
  219.8 9.4 %shard_map.122 = (f32[128,768]{1,0:T(8,128)}, f32[128,768]{1,0:T(8,128)}, f32[16,768]{1,0:T(8,128)S(1)}) custom-call(bf16[9216,768]{1,0:T(8,128)(2,1)} %get-tuple-element.45.matrices, bf16[128,768]{1,0:T(8,128)(2,1)S(1)} %copy-done.6, f32[128,768]{1,0:T(8,128)S(1)} %get-tuple-element.54.refs_1_, f32[128,1]{1,0:T(8,128)S(1)} %copy.19.refs_2_, ...), custom_call_target="tpu_custom_call" | custom-call | tf_op jit(solution)/shard_map/pallas_call | solution.py:786
  236.4 18.1 %collective-permute-done.30 = f32[16,768]{1,0:T(8,128)S(1)} collective-permute-done((f32[16,768]{1,0:T(8,128)S(1)}, f32[16,768]{1,0:T(8,128)S(1)}, u32[]{:S(2)}, u32[]{:S(2)}) %collective-permute-start.30) | collective-permute-done | bytes 49184 | tf_op jit(solution)/shard_map/ppermute | solution.py:409
  258.7 2.8 collective-permute-start.33
  263.7 7.0 %collective-permute-done.39 = bf16[288,768]{1,0:T(8,128)(2,1)S(1)} collective-permute-done((bf16[288,768]{1,0:T(8,128)(2,1)S(1)}, bf16[288,768]{1,0:T(8,128)(2,1)S(1)}, u32[]{:S(2)}, u32[]{:S(2)}) %collective-permute-start.39) | collective-permute-done | bytes 442400 | tf_op jit(solution)/shard_map/ppermute | solution.py:425
  271.2 10.5 %collective-permute-done.33 = f32[16,768]{1,0:T(8,128)S(1)} collective-permute-done((f32[16,768]{1,0:T(8,128)S(1)}, f32[16,768]{1,0:T(8,128)S(1)}, u32[]{:S(2)}, u32[]{:S(2)}) %collective-permute-start.33) | collective-permute-done | bytes 49184 | tf_op jit(solution)/shard_map/ppermute | solution.py:953
  283.5 6.3 %collective-permute-start.41 = (bf16[288,768]{1,0:T(8,128)(2,1)S(1)}, bf16[288,768]{1,0:T(8,128)(2,1)S(1)}, u32[]{:S(2)}, u32[]{:S(2)}) collective-permute-start(bf16[288,768]{1,0:T(8,128)(2,1)S(1)} %fusion.4), channel_id=1, source_target_pairs={{0,1},{1,2},{2,3},{3,0},{4,5},{5,6},{6,7},{7,4},{8,9},{9,10},{10,1... | collective-permute-start | bytes 1327112 | tf_op jit(solution)/shard_map/ppermute | solution.py:425
  290.8 8.2 %collective-permute-done.41 = bf16[288,768]{1,0:T(8,128)(2,1)S(1)} collective-permute-done((bf16[288,768]{1,0:T(8,128)(2,1)S(1)}, bf16[288,768]{1,0:T(8,128)(2,1)S(1)}, u32[]{:S(2)}, u32[]{:S(2)}) %collective-permute-start.41) | collective-permute-done | bytes 442400 | tf_op jit(solution)/shard_map/ppermute | solution.py:425
  301.3 10.7 %collective-permute-done.42.refs_1_ = bf16[288,768]{1,0:T(8,128)(2,1)S(1)} collective-permute-done((bf16[288,768]{1,0:T(8,128)(2,1)S(1)}, bf16[288,768]{1,0:T(8,128)(2,1)S(1)}, u32[]{:S(2)}, u32[]{:S(2)}) %collective-permute-start.42) | collective-permute-done | bytes 442400 | tf_op jit(solution)/shard_map/ppermute | solution.py:409
  312.6 7.8 %collective-permute-done.44.refs_3_ = bf16[288,768]{1,0:T(8,128)(2,1)S(1)} collective-permute-done((bf16[288,768]{1,0:T(8,128)(2,1)S(1)}, bf16[288,768]{1,0:T(8,128)(2,1)S(1)}, u32[]{:S(2)}, u32[]{:S(2)}) %collective-permute-start.44) | collective-permute-done | bytes 442400 | tf_op jit(solution)/shard_map/ppermute | solution.py:409
  323.3 3.0 copy-done.2
  327.0 14.1 %shard_map.123 = (f32[13848,128]{1,0:T(8,128)}, f32[13848,128]{1,0:T(8,128)}) custom-call(s32[9]{0:T(128)S(1)} %stack.397.where, bf16[288,768]{1,0:T(8,128)(2,1)S(1)} %fusion.5.refs_0_, bf16[288,768]{1,0:T(8,128)(2,1)S(1)} %collective-permute-done.42.refs_1_, bf16[288,768]{1,0:T(8,128)(2,1)S(1)} %collective-permute-done.43.refs_2_, ...), custom_call_target="tpu_custom_call" | custom-call | tf_op jit(solution)/shard_map/pallas_call | solution.py:913
  341.2 2.8 fusion
  (219 shorter events, 69.4 us)
Async XLA Ops:
  7.2 316.1 %all-gather.2.cloned.1.call-start = ((), (), s32[]{:S(2)}) async-start(), calls=%async_computation | async-start | bytes 8110080 | tf_op jit(solution)/shard_map/all_gather | solution.py:1050
  11.2 15.4 %collective-permute-start = (bf16[288,768]{1,0:T(8,128)(2,1)S(1)}, bf16[288,768]{1,0:T(8,128)(2,1)}, u32[]{:S(2)}, u32[]{:S(2)}) collective-permute-start(bf16[288,768]{1,0:T(8,128)(2,1)S(1)} %bitcast.130), channel_id=1, source_target_pairs={{0,1},{1,2},{2,3},{3,0},{4,5},{5,6},{6,7},{7,4},{8,9},{9,10},{10,1... | collective-permute-start | bytes 1327112 | tf_op jit(solution)/shard_map/ppermute | solution.py:425
  26.6 13.4 %collective-permute-start.5 = (bf16[288,768]{1,0:T(8,128)(2,1)}, bf16[288,768]{1,0:T(8,128)(2,1)S(1)}, u32[]{:S(2)}, u32[]{:S(2)}) collective-permute-start(bf16[288,768]{1,0:T(8,128)(2,1)} %collective-permute-done), channel_id=1, source_target_pairs={{0,1},{1,2},{2,3},{3,0},{4,5},{5,6},{6,7},{7,4},{8,9},{9,10},{10,1... | collective-permute-start | bytes 1327112 | tf_op jit(solution)/shard_map/ppermute | solution.py:425
  39.9 12.2 %collective-permute-start.10 = (bf16[288,768]{1,0:T(8,128)(2,1)S(1)}, bf16[288,768]{1,0:T(8,128)(2,1)S(1)}, u32[]{:S(2)}, u32[]{:S(2)}) collective-permute-start(bf16[288,768]{1,0:T(8,128)(2,1)S(1)} %collective-permute-done.5), channel_id=1, source_target_pairs={{0,1},{1,2},{2,3},{3,0},{4,5},{5,6},{6,7},{7,4},{8,9},{9,10},{10,1... | collective-permute-start | bytes 1327112 | tf_op jit(solution)/shard_map/ppermute | solution.py:425
  77.0 65.9 %collective-permute-start.18 = (bf16[4,768]{1,0:T(4,128)(2,1)S(1)}, bf16[4,768]{1,0:T(4,128)(2,1)S(1)}, u32[]{:S(2)}, u32[]{:S(2)}) collective-permute-start(bf16[4,768]{1,0:T(4,128)(2,1)S(1)} %pad_maximum_fusion.3), channel_id=1, source_target_pairs={{0,1},{1,2},{2,3},{3,0},{4,5},{5,6},{6,7},{7,4},{8,9},{9,10},{10,1... | collective-permute-start | bytes 18440 | tf_op jit(solution)/shard_map/ppermute | solution.py:953
  77.2 21.9 %collective-permute-start.1 = (bf16[288,768]{1,0:T(8,128)(2,1)}, bf16[288,768]{1,0:T(8,128)(2,1)}, u32[]{:S(2)}, u32[]{:S(2)}) collective-permute-start(bf16[288,768]{1,0:T(8,128)(2,1)} %collective-permute-done), channel_id=1, source_target_pairs={{0,8},{4,20},{8,0},{12,28},{16,24},{20,4},{24,16},{28,12},{1,9},{5... | collective-permute-start | bytes 1327112 | tf_op jit(solution)/shard_map/ppermute | solution.py:409
  79.3 30.5 %collective-permute-start.6 = (bf16[288,768]{1,0:T(8,128)(2,1)S(1)}, bf16[288,768]{1,0:T(8,128)(2,1)S(1)}, u32[]{:S(2)}, u32[]{:S(2)}) collective-permute-start(bf16[288,768]{1,0:T(8,128)(2,1)S(1)} %collective-permute-done.5), channel_id=1, source_target_pairs={{0,8},{4,20},{8,0},{12,28},{16,24},{20,4},{24,16},{28,12},{1,9},{5... | collective-permute-start | bytes 1327112 | tf_op jit(solution)/shard_map/ppermute | solution.py:409
  80.3 30.4 %collective-permute-start.2 = (bf16[288,768]{1,0:T(8,128)(2,1)}, bf16[288,768]{1,0:T(8,128)(2,1)S(1)}, u32[]{:S(2)}, u32[]{:S(2)}) collective-permute-start(bf16[288,768]{1,0:T(8,128)(2,1)} %collective-permute-done), channel_id=1, source_target_pairs={{0,16},{4,12},{8,24},{12,4},{16,0},{20,28},{24,8},{28,20},{1,17},{... | collective-permute-start | bytes 1327112 | tf_op jit(solution)/shard_map/ppermute | solution.py:409
  99.1 13.5 %collective-permute-start.3 = (bf16[288,768]{1,0:T(8,128)(2,1)}, bf16[288,768]{1,0:T(8,128)(2,1)S(1)}, u32[]{:S(2)}, u32[]{:S(2)}) collective-permute-start(bf16[288,768]{1,0:T(8,128)(2,1)} %collective-permute-done.1), channel_id=1, source_target_pairs={{0,16},{4,12},{8,24},{12,4},{16,0},{20,28},{24,8},{28,20},{1,17},{... | collective-permute-start | bytes 1327112 | tf_op jit(solution)/shard_map/ppermute | solution.py:409
  100.5 26.1 %collective-permute-start.7 = (bf16[288,768]{1,0:T(8,128)(2,1)S(1)}, bf16[288,768]{1,0:T(8,128)(2,1)S(1)}, u32[]{:S(2)}, u32[]{:S(2)}) collective-permute-start(bf16[288,768]{1,0:T(8,128)(2,1)S(1)} %collective-permute-done.5), channel_id=1, source_target_pairs={{0,16},{4,12},{8,24},{12,4},{16,0},{20,28},{24,8},{28,20},{1,17},{... | collective-permute-start | bytes 1327112 | tf_op jit(solution)/shard_map/ppermute | solution.py:409
  109.8 27.8 %collective-permute-start.8 = (bf16[288,768]{1,0:T(8,128)(2,1)S(1)}, bf16[288,768]{1,0:T(8,128)(2,1)S(1)}, u32[]{:S(2)}, u32[]{:S(2)}) collective-permute-start(bf16[288,768]{1,0:T(8,128)(2,1)S(1)} %collective-permute-done.6), channel_id=1, source_target_pairs={{0,16},{4,12},{8,24},{12,4},{16,0},{20,28},{24,8},{28,20},{1,17},{... | collective-permute-start | bytes 1327112 | tf_op jit(solution)/shard_map/ppermute | solution.py:409
  110.7 46.6 %collective-permute-start.19 = (bf16[4,768]{1,0:T(4,128)(2,1)S(1)}, bf16[4,768]{1,0:T(4,128)(2,1)S(1)}, u32[]{:S(2)}, u32[]{:S(2)}) collective-permute-start(bf16[4,768]{1,0:T(4,128)(2,1)S(1)} %pad_maximum_fusion.3), channel_id=1, source_target_pairs={{0,2},{1,3},{2,0},{3,1},{4,6},{5,7},{6,4},{7,5},{8,10},{9,11},{10,... | collective-permute-start | bytes 18440 | tf_op jit(solution)/shard_map/ppermute | solution.py:953
  115.1 47.3 %collective-permute-start.4 = (bf16[4,288,768]{2,1,0:T(8,128)(2,1)}, bf16[4,288,768]{2,1,0:T(8,128)(2,1)}, u32[]{:S(2)}, u32[]{:S(2)}) collective-permute-start(bf16[4,288,768]{2,1,0:T(8,128)(2,1)} %pad_maximum_fusion.refs_0_), channel_id=1, source_target_pairs={{0,4},{4,0},{8,12},{12,8},{16,20},{20,16},{24,28},{28,24},{1,5},{5... | collective-permute-start | bytes 5308424 | tf_op jit(solution)/shard_map/ppermute | solution.py:409
  139.1 23.3 %collective-permute-start.9 = (bf16[4,288,768]{2,1,0:T(8,128)(2,1)}, bf16[4,288,768]{2,1,0:T(8,128)(2,1)}, u32[]{:S(2)}, u32[]{:S(2)}) collective-permute-start(bf16[4,288,768]{2,1,0:T(8,128)(2,1)} %pad_maximum_fusion.1.refs_2_), channel_id=1, source_target_pairs={{0,4},{4,0},{8,12},{12,8},{16,20},{20,16},{24,28},{28,24},{1,5},{5... | collective-permute-start | bytes 5308424 | tf_op jit(solution)/shard_map/ppermute | solution.py:409
  141.2 17.4 %collective-permute-start.12 = (bf16[288,768]{1,0:T(8,128)(2,1)S(1)}, bf16[288,768]{1,0:T(8,128)(2,1)}, u32[]{:S(2)}, u32[]{:S(2)}) collective-permute-start(bf16[288,768]{1,0:T(8,128)(2,1)S(1)} %collective-permute-done.10), channel_id=1, source_target_pairs={{0,16},{4,12},{8,24},{12,4},{16,0},{20,28},{24,8},{28,20},{1,17},{... | collective-permute-start | bytes 1327112 | tf_op jit(solution)/shard_map/ppermute | solution.py:409
  142.9 14.4 %collective-permute-start.20 = (bf16[4,768]{1,0:T(4,128)(2,1)S(1)}, bf16[4,768]{1,0:T(4,128)(2,1)S(1)}, u32[]{:S(2)}, u32[]{:S(2)}) collective-permute-start(bf16[4,768]{1,0:T(4,128)(2,1)S(1)} %pad_maximum_fusion.3), channel_id=1, source_target_pairs={{0,3},{1,0},{2,1},{3,2},{4,7},{5,4},{6,5},{7,6},{8,11},{9,8},{10,9... | collective-permute-start | bytes 18440 | tf_op jit(solution)/shard_map/ppermute | solution.py:953
  202.4 13.1 %collective-permute-start.22 = (bf16[2,288,768]{2,1,0:T(8,128)(2,1)S(1)}, bf16[2,288,768]{2,1,0:T(8,128)(2,1)S(1)}, u32[]{:S(2)}, u32[]{:S(2)}) collective-permute-start(bf16[2,288,768]{2,1,0:T(8,128)(2,1)S(1)} %slice.111), channel_id=1, source_target_pairs={{0,8},{4,20},{8,0},{12,28},{16,24},{20,4},{24,16},{28,12},{1,9},{5... | collective-permute-start | bytes 2654216 | tf_op jit(solution)/shard_map/ppermute | solution.py:409
  205.3 23.9 %collective-permute-start.28 = (bf16[2,288,768]{2,1,0:T(8,128)(2,1)}, bf16[2,288,768]{2,1,0:T(8,128)(2,1)}, u32[]{:S(2)}, u32[]{:S(2)}) collective-permute-start(bf16[2,288,768]{2,1,0:T(8,128)(2,1)} %slice.117), channel_id=1, source_target_pairs={{0,8},{4,20},{8,0},{12,28},{16,24},{20,4},{24,16},{28,12},{1,9},{5... | collective-permute-start | bytes 2654216 | tf_op jit(solution)/shard_map/ppermute | solution.py:409
  208.2 26.9 %collective-permute-start.26 = (bf16[2,288,768]{2,1,0:T(8,128)(2,1)}, bf16[2,288,768]{2,1,0:T(8,128)(2,1)}, u32[]{:S(2)}, u32[]{:S(2)}) collective-permute-start(bf16[2,288,768]{2,1,0:T(8,128)(2,1)} %slice.115), channel_id=1, source_target_pairs={{0,8},{4,20},{8,0},{12,28},{16,24},{20,4},{24,16},{28,12},{1,9},{5... | collective-permute-start | bytes 2654216 | tf_op jit(solution)/shard_map/ppermute | solution.py:409
  211.2 44.5 %collective-permute-start.24 = (bf16[2,288,768]{2,1,0:T(8,128)(2,1)}, bf16[2,288,768]{2,1,0:T(8,128)(2,1)}, u32[]{:S(2)}, u32[]{:S(2)}) collective-permute-start(bf16[2,288,768]{2,1,0:T(8,128)(2,1)} %slice.113), channel_id=1, source_target_pairs={{0,8},{4,20},{8,0},{12,28},{16,24},{20,4},{24,16},{28,12},{1,9},{5... | collective-permute-start | bytes 2654216 | tf_op jit(solution)/shard_map/ppermute | solution.py:409
  230.8 24.8 %collective-permute-start.38 = (bf16[288,768]{1,0:T(8,128)(2,1)S(1)}, bf16[288,768]{1,0:T(8,128)(2,1)S(1)}, u32[]{:S(2)}, u32[]{:S(2)}) collective-permute-start(bf16[288,768]{1,0:T(8,128)(2,1)S(1)} %slice_bitcast_fusion), channel_id=1, source_target_pairs={{0,16},{4,12},{8,24},{12,4},{16,0},{20,28},{24,8},{28,20},{1,17},{... | collective-permute-start | bytes 1327112 | tf_op jit(solution)/shard_map/ppermute | solution.py:409
  231.9 30.6 %collective-permute-start.37 = (bf16[288,768]{1,0:T(8,128)(2,1)S(1)}, bf16[288,768]{1,0:T(8,128)(2,1)S(1)}, u32[]{:S(2)}, u32[]{:S(2)}) collective-permute-start(bf16[288,768]{1,0:T(8,128)(2,1)S(1)} %slice_bitcast_fusion.1), channel_id=1, source_target_pairs={{0,16},{4,12},{8,24},{12,4},{16,0},{20,28},{24,8},{28,20},{1,17},{... | collective-permute-start | bytes 1327112 | tf_op jit(solution)/shard_map/ppermute | solution.py:409
  233.0 21.5 %collective-permute-start.30 = (f32[16,768]{1,0:T(8,128)S(1)}, f32[16,768]{1,0:T(8,128)S(1)}, u32[]{:S(2)}, u32[]{:S(2)}) collective-permute-start(f32[16,768]{1,0:T(8,128)S(1)} %add.679), channel_id=1, source_target_pairs={{0,8},{4,12},{8,0},{12,4},{16,24},{20,28},{24,16},{28,20},{1,9},{5... | collective-permute-start | bytes 147464 | tf_op jit(solution)/shard_map/ppermute | solution.py:409
  255.7 15.0 %collective-permute-start.39 = (bf16[288,768]{1,0:T(8,128)(2,1)S(1)}, bf16[288,768]{1,0:T(8,128)(2,1)S(1)}, u32[]{:S(2)}, u32[]{:S(2)}) collective-permute-start(bf16[288,768]{1,0:T(8,128)(2,1)S(1)} %bitcast_add_fusion), channel_id=1, source_target_pairs={{0,1},{1,2},{2,3},{3,0},{4,5},{5,6},{6,7},{7,4},{8,9},{9,10},{10,1... | collective-permute-start | bytes 1327112 | tf_op jit(solution)/shard_map/ppermute | solution.py:425
  258.7 12.6 %collective-permute-start.32 = (f32[16,768]{1,0:T(8,128)S(1)}, f32[16,768]{1,0:T(8,128)S(1)}, u32[]{:S(2)}, u32[]{:S(2)}) collective-permute-start(f32[16,768]{1,0:T(8,128)S(1)} %add.681), channel_id=1, source_target_pairs={{0,1},{1,2},{2,3},{3,0},{4,5},{5,6},{6,7},{7,4},{8,9},{9,10},{10,1... | collective-permute-start | bytes 147464 | tf_op jit(solution)/shard_map/ppermute | solution.py:953
  258.7 23.0 %collective-permute-start.33 = (f32[16,768]{1,0:T(8,128)S(1)}, f32[16,768]{1,0:T(8,128)S(1)}, u32[]{:S(2)}, u32[]{:S(2)}) collective-permute-start(f32[16,768]{1,0:T(8,128)S(1)} %add.681), channel_id=1, source_target_pairs={{0,2},{1,3},{2,0},{3,1},{4,6},{5,7},{6,4},{7,5},{8,10},{9,11},{10,... | collective-permute-start | bytes 147464 | tf_op jit(solution)/shard_map/ppermute | solution.py:953
  261.5 20.3 %collective-permute-start.34 = (f32[16,768]{1,0:T(8,128)S(1)}, f32[16,768]{1,0:T(8,128)S(1)}, u32[]{:S(2)}, u32[]{:S(2)}) collective-permute-start(f32[16,768]{1,0:T(8,128)S(1)} %add.681), channel_id=1, source_target_pairs={{0,3},{1,0},{2,1},{3,2},{4,7},{5,4},{6,5},{7,6},{8,11},{9,8},{10,9... | collective-permute-start | bytes 147464 | tf_op jit(solution)/shard_map/ppermute | solution.py:953
  262.6 20.9 %collective-permute-start.36 = (bf16[288,768]{1,0:T(8,128)(2,1)S(1)}, bf16[288,768]{1,0:T(8,128)(2,1)S(1)}, u32[]{:S(2)}, u32[]{:S(2)}) collective-permute-start(bf16[288,768]{1,0:T(8,128)(2,1)S(1)} %slice_bitcast_fusion.2), channel_id=1, source_target_pairs={{0,16},{4,12},{8,24},{12,4},{16,0},{20,28},{24,8},{28,20},{1,17},{... | collective-permute-start | bytes 1327112 | tf_op jit(solution)/shard_map/ppermute | solution.py:409
  270.8 12.7 %collective-permute-start.40 = (bf16[288,768]{1,0:T(8,128)(2,1)S(1)}, bf16[288,768]{1,0:T(8,128)(2,1)S(1)}, u32[]{:S(2)}, u32[]{:S(2)}) collective-permute-start(bf16[288,768]{1,0:T(8,128)(2,1)S(1)} %fusion.3), channel_id=1, source_target_pairs={{0,1},{1,2},{2,3},{3,0},{4,5},{5,6},{6,7},{7,4},{8,9},{9,10},{10,1... | collective-permute-start | bytes 1327112 | tf_op jit(solution)/shard_map/ppermute | solution.py:425
  283.5 15.4 %collective-permute-start.41 = (bf16[288,768]{1,0:T(8,128)(2,1)S(1)}, bf16[288,768]{1,0:T(8,128)(2,1)S(1)}, u32[]{:S(2)}, u32[]{:S(2)}) collective-permute-start(bf16[288,768]{1,0:T(8,128)(2,1)S(1)} %fusion.4), channel_id=1, source_target_pairs={{0,1},{1,2},{2,3},{3,0},{4,5},{5,6},{6,7},{7,4},{8,9},{9,10},{10,1... | collective-permute-start | bytes 1327112 | tf_op jit(solution)/shard_map/ppermute | solution.py:425
  299.0 13.1 %collective-permute-start.42 = (bf16[288,768]{1,0:T(8,128)(2,1)S(1)}, bf16[288,768]{1,0:T(8,128)(2,1)S(1)}, u32[]{:S(2)}, u32[]{:S(2)}) collective-permute-start(bf16[288,768]{1,0:T(8,128)(2,1)S(1)} %fusion.5.refs_0_), channel_id=1, source_target_pairs={{0,8},{4,20},{8,0},{12,28},{16,24},{20,4},{24,16},{28,12},{1,9},{5... | collective-permute-start | bytes 1327112 | tf_op jit(solution)/shard_map/ppermute | solution.py:409
  300.4 12.2 %collective-permute-start.43 = (bf16[288,768]{1,0:T(8,128)(2,1)S(1)}, bf16[288,768]{1,0:T(8,128)(2,1)S(1)}, u32[]{:S(2)}, u32[]{:S(2)}) collective-permute-start(bf16[288,768]{1,0:T(8,128)(2,1)S(1)} %fusion.5.refs_0_), channel_id=1, source_target_pairs={{0,16},{4,12},{8,24},{12,4},{16,0},{20,28},{24,8},{28,20},{1,17},{... | collective-permute-start | bytes 1327112 | tf_op jit(solution)/shard_map/ppermute | solution.py:409
  (51 other events, 430.3 us)
Sparse Core Ops, SparseCore 0:
  72.2 66.2 all-gather.1

commit v5 on v4

--- a/solution.py
+++ b/solution.py
@@ -510,12 +510,12 @@
             ],
         ),
         out_shape=jax.ShapeDtypeStruct((len(reps), PIECE, D), jnp.bfloat16),
-        compiler_params=pltpu.CompilerParams(vmem_limit_bytes=16 * 2**20),
+        compiler_params=pltpu.CompilerParams(vmem_limit_bytes=56 * 2**20),
     )(jnp.stack([shard] + reps), params.reshape(FLAT_ROWS, LANES))
 
 
 PIECES = SHARDS * REPS
-GROUPS = 9
+GROUPS = 12
 ALL_ROWS = PIECES * PIECE
 
 
@@ -567,21 +567,15 @@
     return jnp.dot(a, b, preferred_element_type=jnp.float32)
 
 
-def gradient_kernel(where, *refs):
+def attention_kernel(where, *refs):
     count = PIECES - REPS
     blocks, own = refs[:GROUPS], refs[GROUPS]
-    (act_one, act_two, grad_y, vecs, rot_cos, rot_up, rot_down, bias) = refs[GROUPS + 1 : GROUPS + 9]
-    outs = refs[GROUPS + 9 : GROUPS + 9 + 14]
-    sent, kept = outs[0:4], outs[4:8]
-    matrices, attn_out, hidden_out, pre_out, mixed_out, sums_out = outs[8:14]
-    held, grads, query, key, value, grad_attn, sems, out_sems = refs[GROUPS + 23 :]
+    (act_one, grad_y, vecs, rot_cos, rot_up, rot_down, bias) = refs[GROUPS + 1 : GROUPS + 8]
+    matrices, attn_out, mixed_out, sums_out = refs[GROUPS + 8 : GROUPS + 12]
+    held, query, key, value, grad_attn, sems, save_sem = refs[GROUPS + 12 :]
     shard = where[0]
     arrive = fetch_pieces([where[1 + t] for t in range(count)], blocks, own, shard, held, sems)
-    slot_row = lambda z, r: pl.multiple_of(where[1 + count + z * REPS + r] * PIECE, 16)
-
-    def keep_rows(z, begin, rows, part):
-        for r in range(part.shape[0] // rows):
-            grads[pl.ds(slot_row(z, r) + begin, rows), :] = part[rows * r : rows * (r + 1), :]
+    sums_out[...] = jnp.zeros_like(sums_out)
 
     arrive(0)
     act1 = act_one[...]
@@ -605,7 +599,7 @@
 
     arrive(2)
     arrive(3)
-    saving = pltpu.make_async_copy(held, matrices, out_sems.at[PIECES])
+    saving = pltpu.make_async_copy(held, matrices, save_sem)
     saving.start()
     low = lax.broadcasted_iota(jnp.int32, (LANES, LANES), 1) < HD
     scale = HD ** (-0.5)
@@ -644,17 +638,71 @@
                     - pltpu.roll(part, 8, 1) * rot_down[...]
                 )
             wide = slice(D * j + LANES * p, D * j + LANES * (p + 1))
-            sums_out[2 + j : 3 + j, lanes] = jnp.sum(part, axis=0, keepdims=True)
+            sums_out[j : j + 1, lanes] = jnp.sum(part, axis=0, keepdims=True)
             mixed_out[:, wide] = part.astype(jnp.bfloat16)
 
+    saving.wait()
+
+
+def attention(scalars, blocks, own, small):
+    anywhere = pl.BlockSpec(memory_space=pl.ANY)
+    vmem = pl.BlockSpec(memory_space=pltpu.VMEM)
+    bf16 = jnp.bfloat16
+    return pl.pallas_call(
+        attention_kernel,
+        grid_spec=pltpu.PrefetchScalarGridSpec(
+            num_scalar_prefetch=1,
+            in_specs=[anywhere] * (len(blocks) + 1) + [vmem] * len(small),
+            out_specs=[anywhere] + [vmem] * 3,
+            scratch_shapes=[
+                pltpu.VMEM((ALL_ROWS, D), bf16),
+                pltpu.VMEM((TOK_DEV, D), bf16),
+                pltpu.VMEM((TOK_DEV, D), bf16),
+                pltpu.VMEM((TOK_DEV, D), bf16),
+                pltpu.VMEM((TOK_DEV, D), bf16),
+                pltpu.SemaphoreType.DMA((PIECES,)),
+                pltpu.SemaphoreType.DMA,
+            ],
+        ),
+        out_shape=[
+            jax.ShapeDtypeStruct((ALL_ROWS, D), bf16),
+            jax.ShapeDtypeStruct((TOK_DEV, D), bf16),
+            jax.ShapeDtypeStruct((TOK_DEV, 3 * D), bf16),
+            jax.ShapeDtypeStruct((8, D), jnp.float32),
+        ],
+        compiler_params=pltpu.CompilerParams(vmem_limit_bytes=40 * 2**20),
+    )(scalars, *blocks, own, *small)
+
+
+def gradient_kernel(where, matrices, *refs):
+    (act_one, act_two, grad_y, vecs, attn_in, mixed_in) = refs[:6]
+    outs = refs[6:22]
+    hidden_out, pre_out, sums_out = refs[22:25]
+    held, grads, sems, out_sems = refs[25:]
+    copies = []
+    for z in range(1, SHARDS):
+        rows = pl.ds(z * REPS * PIECE, REPS * PIECE)
+        copies.append(pltpu.make_async_copy(matrices.at[rows], held.at[rows], sems.at[z]))
+    for copy in copies:
+        copy.start()
+    sums_out[...] = jnp.zeros_like(sums_out)
+    slot_row = lambda z, r: pl.multiple_of(where[z * REPS + r] * PIECE, 16)
+
+    def keep_rows(z, begin, rows, part):
+        for r in range(part.shape[0] // rows):
+            grads[pl.ds(slot_row(z, r) + begin, rows), :] = part[rows * r : rows * (r + 1), :]
+
     gy = grad_y[...]
-    act1_t = act1.T
+    act1_t = act_one[...].T
     for j in range(3):
         keep_rows(
-            0, 96 * j, 96, dot32(act1_t, mixed_out[:, D * j : D * (j + 1)]).astype(jnp.bfloat16)
+            0, 96 * j, 96, dot32(act1_t, mixed_in[:, D * j : D * (j + 1)]).astype(jnp.bfloat16)
         )
-    keep_rows(1, 0, 96, dot32(attn_out[...].T, gy).astype(jnp.bfloat16))
-
+    keep_rows(1, 0, 96, dot32(attn_in[...].T, gy).astype(jnp.bfloat16))
+
+    for copy in copies:
+        copy.wait()
+    gy_t = gy.T
     act2 = act_two[...]
     act2_t = act2.T
     for j in range(4):
@@ -665,7 +713,7 @@
         hidden_out[:, wide] = hidden
         grad_hidden = dot32(w_out2_of(held, j), gy_t).T
         grad_pre = grad_hidden * (bell + pre * jnp.exp(-0.5 * pre * pre) * INV_ROOT_TWO_PI)
-        sums_out[8 + j : 9 + j, :] = jnp.sum(grad_pre, axis=0, keepdims=True)
+        sums_out[j : j + 1, :] = jnp.sum(grad_pre, axis=0, keepdims=True)
         grad_pre16 = grad_pre.astype(jnp.bfloat16)
         pre_out[:, wide] = grad_pre16
         w2 = dot32(hidden.T, gy).astype(jnp.bfloat16)
@@ -684,60 +732,53 @@
         keep_rows(1, 96 + 48 * j, 48, w1[: D // 2])
         keep_rows(2, 48 * j, 48, w1[D // 2 :])
     copies = []
-    for turn, out in enumerate(sent + kept):
-        for p in range(4):
+    for turn, out in enumerate(outs):
+        for p in range(2):
             copies.append(
                 pltpu.make_async_copy(
-                    grads.at[pl.ds((turn * 4 + p) * PIECE, PIECE)],
+                    grads.at[pl.ds((turn * 2 + p) * PIECE, PIECE)],
                     out.at[p],
-                    out_sems.at[turn * 4 + p],
+                    out_sems.at[turn * 2 + p],
                 )
             )
     for copy in copies:
         copy.start()
     for copy in copies:
         copy.wait()
-    saving.wait()
-
-
-def weight_gradients(scalars, blocks, own, small):
-    hbm = pl.BlockSpec(memory_space=pl.ANY)
+
+
+def weight_gradients(slots, matrices, small):
+    anywhere = pl.BlockSpec(memory_space=pl.ANY)
     vmem = pl.BlockSpec(memory_space=pltpu.VMEM)
     bf16 = jnp.bfloat16
-    group = jax.ShapeDtypeStruct((4, PIECE, D), bf16)
     return pl.pallas_call(
         gradient_kernel,
         grid_spec=pltpu.PrefetchScalarGridSpec(
             num_scalar_prefetch=1,
-            in_specs=[hbm] * (len(blocks) + 1) + [vmem] * len(small),
-            out_specs=[hbm] * 9 + [vmem] * 5,
+            in_specs=[anywhere] + [vmem] * len(small),
+            out_specs=[anywhere] * 16 + [vmem] * 3,
             scratch_shapes=[
                 pltpu.VMEM((ALL_ROWS, D), bf16),
                 pltpu.VMEM((ALL_ROWS, D), bf16),
-                pltpu.VMEM((TOK_DEV, D), bf16),
-                pltpu.VMEM((TOK_DEV, D), bf16),
-                pltpu.VMEM((TOK_DEV, D), bf16),
-                pltpu.VMEM((TOK_DEV, D), bf16),
+                pltpu.SemaphoreType.DMA((SHARDS,)),
                 pltpu.SemaphoreType.DMA((PIECES,)),
-                pltpu.SemaphoreType.DMA((PIECES + 1,)),
             ],
         ),
-        out_shape=[group] * 8
+        out_shape=[jax.ShapeDtypeStruct((2, PIECE, D), bf16)] * 16
         + [
-            jax.ShapeDtypeStruct((ALL_ROWS, D), bf16),
-            jax.ShapeDtypeStruct((TOK_DEV, D), bf16),
             jax.ShapeDtypeStruct((TOK_DEV, FF), bf16),
             jax.ShapeDtypeStruct((TOK_DEV, FF), bf16),
-            jax.ShapeDtypeStruct((TOK_DEV, 3 * D), bf16),
-            jax.ShapeDtypeStruct((16, D), jnp.float32),
+            jax.ShapeDtypeStruct((8, D), jnp.float32),
         ],
         compiler_params=pltpu.CompilerParams(vmem_limit_bytes=56 * 2**20),
-    )(scalars, *blocks, own, *small)
+    )(slots, matrices, *small)
 
 
 def result_kernel(matrices, *refs):
-    (tokens, normed, inv_std, grad_y, vecs, attn, hidden, grad_pre, grad_mixed, sums) = refs[:10]
-    output, grad_input, vec_out, held, sems = refs[10:]
+    (tokens, normed, inv_std, grad_y, vecs, attn, grad_mixed, low_sums, hidden, grad_pre, high_sums) = (
+        refs[:11]
+    )
+    output, grad_input, vec_out, held, sems = refs[11:]
     copies = []
     for z in range(SHARDS):
         rows = pl.ds(z * REPS * PIECE, REPS * PIECE)
@@ -750,7 +791,8 @@
     for j in range(4):
         total = total + dot32(hidden[:, D * j : D * (j + 1)], w_out2_of(held, j))
     output[...] = tokens[...].astype(jnp.float32) + (total + vecs[12:13, :])
-    vec_out[...] = sums[...]
+    vec_out[2:5, :] = low_sums[0:3, :]
+    vec_out[8:12, :] = high_sums[0:4, :]
     gy = grad_y[...].astype(jnp.float32)
     total = gy
     for norm, (parts, width, weights) in enumerate(
@@ -831,15 +873,21 @@
 
 def update_kernel(factor, where, *refs):
     blocks = refs[:REPS]
-    vec_ref, params, moments, grad_out, params_out = refs[REPS : REPS + 5]
-    held, grad, weight, moment, sems, out_sems = refs[REPS + 5 :]
+    moments = refs[REPS : 2 * REPS]
+    vec_ref, params, grad_out, params_out = refs[2 * REPS : 2 * REPS + 4]
+    held, grad, weight, moment, sems, out_sems = refs[2 * REPS + 4 :]
     copies = []
     for turn in range(REPS):
         copies.append(
             pltpu.make_async_copy(blocks[turn], held.at[where[1 + turn]], sems.at[turn])
         )
-    copies.append(pltpu.make_async_copy(moments, moment, sems.at[REPS]))
-    copies.append(pltpu.make_async_copy(params, weight, sems.at[REPS + 1]))
+    copies.append(pltpu.make_async_copy(params, weight, sems.at[REPS]))
+    for turn in range(REPS):
+        copies.append(
+            pltpu.make_async_copy(
+                moments[turn], moment.at[where[1 + turn]], sems.at[REPS + 1 + turn]
+            )
+        )
     for copy in copies:
         copy.start()
     for copy in copies[:REPS]:
@@ -914,39 +962,54 @@
         functools.partial(update_kernel, factor),
         grid_spec=pltpu.PrefetchScalarGridSpec(
             num_scalar_prefetch=1,
-            in_specs=[anywhere] * REPS + [pl.BlockSpec(memory_space=pltpu.VMEM)] + [anywhere] * 2,
+            in_specs=[anywhere] * (2 * REPS)
+            + [pl.BlockSpec(memory_space=pltpu.VMEM), anywhere],
             out_specs=[anywhere] * 2,
             scratch_shapes=[
                 pltpu.VMEM((REPS, PIECE, D), jnp.bfloat16),
                 pltpu.VMEM((FLAT_ROWS, LANES), jnp.float32),
                 pltpu.VMEM((FLAT_ROWS, LANES), jnp.float32),
                 pltpu.VMEM((REPS, 2, SHARE_ROWS, LANES), jnp.bfloat16),
-                pltpu.SemaphoreType.DMA((REPS + 2,)),
+                pltpu.SemaphoreType.DMA((2 * REPS + 1,)),
                 pltpu.SemaphoreType.DMA((REPS + 1,)),
             ],
         ),
         out_shape=[flat, flat],
-        compiler_params=pltpu.CompilerParams(vmem_limit_bytes=40 * 2**20),
-    )(jnp.stack([shard] + ids), *blocks, vectors, params.reshape(FLAT_ROWS, LANES), moments)
+        compiler_params=pltpu.CompilerParams(vmem_limit_bytes=56 * 2**20),
+    )(jnp.stack([shard] + ids), *blocks, *moments, vectors, params.reshape(FLAT_ROWS, LANES))
 
 
 def gather_matrices(params, shard, rep):
     piece = pack_pieces(params, shard, [rep])[0]
     own = pack_pieces(params, shard, [rep * 0 + turn for turn in range(REPS)])
-    reps = spread_ids(rep)
-    blocks, ids = [], []
+    fence = lax.optimization_barrier
+    one = ring_step(piece)
+    one, own = fence((one, own))
+    two, first_one, second_one = ring_step(one), first_cross(one), second_cross(one)
+    two, first_one, second_one = fence((two, first_one, second_one))
+    three, first_two, second_two = ring_step(two), first_cross(two), second_cross(two)
+    both_one = second_cross(first_one)
+    three, first_two, second_two, both_one = fence((three, first_two, second_two, both_one))
+    first_three, second_three = first_cross(three), second_cross(three)
+    both_two = second_cross(first_two)
+    mine_one = jnp.stack([one, first_one, second_one, both_one])
+    other_one = core_cross(mine_one)
+    first_three, second_three, both_two, other_one = fence(
+        (first_three, second_three, both_two, other_one)
+    )
+    both_three = second_cross(first_three)
+    mine_two = jnp.stack([two, first_two, second_two, both_two])
+    other_two = core_cross(mine_two)
+    others = [core_cross(value) for value in (three, first_three, second_three)]
+    others, both_three, other_two = fence((others, both_three, other_two))
+    others.append(core_cross(both_three))
+    threes = [three, first_three, second_three, both_three]
+    blocks = [mine_one, other_one, mine_two, other_two] + threes + others
+    ids = []
     for hop in range(1, SHARDS):
-        piece = ring_step(piece)
         owner = (shard + SHARDS - hop) % SHARDS
-        if hop < SHARDS - 1:
-            first = first_cross(piece)
-            mine = jnp.stack([piece, first, second_cross(piece), second_cross(first)])
-            blocks += [mine, core_cross(mine)]
-        else:
-            blocks += spread_in_plane(piece)
-        ids += [owner * REPS + which for which in reps]
-    mine = jnp.stack(blocks[4:8])
-    return blocks[:4] + [mine] + blocks[8:], own.reshape(REPS * PIECE, D), ids
+        ids += [owner * REPS + which for which in spread_ids(rep)]
+    return blocks, own.reshape(REPS * PIECE, D), ids
 
 
 def ring_shift(value, hop):
@@ -988,28 +1051,26 @@
     return slots
 
 
-def scatter_sums(sent, kept, small, results):
+def scatter_sums(parts, moments, small, results):
     carried = None
     for turn in range(SHARDS):
-        chip = kept[turn] + core_cross(sent[turn])
-        pair = chip[2:4] + first_cross(chip[0:2])
-        if turn == 0:
+        sent_far, sent_near = parts[2 * turn], parts[2 * turn + 1]
+        kept_far, kept_near = parts[8 + 2 * turn], parts[9 + 2 * turn]
+        crossed = first_cross(kept_far + core_cross(sent_far))
+        pair = kept_near + core_cross(sent_near) + crossed
+        if turn == 1:
             pair, small = lax.optimization_barrier((pair, small))
             output, grad_input, vectors = results(small)
-        elif turn == 1:
-            pair, vectors = lax.optimization_barrier((pair, vectors))
-            vectors = sum_in_plane(vectors)
         elif turn == 2:
-            pair, vectors = lax.optimization_barrier((pair, vectors))
-            vectors = sum_over_shards(vectors)
-        else:
-            pair, vectors = lax.optimization_barrier((pair, vectors))
+            pair, vectors, moments = lax.optimization_barrier((pair, vectors, moments))
+            vectors = sum_over_shards(sum_in_plane(vectors))
+            moments = moments + [core_cross(value) for value in moments]
         total = pair[0] + second_cross(pair[1])
         if carried is not None:
             total = total + carried
         if turn < SHARDS - 1:
             carried = ring_step(total)
-    return total, output, grad_input, vectors
+    return total, moments, output, grad_input, vectors
 
 
 def shard_vectors(params, shard):
@@ -1043,17 +1104,18 @@
     allowed = (segment_ids[:, None] == segment_ids[None, :]) & (
         slot_ids[None, :] <= slot_ids[:, None]
     )
-    scalars = jnp.stack([shard] + ids + slots_by_piece(shard, rep))
-    small = (act_one, act_two, grad_y, vecs, rot_cos, rot_up, rot_down, allowed.astype(jnp.float32))
-    moments = align_moments(moment_one, moment_two, rep).reshape(2 * SHARE_ROWS, LANES)
-    moments, blocks[-1] = lax.optimization_barrier((moments, blocks[-1]))
-    moments = lax.all_gather(moments, PLANE, axis=0, tiled=True)
-    made = weight_gradients(scalars, blocks, own, small)
-    sent, kept = made[0:4], made[4:8]
-    matrices = made[8]
-    small = (tokens, normed, inv_std, grad_y, vecs) + tuple(made[9:])
-    owned, output, grad_input, vec_grads = scatter_sums(
-        sent, kept, small, lambda small: layer_results(matrices, small)
+    small = (act_one, grad_y, vecs, rot_cos, rot_up, rot_down, allowed.astype(jnp.float32))
+    moments = align_moments(moment_one, moment_two, rep)
+    moments, blocks = lax.optimization_barrier((moments, blocks))
+    first_moments = first_cross(moments)
+    matrices, *attended = attention(jnp.stack([shard] + ids), blocks, own, small)
+    moments, first_moments, attended = lax.optimization_barrier((moments, first_moments, attended))
+    moments = [moments, first_moments, second_cross(moments), second_cross(first_moments)]
+    small = (act_one, act_two, grad_y, vecs, attended[0], attended[1])
+    made = weight_gradients(jnp.stack(slots_by_piece(shard, rep)), matrices, small)
+    small = (tokens, normed, inv_std, grad_y, vecs) + tuple(attended) + tuple(made[16:])
+    owned, moments, output, grad_input, vec_grads = scatter_sums(
+        made[:16], moments, small, lambda small: layer_results(matrices, small)
     )
     own_vectors = lax.dynamic_index_in_dim(
         vec_grads.reshape(SHARDS, 4, D), shard, 0, keepdims=False
@@ -1064,7 +1126,7 @@
         spread_ids(rep),
         own_vectors,
         params,
-        moments.reshape(REPS, 2, SHARE_ROWS, LANES),
+        moments,
         shard,
         1.0 / math.sqrt(tokens_all),
     )

time: 352 us -> 341 us (0.969)
  waiting for transfers between devices: 176 us -> 138 us
  Pallas kernels: 61.2 us -> 78.8 us
  local copies, waits for them, and re-layouts: 29.4 us -> 46.7 us
  between operations: 17.7 us -> 3.83 us
  other arithmetic: 22.4 us -> 31.5 us
    ppermute x37 -> x48, waiting for transfers between devices: 112 us -> 78.4 us  [plane_permute(): lax.ppermute(value, PLANE, [(i, i ^ flips[i % 2]) for i in range(REPS)])]
    pallas_call x0 -> x1, Pallas kernels: none -> 21.7 us  [attention(): pl.pallas_call(attention_kernel, grid_spec=pltpu.PrefetchScalarGridSpec(n...]
    pallas_call x1, Pallas kernels: 32.7 us -> 19.3 us  [weight_gradients(): pl.pallas_call(gradient_kernel, grid_spec=pltpu.PrefetchScalarGridSpec(nu...]
    ppermute x6, waiting for transfers between devices: 53 us -> 44.3 us  [ring_step(): lax.ppermute(value, 'z', [(i, (i + 1) % SHARDS) for i in range(SHARDS)])]
    unnamed x66 -> x130, local copies, waits for them, and re-layouts: 17.1 us -> 24.4 us
    pallas_call x2, Pallas kernels: 3.87 us -> 10.7 us  [pack_pieces(): pl.pallas_call(pack_kernel, grid_spec=pltpu.PrefetchScalarGridSpec(num_sc...]
    ppermute x6, starting transfers between devices: 9.58 us -> 3.31 us  [ring_step(): lax.ppermute(value, 'z', [(i, (i + 1) % SHARDS) for i in range(SHARDS)])]
    ppermute x37 -> x48, starting transfers between devices: 27 us -> 31.2 us  [plane_permute(): lax.ppermute(value, PLANE, [(i, i ^ flips[i % 2]) for i in range(REPS)])]
  transfers between devices with their start and end apart: 50 -> 60, of which waited for: 23 -> 27; matrix products, arithmetic and copies ran while one was open for 9% -> 14% of each run, Pallas kernels for 13% -> 12%
where the time goes in v5:
time: 341 us; the launch traced here: 339 us
  waiting for transfers between devices  138 us (40%)
  Pallas kernels  78.8 us (23%)
  local copies, waits for them, and re-layouts  46.7 us (14%)
  starting transfers between devices  40.7 us (12%)
  other arithmetic  31.5 us (9%)
  between operations  3.83 us (1%)
    ppermute x48, waiting for transfers between devices, plane_permute(): lax.ppermute(value, PLANE, [(i, i ^ flips[i % 2]) for i in range(REPS)])  78.4 us
    ppermute x6, waiting for transfers between devices, ring_step(): lax.ppermute(value, 'z', [(i, (i + 1) % SHARDS) for i in range(SHARDS)])  44.3 us
    ppermute x48, starting transfers between devices, plane_permute(): lax.ppermute(value, PLANE, [(i, i ^ flips[i % 2]) for i in range(REPS)])  31.2 us
    unnamed x130, local copies, waits for them, and re-layouts  24.4 us
    pallas_call x1, Pallas kernels, attention(): pl.pallas_call(attention_kernel, grid_spec=pltpu.PrefetchScalarGridSpec(n...  21.7 us
    pallas_call x1, Pallas kernels, weight_gradients(): pl.pallas_call(gradient_kernel, grid_spec=pltpu.PrefetchScalarGridSpec(nu...  19.3 us
    pallas_call x1, Pallas kernels, update_shard(): pl.pallas_call(functools.partial(update_kernel, factor), grid_spec=pltpu....  17.6 us
    ppermute x6, waiting for transfers between devices, ring_shift(): lax.ppermute(value, 'z', [(i, (i + hop) % SHARDS) for i in range(SHARDS)])  15 us
  transfers between devices with their start and end apart: 60, of which 27 were waited for; matrix products, arithmetic and copies ran while one was open for 14% of the time, Pallas kernels for 12%

profile of v5, /device:TPU:0, one launch (start us, length us, event | category | flops | bytes accessed | tf_op | source)
XLA Modules:
  0.0 339.3 jit_solution(5348303663219862117)
XLA Ops:
  1.2 2.7 shard_map.119
  4.0 3.1 collective-permute-start
  7.7 7.9 %shard_map.120 = bf16[8,288,768]{2,1,0:T(8,128)(2,1)} custom-call(s32[9]{0:T(128)} %stack.316.where, f32[13848,128]{1,0:T(8,128)} %bitcast.125), custom_call_target="tpu_custom_call" | custom-call | tf_op jit(solution)/shard_map/pallas_call | solution.py:501
  15.6 3.8 %collective-permute-done = bf16[288,768]{1,0:T(8,128)(2,1)S(1)} collective-permute-done((bf16[288,768]{1,0:T(8,128)(2,1)}, bf16[288,768]{1,0:T(8,128)(2,1)S(1)}, u32[]{:S(2)}, u32[]{:S(2)}) %collective-permute-start) | collective-permute-done | bytes 442400 | tf_op jit(solution)/shard_map/ppermute | solution.py:425
  22.5 10.1 %collective-permute-done.1 = bf16[288,768]{1,0:T(8,128)(2,1)S(1)} collective-permute-done((bf16[288,768]{1,0:T(8,128)(2,1)S(1)}, bf16[288,768]{1,0:T(8,128)(2,1)S(1)}, u32[]{:S(2)}, u32[]{:S(2)}) %collective-permute-start.1) | collective-permute-done | bytes 442400 | tf_op jit(solution)/shard_map/ppermute | solution.py:425
  36.2 8.9 %collective-permute-done.4.refs_4_ = bf16[288,768]{1,0:T(8,128)(2,1)S(1)} collective-permute-done((bf16[288,768]{1,0:T(8,128)(2,1)S(1)}, bf16[288,768]{1,0:T(8,128)(2,1)S(1)}, u32[]{:S(2)}, u32[]{:S(2)}) %collective-permute-start.4) | collective-permute-done | bytes 442400 | tf_op jit(solution)/shard_map/ppermute | solution.py:425
  45.8 2.4 collective-permute-done.7
  61.9 4.3 %collective-permute-done.10 = bf16[288,768]{1,0:T(8,128)(2,1)} collective-permute-done((bf16[288,768]{1,0:T(8,128)(2,1)}, bf16[288,768]{1,0:T(8,128)(2,1)}, u32[]{:S(2)}, u32[]{:S(2)}) %collective-permute-start.10) | collective-permute-done | bytes 442400 | tf_op jit(solution)/shard_map/ppermute | solution.py:409
  95.2 2.5 collective-permute-start.19
  98.4 2.1 collective-permute-start.20
  111.0 2.1 gather_fusion
  115.5 2.0 fusion.1
  129.4 21.7 %shard_map.121 = (bf16[9216,768]{1,0:T(8,128)(2,1)}, bf16[128,768]{1,0:T(8,128)(2,1)S(1)}, bf16[128,2304]{1,0:T(8,128)(2,1)S(1)}, f32[8,768]{1,0:T(8,128)S(1)}) custom-call(s32[25]{0:T(128)S(1)} %stack.313.where, bf16[4,288,768]{2,1,0:T(8,128)(2,1)S(1)} %pad_maximum_fusion.refs_0_, bf16[4,288,768]{2,1,0:T(8,128)(2,1)S(1)} %copy-done.13, ...), custom_call_target="tpu_custom_call" | custom-call | tf_op jit(solution)/shard_map/pallas_call | solution.py:651
  153.2 19.3 %shard_map.122 = (bf16[2,288,768]{2,1,0:T(8,128)(2,1)}, bf16[2,288,768]{2,1,0:T(8,128)(2,1)}, bf16[2,288,768]{2,1,0:T(8,128)(2,1)}, bf16[2,288,768]{2,1,0:T(8,12...) custom-call(s32[32]{0:T(128)} %stack.373.where, ...), custom_call_target="tpu_custom_call" | custom-call | tf_op jit(solution)/shard_map/pallas_call | solution.py:754
  182.5 12.2 %collective-permute-done.38 = bf16[2,288,768]{2,1,0:T(8,128)(2,1)S(1)} collective-permute-done((bf16[2,288,768]{2,1,0:T(8,128)(2,1)S(1)}, bf16[2,288,768]{2,1,0:T(8,128)(2,1)S(1)}, u32[]{:S(2)}, u32[]{:S(2)}) %collective-permute-start.38) | collective-permute-done | bytes 884768 | tf_op jit(solution)/shard_map/ppermute | solution.py:409
  197.6 16.1 %collective-permute-done.24 = bf16[2,288,768]{2,1,0:T(8,128)(2,1)S(1)} collective-permute-done((bf16[2,288,768]{2,1,0:T(8,128)(2,1)S(1)}, bf16[2,288,768]{2,1,0:T(8,128)(2,1)S(1)}, u32[]{:S(2)}, u32[]{:S(2)}) %collective-permute-start.24) | collective-permute-done | bytes 884768 | tf_op jit(solution)/shard_map/ppermute | solution.py:409
  217.8 9.3 %shard_map.123 = (f32[128,768]{1,0:T(8,128)}, f32[128,768]{1,0:T(8,128)}, f32[16,768]{1,0:T(8,128)S(1)}) custom-call(bf16[9216,768]{1,0:T(8,128)(2,1)} %get-tuple-element.118.matrices, bf16[128,768]{1,0:T(8,128)(2,1)S(1)} %copy-done.6, f32[128,768]{1,0:T(8,128)S(1)} %copy-done.14, f32[128,1]{1,0:T(8,128)S(1)} %copy.19.refs_2_, ...), custom_call_target="tpu_custom_call" | custom-call | tf_op jit(solution)/shard_map/pallas_call | solution.py:828
  227.3 4.8 %collective-permute-done.39 = bf16[288,768]{1,0:T(8,128)(2,1)} collective-permute-done((bf16[288,768]{1,0:T(8,128)(2,1)}, bf16[288,768]{1,0:T(8,128)(2,1)}, u32[]{:S(2)}, u32[]{:S(2)}) %collective-permute-start.39) | collective-permute-done | bytes 442400 | tf_op jit(solution)/shard_map/ppermute | solution.py:409
  237.9 9.3 %collective-permute-done.35 = bf16[288,768]{1,0:T(8,128)(2,1)S(1)} collective-permute-done((bf16[288,768]{1,0:T(8,128)(2,1)S(1)}, bf16[288,768]{1,0:T(8,128)(2,1)S(1)}, u32[]{:S(2)}, u32[]{:S(2)}) %collective-permute-start.35) | collective-permute-done | bytes 442400 | tf_op jit(solution)/shard_map/ppermute | solution.py:409
  247.3 2.0 collective-permute-done.40
  249.4 3.5 %collective-permute-done.27 = bf16[2,288,768]{2,1,0:T(8,128)(2,1)S(1)} collective-permute-done((bf16[2,288,768]{2,1,0:T(8,128)(2,1)S(1)}, bf16[2,288,768]{2,1,0:T(8,128)(2,1)S(1)}, u32[]{:S(2)}, u32[]{:S(2)}) %collective-permute-start.27) | collective-permute-done | bytes 884768 | tf_op jit(solution)/shard_map/ppermute | solution.py:409
  254.5 8.0 %collective-permute-done.41 = bf16[288,768]{1,0:T(8,128)(2,1)S(1)} collective-permute-done((bf16[288,768]{1,0:T(8,128)(2,1)S(1)}, bf16[288,768]{1,0:T(8,128)(2,1)S(1)}, u32[]{:S(2)}, u32[]{:S(2)}) %collective-permute-start.41) | collective-permute-done | bytes 442400 | tf_op jit(solution)/shard_map/ppermute | solution.py:425
  263.2 11.5 %collective-permute-done.42 = bf16[288,768]{1,0:T(8,128)(2,1)S(1)} collective-permute-done((bf16[288,768]{1,0:T(8,128)(2,1)S(1)}, bf16[288,768]{1,0:T(8,128)(2,1)S(1)}, u32[]{:S(2)}, u32[]{:S(2)}) %collective-permute-start.42) | collective-permute-done | bytes 442400 | tf_op jit(solution)/shard_map/ppermute | solution.py:425
  278.2 6.0 %collective-permute-done.55 = f32[16,768]{1,0:T(8,128)S(1)} collective-permute-done((f32[16,768]{1,0:T(8,128)S(1)}, f32[16,768]{1,0:T(8,128)S(1)}, u32[]{:S(2)}, u32[]{:S(2)}) %collective-permute-start.55) | collective-permute-done | bytes 49184 | tf_op jit(solution)/shard_map/ppermute | solution.py:409
  285.2 3.3 collective-permute-done.56
  288.5 5.9 %collective-permute-done.57 = f32[16,768]{1,0:T(8,128)S(1)} collective-permute-done((f32[16,768]{1,0:T(8,128)S(1)}, f32[16,768]{1,0:T(8,128)S(1)}, u32[]{:S(2)}, u32[]{:S(2)}) %collective-permute-start.57) | collective-permute-done | bytes 49184 | tf_op jit(solution)/shard_map/ppermute | solution.py:1016
  294.4 5.0 %collective-permute-done.58 = f32[16,768]{1,0:T(8,128)S(1)} collective-permute-done((f32[16,768]{1,0:T(8,128)S(1)}, f32[16,768]{1,0:T(8,128)S(1)}, u32[]{:S(2)}, u32[]{:S(2)}) %collective-permute-start.58) | collective-permute-done | bytes 49184 | tf_op jit(solution)/shard_map/ppermute | solution.py:1016
  299.3 4.1 %collective-permute-done.59 = f32[16,768]{1,0:T(8,128)S(1)} collective-permute-done((f32[16,768]{1,0:T(8,128)S(1)}, f32[16,768]{1,0:T(8,128)S(1)}, u32[]{:S(2)}, u32[]{:S(2)}) %collective-permute-start.59) | collective-permute-done | bytes 49184 | tf_op jit(solution)/shard_map/ppermute | solution.py:1016
  306.1 5.7 %collective-permute-done.44.refs_2_ = bf16[288,768]{1,0:T(8,128)(2,1)S(1)} collective-permute-done((bf16[288,768]{1,0:T(8,128)(2,1)S(1)}, bf16[288,768]{1,0:T(8,128)(2,1)S(1)}, u32[]{:S(2)}, u32[]{:S(2)}) %collective-permute-start.44) | collective-permute-done | bytes 442400 | tf_op jit(solution)/shard_map/ppermute | solution.py:409
  311.8 4.8 %collective-permute-done.45.refs_3_ = bf16[288,768]{1,0:T(8,128)(2,1)} collective-permute-done((bf16[288,768]{1,0:T(8,128)(2,1)S(1)}, bf16[288,768]{1,0:T(8,128)(2,1)}, u32[]{:S(2)}, u32[]{:S(2)}) %collective-permute-start.45) | collective-permute-done | bytes 442400 | tf_op jit(solution)/shard_map/ppermute | solution.py:409
  318.8 17.6 %shard_map.124 = (f32[13848,128]{1,0:T(8,128)}, f32[13848,128]{1,0:T(8,128)}) custom-call(s32[9]{0:T(128)} %stack.381.where, bf16[288,768]{1,0:T(8,128)(2,1)} %copy-done.43, bf16[288,768]{1,0:T(8,128)(2,1)} %copy-done.58, bf16[288,768]{1,0:T(8,128)(2,1)} %copy-done.59, bf16[288,768]{1,0:T(8,128)(2,1)} %collective-permute-done.45.refs_3_, ...), custom_call_target="tpu_custom_call" | custom-call | tf_op jit(solution)/shard_map/pallas_call | solution.py:961
  336.5 2.8 fusion
  (299 shorter events, 110.4 us)
Async XLA Ops:
  4.0 15.5 %collective-permute-start = (bf16[288,768]{1,0:T(8,128)(2,1)}, bf16[288,768]{1,0:T(8,128)(2,1)S(1)}, u32[]{:S(2)}, u32[]{:S(2)}) collective-permute-start(bf16[288,768]{1,0:T(8,128)(2,1)} %bitcast.135), channel_id=1, source_target_pairs={{0,1},{1,2},{2,3},{3,0},{4,5},{5,6},{6,7},{7,4},{8,9},{9,10},{10,1... | collective-permute-start | bytes 1327112 | tf_op jit(solution)/shard_map/ppermute | solution.py:425
  19.4 13.2 %collective-permute-start.1 = (bf16[288,768]{1,0:T(8,128)(2,1)S(1)}, bf16[288,768]{1,0:T(8,128)(2,1)S(1)}, u32[]{:S(2)}, u32[]{:S(2)}) collective-permute-start(bf16[288,768]{1,0:T(8,128)(2,1)S(1)} %collective-permute-done), channel_id=1, source_target_pairs={{0,1},{1,2},{2,3},{3,0},{4,5},{5,6},{6,7},{7,4},{8,9},{9,10},{10,1... | collective-permute-start | bytes 1327112 | tf_op jit(solution)/shard_map/ppermute | solution.py:425
  19.4 13.2 %collective-permute-start.2 = (bf16[288,768]{1,0:T(8,128)(2,1)S(1)}, bf16[288,768]{1,0:T(8,128)(2,1)S(1)}, u32[]{:S(2)}, u32[]{:S(2)}) collective-permute-start(bf16[288,768]{1,0:T(8,128)(2,1)S(1)} %collective-permute-done), channel_id=1, source_target_pairs={{0,8},{4,20},{8,0},{12,28},{16,24},{20,4},{24,16},{28,12},{1,9},{5... | collective-permute-start | bytes 1327112 | tf_op jit(solution)/shard_map/ppermute | solution.py:409
  32.7 13.1 %collective-permute-start.5 = (bf16[288,768]{1,0:T(8,128)(2,1)S(1)}, bf16[288,768]{1,0:T(8,128)(2,1)S(1)}, u32[]{:S(2)}, u32[]{:S(2)}) collective-permute-start(bf16[288,768]{1,0:T(8,128)(2,1)S(1)} %collective-permute-done.1), channel_id=1, source_target_pairs={{0,8},{4,20},{8,0},{12,28},{16,24},{20,4},{24,16},{28,12},{1,9},{5... | collective-permute-start | bytes 1327112 | tf_op jit(solution)/shard_map/ppermute | solution.py:409
  35.5 12.8 %collective-permute-start.7 = (bf16[288,768]{1,0:T(8,128)(2,1)S(1)}, bf16[288,768]{1,0:T(8,128)(2,1)S(1)}, u32[]{:S(2)}, u32[]{:S(2)}) collective-permute-start(bf16[288,768]{1,0:T(8,128)(2,1)S(1)} %collective-permute-done.2), channel_id=1, source_target_pairs={{0,16},{4,12},{8,24},{12,4},{16,0},{20,28},{24,8},{28,20},{1,17},{... | collective-permute-start | bytes 1327112 | tf_op jit(solution)/shard_map/ppermute | solution.py:409
  48.5 17.7 %collective-permute-start.11 = (bf16[4,288,768]{2,1,0:T(8,128)(2,1)S(1)}, bf16[4,288,768]{2,1,0:T(8,128)(2,1)S(1)}, u32[]{:S(2)}, u32[]{:S(2)}) collective-permute-start(bf16[4,288,768]{2,1,0:T(8,128)(2,1)S(1)} %pad_maximum_fusion.refs_0_), channel_id=1, source_target_pairs={{0,4},{4,0},{8,12},{12,8},{16,20},{20,16},{24,28},{28,24},{1,5},{5... | collective-permute-start | bytes 5308424 | tf_op jit(solution)/shard_map/ppermute | solution.py:409
  48.8 13.1 %collective-permute-start.8 = (bf16[288,768]{1,0:T(8,128)(2,1)}, bf16[288,768]{1,0:T(8,128)(2,1)}, u32[]{:S(2)}, u32[]{:S(2)}) collective-permute-start(bf16[288,768]{1,0:T(8,128)(2,1)} %copy-done.21), channel_id=1, source_target_pairs={{0,8},{4,20},{8,0},{12,28},{16,24},{20,4},{24,16},{28,12},{1,9},{5... | collective-permute-start | bytes 1327112 | tf_op jit(solution)/shard_map/ppermute | solution.py:409
  51.7 14.6 %collective-permute-start.10 = (bf16[288,768]{1,0:T(8,128)(2,1)}, bf16[288,768]{1,0:T(8,128)(2,1)}, u32[]{:S(2)}, u32[]{:S(2)}) collective-permute-start(bf16[288,768]{1,0:T(8,128)(2,1)} %copy-done.56), channel_id=1, source_target_pairs={{0,16},{4,12},{8,24},{12,4},{16,0},{20,28},{24,8},{28,20},{1,17},{... | collective-permute-start | bytes 1327112 | tf_op jit(solution)/shard_map/ppermute | solution.py:409
  69.1 31.5 %collective-permute-start.16 = (bf16[4,288,768]{2,1,0:T(8,128)(2,1)S(1)}, bf16[4,288,768]{2,1,0:T(8,128)(2,1)}, u32[]{:S(2)}, u32[]{:S(2)}) collective-permute-start(bf16[4,288,768]{2,1,0:T(8,128)(2,1)S(1)} %pad_maximum_fusion.1.refs_2_), channel_id=1, source_target_pairs={{0,4},{4,0},{8,12},{12,8},{16,20},{20,16},{24,28},{28,24},{1,5},{5... | collective-permute-start | bytes 5308424 | tf_op jit(solution)/shard_map/ppermute | solution.py:409
  87.6 13.0 %collective-permute-start.15 = (bf16[288,768]{1,0:T(8,128)(2,1)}, bf16[288,768]{1,0:T(8,128)(2,1)S(1)}, u32[]{:S(2)}, u32[]{:S(2)}) collective-permute-start(bf16[288,768]{1,0:T(8,128)(2,1)} %collective-permute-done.8.refs_5_), channel_id=1, source_target_pairs={{0,16},{4,12},{8,24},{12,4},{16,0},{20,28},{24,8},{28,20},{1,17},{... | collective-permute-start | bytes 1327112 | tf_op jit(solution)/shard_map/ppermute | solution.py:409
  92.8 16.8 %collective-permute-start.18 = (bf16[4,768]{1,0:T(4,128)(2,1)}, bf16[4,768]{1,0:T(4,128)(2,1)}, u32[]{:S(2)}, u32[]{:S(2)}) collective-permute-start(bf16[4,768]{1,0:T(4,128)(2,1)} %pad_maximum_fusion.2), channel_id=1, source_target_pairs={{0,1},{1,2},{2,3},{3,0},{4,5},{5,6},{6,7},{7,4},{8,9},{9,10},{10,1... | collective-permute-start | bytes 18440 | tf_op jit(solution)/shard_map/ppermute | solution.py:1016
  95.2 14.5 %collective-permute-start.19 = (bf16[4,768]{1,0:T(4,128)(2,1)}, bf16[4,768]{1,0:T(4,128)(2,1)}, u32[]{:S(2)}, u32[]{:S(2)}) collective-permute-start(bf16[4,768]{1,0:T(4,128)(2,1)} %pad_maximum_fusion.2), channel_id=1, source_target_pairs={{0,2},{1,3},{2,0},{3,1},{4,6},{5,7},{6,4},{7,5},{8,10},{9,11},{10,... | collective-permute-start | bytes 18440 | tf_op jit(solution)/shard_map/ppermute | solution.py:1016
  104.4 48.8 %collective-permute-start.21 = (bf16[2,1760,128]{2,1,0:T(8,128)(2,1)}, bf16[2,1760,128]{2,1,0:T(8,128)(2,1)}, u32[]{:S(2)}, u32[]{:S(2)}) collective-permute-start(bf16[2,1760,128]{2,1,0:T(8,128)(2,1)} %copy-done), channel_id=1, source_target_pairs={{0,8},{4,20},{8,0},{12,28},{16,24},{20,4},{24,16},{28,12},{1,9},{5... | collective-permute-start | bytes 2703368 | tf_op jit(solution)/shard_map/ppermute | solution.py:409
  176.6 18.1 %collective-permute-start.38 = (bf16[2,288,768]{2,1,0:T(8,128)(2,1)S(1)}, bf16[2,288,768]{2,1,0:T(8,128)(2,1)S(1)}, u32[]{:S(2)}, u32[]{:S(2)}) collective-permute-start(bf16[2,288,768]{2,1,0:T(8,128)(2,1)S(1)} %add.704), channel_id=1, source_target_pairs={{0,8},{4,20},{8,0},{12,28},{16,24},{20,4},{24,16},{28,12},{1,9},{5... | collective-permute-start | bytes 2654216 | tf_op jit(solution)/shard_map/ppermute | solution.py:409
  177.4 19.0 %collective-permute-start.22 = (bf16[2,288,768]{2,1,0:T(8,128)(2,1)S(1)}, bf16[2,288,768]{2,1,0:T(8,128)(2,1)S(1)}, u32[]{:S(2)}, u32[]{:S(2)}) collective-permute-start(bf16[2,288,768]{2,1,0:T(8,128)(2,1)S(1)} %copy-done.64), channel_id=1, source_target_pairs={{0,4},{4,0},{8,12},{12,8},{16,20},{20,16},{24,28},{28,24},{1,5},{5... | collective-permute-start | bytes 2654216 | tf_op jit(solution)/shard_map/ppermute | solution.py:409
  177.8 35.9 %collective-permute-start.24 = (bf16[2,288,768]{2,1,0:T(8,128)(2,1)S(1)}, bf16[2,288,768]{2,1,0:T(8,128)(2,1)S(1)}, u32[]{:S(2)}, u32[]{:S(2)}) collective-permute-start(bf16[2,288,768]{2,1,0:T(8,128)(2,1)S(1)} %add.692), channel_id=1, source_target_pairs={{0,8},{4,20},{8,0},{12,28},{16,24},{20,4},{24,16},{28,12},{1,9},{5... | collective-permute-start | bytes 2654216 | tf_op jit(solution)/shard_map/ppermute | solution.py:409
  180.4 46.7 %collective-permute-start.29 = (bf16[2,288,768]{2,1,0:T(8,128)(2,1)}, bf16[2,288,768]{2,1,0:T(8,128)(2,1)}, u32[]{:S(2)}, u32[]{:S(2)}) collective-permute-start(bf16[2,288,768]{2,1,0:T(8,128)(2,1)} %get-tuple-element.151), channel_id=1, source_target_pairs={{0,4},{4,0},{8,12},{12,8},{16,20},{20,16},{24,28},{28,24},{1,5},{5... | collective-permute-start | bytes 2654216 | tf_op jit(solution)/shard_map/ppermute | solution.py:409
  181.6 52.4 %collective-permute-start.32 = (bf16[2,1760,128]{2,1,0:T(8,128)(2,1)S(1)}, bf16[2,1760,128]{2,1,0:T(8,128)(2,1)}, u32[]{:S(2)}, u32[]{:S(2)}) collective-permute-start(bf16[2,1760,128]{2,1,0:T(8,128)(2,1)S(1)} %copy-done.1), channel_id=1, source_target_pairs={{0,16},{4,12},{8,24},{12,4},{16,0},{20,28},{24,8},{28,20},{1,17},{... | collective-permute-start | bytes 2703368 | tf_op jit(solution)/shard_map/ppermute | solution.py:409
  194.8 40.5 %collective-permute-start.31 = (bf16[2,288,768]{2,1,0:T(8,128)(2,1)}, bf16[2,288,768]{2,1,0:T(8,128)(2,1)}, u32[]{:S(2)}, u32[]{:S(2)}) collective-permute-start(bf16[2,288,768]{2,1,0:T(8,128)(2,1)} %add.699), channel_id=1, source_target_pairs={{0,8},{4,20},{8,0},{12,28},{16,24},{20,4},{24,16},{28,12},{1,9},{5... | collective-permute-start | bytes 2654216 | tf_op jit(solution)/shard_map/ppermute | solution.py:409
  196.4 40.5 %collective-permute-start.33 = (bf16[2,1760,128]{2,1,0:T(8,128)(2,1)}, bf16[2,1760,128]{2,1,0:T(8,128)(2,1)}, u32[]{:S(2)}, u32[]{:S(2)}) collective-permute-start(bf16[2,1760,128]{2,1,0:T(8,128)(2,1)} %collective-permute-done.21.refs_9_), channel_id=1, source_target_pairs={{0,16},{4,12},{8,24},{12,4},{16,0},{20,28},{24,8},{28,20},{1,17},{... | collective-permute-start | bytes 2703368 | tf_op jit(solution)/shard_map/ppermute | solution.py:409
  213.7 18.3 %collective-permute-start.39 = (bf16[288,768]{1,0:T(8,128)(2,1)}, bf16[288,768]{1,0:T(8,128)(2,1)}, u32[]{:S(2)}, u32[]{:S(2)}) collective-permute-start(bf16[288,768]{1,0:T(8,128)(2,1)} %slice_bitcast_fusion), channel_id=1, source_target_pairs={{0,16},{4,12},{8,24},{12,4},{16,0},{20,28},{24,8},{28,20},{1,17},{... | collective-permute-start | bytes 1327112 | tf_op jit(solution)/shard_map/ppermute | solution.py:409
  227.2 22.2 %collective-permute-start.25 = (bf16[2,288,768]{2,1,0:T(8,128)(2,1)S(1)}, bf16[2,288,768]{2,1,0:T(8,128)(2,1)S(1)}, u32[]{:S(2)}, u32[]{:S(2)}) collective-permute-start(bf16[2,288,768]{2,1,0:T(8,128)(2,1)S(1)} %copy-done.63), channel_id=1, source_target_pairs={{0,4},{4,0},{8,12},{12,8},{16,20},{20,16},{24,28},{28,24},{1,5},{5... | collective-permute-start | bytes 2654216 | tf_op jit(solution)/shard_map/ppermute | solution.py:409
  232.0 20.8 %collective-permute-start.27 = (bf16[2,288,768]{2,1,0:T(8,128)(2,1)S(1)}, bf16[2,288,768]{2,1,0:T(8,128)(2,1)S(1)}, u32[]{:S(2)}, u32[]{:S(2)}) collective-permute-start(bf16[2,288,768]{2,1,0:T(8,128)(2,1)S(1)} %copy-done.51), channel_id=1, source_target_pairs={{0,8},{4,20},{8,0},{12,28},{16,24},{20,4},{24,16},{28,12},{1,9},{5... | collective-permute-start | bytes 2654216 | tf_op jit(solution)/shard_map/ppermute | solution.py:409
  234.1 13.2 %collective-permute-start.35 = (bf16[288,768]{1,0:T(8,128)(2,1)S(1)}, bf16[288,768]{1,0:T(8,128)(2,1)S(1)}, u32[]{:S(2)}, u32[]{:S(2)}) collective-permute-start(bf16[288,768]{1,0:T(8,128)(2,1)S(1)} %slice_bitcast_fusion.4), channel_id=1, source_target_pairs={{0,16},{4,12},{8,24},{12,4},{16,0},{20,28},{24,8},{28,20},{1,17},{... | collective-permute-start | bytes 1327112 | tf_op jit(solution)/shard_map/ppermute | solution.py:409
  235.3 13.9 %collective-permute-start.40 = (bf16[288,768]{1,0:T(8,128)(2,1)S(1)}, bf16[288,768]{1,0:T(8,128)(2,1)S(1)}, u32[]{:S(2)}, u32[]{:S(2)}) collective-permute-start(bf16[288,768]{1,0:T(8,128)(2,1)S(1)} %fusion.3), channel_id=1, source_target_pairs={{0,1},{1,2},{2,3},{3,0},{4,5},{5,6},{6,7},{7,4},{8,9},{9,10},{10,1... | collective-permute-start | bytes 1327112 | tf_op jit(solution)/shard_map/ppermute | solution.py:425
  237.0 17.5 %collective-permute-start.34 = (bf16[288,768]{1,0:T(8,128)(2,1)S(1)}, bf16[288,768]{1,0:T(8,128)(2,1)S(1)}, u32[]{:S(2)}, u32[]{:S(2)}) collective-permute-start(bf16[288,768]{1,0:T(8,128)(2,1)S(1)} %slice_bitcast_fusion.5), channel_id=1, source_target_pairs={{0,16},{4,12},{8,24},{12,4},{16,0},{20,28},{24,8},{28,20},{1,17},{... | collective-permute-start | bytes 1327112 | tf_op jit(solution)/shard_map/ppermute | solution.py:409
  249.3 13.1 %collective-permute-start.41 = (bf16[288,768]{1,0:T(8,128)(2,1)S(1)}, bf16[288,768]{1,0:T(8,128)(2,1)S(1)}, u32[]{:S(2)}, u32[]{:S(2)}) collective-permute-start(bf16[288,768]{1,0:T(8,128)(2,1)S(1)} %fusion.6), channel_id=1, source_target_pairs={{0,1},{1,2},{2,3},{3,0},{4,5},{5,6},{6,7},{7,4},{8,9},{9,10},{10,1... | collective-permute-start | bytes 1327112 | tf_op jit(solution)/shard_map/ppermute | solution.py:425
  262.6 40.9 %collective-permute-start.50 = (bf16[2,1760,128]{2,1,0:T(8,128)(2,1)S(1)}, bf16[2,1760,128]{2,1,0:T(8,128)(2,1)S(1)}, u32[]{:S(2)}, u32[]{:S(2)}) collective-permute-start(bf16[2,1760,128]{2,1,0:T(8,128)(2,1)S(1)} %copy-done.1), channel_id=1, source_target_pairs={{0,4},{4,0},{8,12},{12,8},{16,20},{20,16},{24,28},{28,24},{1,5},{5... | collective-permute-start | bytes 2703368 | tf_op jit(solution)/shard_map/ppermute | solution.py:409
  262.7 42.9 %collective-permute-start.51 = (bf16[2,1760,128]{2,1,0:T(8,128)(2,1)}, bf16[2,1760,128]{2,1,0:T(8,128)(2,1)S(1)}, u32[]{:S(2)}, u32[]{:S(2)}) collective-permute-start(bf16[2,1760,128]{2,1,0:T(8,128)(2,1)} %collective-permute-done.21.refs_9_), channel_id=1, source_target_pairs={{0,4},{4,0},{8,12},{12,8},{16,20},{20,16},{24,28},{28,24},{1,5},{5... | collective-permute-start | bytes 2703368 | tf_op jit(solution)/shard_map/ppermute | solution.py:409
  263.2 42.4 %collective-permute-start.52 = (bf16[2,1760,128]{2,1,0:T(8,128)(2,1)}, bf16[2,1760,128]{2,1,0:T(8,128)(2,1)S(1)}, u32[]{:S(2)}, u32[]{:S(2)}) collective-permute-start(bf16[2,1760,128]{2,1,0:T(8,128)(2,1)} %collective-permute-done.32.refs_10_), channel_id=1, source_target_pairs={{0,4},{4,0},{8,12},{12,8},{16,20},{20,16},{24,28},{28,24},{1,5},{5... | collective-permute-start | bytes 2703368 | tf_op jit(solution)/shard_map/ppermute | solution.py:409
  274.8 29.5 %collective-permute-start.43 = (bf16[288,768]{1,0:T(8,128)(2,1)S(1)}, bf16[288,768]{1,0:T(8,128)(2,1)S(1)}, u32[]{:S(2)}, u32[]{:S(2)}) collective-permute-start(bf16[288,768]{1,0:T(8,128)(2,1)S(1)} %fusion.5.refs_0_), channel_id=1, source_target_pairs={{0,8},{4,20},{8,0},{12,28},{16,24},{20,4},{24,16},{28,12},{1,9},{5... | collective-permute-start | bytes 1327112 | tf_op jit(solution)/shard_map/ppermute | solution.py:409
  303.4 14.6 %collective-permute-start.53 = (bf16[2,1760,128]{2,1,0:T(8,128)(2,1)}, bf16[2,1760,128]{2,1,0:T(8,128)(2,1)}, u32[]{:S(2)}, u32[]{:S(2)}) collective-permute-start(bf16[2,1760,128]{2,1,0:T(8,128)(2,1)} %collective-permute-done.33.refs_11_), channel_id=1, source_target_pairs={{0,4},{4,0},{8,12},{12,8},{16,20},{20,16},{24,28},{28,24},{1,5},{5... | collective-permute-start | bytes 2703368 | tf_op jit(solution)/shard_map/ppermute | solution.py:409
  (93 other events, 643.6 us)

commit v6 on v5

--- a/solution.py
+++ b/solution.py
@@ -431,20 +431,18 @@
     return (0, first, 6 - first, 6)
 
 
-def spread_in_plane(piece):
-    first = first_cross(piece)
-    second = second_cross(piece)
-    both = second_cross(first)
-    mine = [piece, first, second, both]
-    return mine + [core_cross(value) for value in mine]
-
-
 def spread_ids(rep):
     other = rep ^ 1
     return [rep ^ flip for flip in flips_of(rep)] + [other ^ flip for flip in flips_of(other)]
 
 
-def pack_kernel(where, flat_ref, out_ref, held, sems):
+def window_of(row):
+    return min(6 * row // 8 * 8, FLAT_ROWS - 16)
+
+
+def pack_kernel(where, flat_ref, out_ref, *rest):
+    vec_ref = rest[0] if len(rest) == 4 else None
+    held, windows, sems = rest[-3:]
     shard = where[0]
     turns = out_ref.shape[0]
     for z in range(SHARDS):
@@ -472,6 +470,26 @@
 
             for copy in copies_of(0):
                 copy.start()
+            if vec_ref is not None:
+                cuts = []
+                for slot, row in enumerate(VECTOR_ROWS[z]):
+                    cuts.append(
+                        pltpu.make_async_copy(
+                            flat_ref.at[pl.ds(window_of(row), 16)],
+                            windows.at[slot],
+                            sems.at[2 + slot // 2, slot % 2],
+                        )
+                    )
+                    cuts[-1].start()
+                vec_ref[...] = jnp.zeros_like(vec_ref)
+                for slot, row in enumerate(VECTOR_ROWS[z]):
+                    cuts[slot].wait()
+                    lead = 6 * row - window_of(row)
+                    for col in range(6):
+                        got = windows[slot, lead + col : lead + col + 1, :]
+                        vec_ref[slot : slot + 1, LANES * col : LANES * (col + 1)] = got.astype(
+                            jnp.bfloat16
+                        ).astype(jnp.float32)
 
             @pl.loop(0, turns)
             def _(turn):
@@ -497,21 +515,66 @@
                     at += step + (8 if lead else 0)
 
 
-def pack_pieces(params, shard, reps):
+def pack_pieces(params, shard, reps, vectors):
+    pieces = jax.ShapeDtypeStruct((len(reps), PIECE, D), jnp.bfloat16)
+    rows = jax.ShapeDtypeStruct((8, D), jnp.float32)
+    vmem = pl.BlockSpec(memory_space=pltpu.VMEM)
     return pl.pallas_call(
         pack_kernel,
         grid_spec=pltpu.PrefetchScalarGridSpec(
             num_scalar_prefetch=1,
             in_specs=[pl.BlockSpec(memory_space=pltpu.HBM)],
-            out_specs=pl.BlockSpec(memory_space=pltpu.VMEM),
+            out_specs=[vmem, vmem] if vectors else [vmem],
             scratch_shapes=[
                 pltpu.VMEM((2, MOVED + 16, LANES), jnp.float32),
-                pltpu.SemaphoreType.DMA((2, 2)),
+                pltpu.VMEM((4, 16, LANES), jnp.float32),
+                pltpu.SemaphoreType.DMA((4, 2)),
             ],
         ),
-        out_shape=jax.ShapeDtypeStruct((len(reps), PIECE, D), jnp.bfloat16),
+        out_shape=[pieces, rows] if vectors else [pieces],
         compiler_params=pltpu.CompilerParams(vmem_limit_bytes=56 * 2**20),
     )(jnp.stack([shard] + reps), params.reshape(FLAT_ROWS, LANES))
+
+
+def prepare_kernel(tokens, cotangent, ids, freqs, normed, spread, grad_y, tables):
+    x_wide = tokens[...].astype(jnp.float32)
+    centered = x_wide - jnp.mean(x_wide, axis=1, keepdims=True)
+    variance = jnp.mean(centered * centered, axis=1, keepdims=True)
+    inv_std = lax.rsqrt(variance + EPS_NORM)
+    normed[...] = centered * inv_std
+    spread[...] = jnp.broadcast_to(inv_std, spread.shape)
+    square = (TOK_DEV, TOK_DEV)
+    across = jnp.broadcast_to(ids[...].astype(jnp.float32), square)
+    down = across.T
+    lane = lax.broadcasted_iota(jnp.int32, square, 1)
+    row = lax.broadcasted_iota(jnp.int32, square, 0)
+    begins = (across != pltpu.roll(across, 1, 1)) | (lane == 0)
+    before = jnp.where(begins & (lane <= row), lane.astype(jnp.float32), 0.0)
+    position = row.astype(jnp.float32) - jnp.max(before, axis=1, keepdims=True)
+    angle = position * freqs[...]
+    cosine, sine = jnp.cos(angle), jnp.sin(angle)
+    within = lane % HD
+    tables[0] = jnp.where(within < ROT, cosine, 1.0)
+    tables[1] = jnp.where(within < ROT // 2, -sine, 0.0)
+    tables[2] = jnp.where((within >= ROT // 2) & (within < ROT), sine, 0.0)
+    tables[3] = jnp.where((across == down) & (lane <= row), 1.0, 0.0)
+    cot = cotangent[...].astype(jnp.float32)
+    grad_y[...] = jnp.where(down[:, 0:1] >= 0, cot, 0.0).astype(jnp.bfloat16)
+
+
+def prepare(tokens, cotangent, segment_ids):
+    steps = jnp.arange(LANES, dtype=jnp.int32) % (ROT // 2)
+    freqs = jnp.power(jnp.float32(ROPE_BASE), -2.0 * steps.astype(jnp.float32) / ROT)
+    return pl.pallas_call(
+        prepare_kernel,
+        out_shape=[
+            jax.ShapeDtypeStruct((TOK_DEV, D), jnp.float32),
+            jax.ShapeDtypeStruct((TOK_DEV, LANES), jnp.float32),
+            jax.ShapeDtypeStruct((TOK_DEV, D), jnp.bfloat16),
+            jax.ShapeDtypeStruct((4, TOK_DEV, TOK_DEV), jnp.float32),
+        ],
+        compiler_params=pltpu.CompilerParams(vmem_limit_bytes=16 * 2**20),
+    )(tokens, cotangent, segment_ids.reshape(1, TOK_DEV), freqs.reshape(1, LANES))
 
 
 PIECES = SHARDS * REPS
@@ -570,15 +633,23 @@
 def attention_kernel(where, *refs):
     count = PIECES - REPS
     blocks, own = refs[:GROUPS], refs[GROUPS]
-    (act_one, grad_y, vecs, rot_cos, rot_up, rot_down, bias) = refs[GROUPS + 1 : GROUPS + 8]
-    matrices, attn_out, mixed_out, sums_out = refs[GROUPS + 8 : GROUPS + 12]
-    held, query, key, value, grad_attn, sems, save_sem = refs[GROUPS + 12 :]
+    normed, grad_y, tables = refs[GROUPS + 1 : GROUPS + 4]
+    hops = refs[GROUPS + 4 : GROUPS + 8]
+    matrices, attn_out, mixed_out, sums_out, vecs = refs[GROUPS + 8 : GROUPS + 13]
+    held, query, key, value, grad_attn, sems, save_sem = refs[GROUPS + 13 :]
+    rot_cos, rot_up, rot_down, bias = (tables.at[turn] for turn in range(4))
     shard = where[0]
+    for owner in range(SHARDS):
+        rows = jnp.zeros((4, D), jnp.float32)
+        for hop in range(SHARDS):
+            met = (shard + SHARDS - owner) % SHARDS == hop
+            rows = jnp.where(met, hops[hop][0:4, :], rows)
+        vecs[4 * owner : 4 * owner + 4, :] = rows
     arrive = fetch_pieces([where[1 + t] for t in range(count)], blocks, own, shard, held, sems)
     sums_out[...] = jnp.zeros_like(sums_out)
 
     arrive(0)
-    act1 = act_one[...]
+    act1 = (normed[...] * vecs[0:1, :] + vecs[1:2, :]).astype(jnp.bfloat16)
     for j, out in enumerate((query, key, value)):
         got = dot32(act1, w_qkv_of(held, j)) + vecs[2 + j : 3 + j, :]
         if j < 2:
@@ -653,7 +724,7 @@
         grid_spec=pltpu.PrefetchScalarGridSpec(
             num_scalar_prefetch=1,
             in_specs=[anywhere] * (len(blocks) + 1) + [vmem] * len(small),
-            out_specs=[anywhere] + [vmem] * 3,
+            out_specs=[anywhere] + [vmem] * 4,
             scratch_shapes=[
                 pltpu.VMEM((ALL_ROWS, D), bf16),
                 pltpu.VMEM((TOK_DEV, D), bf16),
@@ -669,16 +740,20 @@
             jax.ShapeDtypeStruct((TOK_DEV, D), bf16),
             jax.ShapeDtypeStruct((TOK_DEV, 3 * D), bf16),
             jax.ShapeDtypeStruct((8, D), jnp.float32),
+            jax.ShapeDtypeStruct((16, D), jnp.float32),
         ],
-        compiler_params=pltpu.CompilerParams(vmem_limit_bytes=40 * 2**20),
+        compiler_params=pltpu.CompilerParams(vmem_limit_bytes=26 * 2**20),
+        cost_estimate=pl.CostEstimate(
+            flops=6 * 10**9, bytes_accessed=60 * 2**20, transcendentals=200000
+        ),
     )(scalars, *blocks, own, *small)
 
 
 def gradient_kernel(where, matrices, *refs):
-    (act_one, act_two, grad_y, vecs, attn_in, mixed_in) = refs[:6]
-    outs = refs[6:22]
-    hidden_out, pre_out, sums_out = refs[22:25]
-    held, grads, sems, out_sems = refs[25:]
+    (normed, grad_y, attn_in, mixed_in, vecs) = refs[:5]
+    outs = refs[5:21]
+    hidden_out, pre_out, sums_out = refs[21:24]
+    held, grads, sems, out_sems = refs[24:]
     copies = []
     for z in range(1, SHARDS):
         rows = pl.ds(z * REPS * PIECE, REPS * PIECE)
@@ -693,7 +768,7 @@
             grads[pl.ds(slot_row(z, r) + begin, rows), :] = part[rows * r : rows * (r + 1), :]
 
     gy = grad_y[...]
-    act1_t = act_one[...].T
+    act1_t = (normed[...] * vecs[0:1, :] + vecs[1:2, :]).astype(jnp.bfloat16).T
     for j in range(3):
         keep_rows(
             0, 96 * j, 96, dot32(act1_t, mixed_in[:, D * j : D * (j + 1)]).astype(jnp.bfloat16)
@@ -703,7 +778,7 @@
     for copy in copies:
         copy.wait()
     gy_t = gy.T
-    act2 = act_two[...]
+    act2 = (normed[...] * vecs[6:7, :] + vecs[7:8, :]).astype(jnp.bfloat16)
     act2_t = act2.T
     for j in range(4):
         wide = slice(D * j, D * (j + 1))
@@ -770,12 +845,15 @@
             jax.ShapeDtypeStruct((TOK_DEV, FF), bf16),
             jax.ShapeDtypeStruct((8, D), jnp.float32),
         ],
-        compiler_params=pltpu.CompilerParams(vmem_limit_bytes=56 * 2**20),
+        compiler_params=pltpu.CompilerParams(vmem_limit_bytes=48 * 2**20),
+        cost_estimate=pl.CostEstimate(
+            flops=10**10, bytes_accessed=60 * 2**20, transcendentals=800000
+        ),
     )(slots, matrices, *small)
 
 
 def result_kernel(matrices, *refs):
-    (tokens, normed, inv_std, grad_y, vecs, attn, grad_mixed, low_sums, hidden, grad_pre, high_sums) = (
+    (tokens, normed, spread, grad_y, attn, grad_mixed, low_sums, vecs, hidden, grad_pre, high_sums) = (
         refs[:11]
     )
     output, grad_input, vec_out, held, sems = refs[11:]
@@ -808,7 +886,7 @@
         vec_out[gain_row : gain_row + 1, :] = jnp.sum(grad_act * unit, axis=0, keepdims=True)
         vec_out[gain_row + 1 : gain_row + 2, :] = jnp.sum(grad_act, axis=0, keepdims=True)
         grad_norm = grad_act * vecs[gain_row : gain_row + 1, :]
-        total = total + inv_std[...] * (
+        total = total + spread[:, 0:1] * (
             grad_norm
             - jnp.mean(grad_norm, axis=1, keepdims=True)
             - unit * jnp.mean(grad_norm * unit, axis=1, keepdims=True)
@@ -834,7 +912,10 @@
             pltpu.SemaphoreType.DMA((SHARDS,)),
         ],
         out_shape=[rows, rows, jax.ShapeDtypeStruct((16, D), jnp.float32)],
-        compiler_params=pltpu.CompilerParams(vmem_limit_bytes=40 * 2**20),
+        compiler_params=pltpu.CompilerParams(vmem_limit_bytes=26 * 2**20),
+        cost_estimate=pl.CostEstimate(
+            flops=4 * 10**9, bytes_accessed=30 * 2**20, transcendentals=0
+        ),
     )(matrices, *small)
 
 
@@ -979,23 +1060,36 @@
     )(jnp.stack([shard] + ids), *blocks, *moments, vectors, params.reshape(FLAT_ROWS, LANES))
 
 
-def gather_matrices(params, shard, rep):
-    piece = pack_pieces(params, shard, [rep])[0]
-    own = pack_pieces(params, shard, [rep * 0 + turn for turn in range(REPS)])
-    fence = lax.optimization_barrier
+def ring_shift(value, hop):
+    return lax.ppermute(value, "z", [(i, (i + hop) % SHARDS) for i in range(SHARDS)])
+
+
+fence = lax.optimization_barrier
+
+
+def gather_matrices(params, shard, rep, early):
+    piece = pack_pieces(params, shard, [rep], False)[0][0]
+    own, vec = pack_pieces(params, shard, [rep * 0 + turn for turn in range(REPS)], True)
     one = ring_step(piece)
-    one, own = fence((one, own))
+    one, own, vec = fence((one, own, vec))
     two, first_one, second_one = ring_step(one), first_cross(one), second_cross(one)
-    two, first_one, second_one = fence((two, first_one, second_one))
+    vec_one = ring_step(vec)
+    two, first_one, second_one, vec_one, early = fence(
+        (two, first_one, second_one, vec_one, early)
+    )
     three, first_two, second_two = ring_step(two), first_cross(two), second_cross(two)
     both_one = second_cross(first_one)
-    three, first_two, second_two, both_one = fence((three, first_two, second_two, both_one))
+    vec_two = ring_step(vec_one)
+    three, first_two, second_two, both_one, vec_two = fence(
+        (three, first_two, second_two, both_one, vec_two)
+    )
     first_three, second_three = first_cross(three), second_cross(three)
     both_two = second_cross(first_two)
     mine_one = jnp.stack([one, first_one, second_one, both_one])
     other_one = core_cross(mine_one)
-    first_three, second_three, both_two, other_one = fence(
-        (first_three, second_three, both_two, other_one)
+    vec_three = ring_step(vec_two)
+    first_three, second_three, both_two, other_one, vec_three = fence(
+        (first_three, second_three, both_two, other_one, vec_three)
     )
     both_three = second_cross(first_three)
     mine_two = jnp.stack([two, first_two, second_two, both_two])
@@ -1009,29 +1103,8 @@
     for hop in range(1, SHARDS):
         owner = (shard + SHARDS - hop) % SHARDS
         ids += [owner * REPS + which for which in spread_ids(rep)]
-    return blocks, own.reshape(REPS * PIECE, D), ids
-
-
-def ring_shift(value, hop):
-    return lax.ppermute(value, "z", [(i, (i + hop) % SHARDS) for i in range(SHARDS)])
-
-
-def gather_vectors(params, shard):
-    mine = shard_vectors(params, shard).astype(jnp.bfloat16)
-    held = [mine] + [ring_shift(mine, hop) for hop in range(1, SHARDS)]
-    turned = jnp.stack(held).astype(jnp.float32)
-    order = (shard + SHARDS - jnp.arange(SHARDS)) % SHARDS
-    return jnp.take(turned, order, axis=0).reshape(16, D)
-
-
-def sum_in_plane(value):
-    for flips in ((1, 1), (2, 2), (4, 4)):
-        value = value + plane_permute(value, flips)
-    return value
-
-
-def sum_over_shards(value):
-    return value + ring_shift(value, 1) + ring_shift(value, 2) + ring_shift(value, 3)
+    hops = [vec, vec_one, vec_two, vec_three]
+    return blocks, own.reshape(REPS * PIECE, D), ids, hops, early
 
 
 def slots_by_piece(shard, rep):
@@ -1052,69 +1125,81 @@
 
 
 def scatter_sums(parts, moments, small, results):
+    sent_far, sent_near, kept_far, kept_near = (
+        [parts[8 * half + 2 * turn + near] for turn in range(SHARDS)]
+        for half in range(2)
+        for near in range(2)
+    )
+    cores = [core_cross(sent_far[0]), core_cross(sent_near[0]), core_cross(sent_far[1])]
+    cores = list(fence(cores))
+    far = [kept_far[0] + cores[0], kept_far[1] + cores[2]]
+    crossed = first_cross(far[0])
+    others = [core_cross(v) for v in (sent_near[1], sent_far[2], sent_near[2], sent_far[3])]
+    crossed, others, small = fence((crossed, others, small))
+    near = [kept_near[0] + cores[1], kept_near[1] + others[0], kept_near[2] + others[2]]
+    far += [kept_far[2] + others[1], kept_far[3] + others[3]]
+
+    pair = near[0] + crossed
+    final = second_cross(pair[1])
+    kept = pair[0]
+    crossed = first_cross(far[1])
+    last_near = core_cross(sent_near[3])
+    output, grad_input, vectors = results(small)
+    final, crossed, last_near, vectors = fence((final, crossed, last_near, vectors))
+    near.append(kept_near[3] + last_near)
+
     carried = None
-    for turn in range(SHARDS):
-        sent_far, sent_near = parts[2 * turn], parts[2 * turn + 1]
-        kept_far, kept_near = parts[8 + 2 * turn], parts[9 + 2 * turn]
-        crossed = first_cross(kept_far + core_cross(sent_far))
-        pair = kept_near + core_cross(sent_near) + crossed
-        if turn == 1:
-            pair, small = lax.optimization_barrier((pair, small))
-            output, grad_input, vectors = results(small)
-        elif turn == 2:
-            pair, vectors, moments = lax.optimization_barrier((pair, vectors, moments))
-            vectors = sum_over_shards(sum_in_plane(vectors))
-            moments = moments + [core_cross(value) for value in moments]
-        total = pair[0] + second_cross(pair[1])
+    for turn in range(1, SHARDS):
+        total = kept + final
         if carried is not None:
             total = total + carried
+        carried = ring_step(total)
+        pair = near[turn] + crossed
+        kept = pair[0]
+        final = second_cross(pair[1])
+        met = plane_permute(vectors, ((1, 1), (2, 2), (4, 4))[turn - 1])
         if turn < SHARDS - 1:
-            carried = ring_step(total)
-    return total, moments, output, grad_input, vectors
-
-
-def shard_vectors(params, shard):
-    rows = jnp.asarray(VECTOR_ROWS, jnp.int32)[shard]
-    return jnp.stack([lax.dynamic_slice_in_dim(params, rows[i] * D, D) for i in range(4)])
+            crossed = first_cross(far[turn + 1])
+            final, crossed, carried, met = fence((final, crossed, carried, met))
+        else:
+            others = [core_cross(value) for value in moments[:2]]
+            final, carried, met, others = fence((final, carried, met, others))
+        vectors = vectors + met
+    total = kept + final + carried
+
+    first, second = first_cross(total), second_cross(total)
+    shifted = [ring_shift(vectors, hop) for hop in range(1, SHARDS)]
+    first, second, shifted = fence((first, second, shifted))
+    vectors = vectors + shifted[0] + shifted[1] + shifted[2]
+    both = second_cross(first)
+    mine = [total, first, second]
+    spread = [core_cross(value) for value in mine]
+    last = core_cross(moments[2])
+    both, spread, last = fence((both, spread, last))
+    spread.append(core_cross(both))
+    others += [last, core_cross(moments[3])]
+    return mine + [both] + spread, moments + others, output, grad_input, vectors
 
 
 def on_device_rows(tokens, segment_ids, cotangent, params, moment_one, moment_two):
     shard = lax.axis_index("z")
     rep = lax.axis_index(PLANE)
-    vecs = gather_vectors(params, shard)
-    blocks, own, ids = gather_matrices(params, shard, rep)
-    x_wide = tokens.astype(jnp.float32)
-    centered = x_wide - jnp.mean(x_wide, axis=1, keepdims=True)
-    variance = jnp.mean(centered * centered, axis=1, keepdims=True)
-    inv_std = lax.rsqrt(variance + EPS_NORM)
-    normed = centered * inv_std
-    act_one = (normed * vecs[0] + vecs[1]).astype(jnp.bfloat16)
-    act_two = (normed * vecs[6] + vecs[7]).astype(jnp.bfloat16)
-    live_rows = (segment_ids >= 0)[:, None]
-    grad_y = jnp.where(live_rows, cotangent, jnp.zeros_like(cotangent))
-    cosine, sine = rotary_tables(positions_of(segment_ids))
-    cosine, sine = cosine[:, 0], sine[:, 0]
-    rest = jnp.ones((TOK_DEV, HD - ROT), jnp.float32)
-    none = jnp.zeros_like(rest)
-    gap = jnp.zeros_like(sine)
-    rot_cos = jnp.concatenate([cosine, cosine, rest] * 2, axis=1)
-    rot_up = jnp.concatenate([-sine, gap, none] * 2, axis=1)
-    rot_down = jnp.concatenate([gap, sine, none] * 2, axis=1)
-    slot_ids = jnp.arange(TOK_DEV, dtype=jnp.int32)
-    allowed = (segment_ids[:, None] == segment_ids[None, :]) & (
-        slot_ids[None, :] <= slot_ids[:, None]
-    )
-    small = (act_one, grad_y, vecs, rot_cos, rot_up, rot_down, allowed.astype(jnp.float32))
-    moments = align_moments(moment_one, moment_two, rep)
-    moments, blocks = lax.optimization_barrier((moments, blocks))
+    early = (prepare(tokens, cotangent, segment_ids), align_moments(moment_one, moment_two, rep))
+    blocks, own, ids, hops, early = gather_matrices(params, shard, rep, early)
+    (normed, inv_std, grad_y, tables), moments = early
+    moments, blocks = fence((moments, blocks))
     first_moments = first_cross(moments)
+    small = (normed, grad_y, tables, *hops)
     matrices, *attended = attention(jnp.stack([shard] + ids), blocks, own, small)
-    moments, first_moments, attended = lax.optimization_barrier((moments, first_moments, attended))
+    moments, first_moments, attended = fence((moments, first_moments, attended))
     moments = [moments, first_moments, second_cross(moments), second_cross(first_moments)]
-    small = (act_one, act_two, grad_y, vecs, attended[0], attended[1])
-    made = weight_gradients(jnp.stack(slots_by_piece(shard, rep)), matrices, small)
-    small = (tokens, normed, inv_std, grad_y, vecs) + tuple(attended) + tuple(made[16:])
-    owned, moments, output, grad_input, vec_grads = scatter_sums(
+    attn, mixed, low_sums, vecs = attended
+    made = weight_gradients(
+        jnp.stack(slots_by_piece(shard, rep)), matrices, (normed, grad_y, attn, mixed, vecs)
+    )
+    made, moments = fence((made, moments))
+    small = (tokens, normed, inv_std, grad_y, attn, mixed, low_sums, vecs) + tuple(made[16:])
+    spread, moments, output, grad_input, vec_grads = scatter_sums(
         made[:16], moments, small, lambda small: layer_results(matrices, small)
     )
     own_vectors = lax.dynamic_index_in_dim(
@@ -1122,7 +1207,7 @@
     )
     tokens_all = tokens.shape[0] * lax.axis_size(EVERY)
     grad_params, new_params = update_shard(
-        spread_in_plane(owned),
+        spread,
         spread_ids(rep),
         own_vectors,
         params,

time: 341 us -> 279 us (0.82)
  other arithmetic: 31.5 us -> 9.17 us
  waiting for transfers between devices: 138 us -> 122 us
  local copies, waits for them, and re-layouts: 46.7 us -> 34.2 us
  starting transfers between devices: 40.7 us -> 32.5 us
    ppermute x6 -> x9, waiting for transfers between devices: 44.3 us -> 35.9 us  [ring_step(): lax.ppermute(value, 'z', [(i, (i + 1) % SHARDS) for i in range(SHARDS)])]
    unnamed x130 -> x134, local copies, waits for them, and re-layouts: 24.4 us -> 32 us
    ppermute x6 -> x3, starting transfers between devices: 6.23 us -> 0.08 us  [ring_shift(): lax.ppermute(value, 'z', [(i, (i + hop) % SHARDS) for i in range(SHARDS)])]
    concatenate x3 -> x0, local copies, waits for them, and re-layouts: 5.33 us -> none  [the longest x1 1.8 us: on_device_rows(): rot_cos = jnp.concatenate([cosine, cosine, rest] * 2, axis=1)]
    ppermute x6 -> x3, waiting for transfers between devices: 15 us -> 9.88 us  [ring_shift(): lax.ppermute(value, 'z', [(i, (i + hop) % SHARDS) for i in range(SHARDS)])]
    another operation x4 -> x0, other arithmetic: 4.97 us -> none
    add x13 -> x14, other arithmetic: 8.08 us -> 4.02 us  [the longest x2 2.79 us: scatter_sums(): far = [kept_far[0] + cores[0], kept_far[1] + cores[2]]]
    another operation x9 -> x0, local copies, waits for them, and re-layouts: 3.79 us -> none  [the longest x8 2.4 us: shard_vectors(): jnp.stack([lax.dynamic_slice_in_dim(params, rows[i] * D, D) for i in rang...]
  transfers between devices with their start and end apart: 60 -> 60, of which waited for: 27 -> 29; matrix products, arithmetic and copies ran while one was open for 14% -> 2% of each run, Pallas kernels for 12% -> 21%
where the time goes in v6:
time: 279 us; the launch traced here: 277 us
  waiting for transfers between devices  122 us (44%)
  Pallas kernels  78.2 us (28%)
  local copies, waits for them, and re-layouts  34.2 us (12%)
  starting transfers between devices  32.5 us (12%)
  other arithmetic  9.17 us (3%)
    ppermute x48, waiting for transfers between devices, plane_permute(): lax.ppermute(value, PLANE, [(i, i ^ flips[i % 2]) for i in range(REPS)])  76.2 us
    ppermute x9, waiting for transfers between devices, ring_step(): lax.ppermute(value, 'z', [(i, (i + 1) % SHARDS) for i in range(SHARDS)])  35.9 us
    unnamed x134, local copies, waits for them, and re-layouts  32 us
    ppermute x48, starting transfers between devices, plane_permute(): lax.ppermute(value, PLANE, [(i, i ^ flips[i % 2]) for i in range(REPS)])  27.9 us
    pallas_call x1, Pallas kernels, attention(): pl.pallas_call(attention_kernel, grid_spec=pltpu.PrefetchScalarGridSpec(n...  24 us
    pallas_call x1, Pallas kernels, weight_gradients(): pl.pallas_call(gradient_kernel, grid_spec=pltpu.PrefetchScalarGridSpec(nu...  18.4 us
    pallas_call x1, Pallas kernels, update_shard(): pl.pallas_call(functools.partial(update_kernel, factor), grid_spec=pltpu....  17.6 us
    pallas_call x2, Pallas kernels, pack_pieces(): pl.pallas_call(pack_kernel, grid_spec=pltpu.PrefetchScalarGridSpec(num_sc...  11.7 us
  transfers between devices with their start and end apart: 60, of which 29 were waited for; matrix products, arithmetic and copies ran while one was open for 2% of the time, Pallas kernels for 21%

profile of v6, /device:TPU:0, one launch (start us, length us, event | category | flops | bytes accessed | tf_op | source)
XLA Modules:
  0.0 277.4 jit_solution(10786154056961716166)
XLA Ops:
  1.2 2.8 shard_map.109
  4.0 3.1 %collective-permute-start = (bf16[288,768]{1,0:T(8,128)(2,1)}, bf16[288,768]{1,0:T(8,128)(2,1)S(1)}, u32[]{:S(2)}, u32[]{:S(2)}) collective-permute-start(bf16[288,768]{1,0:T(8,128)(2,1)} %bitcast.130), channel_id=1, source_target_pairs={{0,1},{1,2},{2,3},{3,0},{4,5},{5,6},{6,7},{7,4},{8,9},{9,10},{10,1... | collective-permute-start | bytes 1327112 | tf_op jit(solution)/shard_map/ppermute | solution.py:425
  7.7 8.9 %shard_map.110 = (bf16[8,288,768]{2,1,0:T(8,128)(2,1)}, f32[8,768]{1,0:T(8,128)}) custom-call(s32[9]{0:T(128)} %stack.273.where, f32[13848,128]{1,0:T(8,128)} %bitcast.120), custom_call_target="tpu_custom_call" | custom-call | tf_op jit(solution)/shard_map/pallas_call | solution.py:522
  16.7 2.8 %collective-permute-done = bf16[288,768]{1,0:T(8,128)(2,1)S(1)} collective-permute-done((bf16[288,768]{1,0:T(8,128)(2,1)}, bf16[288,768]{1,0:T(8,128)(2,1)S(1)}, u32[]{:S(2)}, u32[]{:S(2)}) %collective-permute-start) | collective-permute-done | bytes 442400 | tf_op jit(solution)/shard_map/ppermute | solution.py:425
  19.5 1.5 collective-permute-start.3
  25.2 10.1 %collective-permute-done.4.refs_17_ = f32[8,768]{1,0:T(8,128)S(1)} collective-permute-done((f32[8,768]{1,0:T(8,128)}, f32[8,768]{1,0:T(8,128)S(1)}, u32[]{:S(2)}, u32[]{:S(2)}) %collective-permute-start.4) | collective-permute-done | bytes 24608 | tf_op jit(solution)/shard_map/ppermute | solution.py:425
  35.9 1.5 collective-permute-start.7
  38.0 11.1 %collective-permute-done.9.refs_18_ = f32[8,768]{1,0:T(8,128)S(1)} collective-permute-done((f32[8,768]{1,0:T(8,128)S(1)}, f32[8,768]{1,0:T(8,128)S(1)}, u32[]{:S(2)}, u32[]{:S(2)}) %collective-permute-start.9) | collective-permute-done | bytes 24608 | tf_op jit(solution)/shard_map/ppermute | solution.py:425
  49.1 2.2 collective-permute-done.7
  53.3 1.5 collective-permute-start.11
  55.4 5.6 %collective-permute-done.14.refs_19_ = f32[8,768]{1,0:T(8,128)S(1)} collective-permute-done((f32[8,768]{1,0:T(8,128)S(1)}, f32[8,768]{1,0:T(8,128)S(1)}, u32[]{:S(2)}, u32[]{:S(2)}) %collective-permute-start.14) | collective-permute-done | bytes 24608 | tf_op jit(solution)/shard_map/ppermute | solution.py:425
  61.0 3.9 %collective-permute-done.12 = bf16[288,768]{1,0:T(8,128)(2,1)S(1)} collective-permute-done((bf16[288,768]{1,0:T(8,128)(2,1)S(1)}, bf16[288,768]{1,0:T(8,128)(2,1)S(1)}, u32[]{:S(2)}, u32[]{:S(2)}) %collective-permute-start.12) | collective-permute-done | bytes 442400 | tf_op jit(solution)/shard_map/ppermute | solution.py:409
  65.0 5.7 %collective-permute-done.11.refs_6_ = bf16[288,768]{1,0:T(8,128)(2,1)S(1)} collective-permute-done((bf16[288,768]{1,0:T(8,128)(2,1)S(1)}, bf16[288,768]{1,0:T(8,128)(2,1)S(1)}, u32[]{:S(2)}, u32[]{:S(2)}) %collective-permute-start.11) | collective-permute-done | bytes 442400 | tf_op jit(solution)/shard_map/ppermute | solution.py:409
  78.0 5.0 %collective-permute-done.18.refs_7_ = bf16[288,768]{1,0:T(8,128)(2,1)S(1)} collective-permute-done((bf16[288,768]{1,0:T(8,128)(2,1)S(1)}, bf16[288,768]{1,0:T(8,128)(2,1)S(1)}, u32[]{:S(2)}, u32[]{:S(2)}) %collective-permute-start.18) | collective-permute-done | bytes 442400 | tf_op jit(solution)/shard_map/ppermute | solution.py:409
  89.8 2.0 copy-done.19
  103.8 24.0 %shard_map.113 = (bf16[9216,768]{1,0:T(8,128)(2,1)}, bf16[128,768]{1,0:T(8,128)(2,1)S(1)}, bf16[128,2304]{1,0:T(8,128)(2,1)S(1)}, f32[8,768]{1,0:T(8,128)S(1)}, f32[16,768]{1,0:T(8,128)S(1)}) custom-call(s32[25]{0:T(128)S(1)} %stack.270.where, bf16[4,288,768]{2,1,0:T(8,128)(2,1)S(1)} %pad_maximum_fusion.refs_0_, bf16[4,288,768]{2,1,0:T(8,128)(2,1)S(1)} %copy-done.21, ...), custom_call_target="tpu_custom_call" | custom-call | flops 6000000000 | bytes 62914560 | tf_op jit(solution)/shard_map/pallas_call | solution.py:722
  131.8 18.4 %shard_map.114 = (bf16[2,288,768]{2,1,0:T(8,128)(2,1)S(1)}, bf16[2,288,768]{2,1,0:T(8,128)(2,1)S(1)}, bf16[2,288,768]{2,1,0:T(8,128)(2,1)S(1)}, bf16[2,288,768]{...) custom-call(s32[32]{0:T(128)S(1)} %stack.316.where, ...), custom_call_target="tpu_custom_call" | custom-call | flops 10000000000 | bytes 62914560 | tf_op jit(solution)/shard_map/pallas_call | solution.py:829
  156.1 1.5 collective-permute-done.24
  161.5 1.6 collective-permute-start.27
  165.2 9.4 %collective-permute-done.27 = bf16[2,288,768]{2,1,0:T(8,128)(2,1)S(1)} collective-permute-done((bf16[2,288,768]{2,1,0:T(8,128)(2,1)S(1)}, bf16[2,288,768]{2,1,0:T(8,128)(2,1)S(1)}, u32[]{:S(2)}, u32[]{:S(2)}) %collective-permute-start.27) | collective-permute-done | bytes 884768 | tf_op jit(solution)/shard_map/ppermute | solution.py:409
  177.3 5.7 %shard_map.115 = (f32[128,768]{1,0:T(8,128)}, f32[128,768]{1,0:T(8,128)}, f32[16,768]{1,0:T(8,128)S(1)}) custom-call(bf16[9216,768]{1,0:T(8,128)(2,1)S(1)} %bitcast.114, bf16[128,768]{1,0:T(8,128)(2,1)S(1)} %copy-done.8, f32[128,768]{1,0:T(8,128)S(1)} %copy-done.14, f32[128,128]{1,0:T(8,128)S(1)} %get-tuple-element.246.refs_2_, ...), custom_call_target="tpu_custom_call" | custom-call | flops 4000000000 | bytes 31457280 | tf_op jit(solution)/shard_map/pallas_call | solution.py:906
  183.1 5.8 %collective-permute-done.33 = bf16[2,288,768]{2,1,0:T(8,128)(2,1)S(1)} collective-permute-done((bf16[2,288,768]{2,1,0:T(8,128)(2,1)S(1)}, bf16[2,288,768]{2,1,0:T(8,128)(2,1)S(1)}, u32[]{:S(2)}, u32[]{:S(2)}) %collective-permute-start.33) | collective-permute-done | bytes 884768 | tf_op jit(solution)/shard_map/ppermute | solution.py:409
  190.5 1.5 collective-permute-start.40
  192.0 11.1 %collective-permute-done.36 = bf16[2,288,768]{2,1,0:T(8,128)(2,1)S(1)} collective-permute-done((bf16[2,288,768]{2,1,0:T(8,128)(2,1)S(1)}, bf16[2,288,768]{2,1,0:T(8,128)(2,1)S(1)}, u32[]{:S(2)}, u32[]{:S(2)}) %collective-permute-start.36) | collective-permute-done | bytes 884768 | tf_op jit(solution)/shard_map/ppermute | solution.py:409
  205.6 12.3 %collective-permute-done.40 = bf16[2,288,768]{2,1,0:T(8,128)(2,1)S(1)} collective-permute-done((bf16[2,288,768]{2,1,0:T(8,128)(2,1)S(1)}, bf16[2,288,768]{2,1,0:T(8,128)(2,1)S(1)}, u32[]{:S(2)}, u32[]{:S(2)}) %collective-permute-start.40) | collective-permute-done | bytes 884768 | tf_op jit(solution)/shard_map/ppermute | solution.py:409
  221.0 7.0 %collective-permute-done.45 = f32[16,768]{1,0:T(8,128)S(1)} collective-permute-done((f32[16,768]{1,0:T(8,128)S(1)}, f32[16,768]{1,0:T(8,128)S(1)}, u32[]{:S(2)}, u32[]{:S(2)}) %collective-permute-start.45) | collective-permute-done | bytes 49184 | tf_op jit(solution)/shard_map/ppermute | solution.py:409
  228.0 5.8 %collective-permute-done.44 = bf16[288,768]{1,0:T(8,128)(2,1)S(1)} collective-permute-done((bf16[288,768]{1,0:T(8,128)(2,1)S(1)}, bf16[288,768]{1,0:T(8,128)(2,1)S(1)}, u32[]{:S(2)}, u32[]{:S(2)}) %collective-permute-start.44) | collective-permute-done | bytes 442400 | tf_op jit(solution)/shard_map/ppermute | solution.py:425
  235.6 4.0 %collective-permute-done.52 = f32[16,768]{1,0:T(8,128)S(1)} collective-permute-done((f32[16,768]{1,0:T(8,128)S(1)}, f32[16,768]{1,0:T(8,128)S(1)}, u32[]{:S(2)}, u32[]{:S(2)}) %collective-permute-start.52) | collective-permute-done | bytes 49184 | tf_op jit(solution)/shard_map/ppermute | solution.py:1064
  240.6 4.9 %collective-permute-done.50 = f32[16,768]{1,0:T(8,128)S(1)} collective-permute-done((f32[16,768]{1,0:T(8,128)S(1)}, f32[16,768]{1,0:T(8,128)S(1)}, u32[]{:S(2)}, u32[]{:S(2)}) %collective-permute-start.50) | collective-permute-done | bytes 49184 | tf_op jit(solution)/shard_map/ppermute | solution.py:1064
  248.6 6.0 %collective-permute-done.53.refs_3_ = bf16[288,768]{1,0:T(8,128)(2,1)} collective-permute-done((bf16[288,768]{1,0:T(8,128)(2,1)S(1)}, bf16[288,768]{1,0:T(8,128)(2,1)}, u32[]{:S(2)}, u32[]{:S(2)}) %collective-permute-start.53) | collective-permute-done | bytes 442400 | tf_op jit(solution)/shard_map/ppermute | solution.py:409
  257.0 17.6 %shard_map.116 = (f32[13848,128]{1,0:T(8,128)}, f32[13848,128]{1,0:T(8,128)}) custom-call(s32[9]{0:T(128)} %stack.324.where, bf16[288,768]{1,0:T(8,128)(2,1)} %copy-done.46, bf16[288,768]{1,0:T(8,128)(2,1)} %copy-done.59, bf16[288,768]{1,0:T(8,128)(2,1)} %copy-done.58, bf16[288,768]{1,0:T(8,128)(2,1)} %collective-permute-done.53.refs_3_, ...), custom_call_target="tpu_custom_call" | custom-call | tf_op jit(solution)/shard_map/pallas_call | solution.py:1042
  274.6 2.8 %fusion = (f32[221568]{0:T(1024)}, f32[221568]{0:T(1024)}) fusion(f32[221568]{0:T(1024)S(1)} %copy-done.4, f32[1772544]{0:T(1024)} %bitcast.131, s32[]{:T(128)S(6)} %select_n.334, f32[221568]{0:T(1024)S(1)} %copy-done.2), kind=kLoop, calls=%fused_computation.3 | loop fusion | flops 1550976 | bytes 4431364 | tf_op jit(solution)/shard_map/add | solution.py:352
  (262 shorter events, 68.8 us)
Async XLA Ops:
  4.0 15.5 %collective-permute-start = (bf16[288,768]{1,0:T(8,128)(2,1)}, bf16[288,768]{1,0:T(8,128)(2,1)S(1)}, u32[]{:S(2)}, u32[]{:S(2)}) collective-permute-start(bf16[288,768]{1,0:T(8,128)(2,1)} %bitcast.130), channel_id=1, source_target_pairs={{0,1},{1,2},{2,3},{3,0},{4,5},{5,6},{6,7},{7,4},{8,9},{9,10},{10,1... | collective-permute-start | bytes 1327112 | tf_op jit(solution)/shard_map/ppermute | solution.py:425
  19.5 15.9 %collective-permute-start.3 = (bf16[288,768]{1,0:T(8,128)(2,1)S(1)}, bf16[288,768]{1,0:T(8,128)(2,1)S(1)}, u32[]{:S(2)}, u32[]{:S(2)}) collective-permute-start(bf16[288,768]{1,0:T(8,128)(2,1)S(1)} %collective-permute-done), channel_id=1, source_target_pairs={{0,16},{4,12},{8,24},{12,4},{16,0},{20,28},{24,8},{28,20},{1,17},{... | collective-permute-start | bytes 1327112 | tf_op jit(solution)/shard_map/ppermute | solution.py:409
  21.0 14.4 %collective-permute-start.2 = (bf16[288,768]{1,0:T(8,128)(2,1)S(1)}, bf16[288,768]{1,0:T(8,128)(2,1)S(1)}, u32[]{:S(2)}, u32[]{:S(2)}) collective-permute-start(bf16[288,768]{1,0:T(8,128)(2,1)S(1)} %collective-permute-done), channel_id=1, source_target_pairs={{0,8},{4,20},{8,0},{12,28},{16,24},{20,4},{24,16},{28,12},{1,9},{5... | collective-permute-start | bytes 1327112 | tf_op jit(solution)/shard_map/ppermute | solution.py:409
  22.5 12.9 %collective-permute-start.1 = (bf16[288,768]{1,0:T(8,128)(2,1)S(1)}, bf16[288,768]{1,0:T(8,128)(2,1)S(1)}, u32[]{:S(2)}, u32[]{:S(2)}) collective-permute-start(bf16[288,768]{1,0:T(8,128)(2,1)S(1)} %collective-permute-done), channel_id=1, source_target_pairs={{0,1},{1,2},{2,3},{3,0},{4,5},{5,6},{6,7},{7,4},{8,9},{9,10},{10,1... | collective-permute-start | bytes 1327112 | tf_op jit(solution)/shard_map/ppermute | solution.py:425
  22.5 12.9 %collective-permute-start.4 = (f32[8,768]{1,0:T(8,128)}, f32[8,768]{1,0:T(8,128)S(1)}, u32[]{:S(2)}, u32[]{:S(2)}) collective-permute-start(f32[8,768]{1,0:T(8,128)} %get-tuple-element.159.refs_16_), channel_id=1, source_target_pairs={{0,1},{1,2},{2,3},{3,0},{4,5},{5,6},{6,7},{7,4},{8,9},{9,10},{10,1... | collective-permute-start | bytes 73736 | tf_op jit(solution)/shard_map/ppermute | solution.py:425
  35.4 13.7 %collective-permute-start.8 = (bf16[288,768]{1,0:T(8,128)(2,1)S(1)}, bf16[288,768]{1,0:T(8,128)(2,1)S(1)}, u32[]{:S(2)}, u32[]{:S(2)}) collective-permute-start(bf16[288,768]{1,0:T(8,128)(2,1)S(1)} %collective-permute-done.2), channel_id=1, source_target_pairs={{0,16},{4,12},{8,24},{12,4},{16,0},{20,28},{24,8},{28,20},{1,17},{... | collective-permute-start | bytes 1327112 | tf_op jit(solution)/shard_map/ppermute | solution.py:409
  35.9 15.3 %collective-permute-start.7 = (bf16[288,768]{1,0:T(8,128)(2,1)S(1)}, bf16[288,768]{1,0:T(8,128)(2,1)S(1)}, u32[]{:S(2)}, u32[]{:S(2)}) collective-permute-start(bf16[288,768]{1,0:T(8,128)(2,1)S(1)} %collective-permute-done.1), channel_id=1, source_target_pairs={{0,16},{4,12},{8,24},{12,4},{16,0},{20,28},{24,8},{28,20},{1,17},{... | collective-permute-start | bytes 1327112 | tf_op jit(solution)/shard_map/ppermute | solution.py:409
  37.5 13.8 %collective-permute-start.6 = (bf16[288,768]{1,0:T(8,128)(2,1)S(1)}, bf16[288,768]{1,0:T(8,128)(2,1)S(1)}, u32[]{:S(2)}, u32[]{:S(2)}) collective-permute-start(bf16[288,768]{1,0:T(8,128)(2,1)S(1)} %collective-permute-done.1), channel_id=1, source_target_pairs={{0,8},{4,20},{8,0},{12,28},{16,24},{20,4},{24,16},{28,12},{1,9},{5... | collective-permute-start | bytes 1327112 | tf_op jit(solution)/shard_map/ppermute | solution.py:409
  38.0 13.3 %collective-permute-start.5 = (bf16[288,768]{1,0:T(8,128)(2,1)S(1)}, bf16[288,768]{1,0:T(8,128)(2,1)S(1)}, u32[]{:S(2)}, u32[]{:S(2)}) collective-permute-start(bf16[288,768]{1,0:T(8,128)(2,1)S(1)} %collective-permute-done.1), channel_id=1, source_target_pairs={{0,1},{1,2},{2,3},{3,0},{4,5},{5,6},{6,7},{7,4},{8,9},{9,10},{10,1... | collective-permute-start | bytes 1327112 | tf_op jit(solution)/shard_map/ppermute | solution.py:425
  52.7 17.9 %collective-permute-start.13 = (bf16[4,288,768]{2,1,0:T(8,128)(2,1)S(1)}, bf16[4,288,768]{2,1,0:T(8,128)(2,1)S(1)}, u32[]{:S(2)}, u32[]{:S(2)}) collective-permute-start(bf16[4,288,768]{2,1,0:T(8,128)(2,1)S(1)} %pad_maximum_fusion.refs_0_), channel_id=1, source_target_pairs={{0,4},{4,0},{8,12},{12,8},{16,20},{20,16},{24,28},{28,24},{1,5},{5... | collective-permute-start | bytes 5308424 | tf_op jit(solution)/shard_map/ppermute | solution.py:409
  52.8 12.2 %collective-permute-start.12 = (bf16[288,768]{1,0:T(8,128)(2,1)S(1)}, bf16[288,768]{1,0:T(8,128)(2,1)S(1)}, u32[]{:S(2)}, u32[]{:S(2)}) collective-permute-start(bf16[288,768]{1,0:T(8,128)(2,1)S(1)} %collective-permute-done.6), channel_id=1, source_target_pairs={{0,16},{4,12},{8,24},{12,4},{16,0},{20,28},{24,8},{28,20},{1,17},{... | collective-permute-start | bytes 1327112 | tf_op jit(solution)/shard_map/ppermute | solution.py:409
  53.3 17.3 %collective-permute-start.11 = (bf16[288,768]{1,0:T(8,128)(2,1)S(1)}, bf16[288,768]{1,0:T(8,128)(2,1)S(1)}, u32[]{:S(2)}, u32[]{:S(2)}) collective-permute-start(bf16[288,768]{1,0:T(8,128)(2,1)S(1)} %collective-permute-done.5.refs_4_), channel_id=1, source_target_pairs={{0,16},{4,12},{8,24},{12,4},{16,0},{20,28},{24,8},{28,20},{1,17},{... | collective-permute-start | bytes 1327112 | tf_op jit(solution)/shard_map/ppermute | solution.py:409
  54.9 15.7 %collective-permute-start.10 = (bf16[288,768]{1,0:T(8,128)(2,1)S(1)}, bf16[288,768]{1,0:T(8,128)(2,1)S(1)}, u32[]{:S(2)}, u32[]{:S(2)}) collective-permute-start(bf16[288,768]{1,0:T(8,128)(2,1)S(1)} %collective-permute-done.5.refs_4_), channel_id=1, source_target_pairs={{0,8},{4,20},{8,0},{12,28},{16,24},{20,4},{24,16},{28,12},{1,9},{5... | collective-permute-start | bytes 1327112 | tf_op jit(solution)/shard_map/ppermute | solution.py:409
  72.1 11.7 %collective-permute-start.19 = (bf16[4,288,768]{2,1,0:T(8,128)(2,1)S(1)}, bf16[4,288,768]{2,1,0:T(8,128)(2,1)S(1)}, u32[]{:S(2)}, u32[]{:S(2)}) collective-permute-start(bf16[4,288,768]{2,1,0:T(8,128)(2,1)S(1)} %pad_maximum_fusion.1.refs_2_), channel_id=1, source_target_pairs={{0,4},{4,0},{8,12},{12,8},{16,20},{20,16},{24,28},{28,24},{1,5},{5... | collective-permute-start | bytes 5308424 | tf_op jit(solution)/shard_map/ppermute | solution.py:409
  87.5 40.3 %collective-permute-start.21 = (bf16[2,1760,128]{2,1,0:T(8,128)(2,1)S(1)}, bf16[2,1760,128]{2,1,0:T(8,128)(2,1)}, u32[]{:S(2)}, u32[]{:S(2)}) collective-permute-start(bf16[2,1760,128]{2,1,0:T(8,128)(2,1)S(1)} %shard_map.112.refs_8_), channel_id=1, source_target_pairs={{0,8},{4,20},{8,0},{12,28},{16,24},{20,4},{24,16},{28,12},{1,9},{5... | collective-permute-start | bytes 2703368 | tf_op jit(solution)/shard_map/ppermute | solution.py:409
  127.8 27.1 %collective-permute-start.22 = (bf16[2,1760,128]{2,1,0:T(8,128)(2,1)S(1)}, bf16[2,1760,128]{2,1,0:T(8,128)(2,1)}, u32[]{:S(2)}, u32[]{:S(2)}) collective-permute-start(bf16[2,1760,128]{2,1,0:T(8,128)(2,1)S(1)} %shard_map.112.refs_8_), channel_id=1, source_target_pairs={{0,16},{4,12},{8,24},{12,4},{16,0},{20,28},{24,8},{28,20},{1,17},{... | collective-permute-start | bytes 2703368 | tf_op jit(solution)/shard_map/ppermute | solution.py:409
  128.9 26.0 %collective-permute-start.23 = (bf16[2,1760,128]{2,1,0:T(8,128)(2,1)}, bf16[2,1760,128]{2,1,0:T(8,128)(2,1)}, u32[]{:S(2)}, u32[]{:S(2)}) collective-permute-start(bf16[2,1760,128]{2,1,0:T(8,128)(2,1)} %collective-permute-done.21.refs_9_), channel_id=1, source_target_pairs={{0,16},{4,12},{8,24},{12,4},{16,0},{20,28},{24,8},{28,20},{1,17},{... | collective-permute-start | bytes 2703368 | tf_op jit(solution)/shard_map/ppermute | solution.py:409
  161.5 13.1 %collective-permute-start.27 = (bf16[2,288,768]{2,1,0:T(8,128)(2,1)S(1)}, bf16[2,288,768]{2,1,0:T(8,128)(2,1)S(1)}, u32[]{:S(2)}, u32[]{:S(2)}) collective-permute-start(bf16[2,288,768]{2,1,0:T(8,128)(2,1)S(1)} %add.607), channel_id=1, source_target_pairs={{0,8},{4,20},{8,0},{12,28},{16,24},{20,4},{24,16},{28,12},{1,9},{5... | collective-permute-start | bytes 2654216 | tf_op jit(solution)/shard_map/ppermute | solution.py:409
  164.5 18.5 %collective-permute-start.34 = (bf16[2,288,768]{2,1,0:T(8,128)(2,1)}, bf16[2,288,768]{2,1,0:T(8,128)(2,1)S(1)}, u32[]{:S(2)}, u32[]{:S(2)}) collective-permute-start(bf16[2,288,768]{2,1,0:T(8,128)(2,1)} %get-tuple-element.263), channel_id=1, source_target_pairs={{0,4},{4,0},{8,12},{12,8},{16,20},{20,16},{24,28},{28,24},{1,5},{5... | collective-permute-start | bytes 2654216 | tf_op jit(solution)/shard_map/ppermute | solution.py:409
  164.6 24.3 %collective-permute-start.33 = (bf16[2,288,768]{2,1,0:T(8,128)(2,1)S(1)}, bf16[2,288,768]{2,1,0:T(8,128)(2,1)S(1)}, u32[]{:S(2)}, u32[]{:S(2)}) collective-permute-start(bf16[2,288,768]{2,1,0:T(8,128)(2,1)S(1)} %add.610), channel_id=1, source_target_pairs={{0,8},{4,20},{8,0},{12,28},{16,24},{20,4},{24,16},{28,12},{1,9},{5... | collective-permute-start | bytes 2654216 | tf_op jit(solution)/shard_map/ppermute | solution.py:409
  174.9 14.0 %collective-permute-start.32 = (bf16[288,768]{1,0:T(8,128)(2,1)S(1)}, bf16[288,768]{1,0:T(8,128)(2,1)S(1)}, u32[]{:S(2)}, u32[]{:S(2)}) collective-permute-start(bf16[288,768]{1,0:T(8,128)(2,1)S(1)} %slice_bitcast_fusion.7), channel_id=1, source_target_pairs={{0,16},{4,12},{8,24},{12,4},{16,0},{20,28},{24,8},{28,20},{1,17},{... | collective-permute-start | bytes 1327112 | tf_op jit(solution)/shard_map/ppermute | solution.py:409
  176.2 26.9 %collective-permute-start.36 = (bf16[2,288,768]{2,1,0:T(8,128)(2,1)S(1)}, bf16[2,288,768]{2,1,0:T(8,128)(2,1)S(1)}, u32[]{:S(2)}, u32[]{:S(2)}) collective-permute-start(bf16[2,288,768]{2,1,0:T(8,128)(2,1)S(1)} %add.615), channel_id=1, source_target_pairs={{0,8},{4,20},{8,0},{12,28},{16,24},{20,4},{24,16},{28,12},{1,9},{5... | collective-permute-start | bytes 2654216 | tf_op jit(solution)/shard_map/ppermute | solution.py:409
  189.2 13.9 %collective-permute-start.35 = (bf16[288,768]{1,0:T(8,128)(2,1)S(1)}, bf16[288,768]{1,0:T(8,128)(2,1)S(1)}, u32[]{:S(2)}, u32[]{:S(2)}) collective-permute-start(bf16[288,768]{1,0:T(8,128)(2,1)S(1)} %slice_bitcast_fusion.6), channel_id=1, source_target_pairs={{0,16},{4,12},{8,24},{12,4},{16,0},{20,28},{24,8},{28,20},{1,17},{... | collective-permute-start | bytes 1327112 | tf_op jit(solution)/shard_map/ppermute | solution.py:409
  190.2 13.3 %collective-permute-start.37 = (bf16[288,768]{1,0:T(8,128)(2,1)S(1)}, bf16[288,768]{1,0:T(8,128)(2,1)S(1)}, u32[]{:S(2)}, u32[]{:S(2)}) collective-permute-start(bf16[288,768]{1,0:T(8,128)(2,1)S(1)} %fusion.7), channel_id=1, source_target_pairs={{0,1},{1,2},{2,3},{3,0},{4,5},{5,6},{6,7},{7,4},{8,9},{9,10},{10,1... | collective-permute-start | bytes 1327112 | tf_op jit(solution)/shard_map/ppermute | solution.py:425
  190.5 27.4 %collective-permute-start.40 = (bf16[2,288,768]{2,1,0:T(8,128)(2,1)S(1)}, bf16[2,288,768]{2,1,0:T(8,128)(2,1)S(1)}, u32[]{:S(2)}, u32[]{:S(2)}) collective-permute-start(bf16[2,288,768]{2,1,0:T(8,128)(2,1)S(1)} %add.618), channel_id=1, source_target_pairs={{0,8},{4,20},{8,0},{12,28},{16,24},{20,4},{24,16},{28,12},{1,9},{5... | collective-permute-start | bytes 2654216 | tf_op jit(solution)/shard_map/ppermute | solution.py:409
  203.7 14.6 %collective-permute-start.39 = (bf16[288,768]{1,0:T(8,128)(2,1)S(1)}, bf16[288,768]{1,0:T(8,128)(2,1)S(1)}, u32[]{:S(2)}, u32[]{:S(2)}) collective-permute-start(bf16[288,768]{1,0:T(8,128)(2,1)S(1)} %slice_bitcast_fusion.4), channel_id=1, source_target_pairs={{0,16},{4,12},{8,24},{12,4},{16,0},{20,28},{24,8},{28,20},{1,17},{... | collective-permute-start | bytes 1327112 | tf_op jit(solution)/shard_map/ppermute | solution.py:409
  204.4 13.9 %collective-permute-start.41 = (bf16[288,768]{1,0:T(8,128)(2,1)S(1)}, bf16[288,768]{1,0:T(8,128)(2,1)S(1)}, u32[]{:S(2)}, u32[]{:S(2)}) collective-permute-start(bf16[288,768]{1,0:T(8,128)(2,1)S(1)} %fusion.6), channel_id=1, source_target_pairs={{0,1},{1,2},{2,3},{3,0},{4,5},{5,6},{6,7},{7,4},{8,9},{9,10},{10,1... | collective-permute-start | bytes 1327112 | tf_op jit(solution)/shard_map/ppermute | solution.py:425
  204.5 13.8 %collective-permute-start.42 = (f32[16,768]{1,0:T(8,128)S(1)}, f32[16,768]{1,0:T(8,128)S(1)}, u32[]{:S(2)}, u32[]{:S(2)}) collective-permute-start(f32[16,768]{1,0:T(8,128)S(1)} %add.621), channel_id=1, source_target_pairs={{0,8},{4,12},{8,0},{12,4},{16,24},{20,28},{24,16},{28,20},{1,9},{5... | collective-permute-start | bytes 147464 | tf_op jit(solution)/shard_map/ppermute | solution.py:409
  205.6 14.5 %collective-permute-start.46 = (bf16[2,1760,128]{2,1,0:T(8,128)(2,1)S(1)}, bf16[2,1760,128]{2,1,0:T(8,128)(2,1)S(1)}, u32[]{:S(2)}, u32[]{:S(2)}) collective-permute-start(bf16[2,1760,128]{2,1,0:T(8,128)(2,1)S(1)} %shard_map.112.refs_8_), channel_id=1, source_target_pairs={{0,4},{4,0},{8,12},{12,8},{16,20},{20,16},{24,28},{28,24},{1,5},{5... | collective-permute-start | bytes 2703368 | tf_op jit(solution)/shard_map/ppermute | solution.py:409
  219.7 14.1 %collective-permute-start.44 = (bf16[288,768]{1,0:T(8,128)(2,1)S(1)}, bf16[288,768]{1,0:T(8,128)(2,1)S(1)}, u32[]{:S(2)}, u32[]{:S(2)}) collective-permute-start(bf16[288,768]{1,0:T(8,128)(2,1)S(1)} %fusion.2), channel_id=1, source_target_pairs={{0,1},{1,2},{2,3},{3,0},{4,5},{5,6},{6,7},{7,4},{8,9},{9,10},{10,1... | collective-permute-start | bytes 1327112 | tf_op jit(solution)/shard_map/ppermute | solution.py:425
  219.8 26.4 %collective-permute-start.57 = (bf16[2,1760,128]{2,1,0:T(8,128)(2,1)}, bf16[2,1760,128]{2,1,0:T(8,128)(2,1)S(1)}, u32[]{:S(2)}, u32[]{:S(2)}) collective-permute-start(bf16[2,1760,128]{2,1,0:T(8,128)(2,1)} %collective-permute-done.22.refs_10_), channel_id=1, source_target_pairs={{0,4},{4,0},{8,12},{12,8},{16,20},{20,16},{24,28},{28,24},{1,5},{5... | collective-permute-start | bytes 2703368 | tf_op jit(solution)/shard_map/ppermute | solution.py:409
  240.6 15.4 %collective-permute-start.59 = (bf16[2,1760,128]{2,1,0:T(8,128)(2,1)}, bf16[2,1760,128]{2,1,0:T(8,128)(2,1)S(1)}, u32[]{:S(2)}, u32[]{:S(2)}) collective-permute-start(bf16[2,1760,128]{2,1,0:T(8,128)(2,1)} %collective-permute-done.23.refs_11_), channel_id=1, source_target_pairs={{0,4},{4,0},{8,12},{12,8},{16,20},{20,16},{24,28},{28,24},{1,5},{5... | collective-permute-start | bytes 2703368 | tf_op jit(solution)/shard_map/ppermute | solution.py:409
  (95 other events, 1017.8 us)

commit v7 on v6

--- a/solution.py
+++ b/solution.py
@@ -742,7 +742,7 @@
             jax.ShapeDtypeStruct((8, D), jnp.float32),
             jax.ShapeDtypeStruct((16, D), jnp.float32),
         ],
-        compiler_params=pltpu.CompilerParams(vmem_limit_bytes=26 * 2**20),
+        compiler_params=pltpu.CompilerParams(vmem_limit_bytes=60 * 2**20),
         cost_estimate=pl.CostEstimate(
             flops=6 * 10**9, bytes_accessed=60 * 2**20, transcendentals=200000
         ),
@@ -831,7 +831,7 @@
         grid_spec=pltpu.PrefetchScalarGridSpec(
             num_scalar_prefetch=1,
             in_specs=[anywhere] + [vmem] * len(small),
-            out_specs=[anywhere] * 16 + [vmem] * 3,
+            out_specs=[pl.BlockSpec(memory_space=pltpu.HBM)] * 16 + [vmem] * 3,
             scratch_shapes=[
                 pltpu.VMEM((ALL_ROWS, D), bf16),
                 pltpu.VMEM((ALL_ROWS, D), bf16),
@@ -845,7 +845,7 @@
             jax.ShapeDtypeStruct((TOK_DEV, FF), bf16),
             jax.ShapeDtypeStruct((8, D), jnp.float32),
         ],
-        compiler_params=pltpu.CompilerParams(vmem_limit_bytes=48 * 2**20),
+        compiler_params=pltpu.CompilerParams(vmem_limit_bytes=60 * 2**20),
         cost_estimate=pl.CostEstimate(
             flops=10**10, bytes_accessed=60 * 2**20, transcendentals=800000
         ),
@@ -912,7 +912,7 @@
             pltpu.SemaphoreType.DMA((SHARDS,)),
         ],
         out_shape=[rows, rows, jax.ShapeDtypeStruct((16, D), jnp.float32)],
-        compiler_params=pltpu.CompilerParams(vmem_limit_bytes=26 * 2**20),
+        compiler_params=pltpu.CompilerParams(vmem_limit_bytes=60 * 2**20),
         cost_estimate=pl.CostEstimate(
             flops=4 * 10**9, bytes_accessed=30 * 2**20, transcendentals=0
         ),
@@ -1056,7 +1056,7 @@
             ],
         ),
         out_shape=[flat, flat],
-        compiler_params=pltpu.CompilerParams(vmem_limit_bytes=56 * 2**20),
+        compiler_params=pltpu.CompilerParams(vmem_limit_bytes=60 * 2**20),
     )(jnp.stack([shard] + ids), *blocks, *moments, vectors, params.reshape(FLAT_ROWS, LANES))
 
 
@@ -1144,8 +1144,11 @@
     kept = pair[0]
     crossed = first_cross(far[1])
     last_near = core_cross(sent_near[3])
+    others = [core_cross(value) for value in moments[:2]]
     output, grad_input, vectors = results(small)
-    final, crossed, last_near, vectors = fence((final, crossed, last_near, vectors))
+    final, crossed, last_near, vectors, others = fence(
+        (final, crossed, last_near, vectors, others)
+    )
     near.append(kept_near[3] + last_near)
 
     carried = None
@@ -1160,10 +1163,10 @@
         met = plane_permute(vectors, ((1, 1), (2, 2), (4, 4))[turn - 1])
         if turn < SHARDS - 1:
             crossed = first_cross(far[turn + 1])
-            final, crossed, carried, met = fence((final, crossed, carried, met))
+            others.append(core_cross(moments[turn + 1]))
+            final, crossed, carried, met, others = fence((final, crossed, carried, met, others))
         else:
-            others = [core_cross(value) for value in moments[:2]]
-            final, carried, met, others = fence((final, carried, met, others))
+            final, carried, met = fence((final, carried, met))
         vectors = vectors + met
     total = kept + final + carried
 
@@ -1174,10 +1177,8 @@
     both = second_cross(first)
     mine = [total, first, second]
     spread = [core_cross(value) for value in mine]
-    last = core_cross(moments[2])
-    both, spread, last = fence((both, spread, last))
+    both, spread = fence((both, spread))
     spread.append(core_cross(both))
-    others += [last, core_cross(moments[3])]
     return mine + [both] + spread, moments + others, output, grad_input, vectors
 
 

time: 279 us -> 249 us (0.89)
  local copies, waits for them, and re-layouts: 34.2 us -> 9.33 us
  waiting for transfers between devices: 122 us -> 113 us
  other arithmetic: 9.17 us -> 12.5 us
  starting transfers between devices: 32.5 us -> 35.7 us
    unnamed x134 -> x96, local copies, waits for them, and re-layouts: 32 us -> 5.97 us
    pallas_call x1, Pallas kernels: 24 us -> 16.5 us  [attention(): pl.pallas_call(attention_kernel, grid_spec=pltpu.PrefetchScalarGridSpec(n...]
    pallas_call x1, Pallas kernels: 5.74 us -> 11.2 us  [layer_results(): pl.pallas_call(result_kernel, in_specs=[hbm] + [vmem] * len(small), out_s...]
    ppermute x3, waiting for transfers between devices: 9.88 us -> 4.94 us  [ring_shift(): lax.ppermute(value, 'z', [(i, (i + hop) % SHARDS) for i in range(SHARDS)])]
  transfers between devices with their start and end apart: 60 -> 60, of which waited for: 29 -> 33; matrix products, arithmetic and copies ran while one was open for 2% -> 4% of each run, Pallas kernels for 21% -> 23%
where the time goes in v7:
time: 249 us
  waiting for transfers between devices  113 us (45%)
  Pallas kernels  77 us (31%)
  starting transfers between devices  35.7 us (14%)
  other arithmetic  12.5 us (5%)
  local copies, waits for them, and re-layouts  9.33 us (4%)
    ppermute x48, waiting for transfers between devices, plane_permute(): lax.ppermute(value, PLANE, [(i, i ^ flips[i % 2]) for i in range(REPS)])  73.9 us
    ppermute x9, waiting for transfers between devices, ring_step(): lax.ppermute(value, 'z', [(i, (i + 1) % SHARDS) for i in range(SHARDS)])  33.8 us
    ppermute x48, starting transfers between devices, plane_permute(): lax.ppermute(value, PLANE, [(i, i ^ flips[i % 2]) for i in range(REPS)])  29.2 us
    pallas_call x1, Pallas kernels, weight_gradients(): pl.pallas_call(gradient_kernel, grid_spec=pltpu.PrefetchScalarGridSpec(nu...  19.3 us
    pallas_call x1, Pallas kernels, update_shard(): pl.pallas_call(functools.partial(update_kernel, factor), grid_spec=pltpu....  17.6 us
    pallas_call x1, Pallas kernels, attention(): pl.pallas_call(attention_kernel, grid_spec=pltpu.PrefetchScalarGridSpec(n...  16.5 us
    pallas_call x2, Pallas kernels, pack_pieces(): pl.pallas_call(pack_kernel, grid_spec=pltpu.PrefetchScalarGridSpec(num_sc...  11.6 us
    pallas_call x1, Pallas kernels, layer_results(): pl.pallas_call(result_kernel, in_specs=[hbm] + [vmem] * len(small), out_s...  11.2 us
  transfers between devices with their start and end apart: 60, of which 33 were waited for; matrix products, arithmetic and copies ran while one was open for 4% of the time, Pallas kernels for 23%

profile of v7, /device:TPU:0, one launch (start us, length us, event | category | flops | bytes accessed | tf_op | source)
XLA Modules:
  0.0 248.6 jit_solution(15552171756279155173)
XLA Ops:
  1.2 2.8 %shard_map.109 = bf16[1,288,768]{2,1,0:T(8,128)(2,1)} custom-call(s32[2]{0:T(128)} %pad_add_fusion.where, f32[13848,128]{1,0:T(8,128)} %bitcast.116), custom_call_target="tpu_custom_call" | custom-call | tf_op jit(solution)/shard_map/pallas_call | solution.py:522
  4.0 3.1 %collective-permute-start = (bf16[288,768]{1,0:T(8,128)(2,1)}, bf16[288,768]{1,0:T(8,128)(2,1)S(1)}, u32[]{:S(2)}, u32[]{:S(2)}) collective-permute-start(bf16[288,768]{1,0:T(8,128)(2,1)} %bitcast.127), channel_id=1, source_target_pairs={{0,1},{1,2},{2,3},{3,0},{4,5},{5,6},{6,7},{7,4},{8,9},{9,10},{10,1... | collective-permute-start | bytes 1327112 | tf_op jit(solution)/shard_map/ppermute | solution.py:425
  7.7 8.9 %shard_map.110 = (bf16[8,288,768]{2,1,0:T(8,128)(2,1)}, f32[8,768]{1,0:T(8,128)}) custom-call(s32[9]{0:T(128)} %stack.273.where, f32[13848,128]{1,0:T(8,128)} %bitcast.117), custom_call_target="tpu_custom_call" | custom-call | tf_op jit(solution)/shard_map/pallas_call | solution.py:522
  16.6 2.8 %collective-permute-done = bf16[288,768]{1,0:T(8,128)(2,1)S(1)} collective-permute-done((bf16[288,768]{1,0:T(8,128)(2,1)}, bf16[288,768]{1,0:T(8,128)(2,1)S(1)}, u32[]{:S(2)}, u32[]{:S(2)}) %collective-permute-start) | collective-permute-done | bytes 442400 | tf_op jit(solution)/shard_map/ppermute | solution.py:425
  27.3 8.1 %collective-permute-done.4.refs_17_ = f32[8,768]{1,0:T(8,128)S(1)} collective-permute-done((f32[8,768]{1,0:T(8,128)}, f32[8,768]{1,0:T(8,128)S(1)}, u32[]{:S(2)}, u32[]{:S(2)}) %collective-permute-start.4) | collective-permute-done | bytes 24608 | tf_op jit(solution)/shard_map/ppermute | solution.py:425
  38.0 11.1 %collective-permute-done.9.refs_18_ = f32[8,768]{1,0:T(8,128)S(1)} collective-permute-done((f32[8,768]{1,0:T(8,128)S(1)}, f32[8,768]{1,0:T(8,128)S(1)}, u32[]{:S(2)}, u32[]{:S(2)}) %collective-permute-start.9) | collective-permute-done | bytes 24608 | tf_op jit(solution)/shard_map/ppermute | solution.py:425
  49.1 2.2 collective-permute-done.7
  54.3 5.6 %collective-permute-done.14.refs_19_ = f32[8,768]{1,0:T(8,128)S(1)} collective-permute-done((f32[8,768]{1,0:T(8,128)S(1)}, f32[8,768]{1,0:T(8,128)S(1)}, u32[]{:S(2)}, u32[]{:S(2)}) %collective-permute-start.14) | collective-permute-done | bytes 24608 | tf_op jit(solution)/shard_map/ppermute | solution.py:425
  59.9 3.9 %collective-permute-done.12 = bf16[288,768]{1,0:T(8,128)(2,1)S(1)} collective-permute-done((bf16[288,768]{1,0:T(8,128)(2,1)S(1)}, bf16[288,768]{1,0:T(8,128)(2,1)S(1)}, u32[]{:S(2)}, u32[]{:S(2)}) %collective-permute-start.12) | collective-permute-done | bytes 442400 | tf_op jit(solution)/shard_map/ppermute | solution.py:409
  63.8 5.7 %collective-permute-done.11.refs_6_ = bf16[288,768]{1,0:T(8,128)(2,1)S(1)} collective-permute-done((bf16[288,768]{1,0:T(8,128)(2,1)S(1)}, bf16[288,768]{1,0:T(8,128)(2,1)S(1)}, u32[]{:S(2)}, u32[]{:S(2)}) %collective-permute-start.11) | collective-permute-done | bytes 442400 | tf_op jit(solution)/shard_map/ppermute | solution.py:409
  72.4 3.0 %collective-permute-done.15.refs_8_ = bf16[288,768]{1,0:T(8,128)(2,1)S(1)} collective-permute-done((bf16[288,768]{1,0:T(8,128)(2,1)S(1)}, bf16[288,768]{1,0:T(8,128)(2,1)S(1)}, u32[]{:S(2)}, u32[]{:S(2)}) %collective-permute-start.15) | collective-permute-done | bytes 442400 | tf_op jit(solution)/shard_map/ppermute | solution.py:409
  76.1 3.9 %collective-permute-done.18.refs_7_ = bf16[288,768]{1,0:T(8,128)(2,1)S(1)} collective-permute-done((bf16[288,768]{1,0:T(8,128)(2,1)S(1)}, bf16[288,768]{1,0:T(8,128)(2,1)S(1)}, u32[]{:S(2)}, u32[]{:S(2)}) %collective-permute-start.18) | collective-permute-done | bytes 442400 | tf_op jit(solution)/shard_map/ppermute | solution.py:409
  80.2 1.8 collective-permute-done.20.refs_11_
  84.7 16.5 %shard_map.113 = (bf16[9216,768]{1,0:T(8,128)(2,1)}, bf16[128,768]{1,0:T(8,128)(2,1)}, bf16[128,2304]{1,0:T(8,128)(2,1)}, f32[8,768]{1,0:T(8,128)}, f32[16,768]{1,0:T(8,128)}) custom-call(s32[25]{0:T(128)} %stack.270.where, bf16[4,288,768]{2,1,0:T(8,128)(2,1)} %copy-done.12, bf16[4,288,768]{2,1,0:T(8,128)(2,1)} %copy-done.35, ...), custom_call_target="tpu_custom_call" | custom-call | flops 6000000000 | bytes 62914560 | tf_op jit(solution)/shard_map/pallas_call | solution.py:722
  103.4 19.3 %shard_map.114 = (bf16[2,288,768]{2,1,0:T(8,128)(2,1)}, bf16[2,288,768]{2,1,0:T(8,128)(2,1)}, bf16[2,288,768]{2,1,0:T(8,128)(2,1)}, bf16[2,288,768]{2,1,0:T(8,12...) custom-call(s32[32]{0:T(128)} %stack.316.where, ...), custom_call_target="tpu_custom_call" | custom-call | flops 10000000000 | bytes 62914560 | tf_op jit(solution)/shard_map/pallas_call | solution.py:829
  122.7 1.6 collective-permute-done.23.refs_11_
  125.3 1.6 collective-permute-done.24
  136.0 8.0 %collective-permute-done.27 = bf16[2,288,768]{2,1,0:T(8,128)(2,1)S(1)} collective-permute-done((bf16[2,288,768]{2,1,0:T(8,128)(2,1)S(1)}, bf16[2,288,768]{2,1,0:T(8,128)(2,1)S(1)}, u32[]{:S(2)}, u32[]{:S(2)}) %collective-permute-start.27) | collective-permute-done | bytes 884768 | tf_op jit(solution)/shard_map/ppermute | solution.py:409
  147.3 11.2 %shard_map.115 = (f32[128,768]{1,0:T(8,128)}, f32[128,768]{1,0:T(8,128)}, f32[16,768]{1,0:T(8,128)}) custom-call(bf16[9216,768]{1,0:T(8,128)(2,1)} %get-tuple-element.206.matrices, bf16[128,768]{1,0:T(8,128)(2,1)} %refs_0_, f32[128,768]{1,0:T(8,128)} %copy-done.4, f32[128,128]{1,0:T(8,128)} %copy-done.7, bf16[128,768]{1,0:T(8,128)(2,1)} %copy-done.5, ...), custom_call_target="tpu_custom_call" | custom-call | flops 4000000000 | bytes 31457280 | tf_op jit(solution)/shard_map/pallas_call | solution.py:906
  159.7 1.7 add_add_fusion
  162.8 1.6 collective-permute-start.37
  166.1 10.5 %collective-permute-done.38 = bf16[2,288,768]{2,1,0:T(8,128)(2,1)S(1)} collective-permute-done((bf16[2,288,768]{2,1,0:T(8,128)(2,1)}, bf16[2,288,768]{2,1,0:T(8,128)(2,1)S(1)}, u32[]{:S(2)}, u32[]{:S(2)}) %collective-permute-start.38) | collective-permute-done | bytes 884768 | tf_op jit(solution)/shard_map/ppermute | solution.py:409
  180.1 11.3 %collective-permute-done.43 = bf16[2,288,768]{2,1,0:T(8,128)(2,1)S(1)} collective-permute-done((bf16[2,288,768]{2,1,0:T(8,128)(2,1)S(1)}, bf16[2,288,768]{2,1,0:T(8,128)(2,1)S(1)}, u32[]{:S(2)}, u32[]{:S(2)}) %collective-permute-start.43) | collective-permute-done | bytes 884768 | tf_op jit(solution)/shard_map/ppermute | solution.py:409
  195.6 6.6 %collective-permute-done.49 = f32[16,768]{1,0:T(8,128)S(1)} collective-permute-done((f32[16,768]{1,0:T(8,128)S(1)}, f32[16,768]{1,0:T(8,128)S(1)}, u32[]{:S(2)}, u32[]{:S(2)}) %collective-permute-start.49) | collective-permute-done | bytes 49184 | tf_op jit(solution)/shard_map/ppermute | solution.py:409
  202.2 4.8 %collective-permute-done.48 = bf16[288,768]{1,0:T(8,128)(2,1)S(1)} collective-permute-done((bf16[288,768]{1,0:T(8,128)(2,1)S(1)}, bf16[288,768]{1,0:T(8,128)(2,1)S(1)}, u32[]{:S(2)}, u32[]{:S(2)}) %collective-permute-start.48) | collective-permute-done | bytes 442400 | tf_op jit(solution)/shard_map/ppermute | solution.py:425
  207.1 1.7 collective-permute-start.51
  208.9 1.9 collective-permute-start.52
  210.8 2.1 collective-permute-done.54
  213.9 1.9 collective-permute-done.52
  219.5 6.5 %collective-permute-done.55.refs_3_ = bf16[288,768]{1,0:T(8,128)(2,1)} collective-permute-done((bf16[288,768]{1,0:T(8,128)(2,1)S(1)}, bf16[288,768]{1,0:T(8,128)(2,1)}, u32[]{:S(2)}, u32[]{:S(2)}) %collective-permute-start.55) | collective-permute-done | bytes 442400 | tf_op jit(solution)/shard_map/ppermute | solution.py:409
  228.2 17.6 %shard_map.116 = (f32[13848,128]{1,0:T(8,128)}, f32[13848,128]{1,0:T(8,128)}) custom-call(s32[9]{0:T(128)} %stack.324.where, bf16[288,768]{1,0:T(8,128)(2,1)} %copy-done.14, bf16[288,768]{1,0:T(8,128)(2,1)} %copy-done.30, bf16[288,768]{1,0:T(8,128)(2,1)} %copy-done.29, bf16[288,768]{1,0:T(8,128)(2,1)} %collective-permute-done.55.refs_3_, ...), custom_call_target="tpu_custom_call" | custom-call | tf_op jit(solution)/shard_map/pallas_call | solution.py:1042
  245.8 2.8 %fusion = (f32[221568]{0:T(1024)}, f32[221568]{0:T(1024)}) fusion(f32[221568]{0:T(1024)S(1)} %copy-done.2, f32[1772544]{0:T(1024)} %bitcast.128, s32[]{:T(128)S(6)} %select_n.334, f32[221568]{0:T(1024)S(1)} %copy-done.1), kind=kLoop, calls=%fused_computation.3 | loop fusion | flops 1550976 | bytes 4431364 | tf_op jit(solution)/shard_map/add | solution.py:352
  (223 shorter events, 55.2 us)
Async XLA Ops:
  4.0 15.5 %collective-permute-start = (bf16[288,768]{1,0:T(8,128)(2,1)}, bf16[288,768]{1,0:T(8,128)(2,1)S(1)}, u32[]{:S(2)}, u32[]{:S(2)}) collective-permute-start(bf16[288,768]{1,0:T(8,128)(2,1)} %bitcast.127), channel_id=1, source_target_pairs={{0,1},{1,2},{2,3},{3,0},{4,5},{5,6},{6,7},{7,4},{8,9},{9,10},{10,1... | collective-permute-start | bytes 1327112 | tf_op jit(solution)/shard_map/ppermute | solution.py:425
  19.5 15.9 %collective-permute-start.3 = (bf16[288,768]{1,0:T(8,128)(2,1)S(1)}, bf16[288,768]{1,0:T(8,128)(2,1)S(1)}, u32[]{:S(2)}, u32[]{:S(2)}) collective-permute-start(bf16[288,768]{1,0:T(8,128)(2,1)S(1)} %collective-permute-done), channel_id=1, source_target_pairs={{0,16},{4,12},{8,24},{12,4},{16,0},{20,28},{24,8},{28,20},{1,17},{... | collective-permute-start | bytes 1327112 | tf_op jit(solution)/shard_map/ppermute | solution.py:409
  21.0 14.4 %collective-permute-start.2 = (bf16[288,768]{1,0:T(8,128)(2,1)S(1)}, bf16[288,768]{1,0:T(8,128)(2,1)S(1)}, u32[]{:S(2)}, u32[]{:S(2)}) collective-permute-start(bf16[288,768]{1,0:T(8,128)(2,1)S(1)} %collective-permute-done), channel_id=1, source_target_pairs={{0,8},{4,20},{8,0},{12,28},{16,24},{20,4},{24,16},{28,12},{1,9},{5... | collective-permute-start | bytes 1327112 | tf_op jit(solution)/shard_map/ppermute | solution.py:409
  22.5 12.9 %collective-permute-start.1 = (bf16[288,768]{1,0:T(8,128)(2,1)S(1)}, bf16[288,768]{1,0:T(8,128)(2,1)S(1)}, u32[]{:S(2)}, u32[]{:S(2)}) collective-permute-start(bf16[288,768]{1,0:T(8,128)(2,1)S(1)} %collective-permute-done), channel_id=1, source_target_pairs={{0,1},{1,2},{2,3},{3,0},{4,5},{5,6},{6,7},{7,4},{8,9},{9,10},{10,1... | collective-permute-start | bytes 1327112 | tf_op jit(solution)/shard_map/ppermute | solution.py:425
  22.5 12.9 %collective-permute-start.4 = (f32[8,768]{1,0:T(8,128)}, f32[8,768]{1,0:T(8,128)S(1)}, u32[]{:S(2)}, u32[]{:S(2)}) collective-permute-start(f32[8,768]{1,0:T(8,128)} %get-tuple-element.165.refs_16_), channel_id=1, source_target_pairs={{0,1},{1,2},{2,3},{3,0},{4,5},{5,6},{6,7},{7,4},{8,9},{9,10},{10,1... | collective-permute-start | bytes 73736 | tf_op jit(solution)/shard_map/ppermute | solution.py:425
  35.4 13.7 %collective-permute-start.8 = (bf16[288,768]{1,0:T(8,128)(2,1)S(1)}, bf16[288,768]{1,0:T(8,128)(2,1)S(1)}, u32[]{:S(2)}, u32[]{:S(2)}) collective-permute-start(bf16[288,768]{1,0:T(8,128)(2,1)S(1)} %collective-permute-done.2), channel_id=1, source_target_pairs={{0,16},{4,12},{8,24},{12,4},{16,0},{20,28},{24,8},{28,20},{1,17},{... | collective-permute-start | bytes 1327112 | tf_op jit(solution)/shard_map/ppermute | solution.py:409
  36.0 15.3 %collective-permute-start.7 = (bf16[288,768]{1,0:T(8,128)(2,1)S(1)}, bf16[288,768]{1,0:T(8,128)(2,1)S(1)}, u32[]{:S(2)}, u32[]{:S(2)}) collective-permute-start(bf16[288,768]{1,0:T(8,128)(2,1)S(1)} %collective-permute-done.1), channel_id=1, source_target_pairs={{0,16},{4,12},{8,24},{12,4},{16,0},{20,28},{24,8},{28,20},{1,17},{... | collective-permute-start | bytes 1327112 | tf_op jit(solution)/shard_map/ppermute | solution.py:409
  37.5 13.8 %collective-permute-start.6 = (bf16[288,768]{1,0:T(8,128)(2,1)S(1)}, bf16[288,768]{1,0:T(8,128)(2,1)S(1)}, u32[]{:S(2)}, u32[]{:S(2)}) collective-permute-start(bf16[288,768]{1,0:T(8,128)(2,1)S(1)} %collective-permute-done.1), channel_id=1, source_target_pairs={{0,8},{4,20},{8,0},{12,28},{16,24},{20,4},{24,16},{28,12},{1,9},{5... | collective-permute-start | bytes 1327112 | tf_op jit(solution)/shard_map/ppermute | solution.py:409
  38.0 13.3 %collective-permute-start.5 = (bf16[288,768]{1,0:T(8,128)(2,1)S(1)}, bf16[288,768]{1,0:T(8,128)(2,1)S(1)}, u32[]{:S(2)}, u32[]{:S(2)}) collective-permute-start(bf16[288,768]{1,0:T(8,128)(2,1)S(1)} %collective-permute-done.1), channel_id=1, source_target_pairs={{0,1},{1,2},{2,3},{3,0},{4,5},{5,6},{6,7},{7,4},{8,9},{9,10},{10,1... | collective-permute-start | bytes 1327112 | tf_op jit(solution)/shard_map/ppermute | solution.py:425
  38.0 11.1 %collective-permute-start.9 = (f32[8,768]{1,0:T(8,128)S(1)}, f32[8,768]{1,0:T(8,128)S(1)}, u32[]{:S(2)}, u32[]{:S(2)}) collective-permute-start(f32[8,768]{1,0:T(8,128)S(1)} %collective-permute-done.4.refs_17_), channel_id=1, source_target_pairs={{0,1},{1,2},{2,3},{3,0},{4,5},{5,6},{6,7},{7,4},{8,9},{9,10},{10,1... | collective-permute-start | bytes 73736 | tf_op jit(solution)/shard_map/ppermute | solution.py:425
  51.5 17.9 %collective-permute-start.13 = (bf16[4,288,768]{2,1,0:T(8,128)(2,1)S(1)}, bf16[4,288,768]{2,1,0:T(8,128)(2,1)S(1)}, u32[]{:S(2)}, u32[]{:S(2)}) collective-permute-start(bf16[4,288,768]{2,1,0:T(8,128)(2,1)S(1)} %pad_maximum_fusion.refs_0_), channel_id=1, source_target_pairs={{0,4},{4,0},{8,12},{12,8},{16,20},{20,16},{24,28},{28,24},{1,5},{5... | collective-permute-start | bytes 5308424 | tf_op jit(solution)/shard_map/ppermute | solution.py:409
  51.6 12.2 %collective-permute-start.12 = (bf16[288,768]{1,0:T(8,128)(2,1)S(1)}, bf16[288,768]{1,0:T(8,128)(2,1)S(1)}, u32[]{:S(2)}, u32[]{:S(2)}) collective-permute-start(bf16[288,768]{1,0:T(8,128)(2,1)S(1)} %collective-permute-done.6), channel_id=1, source_target_pairs={{0,16},{4,12},{8,24},{12,4},{16,0},{20,28},{24,8},{28,20},{1,17},{... | collective-permute-start | bytes 1327112 | tf_op jit(solution)/shard_map/ppermute | solution.py:409
  52.2 17.3 %collective-permute-start.11 = (bf16[288,768]{1,0:T(8,128)(2,1)S(1)}, bf16[288,768]{1,0:T(8,128)(2,1)S(1)}, u32[]{:S(2)}, u32[]{:S(2)}) collective-permute-start(bf16[288,768]{1,0:T(8,128)(2,1)S(1)} %collective-permute-done.5.refs_4_), channel_id=1, source_target_pairs={{0,16},{4,12},{8,24},{12,4},{16,0},{20,28},{24,8},{28,20},{1,17},{... | collective-permute-start | bytes 1327112 | tf_op jit(solution)/shard_map/ppermute | solution.py:409
  53.7 15.7 %collective-permute-start.10 = (bf16[288,768]{1,0:T(8,128)(2,1)S(1)}, bf16[288,768]{1,0:T(8,128)(2,1)S(1)}, u32[]{:S(2)}, u32[]{:S(2)}) collective-permute-start(bf16[288,768]{1,0:T(8,128)(2,1)S(1)} %collective-permute-done.5.refs_4_), channel_id=1, source_target_pairs={{0,8},{4,20},{8,0},{12,28},{16,24},{20,4},{24,16},{28,12},{1,9},{5... | collective-permute-start | bytes 1327112 | tf_op jit(solution)/shard_map/ppermute | solution.py:409
  82.8 18.5 %collective-permute-start.21 = (bf16[2,1760,128]{2,1,0:T(8,128)(2,1)S(1)}, bf16[2,1760,128]{2,1,0:T(8,128)(2,1)}, u32[]{:S(2)}, u32[]{:S(2)}) collective-permute-start(bf16[2,1760,128]{2,1,0:T(8,128)(2,1)S(1)} %shard_map.112.refs_8_), channel_id=1, source_target_pairs={{0,8},{4,20},{8,0},{12,28},{16,24},{20,4},{24,16},{28,12},{1,9},{5... | collective-permute-start | bytes 2703368 | tf_op jit(solution)/shard_map/ppermute | solution.py:409
  101.3 21.4 %collective-permute-start.22 = (bf16[2,1760,128]{2,1,0:T(8,128)(2,1)S(1)}, bf16[2,1760,128]{2,1,0:T(8,128)(2,1)}, u32[]{:S(2)}, u32[]{:S(2)}) collective-permute-start(bf16[2,1760,128]{2,1,0:T(8,128)(2,1)S(1)} %shard_map.112.refs_8_), channel_id=1, source_target_pairs={{0,16},{4,12},{8,24},{12,4},{16,0},{20,28},{24,8},{28,20},{1,17},{... | collective-permute-start | bytes 2703368 | tf_op jit(solution)/shard_map/ppermute | solution.py:409
  102.3 22.0 %collective-permute-start.23 = (bf16[2,1760,128]{2,1,0:T(8,128)(2,1)}, bf16[2,1760,128]{2,1,0:T(8,128)(2,1)}, u32[]{:S(2)}, u32[]{:S(2)}) collective-permute-start(bf16[2,1760,128]{2,1,0:T(8,128)(2,1)} %collective-permute-done.21.refs_9_), channel_id=1, source_target_pairs={{0,16},{4,12},{8,24},{12,4},{16,0},{20,28},{24,8},{28,20},{1,17},{... | collective-permute-start | bytes 2703368 | tf_op jit(solution)/shard_map/ppermute | solution.py:409
  130.9 13.1 %collective-permute-start.27 = (bf16[2,288,768]{2,1,0:T(8,128)(2,1)S(1)}, bf16[2,288,768]{2,1,0:T(8,128)(2,1)S(1)}, u32[]{:S(2)}, u32[]{:S(2)}) collective-permute-start(bf16[2,288,768]{2,1,0:T(8,128)(2,1)S(1)} %add.607), channel_id=1, source_target_pairs={{0,8},{4,20},{8,0},{12,28},{16,24},{20,4},{24,16},{28,12},{1,9},{5... | collective-permute-start | bytes 2654216 | tf_op jit(solution)/shard_map/ppermute | solution.py:409
  133.6 24.9 %collective-permute-start.34 = (bf16[2,288,768]{2,1,0:T(8,128)(2,1)}, bf16[2,288,768]{2,1,0:T(8,128)(2,1)}, u32[]{:S(2)}, u32[]{:S(2)}) collective-permute-start(bf16[2,288,768]{2,1,0:T(8,128)(2,1)} %get-tuple-element.269), channel_id=1, source_target_pairs={{0,4},{4,0},{8,12},{12,8},{16,20},{20,16},{24,28},{28,24},{1,5},{5... | collective-permute-start | bytes 2654216 | tf_op jit(solution)/shard_map/ppermute | solution.py:409
  133.6 24.9 %collective-permute-start.35 = (bf16[2,1760,128]{2,1,0:T(8,128)(2,1)S(1)}, bf16[2,1760,128]{2,1,0:T(8,128)(2,1)}, u32[]{:S(2)}, u32[]{:S(2)}) collective-permute-start(bf16[2,1760,128]{2,1,0:T(8,128)(2,1)S(1)} %shard_map.112.refs_8_), channel_id=1, source_target_pairs={{0,4},{4,0},{8,12},{12,8},{16,20},{20,16},{24,28},{28,24},{1,5},{5... | collective-permute-start | bytes 2703368 | tf_op jit(solution)/shard_map/ppermute | solution.py:409
  134.1 25.5 %collective-permute-start.36 = (bf16[2,1760,128]{2,1,0:T(8,128)(2,1)}, bf16[2,1760,128]{2,1,0:T(8,128)(2,1)}, u32[]{:S(2)}, u32[]{:S(2)}) collective-permute-start(bf16[2,1760,128]{2,1,0:T(8,128)(2,1)} %collective-permute-done.21.refs_9_), channel_id=1, source_target_pairs={{0,4},{4,0},{8,12},{12,8},{16,20},{20,16},{24,28},{28,24},{1,5},{5... | collective-permute-start | bytes 2703368 | tf_op jit(solution)/shard_map/ppermute | solution.py:409
  134.6 25.1 %collective-permute-start.33 = (bf16[2,288,768]{2,1,0:T(8,128)(2,1)}, bf16[2,288,768]{2,1,0:T(8,128)(2,1)}, u32[]{:S(2)}, u32[]{:S(2)}) collective-permute-start(bf16[2,288,768]{2,1,0:T(8,128)(2,1)} %add.610), channel_id=1, source_target_pairs={{0,8},{4,20},{8,0},{12,28},{16,24},{20,4},{24,16},{28,12},{1,9},{5... | collective-permute-start | bytes 2654216 | tf_op jit(solution)/shard_map/ppermute | solution.py:409
  145.1 14.5 %collective-permute-start.32 = (bf16[288,768]{1,0:T(8,128)(2,1)S(1)}, bf16[288,768]{1,0:T(8,128)(2,1)}, u32[]{:S(2)}, u32[]{:S(2)}) collective-permute-start(bf16[288,768]{1,0:T(8,128)(2,1)S(1)} %slice_bitcast_fusion.7), channel_id=1, source_target_pairs={{0,16},{4,12},{8,24},{12,4},{16,0},{20,28},{24,8},{28,20},{1,17},{... | collective-permute-start | bytes 1327112 | tf_op jit(solution)/shard_map/ppermute | solution.py:409
  158.6 18.1 %collective-permute-start.38 = (bf16[2,288,768]{2,1,0:T(8,128)(2,1)}, bf16[2,288,768]{2,1,0:T(8,128)(2,1)S(1)}, u32[]{:S(2)}, u32[]{:S(2)}) collective-permute-start(bf16[2,288,768]{2,1,0:T(8,128)(2,1)} %add.615), channel_id=1, source_target_pairs={{0,8},{4,20},{8,0},{12,28},{16,24},{20,4},{24,16},{28,12},{1,9},{5... | collective-permute-start | bytes 2654216 | tf_op jit(solution)/shard_map/ppermute | solution.py:409
  162.8 13.9 %collective-permute-start.37 = (bf16[288,768]{1,0:T(8,128)(2,1)S(1)}, bf16[288,768]{1,0:T(8,128)(2,1)S(1)}, u32[]{:S(2)}, u32[]{:S(2)}) collective-permute-start(bf16[288,768]{1,0:T(8,128)(2,1)S(1)} %slice_bitcast_fusion.6), channel_id=1, source_target_pairs={{0,16},{4,12},{8,24},{12,4},{16,0},{20,28},{24,8},{28,20},{1,17},{... | collective-permute-start | bytes 1327112 | tf_op jit(solution)/shard_map/ppermute | solution.py:409
  164.4 13.7 %collective-permute-start.39 = (bf16[288,768]{1,0:T(8,128)(2,1)S(1)}, bf16[288,768]{1,0:T(8,128)(2,1)S(1)}, u32[]{:S(2)}, u32[]{:S(2)}) collective-permute-start(bf16[288,768]{1,0:T(8,128)(2,1)S(1)} %fusion.7), channel_id=1, source_target_pairs={{0,1},{1,2},{2,3},{3,0},{4,5},{5,6},{6,7},{7,4},{8,9},{9,10},{10,1... | collective-permute-start | bytes 1327112 | tf_op jit(solution)/shard_map/ppermute | solution.py:425
  164.7 15.5 %collective-permute-start.46 = (bf16[2,1760,128]{2,1,0:T(8,128)(2,1)}, bf16[2,1760,128]{2,1,0:T(8,128)(2,1)S(1)}, u32[]{:S(2)}, u32[]{:S(2)}) collective-permute-start(bf16[2,1760,128]{2,1,0:T(8,128)(2,1)} %collective-permute-done.23.refs_11_), channel_id=1, source_target_pairs={{0,4},{4,0},{8,12},{12,8},{16,20},{20,16},{24,28},{28,24},{1,5},{5... | collective-permute-start | bytes 2703368 | tf_op jit(solution)/shard_map/ppermute | solution.py:409
  165.6 25.8 %collective-permute-start.43 = (bf16[2,288,768]{2,1,0:T(8,128)(2,1)S(1)}, bf16[2,288,768]{2,1,0:T(8,128)(2,1)S(1)}, u32[]{:S(2)}, u32[]{:S(2)}) collective-permute-start(bf16[2,288,768]{2,1,0:T(8,128)(2,1)S(1)} %add.618), channel_id=1, source_target_pairs={{0,8},{4,20},{8,0},{12,28},{16,24},{20,4},{24,16},{28,12},{1,9},{5... | collective-permute-start | bytes 2654216 | tf_op jit(solution)/shard_map/ppermute | solution.py:409
  178.3 13.6 %collective-permute-start.42 = (bf16[288,768]{1,0:T(8,128)(2,1)S(1)}, bf16[288,768]{1,0:T(8,128)(2,1)S(1)}, u32[]{:S(2)}, u32[]{:S(2)}) collective-permute-start(bf16[288,768]{1,0:T(8,128)(2,1)S(1)} %slice_bitcast_fusion.4), channel_id=1, source_target_pairs={{0,16},{4,12},{8,24},{12,4},{16,0},{20,28},{24,8},{28,20},{1,17},{... | collective-permute-start | bytes 1327112 | tf_op jit(solution)/shard_map/ppermute | solution.py:409
  178.9 13.0 %collective-permute-start.44 = (bf16[288,768]{1,0:T(8,128)(2,1)S(1)}, bf16[288,768]{1,0:T(8,128)(2,1)S(1)}, u32[]{:S(2)}, u32[]{:S(2)}) collective-permute-start(bf16[288,768]{1,0:T(8,128)(2,1)S(1)} %fusion.6), channel_id=1, source_target_pairs={{0,1},{1,2},{2,3},{3,0},{4,5},{5,6},{6,7},{7,4},{8,9},{9,10},{10,1... | collective-permute-start | bytes 1327112 | tf_op jit(solution)/shard_map/ppermute | solution.py:425
  179.0 12.9 %collective-permute-start.45 = (f32[16,768]{1,0:T(8,128)S(1)}, f32[16,768]{1,0:T(8,128)S(1)}, u32[]{:S(2)}, u32[]{:S(2)}) collective-permute-start(f32[16,768]{1,0:T(8,128)S(1)} %add.621), channel_id=1, source_target_pairs={{0,8},{4,12},{8,0},{12,4},{16,24},{20,28},{24,16},{28,20},{1,9},{5... | collective-permute-start | bytes 147464 | tf_op jit(solution)/shard_map/ppermute | solution.py:409
  194.4 12.5 %collective-permute-start.48 = (bf16[288,768]{1,0:T(8,128)(2,1)S(1)}, bf16[288,768]{1,0:T(8,128)(2,1)S(1)}, u32[]{:S(2)}, u32[]{:S(2)}) collective-permute-start(bf16[288,768]{1,0:T(8,128)(2,1)S(1)} %fusion.2), channel_id=1, source_target_pairs={{0,1},{1,2},{2,3},{3,0},{4,5},{5,6},{6,7},{7,4},{8,9},{9,10},{10,1... | collective-permute-start | bytes 1327112 | tf_op jit(solution)/shard_map/ppermute | solution.py:425
  (76 other events, 682.5 us)

commit v8 on v7

--- a/solution.py
+++ b/solution.py
@@ -588,9 +588,13 @@
         views += [block.at[p] for p in range(4)] if len(block.shape) == 3 else [block]
     ids = ids + [shard * REPS + r for r in range(REPS)]
     views += [own.at[pl.ds(r * PIECE, PIECE)] for r in range(REPS)]
-    for which, view in zip(ids, views):
-        row = pl.multiple_of(which * PIECE, 16)
-        pltpu.make_async_copy(view, held.at[pl.ds(row, PIECE)], sems.at[which]).start()
+    for early in (True, False):
+        for which, view in zip(ids, views):
+
+            @pl.when((which < 2 * REPS) == early)
+            def _(which=which, view=view):
+                row = pl.multiple_of(which * PIECE, 16)
+                pltpu.make_async_copy(view, held.at[pl.ds(row, PIECE)], sems.at[which]).start()
 
     def arrive(owner):
         for r in range(REPS):
@@ -761,6 +765,20 @@
     for copy in copies:
         copy.start()
     sums_out[...] = jnp.zeros_like(sums_out)
+    shard = where[PIECES]
+
+    def send_off(owner):
+        for hop in range(SHARDS):
+
+            @pl.when((shard + SHARDS - HOPS[hop]) % SHARDS == owner)
+            def _(hop=hop):
+                for turn in (2 * hop, 2 * hop + 1, 8 + 2 * hop, 9 + 2 * hop):
+                    pltpu.make_async_copy(
+                        grads.at[pl.ds(turn * 2 * PIECE, 2 * PIECE)],
+                        outs[turn],
+                        out_sems.at[turn],
+                    ).start()
+
     slot_row = lambda z, r: pl.multiple_of(where[z * REPS + r] * PIECE, 16)
 
     def keep_rows(z, begin, rows, part):
@@ -773,6 +791,7 @@
         keep_rows(
             0, 96 * j, 96, dot32(act1_t, mixed_in[:, D * j : D * (j + 1)]).astype(jnp.bfloat16)
         )
+    send_off(0)
     keep_rows(1, 0, 96, dot32(attn_in[...].T, gy).astype(jnp.bfloat16))
 
     for copy in copies:
@@ -803,23 +822,17 @@
                     at - D * (j - 1) : at - D * (j - 1) + rows, :
                 ]
                 at += rows
-        w1 = dot32(act2_t, grad_pre16).astype(jnp.bfloat16)
-        keep_rows(1, 96 + 48 * j, 48, w1[: D // 2])
-        keep_rows(2, 48 * j, 48, w1[D // 2 :])
-    copies = []
+    send_off(3)
+    for half, owner in enumerate((1, 2)):
+        side = act2_t[D // 2 * half : D // 2 * (half + 1), :]
+        for j in range(4):
+            w1 = dot32(side, pre_out[:, D * j : D * (j + 1)]).astype(jnp.bfloat16)
+            keep_rows(owner, (96 if owner == 1 else 0) + 48 * j, 48, w1)
+        send_off(owner)
     for turn, out in enumerate(outs):
-        for p in range(2):
-            copies.append(
-                pltpu.make_async_copy(
-                    grads.at[pl.ds((turn * 2 + p) * PIECE, PIECE)],
-                    out.at[p],
-                    out_sems.at[turn * 2 + p],
-                )
-            )
-    for copy in copies:
-        copy.start()
-    for copy in copies:
-        copy.wait()
+        pltpu.make_async_copy(
+            grads.at[pl.ds(turn * 2 * PIECE, 2 * PIECE)], out, out_sems.at[turn]
+        ).wait()
 
 
 def weight_gradients(slots, matrices, small):
@@ -839,7 +852,7 @@
                 pltpu.SemaphoreType.DMA((PIECES,)),
             ],
         ),
-        out_shape=[jax.ShapeDtypeStruct((2, PIECE, D), bf16)] * 16
+        out_shape=[jax.ShapeDtypeStruct((2 * PIECE, D), bf16)] * 16
         + [
             jax.ShapeDtypeStruct((TOK_DEV, FF), bf16),
             jax.ShapeDtypeStruct((TOK_DEV, FF), bf16),
@@ -912,7 +925,7 @@
             pltpu.SemaphoreType.DMA((SHARDS,)),
         ],
         out_shape=[rows, rows, jax.ShapeDtypeStruct((16, D), jnp.float32)],
-        compiler_params=pltpu.CompilerParams(vmem_limit_bytes=60 * 2**20),
+        compiler_params=pltpu.CompilerParams(vmem_limit_bytes=20 * 2**20),
         cost_estimate=pl.CostEstimate(
             flops=4 * 10**9, bytes_accessed=30 * 2**20, transcendentals=0
         ),
@@ -922,7 +935,7 @@
 SHARE = FLAT_ROWS // REPS
 BEGINS = tuple(SHARE * r // 16 * 16 for r in range(REPS)) + (FLAT_ROWS,)
 SHARE_ROWS = 1760
-STEP = 288
+STEP = 96
 
 
 def align_kernel(where, one_ref, two_ref, out_ref, held):
@@ -969,10 +982,12 @@
                 moments[turn], moment.at[where[1 + turn]], sems.at[REPS + 1 + turn]
             )
         )
-    for copy in copies:
+    for copy in copies[:REPS]:
         copy.start()
     for copy in copies[:REPS]:
         copy.wait()
+    for copy in copies[REPS:]:
+        copy.start()
     shard = where[0]
     for z in range(SHARDS):
 
@@ -1144,11 +1159,8 @@
     kept = pair[0]
     crossed = first_cross(far[1])
     last_near = core_cross(sent_near[3])
-    others = [core_cross(value) for value in moments[:2]]
     output, grad_input, vectors = results(small)
-    final, crossed, last_near, vectors, others = fence(
-        (final, crossed, last_near, vectors, others)
-    )
+    final, crossed, last_near, vectors = fence((final, crossed, last_near, vectors))
     near.append(kept_near[3] + last_near)
 
     carried = None
@@ -1163,10 +1175,13 @@
         met = plane_permute(vectors, ((1, 1), (2, 2), (4, 4))[turn - 1])
         if turn < SHARDS - 1:
             crossed = first_cross(far[turn + 1])
-            others.append(core_cross(moments[turn + 1]))
-            final, crossed, carried, met, others = fence((final, crossed, carried, met, others))
+            final, crossed, carried, met, moments = fence(
+                (final, crossed, carried, met, moments)
+            )
         else:
             final, carried, met = fence((final, carried, met))
+        if turn > 1:
+            moments.append(core_cross(moments[turn]))
         vectors = vectors + met
     total = kept + final + carried
 
@@ -1179,7 +1194,7 @@
     spread = [core_cross(value) for value in mine]
     both, spread = fence((both, spread))
     spread.append(core_cross(both))
-    return mine + [both] + spread, moments + others, output, grad_input, vectors
+    return mine + [both] + spread, moments, output, grad_input, vectors
 
 
 def on_device_rows(tokens, segment_ids, cotangent, params, moment_one, moment_two):
@@ -1194,14 +1209,15 @@
     matrices, *attended = attention(jnp.stack([shard] + ids), blocks, own, small)
     moments, first_moments, attended = fence((moments, first_moments, attended))
     moments = [moments, first_moments, second_cross(moments), second_cross(first_moments)]
+    moments += [core_cross(value) for value in moments[:2]]
     attn, mixed, low_sums, vecs = attended
     made = weight_gradients(
-        jnp.stack(slots_by_piece(shard, rep)), matrices, (normed, grad_y, attn, mixed, vecs)
+        jnp.stack(slots_by_piece(shard, rep) + [shard]), matrices, (normed, grad_y, attn, mixed, vecs)
     )
     made, moments = fence((made, moments))
     small = (tokens, normed, inv_std, grad_y, attn, mixed, low_sums, vecs) + tuple(made[16:])
     spread, moments, output, grad_input, vec_grads = scatter_sums(
-        made[:16], moments, small, lambda small: layer_results(matrices, small)
+        [part.reshape(2, PIECE, D) for part in made[:16]], moments, small, lambda small: layer_results(matrices, small)
     )
     own_vectors = lax.dynamic_index_in_dim(
         vec_grads.reshape(SHARDS, 4, D), shard, 0, keepdims=False

time: 249 us -> 247 us (level)
  waiting for transfers between devices: 113 us -> 121 us
  Pallas kernels: 77 us -> 71 us
  other arithmetic: 12.5 us -> 6.83 us
  local copies, waits for them, and re-layouts: 9.33 us -> 12.6 us
  starting transfers between devices: 35.7 us -> 33.2 us
    pallas_call x1, Pallas kernels: 11.2 us -> 5.79 us  [layer_results(): pl.pallas_call(result_kernel, in_specs=[hbm] + [vmem] * len(small), out_s...]
    ppermute x3, waiting for transfers between devices: 4.94 us -> 9.9 us  [ring_shift(): lax.ppermute(value, 'z', [(i, (i + hop) % SHARDS) for i in range(SHARDS)])]
    ppermute x48, waiting for transfers between devices: 73.9 us -> 77.7 us  [plane_permute(): lax.ppermute(value, PLANE, [(i, i ^ flips[i % 2]) for i in range(REPS)])]
    unnamed x96, local copies, waits for them, and re-layouts: 5.97 us -> 9.46 us
    add x3, other arithmetic: 3.16 us -> 0.43 us  [scatter_sums(): pair = near[turn] + crossed]
  transfers between devices with their start and end apart: 60 -> 60, of which waited for: 33 -> 31; matrix products, arithmetic and copies ran while one was open for 4% -> 2% of each run, Pallas kernels for 23% -> 20%
where the time goes in v8:
time: 247 us; the launch traced here: 246 us
  waiting for transfers between devices  121 us (49%)
  Pallas kernels  71 us (29%)
  starting transfers between devices  33.2 us (13%)
  local copies, waits for them, and re-layouts  12.6 us (5%)
  other arithmetic  6.83 us (3%)
    ppermute x48, waiting for transfers between devices, plane_permute(): lax.ppermute(value, PLANE, [(i, i ^ flips[i % 2]) for i in range(REPS)])  77.7 us
    ppermute x9, waiting for transfers between devices, ring_step(): lax.ppermute(value, 'z', [(i, (i + 1) % SHARDS) for i in range(SHARDS)])  33.2 us
    ppermute x48, starting transfers between devices, plane_permute(): lax.ppermute(value, PLANE, [(i, i ^ flips[i % 2]) for i in range(REPS)])  28.6 us
    pallas_call x1, Pallas kernels, update_shard(): pl.pallas_call(functools.partial(update_kernel, factor), grid_spec=pltpu....  20 us
    pallas_call x1, Pallas kernels, weight_gradients(): pl.pallas_call(gradient_kernel, grid_spec=pltpu.PrefetchScalarGridSpec(nu...  17.9 us
    pallas_call x1, Pallas kernels, attention(): pl.pallas_call(attention_kernel, grid_spec=pltpu.PrefetchScalarGridSpec(n...  14.9 us
    pallas_call x2, Pallas kernels, pack_pieces(): pl.pallas_call(pack_kernel, grid_spec=pltpu.PrefetchScalarGridSpec(num_sc...  11.6 us
    ppermute x3, waiting for transfers between devices, ring_shift(): lax.ppermute(value, 'z', [(i, (i + hop) % SHARDS) for i in range(SHARDS)])  9.9 us
  transfers between devices with their start and end apart: 60, of which 31 were waited for; matrix products, arithmetic and copies ran while one was open for 2% of the time, Pallas kernels for 20%

profile of v8, /device:TPU:0, one launch (start us, length us, event | category | flops | bytes accessed | tf_op | source)
XLA Modules:
  0.0 246.0 jit_solution(1062558395370747856)
XLA Ops:
  1.2 2.8 %shard_map.109 = bf16[1,288,768]{2,1,0:T(8,128)(2,1)} custom-call(s32[2]{0:T(128)} %pad_add_fusion.where, f32[13848,128]{1,0:T(8,128)} %bitcast.132), custom_call_target="tpu_custom_call" | custom-call | tf_op jit(solution)/shard_map/pallas_call | solution.py:522
  4.0 3.1 %collective-permute-start = (bf16[288,768]{1,0:T(8,128)(2,1)}, bf16[288,768]{1,0:T(8,128)(2,1)S(1)}, u32[]{:S(2)}, u32[]{:S(2)}) collective-permute-start(bf16[288,768]{1,0:T(8,128)(2,1)} %bitcast.151), channel_id=1, source_target_pairs={{0,1},{1,2},{2,3},{3,0},{4,5},{5,6},{6,7},{7,4},{8,9},{9,10},{10,1... | collective-permute-start | bytes 1327112 | tf_op jit(solution)/shard_map/ppermute | solution.py:425
  7.7 8.9 %shard_map.110 = (bf16[8,288,768]{2,1,0:T(8,128)(2,1)}, f32[8,768]{1,0:T(8,128)}) custom-call(s32[9]{0:T(128)} %stack.274.where, f32[13848,128]{1,0:T(8,128)} %bitcast.133), custom_call_target="tpu_custom_call" | custom-call | tf_op jit(solution)/shard_map/pallas_call | solution.py:522
  16.6 2.8 %collective-permute-done = bf16[288,768]{1,0:T(8,128)(2,1)S(1)} collective-permute-done((bf16[288,768]{1,0:T(8,128)(2,1)}, bf16[288,768]{1,0:T(8,128)(2,1)S(1)}, u32[]{:S(2)}, u32[]{:S(2)}) %collective-permute-start) | collective-permute-done | bytes 442400 | tf_op jit(solution)/shard_map/ppermute | solution.py:425
  26.7 8.7 %collective-permute-done.4.refs_17_ = f32[8,768]{1,0:T(8,128)S(1)} collective-permute-done((f32[8,768]{1,0:T(8,128)}, f32[8,768]{1,0:T(8,128)S(1)}, u32[]{:S(2)}, u32[]{:S(2)}) %collective-permute-start.4) | collective-permute-done | bytes 24608 | tf_op jit(solution)/shard_map/ppermute | solution.py:425
  38.0 11.1 %collective-permute-done.9.refs_18_ = f32[8,768]{1,0:T(8,128)S(1)} collective-permute-done((f32[8,768]{1,0:T(8,128)S(1)}, f32[8,768]{1,0:T(8,128)S(1)}, u32[]{:S(2)}, u32[]{:S(2)}) %collective-permute-start.9) | collective-permute-done | bytes 24608 | tf_op jit(solution)/shard_map/ppermute | solution.py:425
  49.1 2.2 collective-permute-done.7
  52.2 1.5 collective-permute-start.11
  54.3 5.6 %collective-permute-done.14.refs_19_ = f32[8,768]{1,0:T(8,128)S(1)} collective-permute-done((f32[8,768]{1,0:T(8,128)S(1)}, f32[8,768]{1,0:T(8,128)S(1)}, u32[]{:S(2)}, u32[]{:S(2)}) %collective-permute-start.14) | collective-permute-done | bytes 24608 | tf_op jit(solution)/shard_map/ppermute | solution.py:425
  59.9 3.9 %collective-permute-done.12 = bf16[288,768]{1,0:T(8,128)(2,1)S(1)} collective-permute-done((bf16[288,768]{1,0:T(8,128)(2,1)S(1)}, bf16[288,768]{1,0:T(8,128)(2,1)S(1)}, u32[]{:S(2)}, u32[]{:S(2)}) %collective-permute-start.12) | collective-permute-done | bytes 442400 | tf_op jit(solution)/shard_map/ppermute | solution.py:409
  63.8 5.7 %collective-permute-done.11.refs_6_ = bf16[288,768]{1,0:T(8,128)(2,1)S(1)} collective-permute-done((bf16[288,768]{1,0:T(8,128)(2,1)S(1)}, bf16[288,768]{1,0:T(8,128)(2,1)S(1)}, u32[]{:S(2)}, u32[]{:S(2)}) %collective-permute-start.11) | collective-permute-done | bytes 442400 | tf_op jit(solution)/shard_map/ppermute | solution.py:409
  72.4 3.0 %collective-permute-done.15.refs_8_ = bf16[288,768]{1,0:T(8,128)(2,1)S(1)} collective-permute-done((bf16[288,768]{1,0:T(8,128)(2,1)S(1)}, bf16[288,768]{1,0:T(8,128)(2,1)S(1)}, u32[]{:S(2)}, u32[]{:S(2)}) %collective-permute-start.15) | collective-permute-done | bytes 442400 | tf_op jit(solution)/shard_map/ppermute | solution.py:409
  76.1 3.9 %collective-permute-done.18.refs_7_ = bf16[288,768]{1,0:T(8,128)(2,1)S(1)} collective-permute-done((bf16[288,768]{1,0:T(8,128)(2,1)S(1)}, bf16[288,768]{1,0:T(8,128)(2,1)S(1)}, u32[]{:S(2)}, u32[]{:S(2)}) %collective-permute-start.18) | collective-permute-done | bytes 442400 | tf_op jit(solution)/shard_map/ppermute | solution.py:409
  80.2 1.8 collective-permute-done.20.refs_11_
  84.6 14.9 %shard_map.113 = (bf16[9216,768]{1,0:T(8,128)(2,1)}, bf16[128,768]{1,0:T(8,128)(2,1)}, bf16[128,2304]{1,0:T(8,128)(2,1)}, f32[8,768]{1,0:T(8,128)}, f32[16,768]{1,0:T(8,128)}) custom-call(s32[25]{0:T(128)} %stack.271.where, bf16[4,288,768]{2,1,0:T(8,128)(2,1)} %copy-done.19, bf16[4,288,768]{2,1,0:T(8,128)(2,1)} %copy-done.34, ...), custom_call_target="tpu_custom_call" | custom-call | flops 6000000000 | bytes 62914560 | tf_op jit(solution)/shard_map/pallas_call | solution.py:726
  101.8 17.9 %shard_map.114 = (bf16[576,768]{1,0:T(8,128)(2,1)}, bf16[576,768]{1,0:T(8,128)(2,1)}, bf16[576,768]{1,0:T(8,128)(2,1)}, bf16[576,768]{1,0:T(8,128)(2,1)}, bf16[5...) custom-call(s32[33]{0:T(128)} %stack.317.where, ...), custom_call_target="tpu_custom_call" | custom-call | flops 10000000000 | bytes 62914560 | tf_op jit(solution)/shard_map/pallas_call | solution.py:842
  119.8 2.9 %collective-permute-done.23.refs_11_ = bf16[2,1760,128]{2,1,0:T(8,128)(2,1)} collective-permute-done((bf16[2,1760,128]{2,1,0:T(8,128)(2,1)}, bf16[2,1760,128]{2,1,0:T(8,128)(2,1)}, u32[]{:S(2)}, u32[]{:S(2)}) %collective-permute-start.23) | collective-permute-done | bytes 901152 | tf_op jit(solution)/shard_map/ppermute | solution.py:409
  123.6 1.6 collective-permute-done.26
  129.2 1.6 collective-permute-start.29
  132.8 9.5 %collective-permute-done.29 = bf16[2,288,768]{2,1,0:T(8,128)(2,1)S(1)} collective-permute-done((bf16[2,288,768]{2,1,0:T(8,128)(2,1)S(1)}, bf16[2,288,768]{2,1,0:T(8,128)(2,1)S(1)}, u32[]{:S(2)}, u32[]{:S(2)}) %collective-permute-start.29) | collective-permute-done | bytes 884768 | tf_op jit(solution)/shard_map/ppermute | solution.py:409
  145.4 5.0 %copy-done = bf16[9216,768]{1,0:T(8,128)(2,1)S(1)} copy-done((bf16[9216,768]{1,0:T(8,128)(2,1)S(1)}, bf16[9216,768]{1,0:T(8,128)(2,1)}, u32[]{:S(2)}) %copy-start) | copy-done | bytes 14155800
  150.4 5.8 %shard_map.115 = (f32[128,768]{1,0:T(8,128)}, f32[128,768]{1,0:T(8,128)}, f32[16,768]{1,0:T(8,128)S(1)}) custom-call(bf16[9216,768]{1,0:T(8,128)(2,1)S(1)} %copy-done, bf16[128,768]{1,0:T(8,128)(2,1)S(1)} %copy-done.4, f32[128,768]{1,0:T(8,128)S(1)} %copy-done.9, f32[128,128]{1,0:T(8,128)S(1)} %get-tuple-element.257.refs_2_, ...), custom_call_target="tpu_custom_call" | custom-call | flops 4000000000 | bytes 31457280 | tf_op jit(solution)/shard_map/pallas_call | solution.py:919
  159.7 11.1 %collective-permute-done.38 = bf16[2,288,768]{2,1,0:T(8,128)(2,1)S(1)} collective-permute-done((bf16[2,288,768]{2,1,0:T(8,128)(2,1)S(1)}, bf16[2,288,768]{2,1,0:T(8,128)(2,1)S(1)}, u32[]{:S(2)}, u32[]{:S(2)}) %collective-permute-start.38) | collective-permute-done | bytes 884768 | tf_op jit(solution)/shard_map/ppermute | solution.py:409
  173.4 12.1 %collective-permute-done.42 = bf16[2,288,768]{2,1,0:T(8,128)(2,1)S(1)} collective-permute-done((bf16[2,288,768]{2,1,0:T(8,128)(2,1)S(1)}, bf16[2,288,768]{2,1,0:T(8,128)(2,1)S(1)}, u32[]{:S(2)}, u32[]{:S(2)}) %collective-permute-start.42) | collective-permute-done | bytes 884768 | tf_op jit(solution)/shard_map/ppermute | solution.py:409
  188.6 6.6 %collective-permute-done.47 = f32[16,768]{1,0:T(8,128)S(1)} collective-permute-done((f32[16,768]{1,0:T(8,128)S(1)}, f32[16,768]{1,0:T(8,128)S(1)}, u32[]{:S(2)}, u32[]{:S(2)}) %collective-permute-start.47) | collective-permute-done | bytes 49184 | tf_op jit(solution)/shard_map/ppermute | solution.py:409
  195.2 4.6 %collective-permute-done.46 = bf16[288,768]{1,0:T(8,128)(2,1)S(1)} collective-permute-done((bf16[288,768]{1,0:T(8,128)(2,1)S(1)}, bf16[288,768]{1,0:T(8,128)(2,1)S(1)}, u32[]{:S(2)}, u32[]{:S(2)}) %collective-permute-start.46) | collective-permute-done | bytes 442400 | tf_op jit(solution)/shard_map/ppermute | solution.py:425
  201.9 4.0 %collective-permute-done.52 = f32[16,768]{1,0:T(8,128)S(1)} collective-permute-done((f32[16,768]{1,0:T(8,128)S(1)}, f32[16,768]{1,0:T(8,128)S(1)}, u32[]{:S(2)}, u32[]{:S(2)}) %collective-permute-start.52) | collective-permute-done | bytes 49184 | tf_op jit(solution)/shard_map/ppermute | solution.py:1079
  207.0 4.8 %collective-permute-done.50 = f32[16,768]{1,0:T(8,128)S(1)} collective-permute-done((f32[16,768]{1,0:T(8,128)S(1)}, f32[16,768]{1,0:T(8,128)S(1)}, u32[]{:S(2)}, u32[]{:S(2)}) %collective-permute-start.50) | collective-permute-done | bytes 49184 | tf_op jit(solution)/shard_map/ppermute | solution.py:1079
  213.0 1.9 collective-permute-done.56.refs_6_
  215.5 5.4 %collective-permute-done.53.refs_3_ = bf16[288,768]{1,0:T(8,128)(2,1)} collective-permute-done((bf16[288,768]{1,0:T(8,128)(2,1)S(1)}, bf16[288,768]{1,0:T(8,128)(2,1)}, u32[]{:S(2)}, u32[]{:S(2)}) %collective-permute-start.53) | collective-permute-done | bytes 442400 | tf_op jit(solution)/shard_map/ppermute | solution.py:409
  223.1 20.0 %shard_map.116 = (f32[13848,128]{1,0:T(8,128)}, f32[13848,128]{1,0:T(8,128)}) custom-call(s32[9]{0:T(128)} %stack.325.where, bf16[288,768]{1,0:T(8,128)(2,1)} %copy-done.21, bf16[288,768]{1,0:T(8,128)(2,1)} %copy-done.30, bf16[288,768]{1,0:T(8,128)(2,1)} %copy-done.29, bf16[288,768]{1,0:T(8,128)(2,1)} %collective-permute-done.53.refs_3_, ...), custom_call_target="tpu_custom_call" | custom-call | tf_op jit(solution)/shard_map/pallas_call | solution.py:1057
  243.2 2.8 %fusion = (f32[221568]{0:T(1024)}, f32[221568]{0:T(1024)}) fusion(f32[221568]{0:T(1024)S(1)} %copy-done.3, f32[1772544]{0:T(1024)} %bitcast.152, s32[]{:T(128)S(6)} %select_n.334, f32[221568]{0:T(1024)S(1)} %copy-done.2), kind=kLoop, calls=%fused_computation.3 | loop fusion | flops 1550976 | bytes 4431364 | tf_op jit(solution)/shard_map/add | solution.py:352
  (223 shorter events, 47.0 us)
Async XLA Ops:
  4.0 15.5 %collective-permute-start = (bf16[288,768]{1,0:T(8,128)(2,1)}, bf16[288,768]{1,0:T(8,128)(2,1)S(1)}, u32[]{:S(2)}, u32[]{:S(2)}) collective-permute-start(bf16[288,768]{1,0:T(8,128)(2,1)} %bitcast.151), channel_id=1, source_target_pairs={{0,1},{1,2},{2,3},{3,0},{4,5},{5,6},{6,7},{7,4},{8,9},{9,10},{10,1... | collective-permute-start | bytes 1327112 | tf_op jit(solution)/shard_map/ppermute | solution.py:425
  19.5 15.9 %collective-permute-start.3 = (bf16[288,768]{1,0:T(8,128)(2,1)S(1)}, bf16[288,768]{1,0:T(8,128)(2,1)S(1)}, u32[]{:S(2)}, u32[]{:S(2)}) collective-permute-start(bf16[288,768]{1,0:T(8,128)(2,1)S(1)} %collective-permute-done), channel_id=1, source_target_pairs={{0,16},{4,12},{8,24},{12,4},{16,0},{20,28},{24,8},{28,20},{1,17},{... | collective-permute-start | bytes 1327112 | tf_op jit(solution)/shard_map/ppermute | solution.py:409
  21.0 14.4 %collective-permute-start.2 = (bf16[288,768]{1,0:T(8,128)(2,1)S(1)}, bf16[288,768]{1,0:T(8,128)(2,1)S(1)}, u32[]{:S(2)}, u32[]{:S(2)}) collective-permute-start(bf16[288,768]{1,0:T(8,128)(2,1)S(1)} %collective-permute-done), channel_id=1, source_target_pairs={{0,8},{4,20},{8,0},{12,28},{16,24},{20,4},{24,16},{28,12},{1,9},{5... | collective-permute-start | bytes 1327112 | tf_op jit(solution)/shard_map/ppermute | solution.py:409
  22.5 12.9 %collective-permute-start.1 = (bf16[288,768]{1,0:T(8,128)(2,1)S(1)}, bf16[288,768]{1,0:T(8,128)(2,1)S(1)}, u32[]{:S(2)}, u32[]{:S(2)}) collective-permute-start(bf16[288,768]{1,0:T(8,128)(2,1)S(1)} %collective-permute-done), channel_id=1, source_target_pairs={{0,1},{1,2},{2,3},{3,0},{4,5},{5,6},{6,7},{7,4},{8,9},{9,10},{10,1... | collective-permute-start | bytes 1327112 | tf_op jit(solution)/shard_map/ppermute | solution.py:425
  22.5 12.9 %collective-permute-start.4 = (f32[8,768]{1,0:T(8,128)}, f32[8,768]{1,0:T(8,128)S(1)}, u32[]{:S(2)}, u32[]{:S(2)}) collective-permute-start(f32[8,768]{1,0:T(8,128)} %get-tuple-element.170.refs_16_), channel_id=1, source_target_pairs={{0,1},{1,2},{2,3},{3,0},{4,5},{5,6},{6,7},{7,4},{8,9},{9,10},{10,1... | collective-permute-start | bytes 73736 | tf_op jit(solution)/shard_map/ppermute | solution.py:425
  35.4 13.7 %collective-permute-start.8 = (bf16[288,768]{1,0:T(8,128)(2,1)S(1)}, bf16[288,768]{1,0:T(8,128)(2,1)S(1)}, u32[]{:S(2)}, u32[]{:S(2)}) collective-permute-start(bf16[288,768]{1,0:T(8,128)(2,1)S(1)} %collective-permute-done.2), channel_id=1, source_target_pairs={{0,16},{4,12},{8,24},{12,4},{16,0},{20,28},{24,8},{28,20},{1,17},{... | collective-permute-start | bytes 1327112 | tf_op jit(solution)/shard_map/ppermute | solution.py:409
  36.0 15.3 %collective-permute-start.7 = (bf16[288,768]{1,0:T(8,128)(2,1)S(1)}, bf16[288,768]{1,0:T(8,128)(2,1)S(1)}, u32[]{:S(2)}, u32[]{:S(2)}) collective-permute-start(bf16[288,768]{1,0:T(8,128)(2,1)S(1)} %collective-permute-done.1), channel_id=1, source_target_pairs={{0,16},{4,12},{8,24},{12,4},{16,0},{20,28},{24,8},{28,20},{1,17},{... | collective-permute-start | bytes 1327112 | tf_op jit(solution)/shard_map/ppermute | solution.py:409
  37.5 13.8 %collective-permute-start.6 = (bf16[288,768]{1,0:T(8,128)(2,1)S(1)}, bf16[288,768]{1,0:T(8,128)(2,1)S(1)}, u32[]{:S(2)}, u32[]{:S(2)}) collective-permute-start(bf16[288,768]{1,0:T(8,128)(2,1)S(1)} %collective-permute-done.1), channel_id=1, source_target_pairs={{0,8},{4,20},{8,0},{12,28},{16,24},{20,4},{24,16},{28,12},{1,9},{5... | collective-permute-start | bytes 1327112 | tf_op jit(solution)/shard_map/ppermute | solution.py:409
  38.0 13.3 %collective-permute-start.5 = (bf16[288,768]{1,0:T(8,128)(2,1)S(1)}, bf16[288,768]{1,0:T(8,128)(2,1)S(1)}, u32[]{:S(2)}, u32[]{:S(2)}) collective-permute-start(bf16[288,768]{1,0:T(8,128)(2,1)S(1)} %collective-permute-done.1), channel_id=1, source_target_pairs={{0,1},{1,2},{2,3},{3,0},{4,5},{5,6},{6,7},{7,4},{8,9},{9,10},{10,1... | collective-permute-start | bytes 1327112 | tf_op jit(solution)/shard_map/ppermute | solution.py:425
  51.5 17.9 %collective-permute-start.13 = (bf16[4,288,768]{2,1,0:T(8,128)(2,1)S(1)}, bf16[4,288,768]{2,1,0:T(8,128)(2,1)S(1)}, u32[]{:S(2)}, u32[]{:S(2)}) collective-permute-start(bf16[4,288,768]{2,1,0:T(8,128)(2,1)S(1)} %pad_maximum_fusion.refs_0_), channel_id=1, source_target_pairs={{0,4},{4,0},{8,12},{12,8},{16,20},{20,16},{24,28},{28,24},{1,5},{5... | collective-permute-start | bytes 5308424 | tf_op jit(solution)/shard_map/ppermute | solution.py:409
  51.6 12.2 %collective-permute-start.12 = (bf16[288,768]{1,0:T(8,128)(2,1)S(1)}, bf16[288,768]{1,0:T(8,128)(2,1)S(1)}, u32[]{:S(2)}, u32[]{:S(2)}) collective-permute-start(bf16[288,768]{1,0:T(8,128)(2,1)S(1)} %collective-permute-done.6), channel_id=1, source_target_pairs={{0,16},{4,12},{8,24},{12,4},{16,0},{20,28},{24,8},{28,20},{1,17},{... | collective-permute-start | bytes 1327112 | tf_op jit(solution)/shard_map/ppermute | solution.py:409
  52.2 17.3 %collective-permute-start.11 = (bf16[288,768]{1,0:T(8,128)(2,1)S(1)}, bf16[288,768]{1,0:T(8,128)(2,1)S(1)}, u32[]{:S(2)}, u32[]{:S(2)}) collective-permute-start(bf16[288,768]{1,0:T(8,128)(2,1)S(1)} %collective-permute-done.5.refs_4_), channel_id=1, source_target_pairs={{0,16},{4,12},{8,24},{12,4},{16,0},{20,28},{24,8},{28,20},{1,17},{... | collective-permute-start | bytes 1327112 | tf_op jit(solution)/shard_map/ppermute | solution.py:409
  53.7 15.7 %collective-permute-start.10 = (bf16[288,768]{1,0:T(8,128)(2,1)S(1)}, bf16[288,768]{1,0:T(8,128)(2,1)S(1)}, u32[]{:S(2)}, u32[]{:S(2)}) collective-permute-start(bf16[288,768]{1,0:T(8,128)(2,1)S(1)} %collective-permute-done.5.refs_4_), channel_id=1, source_target_pairs={{0,8},{4,20},{8,0},{12,28},{16,24},{20,4},{24,16},{28,12},{1,9},{5... | collective-permute-start | bytes 1327112 | tf_op jit(solution)/shard_map/ppermute | solution.py:409
  82.8 16.7 %collective-permute-start.21 = (bf16[2,1760,128]{2,1,0:T(8,128)(2,1)S(1)}, bf16[2,1760,128]{2,1,0:T(8,128)(2,1)}, u32[]{:S(2)}, u32[]{:S(2)}) collective-permute-start(bf16[2,1760,128]{2,1,0:T(8,128)(2,1)S(1)} %shard_map.112.refs_8_), channel_id=1, source_target_pairs={{0,8},{4,20},{8,0},{12,28},{16,24},{20,4},{24,16},{28,12},{1,9},{5... | collective-permute-start | bytes 2703368 | tf_op jit(solution)/shard_map/ppermute | solution.py:409
  99.5 20.2 %collective-permute-start.24 = (bf16[2,1760,128]{2,1,0:T(8,128)(2,1)S(1)}, bf16[2,1760,128]{2,1,0:T(8,128)(2,1)}, u32[]{:S(2)}, u32[]{:S(2)}) collective-permute-start(bf16[2,1760,128]{2,1,0:T(8,128)(2,1)S(1)} %shard_map.112.refs_8_), channel_id=1, source_target_pairs={{0,4},{4,0},{8,12},{12,8},{16,20},{20,16},{24,28},{28,24},{1,5},{5... | collective-permute-start | bytes 2703368 | tf_op jit(solution)/shard_map/ppermute | solution.py:409
  99.6 20.2 %collective-permute-start.22 = (bf16[2,1760,128]{2,1,0:T(8,128)(2,1)S(1)}, bf16[2,1760,128]{2,1,0:T(8,128)(2,1)}, u32[]{:S(2)}, u32[]{:S(2)}) collective-permute-start(bf16[2,1760,128]{2,1,0:T(8,128)(2,1)S(1)} %shard_map.112.refs_8_), channel_id=1, source_target_pairs={{0,16},{4,12},{8,24},{12,4},{16,0},{20,28},{24,8},{28,20},{1,17},{... | collective-permute-start | bytes 2703368 | tf_op jit(solution)/shard_map/ppermute | solution.py:409
  100.9 18.8 %collective-permute-start.25 = (bf16[2,1760,128]{2,1,0:T(8,128)(2,1)}, bf16[2,1760,128]{2,1,0:T(8,128)(2,1)}, u32[]{:S(2)}, u32[]{:S(2)}) collective-permute-start(bf16[2,1760,128]{2,1,0:T(8,128)(2,1)} %collective-permute-done.21.refs_9_), channel_id=1, source_target_pairs={{0,4},{4,0},{8,12},{12,8},{16,20},{20,16},{24,28},{28,24},{1,5},{5... | collective-permute-start | bytes 2703368 | tf_op jit(solution)/shard_map/ppermute | solution.py:409
  101.3 21.3 %collective-permute-start.23 = (bf16[2,1760,128]{2,1,0:T(8,128)(2,1)}, bf16[2,1760,128]{2,1,0:T(8,128)(2,1)}, u32[]{:S(2)}, u32[]{:S(2)}) collective-permute-start(bf16[2,1760,128]{2,1,0:T(8,128)(2,1)} %collective-permute-done.21.refs_9_), channel_id=1, source_target_pairs={{0,16},{4,12},{8,24},{12,4},{16,0},{20,28},{24,8},{28,20},{1,17},{... | collective-permute-start | bytes 2703368 | tf_op jit(solution)/shard_map/ppermute | solution.py:409
  129.2 13.1 %collective-permute-start.29 = (bf16[2,288,768]{2,1,0:T(8,128)(2,1)S(1)}, bf16[2,288,768]{2,1,0:T(8,128)(2,1)S(1)}, u32[]{:S(2)}, u32[]{:S(2)}) collective-permute-start(bf16[2,288,768]{2,1,0:T(8,128)(2,1)S(1)} %add.607), channel_id=1, source_target_pairs={{0,8},{4,20},{8,0},{12,28},{16,24},{20,4},{24,16},{28,12},{1,9},{5... | collective-permute-start | bytes 2654216 | tf_op jit(solution)/shard_map/ppermute | solution.py:409
  131.1 25.1 %collective-permute-start.36 = (bf16[2,288,768]{2,1,0:T(8,128)(2,1)S(1)}, bf16[2,288,768]{2,1,0:T(8,128)(2,1)S(1)}, u32[]{:S(2)}, u32[]{:S(2)}) collective-permute-start(bf16[2,288,768]{2,1,0:T(8,128)(2,1)S(1)} %bitcast.156), channel_id=1, source_target_pairs={{0,4},{4,0},{8,12},{12,8},{16,20},{20,16},{24,28},{28,24},{1,5},{5... | collective-permute-start | bytes 2654216 | tf_op jit(solution)/shard_map/ppermute | solution.py:409
  131.1 25.4 %collective-permute-start.35 = (bf16[2,288,768]{2,1,0:T(8,128)(2,1)S(1)}, bf16[2,288,768]{2,1,0:T(8,128)(2,1)S(1)}, u32[]{:S(2)}, u32[]{:S(2)}) collective-permute-start(bf16[2,288,768]{2,1,0:T(8,128)(2,1)S(1)} %add.610), channel_id=1, source_target_pairs={{0,8},{4,20},{8,0},{12,28},{16,24},{20,4},{24,16},{28,12},{1,9},{5... | collective-permute-start | bytes 2654216 | tf_op jit(solution)/shard_map/ppermute | solution.py:409
  142.6 13.9 %collective-permute-start.34 = (bf16[288,768]{1,0:T(8,128)(2,1)S(1)}, bf16[288,768]{1,0:T(8,128)(2,1)S(1)}, u32[]{:S(2)}, u32[]{:S(2)}) collective-permute-start(bf16[288,768]{1,0:T(8,128)(2,1)S(1)} %slice_bitcast_fusion.7), channel_id=1, source_target_pairs={{0,16},{4,12},{8,24},{12,4},{16,0},{20,28},{24,8},{28,20},{1,17},{... | collective-permute-start | bytes 1327112 | tf_op jit(solution)/shard_map/ppermute | solution.py:409
  144.2 26.6 %collective-permute-start.38 = (bf16[2,288,768]{2,1,0:T(8,128)(2,1)S(1)}, bf16[2,288,768]{2,1,0:T(8,128)(2,1)S(1)}, u32[]{:S(2)}, u32[]{:S(2)}) collective-permute-start(bf16[2,288,768]{2,1,0:T(8,128)(2,1)S(1)} %add.615), channel_id=1, source_target_pairs={{0,8},{4,20},{8,0},{12,28},{16,24},{20,4},{24,16},{28,12},{1,9},{5... | collective-permute-start | bytes 2654216 | tf_op jit(solution)/shard_map/ppermute | solution.py:409
  156.8 14.0 %collective-permute-start.37 = (bf16[288,768]{1,0:T(8,128)(2,1)S(1)}, bf16[288,768]{1,0:T(8,128)(2,1)S(1)}, u32[]{:S(2)}, u32[]{:S(2)}) collective-permute-start(bf16[288,768]{1,0:T(8,128)(2,1)S(1)} %slice_bitcast_fusion.6), channel_id=1, source_target_pairs={{0,16},{4,12},{8,24},{12,4},{16,0},{20,28},{24,8},{28,20},{1,17},{... | collective-permute-start | bytes 1327112 | tf_op jit(solution)/shard_map/ppermute | solution.py:409
  158.1 13.0 %collective-permute-start.39 = (bf16[288,768]{1,0:T(8,128)(2,1)S(1)}, bf16[288,768]{1,0:T(8,128)(2,1)S(1)}, u32[]{:S(2)}, u32[]{:S(2)}) collective-permute-start(bf16[288,768]{1,0:T(8,128)(2,1)S(1)} %fusion.7), channel_id=1, source_target_pairs={{0,1},{1,2},{2,3},{3,0},{4,5},{5,6},{6,7},{7,4},{8,9},{9,10},{10,1... | collective-permute-start | bytes 1327112 | tf_op jit(solution)/shard_map/ppermute | solution.py:425
  158.4 27.1 %collective-permute-start.42 = (bf16[2,288,768]{2,1,0:T(8,128)(2,1)S(1)}, bf16[2,288,768]{2,1,0:T(8,128)(2,1)S(1)}, u32[]{:S(2)}, u32[]{:S(2)}) collective-permute-start(bf16[2,288,768]{2,1,0:T(8,128)(2,1)S(1)} %add.618), channel_id=1, source_target_pairs={{0,8},{4,20},{8,0},{12,28},{16,24},{20,4},{24,16},{28,12},{1,9},{5... | collective-permute-start | bytes 2654216 | tf_op jit(solution)/shard_map/ppermute | solution.py:409
  171.3 14.7 %collective-permute-start.41 = (bf16[288,768]{1,0:T(8,128)(2,1)S(1)}, bf16[288,768]{1,0:T(8,128)(2,1)S(1)}, u32[]{:S(2)}, u32[]{:S(2)}) collective-permute-start(bf16[288,768]{1,0:T(8,128)(2,1)S(1)} %slice_bitcast_fusion.4), channel_id=1, source_target_pairs={{0,16},{4,12},{8,24},{12,4},{16,0},{20,28},{24,8},{28,20},{1,17},{... | collective-permute-start | bytes 1327112 | tf_op jit(solution)/shard_map/ppermute | solution.py:409
  172.4 13.7 %collective-permute-start.43 = (bf16[288,768]{1,0:T(8,128)(2,1)S(1)}, bf16[288,768]{1,0:T(8,128)(2,1)S(1)}, u32[]{:S(2)}, u32[]{:S(2)}) collective-permute-start(bf16[288,768]{1,0:T(8,128)(2,1)S(1)} %fusion.6), channel_id=1, source_target_pairs={{0,1},{1,2},{2,3},{3,0},{4,5},{5,6},{6,7},{7,4},{8,9},{9,10},{10,1... | collective-permute-start | bytes 1327112 | tf_op jit(solution)/shard_map/ppermute | solution.py:425
  172.5 13.6 %collective-permute-start.44 = (f32[16,768]{1,0:T(8,128)S(1)}, f32[16,768]{1,0:T(8,128)S(1)}, u32[]{:S(2)}, u32[]{:S(2)}) collective-permute-start(f32[16,768]{1,0:T(8,128)S(1)} %add.621), channel_id=1, source_target_pairs={{0,8},{4,12},{8,0},{12,4},{16,24},{20,28},{24,16},{28,20},{1,9},{5... | collective-permute-start | bytes 147464 | tf_op jit(solution)/shard_map/ppermute | solution.py:409
  187.7 12.1 %collective-permute-start.46 = (bf16[288,768]{1,0:T(8,128)(2,1)S(1)}, bf16[288,768]{1,0:T(8,128)(2,1)S(1)}, u32[]{:S(2)}, u32[]{:S(2)}) collective-permute-start(bf16[288,768]{1,0:T(8,128)(2,1)S(1)} %fusion.2), channel_id=1, source_target_pairs={{0,1},{1,2},{2,3},{3,0},{4,5},{5,6},{6,7},{7,4},{8,9},{9,10},{10,1... | collective-permute-start | bytes 1327112 | tf_op jit(solution)/shard_map/ppermute | solution.py:425
  199.9 11.9 %collective-permute-start.49 = (bf16[288,768]{1,0:T(8,128)(2,1)S(1)}, bf16[288,768]{1,0:T(8,128)(2,1)S(1)}, u32[]{:S(2)}, u32[]{:S(2)}) collective-permute-start(bf16[288,768]{1,0:T(8,128)(2,1)S(1)} %fusion.4.refs_0_), channel_id=1, source_target_pairs={{0,16},{4,12},{8,24},{12,4},{16,0},{20,28},{24,8},{28,20},{1,17},{... | collective-permute-start | bytes 1327112 | tf_op jit(solution)/shard_map/ppermute | solution.py:409
  207.0 15.3 %collective-permute-start.58 = (bf16[2,1760,128]{2,1,0:T(8,128)(2,1)}, bf16[2,1760,128]{2,1,0:T(8,128)(2,1)}, u32[]{:S(2)}, u32[]{:S(2)}) collective-permute-start(bf16[2,1760,128]{2,1,0:T(8,128)(2,1)} %collective-permute-done.22.refs_10_), channel_id=1, source_target_pairs={{0,4},{4,0},{8,12},{12,8},{16,20},{20,16},{24,28},{28,24},{1,5},{5... | collective-permute-start | bytes 2703368 | tf_op jit(solution)/shard_map/ppermute | solution.py:409
  (76 other events, 609.1 us)

commit v9 on v8

--- a/solution.py
+++ b/solution.py
@@ -935,7 +935,7 @@
 SHARE = FLAT_ROWS // REPS
 BEGINS = tuple(SHARE * r // 16 * 16 for r in range(REPS)) + (FLAT_ROWS,)
 SHARE_ROWS = 1760
-STEP = 96
+STEP = 576
 
 
 def align_kernel(where, one_ref, two_ref, out_ref, held):
@@ -975,19 +975,23 @@
         copies.append(
             pltpu.make_async_copy(blocks[turn], held.at[where[1 + turn]], sems.at[turn])
         )
-    copies.append(pltpu.make_async_copy(params, weight, sems.at[REPS]))
+    fetched = []
+    for r in range(REPS):
+        rows = pl.ds(BEGINS[r], BEGINS[r + 1] - BEGINS[r])
+        fetched.append(
+            pltpu.make_async_copy(params.at[rows], weight.at[rows], sems.at[REPS + r])
+        )
     for turn in range(REPS):
+        which = where[1 + turn]
         copies.append(
             pltpu.make_async_copy(
-                moments[turn], moment.at[where[1 + turn]], sems.at[REPS + 1 + turn]
+                moments[turn], moment.at[which], sems.at[2 * REPS + which]
             )
         )
-    for copy in copies[:REPS]:
+    for copy in copies + fetched:
         copy.start()
     for copy in copies[:REPS]:
         copy.wait()
-    for copy in copies[REPS:]:
-        copy.start()
     shard = where[0]
     for z in range(SHARDS):
 
@@ -1014,13 +1018,18 @@
                                 got.astype(jnp.float32) * factor
                             )
 
-    saving = [pltpu.make_async_copy(grad, grad_out, out_sems.at[REPS])]
-    saving[0].start()
-    for copy in copies[REPS:]:
-        copy.wait()
+    saving = []
+    for r in range(REPS):
+        rows = pl.ds(BEGINS[r], BEGINS[r + 1] - BEGINS[r])
+        saving.append(
+            pltpu.make_async_copy(grad.at[rows], grad_out.at[rows], out_sems.at[REPS + r])
+        )
+        saving[-1].start()
     for r in range(REPS):
         base = BEGINS[r]
         length = BEGINS[r + 1] - base
+        pltpu.make_async_copy(moments[0], moment.at[r], sems.at[2 * REPS + r]).wait()
+        fetched[r].wait()
         if r > 0:
             tail = base - BEGINS[r - 1]
             moment[r, :, 0:16, :] = moment[r, :, 0:16, :] + moment[r - 1, :, tail : tail + 16, :]
@@ -1066,8 +1075,8 @@
                 pltpu.VMEM((FLAT_ROWS, LANES), jnp.float32),
                 pltpu.VMEM((FLAT_ROWS, LANES), jnp.float32),
                 pltpu.VMEM((REPS, 2, SHARE_ROWS, LANES), jnp.bfloat16),
-                pltpu.SemaphoreType.DMA((2 * REPS + 1,)),
-                pltpu.SemaphoreType.DMA((REPS + 1,)),
+                pltpu.SemaphoreType.DMA((3 * REPS,)),
+                pltpu.SemaphoreType.DMA((2 * REPS,)),
             ],
         ),
         out_shape=[flat, flat],

time: 247 us -> 242 us (0.980)
  Pallas kernels: 71 us -> 66.2 us
    pallas_call x1, Pallas kernels: 20 us -> 15.3 us  [update_shard(): pl.pallas_call(functools.partial(update_kernel, factor), grid_spec=pltpu....]
where the time goes in v9:
time: 242 us; the launch traced here: 241 us
  waiting for transfers between devices  121 us (50%)
  Pallas kernels  66.2 us (27%)
  starting transfers between devices  33.2 us (14%)
  local copies, waits for them, and re-layouts  12.6 us (5%)
  other arithmetic  6.83 us (3%)
    ppermute x48, waiting for transfers between devices, plane_permute(): lax.ppermute(value, PLANE, [(i, i ^ flips[i % 2]) for i in range(REPS)])  77.7 us
    ppermute x9, waiting for transfers between devices, ring_step(): lax.ppermute(value, 'z', [(i, (i + 1) % SHARDS) for i in range(SHARDS)])  33.2 us
    ppermute x48, starting transfers between devices, plane_permute(): lax.ppermute(value, PLANE, [(i, i ^ flips[i % 2]) for i in range(REPS)])  28.6 us
    pallas_call x1, Pallas kernels, weight_gradients(): pl.pallas_call(gradient_kernel, grid_spec=pltpu.PrefetchScalarGridSpec(nu...  17.9 us
    pallas_call x1, Pallas kernels, update_shard(): pl.pallas_call(functools.partial(update_kernel, factor), grid_spec=pltpu....  15.3 us
    pallas_call x1, Pallas kernels, attention(): pl.pallas_call(attention_kernel, grid_spec=pltpu.PrefetchScalarGridSpec(n...  14.9 us
    pallas_call x2, Pallas kernels, pack_pieces(): pl.pallas_call(pack_kernel, grid_spec=pltpu.PrefetchScalarGridSpec(num_sc...  11.6 us
    ppermute x3, waiting for transfers between devices, ring_shift(): lax.ppermute(value, 'z', [(i, (i + hop) % SHARDS) for i in range(SHARDS)])  9.9 us
  transfers between devices with their start and end apart: 60, of which 31 were waited for; matrix products, arithmetic and copies ran while one was open for 2% of the time, Pallas kernels for 20%

profile of v9, /device:TPU:0, one launch (start us, length us, event | category | flops | bytes accessed | tf_op | source)
XLA Modules:
  0.0 241.2 jit_solution(2112631636334404522)
XLA Ops:
  1.2 2.8 %shard_map.109 = bf16[1,288,768]{2,1,0:T(8,128)(2,1)} custom-call(s32[2]{0:T(128)} %pad_add_fusion.where, f32[13848,128]{1,0:T(8,128)} %bitcast.132), custom_call_target="tpu_custom_call" | custom-call | tf_op jit(solution)/shard_map/pallas_call | solution.py:522
  4.0 3.1 %collective-permute-start = (bf16[288,768]{1,0:T(8,128)(2,1)}, bf16[288,768]{1,0:T(8,128)(2,1)S(1)}, u32[]{:S(2)}, u32[]{:S(2)}) collective-permute-start(bf16[288,768]{1,0:T(8,128)(2,1)} %bitcast.151), channel_id=1, source_target_pairs={{0,1},{1,2},{2,3},{3,0},{4,5},{5,6},{6,7},{7,4},{8,9},{9,10},{10,1... | collective-permute-start | bytes 1327112 | tf_op jit(solution)/shard_map/ppermute | solution.py:425
  7.7 8.9 %shard_map.110 = (bf16[8,288,768]{2,1,0:T(8,128)(2,1)}, f32[8,768]{1,0:T(8,128)}) custom-call(s32[9]{0:T(128)} %stack.274.where, f32[13848,128]{1,0:T(8,128)} %bitcast.133), custom_call_target="tpu_custom_call" | custom-call | tf_op jit(solution)/shard_map/pallas_call | solution.py:522
  16.6 2.8 %collective-permute-done = bf16[288,768]{1,0:T(8,128)(2,1)S(1)} collective-permute-done((bf16[288,768]{1,0:T(8,128)(2,1)}, bf16[288,768]{1,0:T(8,128)(2,1)S(1)}, u32[]{:S(2)}, u32[]{:S(2)}) %collective-permute-start) | collective-permute-done | bytes 442400 | tf_op jit(solution)/shard_map/ppermute | solution.py:425
  26.7 8.7 %collective-permute-done.4.refs_17_ = f32[8,768]{1,0:T(8,128)S(1)} collective-permute-done((f32[8,768]{1,0:T(8,128)}, f32[8,768]{1,0:T(8,128)S(1)}, u32[]{:S(2)}, u32[]{:S(2)}) %collective-permute-start.4) | collective-permute-done | bytes 24608 | tf_op jit(solution)/shard_map/ppermute | solution.py:425
  38.0 11.1 %collective-permute-done.9.refs_18_ = f32[8,768]{1,0:T(8,128)S(1)} collective-permute-done((f32[8,768]{1,0:T(8,128)S(1)}, f32[8,768]{1,0:T(8,128)S(1)}, u32[]{:S(2)}, u32[]{:S(2)}) %collective-permute-start.9) | collective-permute-done | bytes 24608 | tf_op jit(solution)/shard_map/ppermute | solution.py:425
  49.1 2.2 collective-permute-done.7
  52.2 1.5 collective-permute-start.11
  54.3 5.6 %collective-permute-done.14.refs_19_ = f32[8,768]{1,0:T(8,128)S(1)} collective-permute-done((f32[8,768]{1,0:T(8,128)S(1)}, f32[8,768]{1,0:T(8,128)S(1)}, u32[]{:S(2)}, u32[]{:S(2)}) %collective-permute-start.14) | collective-permute-done | bytes 24608 | tf_op jit(solution)/shard_map/ppermute | solution.py:425
  59.9 3.9 %collective-permute-done.12 = bf16[288,768]{1,0:T(8,128)(2,1)S(1)} collective-permute-done((bf16[288,768]{1,0:T(8,128)(2,1)S(1)}, bf16[288,768]{1,0:T(8,128)(2,1)S(1)}, u32[]{:S(2)}, u32[]{:S(2)}) %collective-permute-start.12) | collective-permute-done | bytes 442400 | tf_op jit(solution)/shard_map/ppermute | solution.py:409
  63.8 5.7 %collective-permute-done.11.refs_6_ = bf16[288,768]{1,0:T(8,128)(2,1)S(1)} collective-permute-done((bf16[288,768]{1,0:T(8,128)(2,1)S(1)}, bf16[288,768]{1,0:T(8,128)(2,1)S(1)}, u32[]{:S(2)}, u32[]{:S(2)}) %collective-permute-start.11) | collective-permute-done | bytes 442400 | tf_op jit(solution)/shard_map/ppermute | solution.py:409
  72.4 3.0 %collective-permute-done.15.refs_8_ = bf16[288,768]{1,0:T(8,128)(2,1)S(1)} collective-permute-done((bf16[288,768]{1,0:T(8,128)(2,1)S(1)}, bf16[288,768]{1,0:T(8,128)(2,1)S(1)}, u32[]{:S(2)}, u32[]{:S(2)}) %collective-permute-start.15) | collective-permute-done | bytes 442400 | tf_op jit(solution)/shard_map/ppermute | solution.py:409
  76.1 3.9 %collective-permute-done.18.refs_7_ = bf16[288,768]{1,0:T(8,128)(2,1)S(1)} collective-permute-done((bf16[288,768]{1,0:T(8,128)(2,1)S(1)}, bf16[288,768]{1,0:T(8,128)(2,1)S(1)}, u32[]{:S(2)}, u32[]{:S(2)}) %collective-permute-start.18) | collective-permute-done | bytes 442400 | tf_op jit(solution)/shard_map/ppermute | solution.py:409
  80.2 1.8 collective-permute-done.20.refs_11_
  84.6 14.9 %shard_map.113 = (bf16[9216,768]{1,0:T(8,128)(2,1)}, bf16[128,768]{1,0:T(8,128)(2,1)}, bf16[128,2304]{1,0:T(8,128)(2,1)}, f32[8,768]{1,0:T(8,128)}, f32[16,768]{1,0:T(8,128)}) custom-call(s32[25]{0:T(128)} %stack.271.where, bf16[4,288,768]{2,1,0:T(8,128)(2,1)} %copy-done.19, bf16[4,288,768]{2,1,0:T(8,128)(2,1)} %copy-done.34, ...), custom_call_target="tpu_custom_call" | custom-call | flops 6000000000 | bytes 62914560 | tf_op jit(solution)/shard_map/pallas_call | solution.py:726
  101.8 17.9 %shard_map.114 = (bf16[576,768]{1,0:T(8,128)(2,1)}, bf16[576,768]{1,0:T(8,128)(2,1)}, bf16[576,768]{1,0:T(8,128)(2,1)}, bf16[576,768]{1,0:T(8,128)(2,1)}, bf16[5...) custom-call(s32[33]{0:T(128)} %stack.317.where, ...), custom_call_target="tpu_custom_call" | custom-call | flops 10000000000 | bytes 62914560 | tf_op jit(solution)/shard_map/pallas_call | solution.py:842
  119.8 2.9 %collective-permute-done.23.refs_11_ = bf16[2,1760,128]{2,1,0:T(8,128)(2,1)} collective-permute-done((bf16[2,1760,128]{2,1,0:T(8,128)(2,1)}, bf16[2,1760,128]{2,1,0:T(8,128)(2,1)}, u32[]{:S(2)}, u32[]{:S(2)}) %collective-permute-start.23) | collective-permute-done | bytes 901152 | tf_op jit(solution)/shard_map/ppermute | solution.py:409
  123.6 1.6 collective-permute-done.26
  129.2 1.6 collective-permute-start.29
  132.8 9.5 %collective-permute-done.29 = bf16[2,288,768]{2,1,0:T(8,128)(2,1)S(1)} collective-permute-done((bf16[2,288,768]{2,1,0:T(8,128)(2,1)S(1)}, bf16[2,288,768]{2,1,0:T(8,128)(2,1)S(1)}, u32[]{:S(2)}, u32[]{:S(2)}) %collective-permute-start.29) | collective-permute-done | bytes 884768 | tf_op jit(solution)/shard_map/ppermute | solution.py:409
  145.4 5.0 %copy-done = bf16[9216,768]{1,0:T(8,128)(2,1)S(1)} copy-done((bf16[9216,768]{1,0:T(8,128)(2,1)S(1)}, bf16[9216,768]{1,0:T(8,128)(2,1)}, u32[]{:S(2)}) %copy-start) | copy-done | bytes 14155800
  150.4 5.8 %shard_map.115 = (f32[128,768]{1,0:T(8,128)}, f32[128,768]{1,0:T(8,128)}, f32[16,768]{1,0:T(8,128)S(1)}) custom-call(bf16[9216,768]{1,0:T(8,128)(2,1)S(1)} %copy-done, bf16[128,768]{1,0:T(8,128)(2,1)S(1)} %copy-done.4, f32[128,768]{1,0:T(8,128)S(1)} %copy-done.9, f32[128,128]{1,0:T(8,128)S(1)} %get-tuple-element.257.refs_2_, ...), custom_call_target="tpu_custom_call" | custom-call | flops 4000000000 | bytes 31457280 | tf_op jit(solution)/shard_map/pallas_call | solution.py:919
  159.7 11.1 %collective-permute-done.38 = bf16[2,288,768]{2,1,0:T(8,128)(2,1)S(1)} collective-permute-done((bf16[2,288,768]{2,1,0:T(8,128)(2,1)S(1)}, bf16[2,288,768]{2,1,0:T(8,128)(2,1)S(1)}, u32[]{:S(2)}, u32[]{:S(2)}) %collective-permute-start.38) | collective-permute-done | bytes 884768 | tf_op jit(solution)/shard_map/ppermute | solution.py:409
  173.4 12.1 %collective-permute-done.42 = bf16[2,288,768]{2,1,0:T(8,128)(2,1)S(1)} collective-permute-done((bf16[2,288,768]{2,1,0:T(8,128)(2,1)S(1)}, bf16[2,288,768]{2,1,0:T(8,128)(2,1)S(1)}, u32[]{:S(2)}, u32[]{:S(2)}) %collective-permute-start.42) | collective-permute-done | bytes 884768 | tf_op jit(solution)/shard_map/ppermute | solution.py:409
  188.6 6.6 %collective-permute-done.47 = f32[16,768]{1,0:T(8,128)S(1)} collective-permute-done((f32[16,768]{1,0:T(8,128)S(1)}, f32[16,768]{1,0:T(8,128)S(1)}, u32[]{:S(2)}, u32[]{:S(2)}) %collective-permute-start.47) | collective-permute-done | bytes 49184 | tf_op jit(solution)/shard_map/ppermute | solution.py:409
  195.2 4.6 %collective-permute-done.46 = bf16[288,768]{1,0:T(8,128)(2,1)S(1)} collective-permute-done((bf16[288,768]{1,0:T(8,128)(2,1)S(1)}, bf16[288,768]{1,0:T(8,128)(2,1)S(1)}, u32[]{:S(2)}, u32[]{:S(2)}) %collective-permute-start.46) | collective-permute-done | bytes 442400 | tf_op jit(solution)/shard_map/ppermute | solution.py:425
  201.9 4.0 %collective-permute-done.52 = f32[16,768]{1,0:T(8,128)S(1)} collective-permute-done((f32[16,768]{1,0:T(8,128)S(1)}, f32[16,768]{1,0:T(8,128)S(1)}, u32[]{:S(2)}, u32[]{:S(2)}) %collective-permute-start.52) | collective-permute-done | bytes 49184 | tf_op jit(solution)/shard_map/ppermute | solution.py:1088
  207.0 4.8 %collective-permute-done.50 = f32[16,768]{1,0:T(8,128)S(1)} collective-permute-done((f32[16,768]{1,0:T(8,128)S(1)}, f32[16,768]{1,0:T(8,128)S(1)}, u32[]{:S(2)}, u32[]{:S(2)}) %collective-permute-start.50) | collective-permute-done | bytes 49184 | tf_op jit(solution)/shard_map/ppermute | solution.py:1088
  213.0 1.9 collective-permute-done.56.refs_6_
  215.5 5.4 %collective-permute-done.53.refs_3_ = bf16[288,768]{1,0:T(8,128)(2,1)} collective-permute-done((bf16[288,768]{1,0:T(8,128)(2,1)S(1)}, bf16[288,768]{1,0:T(8,128)(2,1)}, u32[]{:S(2)}, u32[]{:S(2)}) %collective-permute-start.53) | collective-permute-done | bytes 442400 | tf_op jit(solution)/shard_map/ppermute | solution.py:409
  223.1 15.3 %shard_map.116 = (f32[13848,128]{1,0:T(8,128)}, f32[13848,128]{1,0:T(8,128)}) custom-call(s32[9]{0:T(128)} %stack.325.where, bf16[288,768]{1,0:T(8,128)(2,1)} %copy-done.21, bf16[288,768]{1,0:T(8,128)(2,1)} %copy-done.30, bf16[288,768]{1,0:T(8,128)(2,1)} %copy-done.29, bf16[288,768]{1,0:T(8,128)(2,1)} %collective-permute-done.53.refs_3_, ...), custom_call_target="tpu_custom_call" | custom-call | tf_op jit(solution)/shard_map/pallas_call | solution.py:1066
  238.4 2.8 %fusion = (f32[221568]{0:T(1024)}, f32[221568]{0:T(1024)}) fusion(f32[221568]{0:T(1024)S(1)} %copy-done.3, f32[1772544]{0:T(1024)} %bitcast.152, s32[]{:T(128)S(6)} %select_n.334, f32[221568]{0:T(1024)S(1)} %copy-done.2), kind=kLoop, calls=%fused_computation.3 | loop fusion | flops 1550976 | bytes 4431364 | tf_op jit(solution)/shard_map/add | solution.py:352
  (223 shorter events, 47.0 us)
Async XLA Ops:
  4.0 15.5 %collective-permute-start = (bf16[288,768]{1,0:T(8,128)(2,1)}, bf16[288,768]{1,0:T(8,128)(2,1)S(1)}, u32[]{:S(2)}, u32[]{:S(2)}) collective-permute-start(bf16[288,768]{1,0:T(8,128)(2,1)} %bitcast.151), channel_id=1, source_target_pairs={{0,1},{1,2},{2,3},{3,0},{4,5},{5,6},{6,7},{7,4},{8,9},{9,10},{10,1... | collective-permute-start | bytes 1327112 | tf_op jit(solution)/shard_map/ppermute | solution.py:425
  19.5 15.9 %collective-permute-start.3 = (bf16[288,768]{1,0:T(8,128)(2,1)S(1)}, bf16[288,768]{1,0:T(8,128)(2,1)S(1)}, u32[]{:S(2)}, u32[]{:S(2)}) collective-permute-start(bf16[288,768]{1,0:T(8,128)(2,1)S(1)} %collective-permute-done), channel_id=1, source_target_pairs={{0,16},{4,12},{8,24},{12,4},{16,0},{20,28},{24,8},{28,20},{1,17},{... | collective-permute-start | bytes 1327112 | tf_op jit(solution)/shard_map/ppermute | solution.py:409
  21.0 14.4 %collective-permute-start.2 = (bf16[288,768]{1,0:T(8,128)(2,1)S(1)}, bf16[288,768]{1,0:T(8,128)(2,1)S(1)}, u32[]{:S(2)}, u32[]{:S(2)}) collective-permute-start(bf16[288,768]{1,0:T(8,128)(2,1)S(1)} %collective-permute-done), channel_id=1, source_target_pairs={{0,8},{4,20},{8,0},{12,28},{16,24},{20,4},{24,16},{28,12},{1,9},{5... | collective-permute-start | bytes 1327112 | tf_op jit(solution)/shard_map/ppermute | solution.py:409
  22.5 12.9 %collective-permute-start.1 = (bf16[288,768]{1,0:T(8,128)(2,1)S(1)}, bf16[288,768]{1,0:T(8,128)(2,1)S(1)}, u32[]{:S(2)}, u32[]{:S(2)}) collective-permute-start(bf16[288,768]{1,0:T(8,128)(2,1)S(1)} %collective-permute-done), channel_id=1, source_target_pairs={{0,1},{1,2},{2,3},{3,0},{4,5},{5,6},{6,7},{7,4},{8,9},{9,10},{10,1... | collective-permute-start | bytes 1327112 | tf_op jit(solution)/shard_map/ppermute | solution.py:425
  22.5 12.9 %collective-permute-start.4 = (f32[8,768]{1,0:T(8,128)}, f32[8,768]{1,0:T(8,128)S(1)}, u32[]{:S(2)}, u32[]{:S(2)}) collective-permute-start(f32[8,768]{1,0:T(8,128)} %get-tuple-element.170.refs_16_), channel_id=1, source_target_pairs={{0,1},{1,2},{2,3},{3,0},{4,5},{5,6},{6,7},{7,4},{8,9},{9,10},{10,1... | collective-permute-start | bytes 73736 | tf_op jit(solution)/shard_map/ppermute | solution.py:425
  35.4 13.7 %collective-permute-start.8 = (bf16[288,768]{1,0:T(8,128)(2,1)S(1)}, bf16[288,768]{1,0:T(8,128)(2,1)S(1)}, u32[]{:S(2)}, u32[]{:S(2)}) collective-permute-start(bf16[288,768]{1,0:T(8,128)(2,1)S(1)} %collective-permute-done.2), channel_id=1, source_target_pairs={{0,16},{4,12},{8,24},{12,4},{16,0},{20,28},{24,8},{28,20},{1,17},{... | collective-permute-start | bytes 1327112 | tf_op jit(solution)/shard_map/ppermute | solution.py:409
  36.0 15.3 %collective-permute-start.7 = (bf16[288,768]{1,0:T(8,128)(2,1)S(1)}, bf16[288,768]{1,0:T(8,128)(2,1)S(1)}, u32[]{:S(2)}, u32[]{:S(2)}) collective-permute-start(bf16[288,768]{1,0:T(8,128)(2,1)S(1)} %collective-permute-done.1), channel_id=1, source_target_pairs={{0,16},{4,12},{8,24},{12,4},{16,0},{20,28},{24,8},{28,20},{1,17},{... | collective-permute-start | bytes 1327112 | tf_op jit(solution)/shard_map/ppermute | solution.py:409
  37.5 13.8 %collective-permute-start.6 = (bf16[288,768]{1,0:T(8,128)(2,1)S(1)}, bf16[288,768]{1,0:T(8,128)(2,1)S(1)}, u32[]{:S(2)}, u32[]{:S(2)}) collective-permute-start(bf16[288,768]{1,0:T(8,128)(2,1)S(1)} %collective-permute-done.1), channel_id=1, source_target_pairs={{0,8},{4,20},{8,0},{12,28},{16,24},{20,4},{24,16},{28,12},{1,9},{5... | collective-permute-start | bytes 1327112 | tf_op jit(solution)/shard_map/ppermute | solution.py:409
  38.0 13.3 %collective-permute-start.5 = (bf16[288,768]{1,0:T(8,128)(2,1)S(1)}, bf16[288,768]{1,0:T(8,128)(2,1)S(1)}, u32[]{:S(2)}, u32[]{:S(2)}) collective-permute-start(bf16[288,768]{1,0:T(8,128)(2,1)S(1)} %collective-permute-done.1), channel_id=1, source_target_pairs={{0,1},{1,2},{2,3},{3,0},{4,5},{5,6},{6,7},{7,4},{8,9},{9,10},{10,1... | collective-permute-start | bytes 1327112 | tf_op jit(solution)/shard_map/ppermute | solution.py:425
  51.5 17.9 %collective-permute-start.13 = (bf16[4,288,768]{2,1,0:T(8,128)(2,1)S(1)}, bf16[4,288,768]{2,1,0:T(8,128)(2,1)S(1)}, u32[]{:S(2)}, u32[]{:S(2)}) collective-permute-start(bf16[4,288,768]{2,1,0:T(8,128)(2,1)S(1)} %pad_maximum_fusion.refs_0_), channel_id=1, source_target_pairs={{0,4},{4,0},{8,12},{12,8},{16,20},{20,16},{24,28},{28,24},{1,5},{5... | collective-permute-start | bytes 5308424 | tf_op jit(solution)/shard_map/ppermute | solution.py:409
  51.6 12.2 %collective-permute-start.12 = (bf16[288,768]{1,0:T(8,128)(2,1)S(1)}, bf16[288,768]{1,0:T(8,128)(2,1)S(1)}, u32[]{:S(2)}, u32[]{:S(2)}) collective-permute-start(bf16[288,768]{1,0:T(8,128)(2,1)S(1)} %collective-permute-done.6), channel_id=1, source_target_pairs={{0,16},{4,12},{8,24},{12,4},{16,0},{20,28},{24,8},{28,20},{1,17},{... | collective-permute-start | bytes 1327112 | tf_op jit(solution)/shard_map/ppermute | solution.py:409
  52.2 17.3 %collective-permute-start.11 = (bf16[288,768]{1,0:T(8,128)(2,1)S(1)}, bf16[288,768]{1,0:T(8,128)(2,1)S(1)}, u32[]{:S(2)}, u32[]{:S(2)}) collective-permute-start(bf16[288,768]{1,0:T(8,128)(2,1)S(1)} %collective-permute-done.5.refs_4_), channel_id=1, source_target_pairs={{0,16},{4,12},{8,24},{12,4},{16,0},{20,28},{24,8},{28,20},{1,17},{... | collective-permute-start | bytes 1327112 | tf_op jit(solution)/shard_map/ppermute | solution.py:409
  53.7 15.7 %collective-permute-start.10 = (bf16[288,768]{1,0:T(8,128)(2,1)S(1)}, bf16[288,768]{1,0:T(8,128)(2,1)S(1)}, u32[]{:S(2)}, u32[]{:S(2)}) collective-permute-start(bf16[288,768]{1,0:T(8,128)(2,1)S(1)} %collective-permute-done.5.refs_4_), channel_id=1, source_target_pairs={{0,8},{4,20},{8,0},{12,28},{16,24},{20,4},{24,16},{28,12},{1,9},{5... | collective-permute-start | bytes 1327112 | tf_op jit(solution)/shard_map/ppermute | solution.py:409
  82.8 16.7 %collective-permute-start.21 = (bf16[2,1760,128]{2,1,0:T(8,128)(2,1)S(1)}, bf16[2,1760,128]{2,1,0:T(8,128)(2,1)}, u32[]{:S(2)}, u32[]{:S(2)}) collective-permute-start(bf16[2,1760,128]{2,1,0:T(8,128)(2,1)S(1)} %shard_map.112.refs_8_), channel_id=1, source_target_pairs={{0,8},{4,20},{8,0},{12,28},{16,24},{20,4},{24,16},{28,12},{1,9},{5... | collective-permute-start | bytes 2703368 | tf_op jit(solution)/shard_map/ppermute | solution.py:409
  99.5 20.2 %collective-permute-start.24 = (bf16[2,1760,128]{2,1,0:T(8,128)(2,1)S(1)}, bf16[2,1760,128]{2,1,0:T(8,128)(2,1)}, u32[]{:S(2)}, u32[]{:S(2)}) collective-permute-start(bf16[2,1760,128]{2,1,0:T(8,128)(2,1)S(1)} %shard_map.112.refs_8_), channel_id=1, source_target_pairs={{0,4},{4,0},{8,12},{12,8},{16,20},{20,16},{24,28},{28,24},{1,5},{5... | collective-permute-start | bytes 2703368 | tf_op jit(solution)/shard_map/ppermute | solution.py:409
  99.6 20.2 %collective-permute-start.22 = (bf16[2,1760,128]{2,1,0:T(8,128)(2,1)S(1)}, bf16[2,1760,128]{2,1,0:T(8,128)(2,1)}, u32[]{:S(2)}, u32[]{:S(2)}) collective-permute-start(bf16[2,1760,128]{2,1,0:T(8,128)(2,1)S(1)} %shard_map.112.refs_8_), channel_id=1, source_target_pairs={{0,16},{4,12},{8,24},{12,4},{16,0},{20,28},{24,8},{28,20},{1,17},{... | collective-permute-start | bytes 2703368 | tf_op jit(solution)/shard_map/ppermute | solution.py:409
  100.9 18.8 %collective-permute-start.25 = (bf16[2,1760,128]{2,1,0:T(8,128)(2,1)}, bf16[2,1760,128]{2,1,0:T(8,128)(2,1)}, u32[]{:S(2)}, u32[]{:S(2)}) collective-permute-start(bf16[2,1760,128]{2,1,0:T(8,128)(2,1)} %collective-permute-done.21.refs_9_), channel_id=1, source_target_pairs={{0,4},{4,0},{8,12},{12,8},{16,20},{20,16},{24,28},{28,24},{1,5},{5... | collective-permute-start | bytes 2703368 | tf_op jit(solution)/shard_map/ppermute | solution.py:409
  101.3 21.3 %collective-permute-start.23 = (bf16[2,1760,128]{2,1,0:T(8,128)(2,1)}, bf16[2,1760,128]{2,1,0:T(8,128)(2,1)}, u32[]{:S(2)}, u32[]{:S(2)}) collective-permute-start(bf16[2,1760,128]{2,1,0:T(8,128)(2,1)} %collective-permute-done.21.refs_9_), channel_id=1, source_target_pairs={{0,16},{4,12},{8,24},{12,4},{16,0},{20,28},{24,8},{28,20},{1,17},{... | collective-permute-start | bytes 2703368 | tf_op jit(solution)/shard_map/ppermute | solution.py:409
  129.2 13.1 %collective-permute-start.29 = (bf16[2,288,768]{2,1,0:T(8,128)(2,1)S(1)}, bf16[2,288,768]{2,1,0:T(8,128)(2,1)S(1)}, u32[]{:S(2)}, u32[]{:S(2)}) collective-permute-start(bf16[2,288,768]{2,1,0:T(8,128)(2,1)S(1)} %add.607), channel_id=1, source_target_pairs={{0,8},{4,20},{8,0},{12,28},{16,24},{20,4},{24,16},{28,12},{1,9},{5... | collective-permute-start | bytes 2654216 | tf_op jit(solution)/shard_map/ppermute | solution.py:409
  131.1 25.1 %collective-permute-start.36 = (bf16[2,288,768]{2,1,0:T(8,128)(2,1)S(1)}, bf16[2,288,768]{2,1,0:T(8,128)(2,1)S(1)}, u32[]{:S(2)}, u32[]{:S(2)}) collective-permute-start(bf16[2,288,768]{2,1,0:T(8,128)(2,1)S(1)} %bitcast.156), channel_id=1, source_target_pairs={{0,4},{4,0},{8,12},{12,8},{16,20},{20,16},{24,28},{28,24},{1,5},{5... | collective-permute-start | bytes 2654216 | tf_op jit(solution)/shard_map/ppermute | solution.py:409
  131.1 25.4 %collective-permute-start.35 = (bf16[2,288,768]{2,1,0:T(8,128)(2,1)S(1)}, bf16[2,288,768]{2,1,0:T(8,128)(2,1)S(1)}, u32[]{:S(2)}, u32[]{:S(2)}) collective-permute-start(bf16[2,288,768]{2,1,0:T(8,128)(2,1)S(1)} %add.610), channel_id=1, source_target_pairs={{0,8},{4,20},{8,0},{12,28},{16,24},{20,4},{24,16},{28,12},{1,9},{5... | collective-permute-start | bytes 2654216 | tf_op jit(solution)/shard_map/ppermute | solution.py:409
  142.6 13.9 %collective-permute-start.34 = (bf16[288,768]{1,0:T(8,128)(2,1)S(1)}, bf16[288,768]{1,0:T(8,128)(2,1)S(1)}, u32[]{:S(2)}, u32[]{:S(2)}) collective-permute-start(bf16[288,768]{1,0:T(8,128)(2,1)S(1)} %slice_bitcast_fusion.7), channel_id=1, source_target_pairs={{0,16},{4,12},{8,24},{12,4},{16,0},{20,28},{24,8},{28,20},{1,17},{... | collective-permute-start | bytes 1327112 | tf_op jit(solution)/shard_map/ppermute | solution.py:409
  144.2 26.6 %collective-permute-start.38 = (bf16[2,288,768]{2,1,0:T(8,128)(2,1)S(1)}, bf16[2,288,768]{2,1,0:T(8,128)(2,1)S(1)}, u32[]{:S(2)}, u32[]{:S(2)}) collective-permute-start(bf16[2,288,768]{2,1,0:T(8,128)(2,1)S(1)} %add.615), channel_id=1, source_target_pairs={{0,8},{4,20},{8,0},{12,28},{16,24},{20,4},{24,16},{28,12},{1,9},{5... | collective-permute-start | bytes 2654216 | tf_op jit(solution)/shard_map/ppermute | solution.py:409
  156.8 14.0 %collective-permute-start.37 = (bf16[288,768]{1,0:T(8,128)(2,1)S(1)}, bf16[288,768]{1,0:T(8,128)(2,1)S(1)}, u32[]{:S(2)}, u32[]{:S(2)}) collective-permute-start(bf16[288,768]{1,0:T(8,128)(2,1)S(1)} %slice_bitcast_fusion.6), channel_id=1, source_target_pairs={{0,16},{4,12},{8,24},{12,4},{16,0},{20,28},{24,8},{28,20},{1,17},{... | collective-permute-start | bytes 1327112 | tf_op jit(solution)/shard_map/ppermute | solution.py:409
  158.1 13.0 %collective-permute-start.39 = (bf16[288,768]{1,0:T(8,128)(2,1)S(1)}, bf16[288,768]{1,0:T(8,128)(2,1)S(1)}, u32[]{:S(2)}, u32[]{:S(2)}) collective-permute-start(bf16[288,768]{1,0:T(8,128)(2,1)S(1)} %fusion.7), channel_id=1, source_target_pairs={{0,1},{1,2},{2,3},{3,0},{4,5},{5,6},{6,7},{7,4},{8,9},{9,10},{10,1... | collective-permute-start | bytes 1327112 | tf_op jit(solution)/shard_map/ppermute | solution.py:425
  158.4 27.1 %collective-permute-start.42 = (bf16[2,288,768]{2,1,0:T(8,128)(2,1)S(1)}, bf16[2,288,768]{2,1,0:T(8,128)(2,1)S(1)}, u32[]{:S(2)}, u32[]{:S(2)}) collective-permute-start(bf16[2,288,768]{2,1,0:T(8,128)(2,1)S(1)} %add.618), channel_id=1, source_target_pairs={{0,8},{4,20},{8,0},{12,28},{16,24},{20,4},{24,16},{28,12},{1,9},{5... | collective-permute-start | bytes 2654216 | tf_op jit(solution)/shard_map/ppermute | solution.py:409
  171.3 14.7 %collective-permute-start.41 = (bf16[288,768]{1,0:T(8,128)(2,1)S(1)}, bf16[288,768]{1,0:T(8,128)(2,1)S(1)}, u32[]{:S(2)}, u32[]{:S(2)}) collective-permute-start(bf16[288,768]{1,0:T(8,128)(2,1)S(1)} %slice_bitcast_fusion.4), channel_id=1, source_target_pairs={{0,16},{4,12},{8,24},{12,4},{16,0},{20,28},{24,8},{28,20},{1,17},{... | collective-permute-start | bytes 1327112 | tf_op jit(solution)/shard_map/ppermute | solution.py:409
  172.4 13.7 %collective-permute-start.43 = (bf16[288,768]{1,0:T(8,128)(2,1)S(1)}, bf16[288,768]{1,0:T(8,128)(2,1)S(1)}, u32[]{:S(2)}, u32[]{:S(2)}) collective-permute-start(bf16[288,768]{1,0:T(8,128)(2,1)S(1)} %fusion.6), channel_id=1, source_target_pairs={{0,1},{1,2},{2,3},{3,0},{4,5},{5,6},{6,7},{7,4},{8,9},{9,10},{10,1... | collective-permute-start | bytes 1327112 | tf_op jit(solution)/shard_map/ppermute | solution.py:425
  172.5 13.6 %collective-permute-start.44 = (f32[16,768]{1,0:T(8,128)S(1)}, f32[16,768]{1,0:T(8,128)S(1)}, u32[]{:S(2)}, u32[]{:S(2)}) collective-permute-start(f32[16,768]{1,0:T(8,128)S(1)} %add.621), channel_id=1, source_target_pairs={{0,8},{4,12},{8,0},{12,4},{16,24},{20,28},{24,16},{28,20},{1,9},{5... | collective-permute-start | bytes 147464 | tf_op jit(solution)/shard_map/ppermute | solution.py:409
  187.7 12.1 %collective-permute-start.46 = (bf16[288,768]{1,0:T(8,128)(2,1)S(1)}, bf16[288,768]{1,0:T(8,128)(2,1)S(1)}, u32[]{:S(2)}, u32[]{:S(2)}) collective-permute-start(bf16[288,768]{1,0:T(8,128)(2,1)S(1)} %fusion.2), channel_id=1, source_target_pairs={{0,1},{1,2},{2,3},{3,0},{4,5},{5,6},{6,7},{7,4},{8,9},{9,10},{10,1... | collective-permute-start | bytes 1327112 | tf_op jit(solution)/shard_map/ppermute | solution.py:425
  199.9 11.9 %collective-permute-start.49 = (bf16[288,768]{1,0:T(8,128)(2,1)S(1)}, bf16[288,768]{1,0:T(8,128)(2,1)S(1)}, u32[]{:S(2)}, u32[]{:S(2)}) collective-permute-start(bf16[288,768]{1,0:T(8,128)(2,1)S(1)} %fusion.4.refs_0_), channel_id=1, source_target_pairs={{0,16},{4,12},{8,24},{12,4},{16,0},{20,28},{24,8},{28,20},{1,17},{... | collective-permute-start | bytes 1327112 | tf_op jit(solution)/shard_map/ppermute | solution.py:409
  207.0 15.3 %collective-permute-start.58 = (bf16[2,1760,128]{2,1,0:T(8,128)(2,1)}, bf16[2,1760,128]{2,1,0:T(8,128)(2,1)}, u32[]{:S(2)}, u32[]{:S(2)}) collective-permute-start(bf16[2,1760,128]{2,1,0:T(8,128)(2,1)} %collective-permute-done.22.refs_10_), channel_id=1, source_target_pairs={{0,4},{4,0},{8,12},{12,8},{16,20},{20,16},{24,28},{28,24},{1,5},{5... | collective-permute-start | bytes 2703368 | tf_op jit(solution)/shard_map/ppermute | solution.py:409
  (76 other events, 609.1 us)

commit v10 on v9

--- a/solution.py
+++ b/solution.py
@@ -532,6 +532,9 @@
             ],
         ),
         out_shape=[pieces, rows] if vectors else [pieces],
+        cost_estimate=pl.CostEstimate(
+            flops=0, bytes_accessed=len(reps) * 3 * 2**20, transcendentals=0
+        ),
         compiler_params=pltpu.CompilerParams(vmem_limit_bytes=56 * 2**20),
     )(jnp.stack([shard] + reps), params.reshape(FLAT_ROWS, LANES))
 
@@ -634,23 +637,27 @@
     return jnp.dot(a, b, preferred_element_type=jnp.float32)
 
 
-def attention_kernel(where, *refs):
+def layer_kernel(where, *refs):
     count = PIECES - REPS
     blocks, own = refs[:GROUPS], refs[GROUPS]
     normed, grad_y, tables = refs[GROUPS + 1 : GROUPS + 4]
     hops = refs[GROUPS + 4 : GROUPS + 8]
-    matrices, attn_out, mixed_out, sums_out, vecs = refs[GROUPS + 8 : GROUPS + 13]
-    held, query, key, value, grad_attn, sems, save_sem = refs[GROUPS + 13 :]
+    outs = refs[GROUPS + 8 : GROUPS + 24]
+    (attn_out, mixed_out, low_sums, vecs, hidden_out, pre_out, high_sums) = refs[
+        GROUPS + 24 : GROUPS + 31
+    ]
+    held, grads, query, key, value, grad_attn, sems, out_sems = refs[GROUPS + 31 :]
     rot_cos, rot_up, rot_down, bias = (tables.at[turn] for turn in range(4))
     shard = where[0]
+    arrive = fetch_pieces([where[1 + t] for t in range(count)], blocks, own, shard, held, sems)
+    low_sums[...] = jnp.zeros_like(low_sums)
+    high_sums[...] = jnp.zeros_like(high_sums)
     for owner in range(SHARDS):
         rows = jnp.zeros((4, D), jnp.float32)
         for hop in range(SHARDS):
             met = (shard + SHARDS - owner) % SHARDS == hop
             rows = jnp.where(met, hops[hop][0:4, :], rows)
         vecs[4 * owner : 4 * owner + 4, :] = rows
-    arrive = fetch_pieces([where[1 + t] for t in range(count)], blocks, own, shard, held, sems)
-    sums_out[...] = jnp.zeros_like(sums_out)
 
     arrive(0)
     act1 = (normed[...] * vecs[0:1, :] + vecs[1:2, :]).astype(jnp.bfloat16)
@@ -674,8 +681,6 @@
 
     arrive(2)
     arrive(3)
-    saving = pltpu.make_async_copy(held, matrices, save_sem)
-    saving.start()
     low = lax.broadcasted_iota(jnp.int32, (LANES, LANES), 1) < HD
     scale = HD ** (-0.5)
     for p in range(6):
@@ -713,59 +718,9 @@
                     - pltpu.roll(part, 8, 1) * rot_down[...]
                 )
             wide = slice(D * j + LANES * p, D * j + LANES * (p + 1))
-            sums_out[j : j + 1, lanes] = jnp.sum(part, axis=0, keepdims=True)
+            low_sums[j : j + 1, lanes] = jnp.sum(part, axis=0, keepdims=True)
             mixed_out[:, wide] = part.astype(jnp.bfloat16)
 
-    saving.wait()
-
-
-def attention(scalars, blocks, own, small):
-    anywhere = pl.BlockSpec(memory_space=pl.ANY)
-    vmem = pl.BlockSpec(memory_space=pltpu.VMEM)
-    bf16 = jnp.bfloat16
-    return pl.pallas_call(
-        attention_kernel,
-        grid_spec=pltpu.PrefetchScalarGridSpec(
-            num_scalar_prefetch=1,
-            in_specs=[anywhere] * (len(blocks) + 1) + [vmem] * len(small),
-            out_specs=[anywhere] + [vmem] * 4,
-            scratch_shapes=[
-                pltpu.VMEM((ALL_ROWS, D), bf16),
-                pltpu.VMEM((TOK_DEV, D), bf16),
-                pltpu.VMEM((TOK_DEV, D), bf16),
-                pltpu.VMEM((TOK_DEV, D), bf16),
-                pltpu.VMEM((TOK_DEV, D), bf16),
-                pltpu.SemaphoreType.DMA((PIECES,)),
-                pltpu.SemaphoreType.DMA,
-            ],
-        ),
-        out_shape=[
-            jax.ShapeDtypeStruct((ALL_ROWS, D), bf16),
-            jax.ShapeDtypeStruct((TOK_DEV, D), bf16),
-            jax.ShapeDtypeStruct((TOK_DEV, 3 * D), bf16),
-            jax.ShapeDtypeStruct((8, D), jnp.float32),
-            jax.ShapeDtypeStruct((16, D), jnp.float32),
-        ],
-        compiler_params=pltpu.CompilerParams(vmem_limit_bytes=60 * 2**20),
-        cost_estimate=pl.CostEstimate(
-            flops=6 * 10**9, bytes_accessed=60 * 2**20, transcendentals=200000
-        ),
-    )(scalars, *blocks, own, *small)
-
-
-def gradient_kernel(where, matrices, *refs):
-    (normed, grad_y, attn_in, mixed_in, vecs) = refs[:5]
-    outs = refs[5:21]
-    hidden_out, pre_out, sums_out = refs[21:24]
-    held, grads, sems, out_sems = refs[24:]
-    copies = []
-    for z in range(1, SHARDS):
-        rows = pl.ds(z * REPS * PIECE, REPS * PIECE)
-        copies.append(pltpu.make_async_copy(matrices.at[rows], held.at[rows], sems.at[z]))
-    for copy in copies:
-        copy.start()
-    sums_out[...] = jnp.zeros_like(sums_out)
-    shard = where[PIECES]
 
     def send_off(owner):
         for hop in range(SHARDS):
@@ -779,7 +734,7 @@
                         out_sems.at[turn],
                     ).start()
 
-    slot_row = lambda z, r: pl.multiple_of(where[z * REPS + r] * PIECE, 16)
+    slot_row = lambda z, r: pl.multiple_of(where[1 + count + z * REPS + r] * PIECE, 16)
 
     def keep_rows(z, begin, rows, part):
         for r in range(part.shape[0] // rows):
@@ -789,14 +744,11 @@
     act1_t = (normed[...] * vecs[0:1, :] + vecs[1:2, :]).astype(jnp.bfloat16).T
     for j in range(3):
         keep_rows(
-            0, 96 * j, 96, dot32(act1_t, mixed_in[:, D * j : D * (j + 1)]).astype(jnp.bfloat16)
+            0, 96 * j, 96, dot32(act1_t, mixed_out[:, D * j : D * (j + 1)]).astype(jnp.bfloat16)
         )
     send_off(0)
-    keep_rows(1, 0, 96, dot32(attn_in[...].T, gy).astype(jnp.bfloat16))
-
-    for copy in copies:
-        copy.wait()
-    gy_t = gy.T
+    keep_rows(1, 0, 96, dot32(attn_out[...].T, gy).astype(jnp.bfloat16))
+
     act2 = (normed[...] * vecs[6:7, :] + vecs[7:8, :]).astype(jnp.bfloat16)
     act2_t = act2.T
     for j in range(4):
@@ -807,7 +759,7 @@
         hidden_out[:, wide] = hidden
         grad_hidden = dot32(w_out2_of(held, j), gy_t).T
         grad_pre = grad_hidden * (bell + pre * jnp.exp(-0.5 * pre * pre) * INV_ROOT_TWO_PI)
-        sums_out[j : j + 1, :] = jnp.sum(grad_pre, axis=0, keepdims=True)
+        high_sums[j : j + 1, :] = jnp.sum(grad_pre, axis=0, keepdims=True)
         grad_pre16 = grad_pre.astype(jnp.bfloat16)
         pre_out[:, wide] = grad_pre16
         w2 = dot32(hidden.T, gy).astype(jnp.bfloat16)
@@ -835,49 +787,56 @@
         ).wait()
 
 
-def weight_gradients(slots, matrices, small):
+def layer_gradients(scalars, blocks, own, small):
     anywhere = pl.BlockSpec(memory_space=pl.ANY)
     vmem = pl.BlockSpec(memory_space=pltpu.VMEM)
     bf16 = jnp.bfloat16
+    rows = jax.ShapeDtypeStruct((8, D), jnp.float32)
     return pl.pallas_call(
-        gradient_kernel,
+        layer_kernel,
         grid_spec=pltpu.PrefetchScalarGridSpec(
             num_scalar_prefetch=1,
-            in_specs=[anywhere] + [vmem] * len(small),
-            out_specs=[pl.BlockSpec(memory_space=pltpu.HBM)] * 16 + [vmem] * 3,
+            in_specs=[anywhere] * (len(blocks) + 1) + [vmem] * len(small),
+            out_specs=[pl.BlockSpec(memory_space=pltpu.HBM)] * 16 + [vmem] * 7,
             scratch_shapes=[
                 pltpu.VMEM((ALL_ROWS, D), bf16),
                 pltpu.VMEM((ALL_ROWS, D), bf16),
-                pltpu.SemaphoreType.DMA((SHARDS,)),
+                pltpu.VMEM((TOK_DEV, D), bf16),
+                pltpu.VMEM((TOK_DEV, D), bf16),
+                pltpu.VMEM((TOK_DEV, D), bf16),
+                pltpu.VMEM((TOK_DEV, D), bf16),
                 pltpu.SemaphoreType.DMA((PIECES,)),
+                pltpu.SemaphoreType.DMA((16,)),
             ],
         ),
         out_shape=[jax.ShapeDtypeStruct((2 * PIECE, D), bf16)] * 16
         + [
+            jax.ShapeDtypeStruct((TOK_DEV, D), bf16),
+            jax.ShapeDtypeStruct((TOK_DEV, 3 * D), bf16),
+            rows,
+            jax.ShapeDtypeStruct((16, D), jnp.float32),
             jax.ShapeDtypeStruct((TOK_DEV, FF), bf16),
             jax.ShapeDtypeStruct((TOK_DEV, FF), bf16),
-            jax.ShapeDtypeStruct((8, D), jnp.float32),
+            rows,
         ],
         compiler_params=pltpu.CompilerParams(vmem_limit_bytes=60 * 2**20),
         cost_estimate=pl.CostEstimate(
-            flops=10**10, bytes_accessed=60 * 2**20, transcendentals=800000
+            flops=2 * 10**10, bytes_accessed=80 * 2**20, transcendentals=10**6
         ),
-    )(slots, matrices, *small)
-
-
-def result_kernel(matrices, *refs):
+    )(scalars, *blocks, own, *small)
+
+
+def result_kernel(where, *refs):
+    count = PIECES - REPS
+    blocks, own = refs[:GROUPS], refs[GROUPS]
     (tokens, normed, spread, grad_y, attn, grad_mixed, low_sums, vecs, hidden, grad_pre, high_sums) = (
-        refs[:11]
-    )
-    output, grad_input, vec_out, held, sems = refs[11:]
-    copies = []
-    for z in range(SHARDS):
-        rows = pl.ds(z * REPS * PIECE, REPS * PIECE)
-        copies.append(pltpu.make_async_copy(matrices.at[rows], held.at[rows], sems.at[z]))
-    for copy in copies:
-        copy.start()
-    for copy in copies:
-        copy.wait()
+        refs[GROUPS + 1 : GROUPS + 12]
+    )
+    output, grad_input, vec_out, held, sems = refs[GROUPS + 12 :]
+    ids = [where[1 + t] for t in range(count)]
+    arrive = fetch_pieces(ids, blocks, own, where[0], held, sems)
+    for owner in range(SHARDS):
+        arrive(owner)
     total = dot32(attn[...], w_out_of(held)) + vecs[5:6, :]
     for j in range(4):
         total = total + dot32(hidden[:, D * j : D * (j + 1)], w_out2_of(held, j))
@@ -912,24 +871,27 @@
     vec_out[...] = vec_out[...].astype(jnp.bfloat16).astype(jnp.float32)
 
 
-def layer_results(matrices, small):
-    hbm = pl.BlockSpec(memory_space=pl.ANY)
+def layer_results(scalars, blocks, own, small):
+    anywhere = pl.BlockSpec(memory_space=pl.ANY)
     vmem = pl.BlockSpec(memory_space=pltpu.VMEM)
     rows = jax.ShapeDtypeStruct((TOK_DEV, D), jnp.float32)
     return pl.pallas_call(
         result_kernel,
-        in_specs=[hbm] + [vmem] * len(small),
-        out_specs=[vmem] * 3,
-        scratch_shapes=[
-            pltpu.VMEM((ALL_ROWS, D), jnp.bfloat16),
-            pltpu.SemaphoreType.DMA((SHARDS,)),
-        ],
+        grid_spec=pltpu.PrefetchScalarGridSpec(
+            num_scalar_prefetch=1,
+            in_specs=[anywhere] * (len(blocks) + 1) + [vmem] * len(small),
+            out_specs=[vmem] * 3,
+            scratch_shapes=[
+                pltpu.VMEM((ALL_ROWS, D), jnp.bfloat16),
+                pltpu.SemaphoreType.DMA((PIECES,)),
+            ],
+        ),
         out_shape=[rows, rows, jax.ShapeDtypeStruct((16, D), jnp.float32)],
-        compiler_params=pltpu.CompilerParams(vmem_limit_bytes=20 * 2**20),
+        compiler_params=pltpu.CompilerParams(vmem_limit_bytes=60 * 2**20),
         cost_estimate=pl.CostEstimate(
             flops=4 * 10**9, bytes_accessed=30 * 2**20, transcendentals=0
         ),
-    )(matrices, *small)
+    )(scalars, *blocks, own, *small)
 
 
 SHARE = FLAT_ROWS // REPS
@@ -962,6 +924,7 @@
         ),
         out_shape=jax.ShapeDtypeStruct((2, SHARE_ROWS, LANES), jnp.bfloat16),
         compiler_params=pltpu.CompilerParams(vmem_limit_bytes=16 * 2**20),
+        cost_estimate=pl.CostEstimate(flops=0, bytes_accessed=6 * 2**20, transcendentals=0),
     )(jnp.stack([rep]), moment_one.reshape(SHARE, LANES), moment_two.reshape(SHARE, LANES))
 
 
@@ -1091,11 +1054,14 @@
 fence = lax.optimization_barrier
 
 
-def gather_matrices(params, shard, rep, early):
+def gather_matrices(params, shard, rep, early, moment_one, moment_two):
     piece = pack_pieces(params, shard, [rep], False)[0][0]
     own, vec = pack_pieces(params, shard, [rep * 0 + turn for turn in range(REPS)], True)
     one = ring_step(piece)
-    one, own, vec = fence((one, own, vec))
+    _, moment_one, moment_two = fence((piece, moment_one, moment_two))
+    moments = align_moments(moment_one, moment_two, rep)
+    first_moments = first_cross(moments)
+    one, own, vec, first_moments = fence((one, own, vec, first_moments))
     two, first_one, second_one = ring_step(one), first_cross(one), second_cross(one)
     vec_one = ring_step(vec)
     two, first_one, second_one, vec_one, early = fence(
@@ -1128,7 +1094,7 @@
         owner = (shard + SHARDS - hop) % SHARDS
         ids += [owner * REPS + which for which in spread_ids(rep)]
     hops = [vec, vec_one, vec_two, vec_three]
-    return blocks, own.reshape(REPS * PIECE, D), ids, hops, early
+    return blocks, own.reshape(REPS * PIECE, D), ids, hops, early, [moments, first_moments]
 
 
 def slots_by_piece(shard, rep):
@@ -1209,24 +1175,20 @@
 def on_device_rows(tokens, segment_ids, cotangent, params, moment_one, moment_two):
     shard = lax.axis_index("z")
     rep = lax.axis_index(PLANE)
-    early = (prepare(tokens, cotangent, segment_ids), align_moments(moment_one, moment_two, rep))
-    blocks, own, ids, hops, early = gather_matrices(params, shard, rep, early)
-    (normed, inv_std, grad_y, tables), moments = early
+    early = prepare(tokens, cotangent, segment_ids)
+    blocks, own, ids, hops, early, moments = gather_matrices(
+        params, shard, rep, early, moment_one, moment_two
+    )
+    normed, inv_std, grad_y, tables = early
     moments, blocks = fence((moments, blocks))
-    first_moments = first_cross(moments)
-    small = (normed, grad_y, tables, *hops)
-    matrices, *attended = attention(jnp.stack([shard] + ids), blocks, own, small)
-    moments, first_moments, attended = fence((moments, first_moments, attended))
-    moments = [moments, first_moments, second_cross(moments), second_cross(first_moments)]
+    moments += [second_cross(value) for value in moments]
     moments += [core_cross(value) for value in moments[:2]]
-    attn, mixed, low_sums, vecs = attended
-    made = weight_gradients(
-        jnp.stack(slots_by_piece(shard, rep) + [shard]), matrices, (normed, grad_y, attn, mixed, vecs)
-    )
+    scalars = jnp.stack([shard] + ids + slots_by_piece(shard, rep))
+    made = layer_gradients(scalars, blocks, own, (normed, grad_y, tables, *hops))
     made, moments = fence((made, moments))
-    small = (tokens, normed, inv_std, grad_y, attn, mixed, low_sums, vecs) + tuple(made[16:])
+    small = (tokens, normed, inv_std, grad_y) + tuple(made[16:])
     spread, moments, output, grad_input, vec_grads = scatter_sums(
-        [part.reshape(2, PIECE, D) for part in made[:16]], moments, small, lambda small: layer_results(matrices, small)
+        [part.reshape(2, PIECE, D) for part in made[:16]], moments, small, lambda small: layer_results(scalars, blocks, own, small)
     )
     own_vectors = lax.dynamic_index_in_dim(
         vec_grads.reshape(SHARDS, 4, D), shard, 0, keepdims=False

time: 242 us -> 239 us (0.988)
  other arithmetic: 6.83 us -> 13.9 us
  waiting for transfers between devices: 121 us -> 114 us
  local copies, waits for them, and re-layouts: 12.6 us -> 9.36 us
    ppermute x48, waiting for transfers between devices: 77.7 us -> 66.1 us  [plane_permute(): lax.ppermute(value, PLANE, [(i, i ^ flips[i % 2]) for i in range(REPS)])]
    ppermute x9, waiting for transfers between devices: 33.2 us -> 37.7 us  [ring_step(): lax.ppermute(value, 'z', [(i, (i + 1) % SHARDS) for i in range(SHARDS)])]
    add x3, other arithmetic: 0.43 us -> 4.51 us  [scatter_sums(): pair = near[turn] + crossed]
    unnamed x96 -> x84, local copies, waits for them, and re-layouts: 9.46 us -> 6.59 us
    ppermute x48, starting transfers between devices: 28.6 us -> 31.3 us  [plane_permute(): lax.ppermute(value, PLANE, [(i, i ^ flips[i % 2]) for i in range(REPS)])]
    pallas_call x3 -> x2, Pallas kernels: 38.6 us -> 36.6 us  [the longest x1 24.7 us: layer_gradients(): pl.pallas_call(layer_kernel, grid_spec=pltpu.PrefetchScalarGridSpec(num_s...]
  transfers between devices with their start and end apart: 60 -> 60, of which waited for: 31 -> 31; matrix products, arithmetic and copies ran while one was open for 2% -> 4% of each run, Pallas kernels for 20% -> 19%
where the time goes in v10:
time: 239 us; the launch traced here: 238 us
  waiting for transfers between devices  114 us (48%)
  Pallas kernels  64.4 us (27%)
  starting transfers between devices  35.3 us (15%)
  other arithmetic  13.9 us (6%)
  local copies, waits for them, and re-layouts  9.36 us (4%)
    ppermute x48, waiting for transfers between devices, plane_permute(): lax.ppermute(value, PLANE, [(i, i ^ flips[i % 2]) for i in range(REPS)])  66.1 us
    ppermute x9, waiting for transfers between devices, ring_step(): lax.ppermute(value, 'z', [(i, (i + 1) % SHARDS) for i in range(SHARDS)])  37.7 us
    ppermute x48, starting transfers between devices, plane_permute(): lax.ppermute(value, PLANE, [(i, i ^ flips[i % 2]) for i in range(REPS)])  31.3 us
    pallas_call x1, Pallas kernels, layer_gradients(): pl.pallas_call(layer_kernel, grid_spec=pltpu.PrefetchScalarGridSpec(num_s...  24.7 us
    pallas_call x1, Pallas kernels, update_shard(): pl.pallas_call(functools.partial(update_kernel, factor), grid_spec=pltpu....  15.3 us
    pallas_call x1, Pallas kernels, layer_results(): pl.pallas_call(result_kernel, grid_spec=pltpu.PrefetchScalarGridSpec(num_...  11.9 us
    pallas_call x2, Pallas kernels, pack_pieces(): pl.pallas_call(pack_kernel, grid_spec=pltpu.PrefetchScalarGridSpec(num_sc...  11.8 us
    ppermute x3, waiting for transfers between devices, ring_shift(): lax.ppermute(value, 'z', [(i, (i + hop) % SHARDS) for i in range(SHARDS)])  9.9 us
  transfers between devices with their start and end apart: 60, of which 31 were waited for; matrix products, arithmetic and copies ran while one was open for 4% of the time, Pallas kernels for 19%

profile of v10, /device:TPU:0, one launch (start us, length us, event | category | flops | bytes accessed | tf_op | source)
XLA Modules:
  0.0 238.0 jit_solution(9805120300151658304)
XLA Ops:
  1.2 2.9 %shard_map.109 = bf16[1,288,768]{2,1,0:T(8,128)(2,1)} custom-call(s32[2]{0:T(128)} %pad_add_fusion.where, f32[13848,128]{1,0:T(8,128)} %bitcast.132), custom_call_target="tpu_custom_call" | custom-call | bytes 3145728 | tf_op jit(solution)/shard_map/pallas_call | solution.py:522
  4.4 3.1 %collective-permute-start.1 = (bf16[2,1760,128]{2,1,0:T(8,128)(2,1)S(1)}, bf16[2,1760,128]{2,1,0:T(8,128)(2,1)}, u32[]{:S(2)}, u32[]{:S(2)}) collective-permute-start(bf16[2,1760,128]{2,1,0:T(8,128)(2,1)S(1)} %shard_map.110.refs_8_), channel_id=1, source_target_pairs={{0,8},{4,20},{8,0},{12,28},{16,24},{20,4},{24,16},{28,12},{1,9},{5... | collective-permute-start | bytes 2703368 | tf_op jit(solution)/shard_map/ppermute | solution.py:409
  9.6 8.9 %shard_map.111 = (bf16[8,288,768]{2,1,0:T(8,128)(2,1)}, f32[8,768]{1,0:T(8,128)}) custom-call(s32[9]{0:T(128)} %stack.302.where, f32[13848,128]{1,0:T(8,128)} %bitcast.133), custom_call_target="tpu_custom_call" | custom-call | bytes 25165824 | tf_op jit(solution)/shard_map/pallas_call | solution.py:522
  18.6 2.7 %collective-permute-done = bf16[288,768]{1,0:T(8,128)(2,1)} collective-permute-done((bf16[288,768]{1,0:T(8,128)(2,1)}, bf16[288,768]{1,0:T(8,128)(2,1)}, u32[]{:S(2)}, u32[]{:S(2)}) %collective-permute-start) | collective-permute-done | bytes 442400 | tf_op jit(solution)/shard_map/ppermute | solution.py:425
  28.0 9.1 %collective-permute-done.5.refs_17_ = f32[8,768]{1,0:T(8,128)S(1)} collective-permute-done((f32[8,768]{1,0:T(8,128)}, f32[8,768]{1,0:T(8,128)S(1)}, u32[]{:S(2)}, u32[]{:S(2)}) %collective-permute-start.5) | collective-permute-done | bytes 24608 | tf_op jit(solution)/shard_map/ppermute | solution.py:425
  37.1 1.8 collective-permute-start.9
  39.6 13.5 %collective-permute-done.10.refs_18_ = f32[8,768]{1,0:T(8,128)S(1)} collective-permute-done((f32[8,768]{1,0:T(8,128)S(1)}, f32[8,768]{1,0:T(8,128)S(1)}, u32[]{:S(2)}, u32[]{:S(2)}) %collective-permute-start.10) | collective-permute-done | bytes 24608 | tf_op jit(solution)/shard_map/ppermute | solution.py:425
  55.6 1.8 collective-permute-start.13
  58.0 5.9 %collective-permute-done.15.refs_19_ = f32[8,768]{1,0:T(8,128)S(1)} collective-permute-done((f32[8,768]{1,0:T(8,128)S(1)}, f32[8,768]{1,0:T(8,128)S(1)}, u32[]{:S(2)}, u32[]{:S(2)}) %collective-permute-start.15) | collective-permute-done | bytes 24608 | tf_op jit(solution)/shard_map/ppermute | solution.py:425
  63.9 3.9 %collective-permute-done.13 = bf16[288,768]{1,0:T(8,128)(2,1)S(1)} collective-permute-done((bf16[288,768]{1,0:T(8,128)(2,1)S(1)}, bf16[288,768]{1,0:T(8,128)(2,1)S(1)}, u32[]{:S(2)}, u32[]{:S(2)}) %collective-permute-start.13) | collective-permute-done | bytes 442400 | tf_op jit(solution)/shard_map/ppermute | solution.py:409
  67.8 5.7 %collective-permute-done.12.refs_6_ = bf16[288,768]{1,0:T(8,128)(2,1)S(1)} collective-permute-done((bf16[288,768]{1,0:T(8,128)(2,1)S(1)}, bf16[288,768]{1,0:T(8,128)(2,1)S(1)}, u32[]{:S(2)}, u32[]{:S(2)}) %collective-permute-start.12) | collective-permute-done | bytes 442400 | tf_op jit(solution)/shard_map/ppermute | solution.py:409
  76.6 1.7 collective-permute-start.19
  79.9 5.1 %collective-permute-done.19.refs_7_ = bf16[288,768]{1,0:T(8,128)(2,1)} collective-permute-done((bf16[288,768]{1,0:T(8,128)(2,1)S(1)}, bf16[288,768]{1,0:T(8,128)(2,1)}, u32[]{:S(2)}, u32[]{:S(2)}) %collective-permute-start.19) | collective-permute-done | bytes 442400 | tf_op jit(solution)/shard_map/ppermute | solution.py:409
  89.2 1.7 collective-permute-start.22
  91.4 24.7 %shard_map.113 = (bf16[576,768]{1,0:T(8,128)(2,1)}, bf16[576,768]{1,0:T(8,128)(2,1)}, bf16[576,768]{1,0:T(8,128)(2,1)}, bf16[576,768]{1,0:T(8,128)(2,1)}, bf16[5...) custom-call(s32[57]{0:T(128)} %stack.299.where, ...), custom_call_target="tpu_custom_call" | custom-call | flops 20000000000 | bytes 83886080 | tf_op jit(solution)/shard_map/pallas_call | solution.py:795
  122.9 1.7 collective-permute-start.29
  126.5 9.5 %collective-permute-done.29 = bf16[2,288,768]{2,1,0:T(8,128)(2,1)S(1)} collective-permute-done((bf16[2,288,768]{2,1,0:T(8,128)(2,1)S(1)}, bf16[2,288,768]{2,1,0:T(8,128)(2,1)S(1)}, u32[]{:S(2)}, u32[]{:S(2)}) %collective-permute-start.29) | collective-permute-done | bytes 884768 | tf_op jit(solution)/shard_map/ppermute | solution.py:409
  136.2 1.6 collective-permute-start.34
  140.0 11.9 %shard_map.114 = (f32[128,768]{1,0:T(8,128)}, f32[128,768]{1,0:T(8,128)}, f32[16,768]{1,0:T(8,128)}) custom-call(s32[57]{0:T(128)} %stack.299.where, bf16[4,288,768]{2,1,0:T(8,128)(2,1)} %copy-done.10, bf16[4,288,768]{2,1,0:T(8,128)(2,1)} %copy-done.12, bf16[4,288,768]{2,1,0:T(8,128)(2,1)} %copy-done.11, bf16[4,288,768]{2,1,0:T(8,128)(2,1)} %copy-done.13, ...), custom_call_target="tpu_custom_call" | custom-call | flops 4000000000 | bytes 31457280 | tf_op jit(solution)/shard_map/pallas_call | solution.py:878
  151.9 1.8 add_add_fusion
  156.6 7.3 %collective-permute-done.38 = bf16[2,288,768]{2,1,0:T(8,128)(2,1)} collective-permute-done((bf16[2,288,768]{2,1,0:T(8,128)(2,1)}, bf16[2,288,768]{2,1,0:T(8,128)(2,1)}, u32[]{:S(2)}, u32[]{:S(2)}) %collective-permute-start.38) | collective-permute-done | bytes 884768 | tf_op jit(solution)/shard_map/ppermute | solution.py:409
  163.9 3.2 %collective-permute-done.37 = bf16[288,768]{1,0:T(8,128)(2,1)S(1)} collective-permute-done((bf16[288,768]{1,0:T(8,128)(2,1)S(1)}, bf16[288,768]{1,0:T(8,128)(2,1)S(1)}, u32[]{:S(2)}, u32[]{:S(2)}) %collective-permute-start.37) | collective-permute-done | bytes 442400 | tf_op jit(solution)/shard_map/ppermute | solution.py:409
  171.1 7.5 %collective-permute-done.42 = bf16[2,288,768]{2,1,0:T(8,128)(2,1)S(1)} collective-permute-done((bf16[2,288,768]{2,1,0:T(8,128)(2,1)S(1)}, bf16[2,288,768]{2,1,0:T(8,128)(2,1)S(1)}, u32[]{:S(2)}, u32[]{:S(2)}) %collective-permute-start.42) | collective-permute-done | bytes 884768 | tf_op jit(solution)/shard_map/ppermute | solution.py:409
  179.6 1.8 collective-permute-done.43
  185.2 6.6 %collective-permute-done.47 = f32[16,768]{1,0:T(8,128)S(1)} collective-permute-done((f32[16,768]{1,0:T(8,128)S(1)}, f32[16,768]{1,0:T(8,128)S(1)}, u32[]{:S(2)}, u32[]{:S(2)}) %collective-permute-start.47) | collective-permute-done | bytes 49184 | tf_op jit(solution)/shard_map/ppermute | solution.py:409
  191.8 4.5 %collective-permute-done.46 = bf16[288,768]{1,0:T(8,128)(2,1)S(1)} collective-permute-done((bf16[288,768]{1,0:T(8,128)(2,1)S(1)}, bf16[288,768]{1,0:T(8,128)(2,1)S(1)}, u32[]{:S(2)}, u32[]{:S(2)}) %collective-permute-start.46) | collective-permute-done | bytes 442400 | tf_op jit(solution)/shard_map/ppermute | solution.py:425
  198.7 4.0 %collective-permute-done.52 = f32[16,768]{1,0:T(8,128)S(1)} collective-permute-done((f32[16,768]{1,0:T(8,128)S(1)}, f32[16,768]{1,0:T(8,128)S(1)}, u32[]{:S(2)}, u32[]{:S(2)}) %collective-permute-start.52) | collective-permute-done | bytes 49184 | tf_op jit(solution)/shard_map/ppermute | solution.py:1051
  203.8 4.8 %collective-permute-done.50 = f32[16,768]{1,0:T(8,128)S(1)} collective-permute-done((f32[16,768]{1,0:T(8,128)S(1)}, f32[16,768]{1,0:T(8,128)S(1)}, u32[]{:S(2)}, u32[]{:S(2)}) %collective-permute-start.50) | collective-permute-done | bytes 49184 | tf_op jit(solution)/shard_map/ppermute | solution.py:1051
  210.0 1.7 collective-permute-done.56.refs_6_
  212.3 5.4 %collective-permute-done.53.refs_3_ = bf16[288,768]{1,0:T(8,128)(2,1)} collective-permute-done((bf16[288,768]{1,0:T(8,128)(2,1)S(1)}, bf16[288,768]{1,0:T(8,128)(2,1)}, u32[]{:S(2)}, u32[]{:S(2)}) %collective-permute-start.53) | collective-permute-done | bytes 442400 | tf_op jit(solution)/shard_map/ppermute | solution.py:409
  219.9 15.3 %shard_map.115 = (f32[13848,128]{1,0:T(8,128)}, f32[13848,128]{1,0:T(8,128)}) custom-call(s32[9]{0:T(128)} %stack.320.where, bf16[288,768]{1,0:T(8,128)(2,1)} %copy-done.14, bf16[288,768]{1,0:T(8,128)(2,1)} %copy-done.34, bf16[288,768]{1,0:T(8,128)(2,1)} %copy-done.33, bf16[288,768]{1,0:T(8,128)(2,1)} %collective-permute-done.53.refs_3_, ...), custom_call_target="tpu_custom_call" | custom-call | tf_op jit(solution)/shard_map/pallas_call | solution.py:1029
  235.2 2.8 %fusion = (f32[221568]{0:T(1024)}, f32[221568]{0:T(1024)}) fusion(f32[221568]{0:T(1024)S(1)} %copy-done.2, f32[1772544]{0:T(1024)} %bitcast.152, s32[]{:T(128)S(6)} %select_n.334, f32[221568]{0:T(1024)S(1)} %copy-done.1), kind=kLoop, calls=%fused_computation.3 | loop fusion | flops 1550976 | bytes 4431364 | tf_op jit(solution)/shard_map/add | solution.py:352
  (209 shorter events, 52.7 us)
Async XLA Ops:
  4.4 16.9 %collective-permute-start.1 = (bf16[2,1760,128]{2,1,0:T(8,128)(2,1)S(1)}, bf16[2,1760,128]{2,1,0:T(8,128)(2,1)}, u32[]{:S(2)}, u32[]{:S(2)}) collective-permute-start(bf16[2,1760,128]{2,1,0:T(8,128)(2,1)S(1)} %shard_map.110.refs_8_), channel_id=1, source_target_pairs={{0,8},{4,20},{8,0},{12,28},{16,24},{20,4},{24,16},{28,12},{1,9},{5... | collective-permute-start | bytes 2703368 | tf_op jit(solution)/shard_map/ppermute | solution.py:409
  7.4 13.8 %collective-permute-start = (bf16[288,768]{1,0:T(8,128)(2,1)}, bf16[288,768]{1,0:T(8,128)(2,1)}, u32[]{:S(2)}, u32[]{:S(2)}) collective-permute-start(bf16[288,768]{1,0:T(8,128)(2,1)} %bitcast.59), channel_id=1, source_target_pairs={{0,1},{1,2},{2,3},{3,0},{4,5},{5,6},{6,7},{7,4},{8,9},{9,10},{10,1... | collective-permute-start | bytes 1327112 | tf_op jit(solution)/shard_map/ppermute | solution.py:425
  21.3 15.9 %collective-permute-start.4 = (bf16[288,768]{1,0:T(8,128)(2,1)}, bf16[288,768]{1,0:T(8,128)(2,1)S(1)}, u32[]{:S(2)}, u32[]{:S(2)}) collective-permute-start(bf16[288,768]{1,0:T(8,128)(2,1)} %collective-permute-done), channel_id=1, source_target_pairs={{0,16},{4,12},{8,24},{12,4},{16,0},{20,28},{24,8},{28,20},{1,17},{... | collective-permute-start | bytes 1327112 | tf_op jit(solution)/shard_map/ppermute | solution.py:409
  21.8 15.4 %collective-permute-start.3 = (bf16[288,768]{1,0:T(8,128)(2,1)}, bf16[288,768]{1,0:T(8,128)(2,1)S(1)}, u32[]{:S(2)}, u32[]{:S(2)}) collective-permute-start(bf16[288,768]{1,0:T(8,128)(2,1)} %collective-permute-done), channel_id=1, source_target_pairs={{0,8},{4,20},{8,0},{12,28},{16,24},{20,4},{24,16},{28,12},{1,9},{5... | collective-permute-start | bytes 1327112 | tf_op jit(solution)/shard_map/ppermute | solution.py:409
  23.3 13.9 %collective-permute-start.2 = (bf16[288,768]{1,0:T(8,128)(2,1)}, bf16[288,768]{1,0:T(8,128)(2,1)S(1)}, u32[]{:S(2)}, u32[]{:S(2)}) collective-permute-start(bf16[288,768]{1,0:T(8,128)(2,1)} %collective-permute-done), channel_id=1, source_target_pairs={{0,1},{1,2},{2,3},{3,0},{4,5},{5,6},{6,7},{7,4},{8,9},{9,10},{10,1... | collective-permute-start | bytes 1327112 | tf_op jit(solution)/shard_map/ppermute | solution.py:425
  23.9 13.2 %collective-permute-start.5 = (f32[8,768]{1,0:T(8,128)}, f32[8,768]{1,0:T(8,128)S(1)}, u32[]{:S(2)}, u32[]{:S(2)}) collective-permute-start(f32[8,768]{1,0:T(8,128)} %get-tuple-element.173.refs_16_), channel_id=1, source_target_pairs={{0,1},{1,2},{2,3},{3,0},{4,5},{5,6},{6,7},{7,4},{8,9},{9,10},{10,1... | collective-permute-start | bytes 73736 | tf_op jit(solution)/shard_map/ppermute | solution.py:425
  37.1 16.0 %collective-permute-start.9 = (bf16[288,768]{1,0:T(8,128)(2,1)S(1)}, bf16[288,768]{1,0:T(8,128)(2,1)S(1)}, u32[]{:S(2)}, u32[]{:S(2)}) collective-permute-start(bf16[288,768]{1,0:T(8,128)(2,1)S(1)} %collective-permute-done.3), channel_id=1, source_target_pairs={{0,16},{4,12},{8,24},{12,4},{16,0},{20,28},{24,8},{28,20},{1,17},{... | collective-permute-start | bytes 1327112 | tf_op jit(solution)/shard_map/ppermute | solution.py:409
  39.0 15.1 %collective-permute-start.8 = (bf16[288,768]{1,0:T(8,128)(2,1)S(1)}, bf16[288,768]{1,0:T(8,128)(2,1)S(1)}, u32[]{:S(2)}, u32[]{:S(2)}) collective-permute-start(bf16[288,768]{1,0:T(8,128)(2,1)S(1)} %collective-permute-done.2), channel_id=1, source_target_pairs={{0,16},{4,12},{8,24},{12,4},{16,0},{20,28},{24,8},{28,20},{1,17},{... | collective-permute-start | bytes 1327112 | tf_op jit(solution)/shard_map/ppermute | solution.py:409
  39.2 14.8 %collective-permute-start.7 = (bf16[288,768]{1,0:T(8,128)(2,1)S(1)}, bf16[288,768]{1,0:T(8,128)(2,1)S(1)}, u32[]{:S(2)}, u32[]{:S(2)}) collective-permute-start(bf16[288,768]{1,0:T(8,128)(2,1)S(1)} %collective-permute-done.2), channel_id=1, source_target_pairs={{0,8},{4,20},{8,0},{12,28},{16,24},{20,4},{24,16},{28,12},{1,9},{5... | collective-permute-start | bytes 1327112 | tf_op jit(solution)/shard_map/ppermute | solution.py:409
  39.6 14.5 %collective-permute-start.6 = (bf16[288,768]{1,0:T(8,128)(2,1)S(1)}, bf16[288,768]{1,0:T(8,128)(2,1)S(1)}, u32[]{:S(2)}, u32[]{:S(2)}) collective-permute-start(bf16[288,768]{1,0:T(8,128)(2,1)S(1)} %collective-permute-done.2), channel_id=1, source_target_pairs={{0,1},{1,2},{2,3},{3,0},{4,5},{5,6},{6,7},{7,4},{8,9},{9,10},{10,1... | collective-permute-start | bytes 1327112 | tf_op jit(solution)/shard_map/ppermute | solution.py:425
  39.6 13.5 %collective-permute-start.10 = (f32[8,768]{1,0:T(8,128)S(1)}, f32[8,768]{1,0:T(8,128)S(1)}, u32[]{:S(2)}, u32[]{:S(2)}) collective-permute-start(f32[8,768]{1,0:T(8,128)S(1)} %collective-permute-done.5.refs_17_), channel_id=1, source_target_pairs={{0,1},{1,2},{2,3},{3,0},{4,5},{5,6},{6,7},{7,4},{8,9},{9,10},{10,1... | collective-permute-start | bytes 73736 | tf_op jit(solution)/shard_map/ppermute | solution.py:425
  55.5 17.9 %collective-permute-start.14 = (bf16[4,288,768]{2,1,0:T(8,128)(2,1)S(1)}, bf16[4,288,768]{2,1,0:T(8,128)(2,1)S(1)}, u32[]{:S(2)}, u32[]{:S(2)}) collective-permute-start(bf16[4,288,768]{2,1,0:T(8,128)(2,1)S(1)} %pad_maximum_fusion.refs_0_), channel_id=1, source_target_pairs={{0,4},{4,0},{8,12},{12,8},{16,20},{20,16},{24,28},{28,24},{1,5},{5... | collective-permute-start | bytes 5308424 | tf_op jit(solution)/shard_map/ppermute | solution.py:409
  55.6 12.2 %collective-permute-start.13 = (bf16[288,768]{1,0:T(8,128)(2,1)S(1)}, bf16[288,768]{1,0:T(8,128)(2,1)S(1)}, u32[]{:S(2)}, u32[]{:S(2)}) collective-permute-start(bf16[288,768]{1,0:T(8,128)(2,1)S(1)} %collective-permute-done.7), channel_id=1, source_target_pairs={{0,16},{4,12},{8,24},{12,4},{16,0},{20,28},{24,8},{28,20},{1,17},{... | collective-permute-start | bytes 1327112 | tf_op jit(solution)/shard_map/ppermute | solution.py:409
  57.4 16.0 %collective-permute-start.12 = (bf16[288,768]{1,0:T(8,128)(2,1)S(1)}, bf16[288,768]{1,0:T(8,128)(2,1)S(1)}, u32[]{:S(2)}, u32[]{:S(2)}) collective-permute-start(bf16[288,768]{1,0:T(8,128)(2,1)S(1)} %collective-permute-done.6.refs_4_), channel_id=1, source_target_pairs={{0,16},{4,12},{8,24},{12,4},{16,0},{20,28},{24,8},{28,20},{1,17},{... | collective-permute-start | bytes 1327112 | tf_op jit(solution)/shard_map/ppermute | solution.py:409
  57.7 15.8 %collective-permute-start.11 = (bf16[288,768]{1,0:T(8,128)(2,1)S(1)}, bf16[288,768]{1,0:T(8,128)(2,1)S(1)}, u32[]{:S(2)}, u32[]{:S(2)}) collective-permute-start(bf16[288,768]{1,0:T(8,128)(2,1)S(1)} %collective-permute-done.6.refs_4_), channel_id=1, source_target_pairs={{0,8},{4,20},{8,0},{12,28},{16,24},{20,4},{24,16},{28,12},{1,9},{5... | collective-permute-start | bytes 1327112 | tf_op jit(solution)/shard_map/ppermute | solution.py:409
  89.1 27.1 %collective-permute-start.24 = (bf16[2,1760,128]{2,1,0:T(8,128)(2,1)S(1)}, bf16[2,1760,128]{2,1,0:T(8,128)(2,1)}, u32[]{:S(2)}, u32[]{:S(2)}) collective-permute-start(bf16[2,1760,128]{2,1,0:T(8,128)(2,1)S(1)} %shard_map.110.refs_8_), channel_id=1, source_target_pairs={{0,4},{4,0},{8,12},{12,8},{16,20},{20,16},{24,28},{28,24},{1,5},{5... | collective-permute-start | bytes 2703368 | tf_op jit(solution)/shard_map/ppermute | solution.py:409
  89.2 26.9 %collective-permute-start.22 = (bf16[2,1760,128]{2,1,0:T(8,128)(2,1)S(1)}, bf16[2,1760,128]{2,1,0:T(8,128)(2,1)}, u32[]{:S(2)}, u32[]{:S(2)}) collective-permute-start(bf16[2,1760,128]{2,1,0:T(8,128)(2,1)S(1)} %shard_map.110.refs_8_), channel_id=1, source_target_pairs={{0,16},{4,12},{8,24},{12,4},{16,0},{20,28},{24,8},{28,20},{1,17},{... | collective-permute-start | bytes 2703368 | tf_op jit(solution)/shard_map/ppermute | solution.py:409
  91.0 25.2 %collective-permute-start.25 = (bf16[2,1760,128]{2,1,0:T(8,128)(2,1)}, bf16[2,1760,128]{2,1,0:T(8,128)(2,1)}, u32[]{:S(2)}, u32[]{:S(2)}) collective-permute-start(bf16[2,1760,128]{2,1,0:T(8,128)(2,1)} %collective-permute-done.1.refs_9_), channel_id=1, source_target_pairs={{0,4},{4,0},{8,12},{12,8},{16,20},{20,16},{24,28},{28,24},{1,5},{5... | collective-permute-start | bytes 2703368 | tf_op jit(solution)/shard_map/ppermute | solution.py:409
  91.0 25.2 %collective-permute-start.23 = (bf16[2,1760,128]{2,1,0:T(8,128)(2,1)}, bf16[2,1760,128]{2,1,0:T(8,128)(2,1)}, u32[]{:S(2)}, u32[]{:S(2)}) collective-permute-start(bf16[2,1760,128]{2,1,0:T(8,128)(2,1)} %collective-permute-done.1.refs_9_), channel_id=1, source_target_pairs={{0,16},{4,12},{8,24},{12,4},{16,0},{20,28},{24,8},{28,20},{1,17},{... | collective-permute-start | bytes 2703368 | tf_op jit(solution)/shard_map/ppermute | solution.py:409
  122.9 13.1 %collective-permute-start.29 = (bf16[2,288,768]{2,1,0:T(8,128)(2,1)S(1)}, bf16[2,288,768]{2,1,0:T(8,128)(2,1)S(1)}, u32[]{:S(2)}, u32[]{:S(2)}) collective-permute-start(bf16[2,288,768]{2,1,0:T(8,128)(2,1)S(1)} %add.607), channel_id=1, source_target_pairs={{0,8},{4,20},{8,0},{12,28},{16,24},{20,4},{24,16},{28,12},{1,9},{5... | collective-permute-start | bytes 2654216 | tf_op jit(solution)/shard_map/ppermute | solution.py:409
  125.7 26.2 %collective-permute-start.36 = (bf16[2,288,768]{2,1,0:T(8,128)(2,1)}, bf16[2,288,768]{2,1,0:T(8,128)(2,1)}, u32[]{:S(2)}, u32[]{:S(2)}) collective-permute-start(bf16[2,288,768]{2,1,0:T(8,128)(2,1)} %bitcast.91), channel_id=1, source_target_pairs={{0,4},{4,0},{8,12},{12,8},{16,20},{20,16},{24,28},{28,24},{1,5},{5... | collective-permute-start | bytes 2654216 | tf_op jit(solution)/shard_map/ppermute | solution.py:409
  125.8 26.2 %collective-permute-start.35 = (bf16[2,288,768]{2,1,0:T(8,128)(2,1)}, bf16[2,288,768]{2,1,0:T(8,128)(2,1)}, u32[]{:S(2)}, u32[]{:S(2)}) collective-permute-start(bf16[2,288,768]{2,1,0:T(8,128)(2,1)} %add.610), channel_id=1, source_target_pairs={{0,8},{4,20},{8,0},{12,28},{16,24},{20,4},{24,16},{28,12},{1,9},{5... | collective-permute-start | bytes 2654216 | tf_op jit(solution)/shard_map/ppermute | solution.py:409
  136.2 15.7 %collective-permute-start.34 = (bf16[288,768]{1,0:T(8,128)(2,1)S(1)}, bf16[288,768]{1,0:T(8,128)(2,1)S(1)}, u32[]{:S(2)}, u32[]{:S(2)}) collective-permute-start(bf16[288,768]{1,0:T(8,128)(2,1)S(1)} %slice_bitcast_fusion.7), channel_id=1, source_target_pairs={{0,16},{4,12},{8,24},{12,4},{16,0},{20,28},{24,8},{28,20},{1,17},{... | collective-permute-start | bytes 1327112 | tf_op jit(solution)/shard_map/ppermute | solution.py:409
  139.0 24.9 %collective-permute-start.38 = (bf16[2,288,768]{2,1,0:T(8,128)(2,1)}, bf16[2,288,768]{2,1,0:T(8,128)(2,1)}, u32[]{:S(2)}, u32[]{:S(2)}) collective-permute-start(bf16[2,288,768]{2,1,0:T(8,128)(2,1)} %add.615), channel_id=1, source_target_pairs={{0,8},{4,20},{8,0},{12,28},{16,24},{20,4},{24,16},{28,12},{1,9},{5... | collective-permute-start | bytes 2654216 | tf_op jit(solution)/shard_map/ppermute | solution.py:409
  153.9 13.2 %collective-permute-start.37 = (bf16[288,768]{1,0:T(8,128)(2,1)S(1)}, bf16[288,768]{1,0:T(8,128)(2,1)S(1)}, u32[]{:S(2)}, u32[]{:S(2)}) collective-permute-start(bf16[288,768]{1,0:T(8,128)(2,1)S(1)} %slice_bitcast_fusion.6), channel_id=1, source_target_pairs={{0,16},{4,12},{8,24},{12,4},{16,0},{20,28},{24,8},{28,20},{1,17},{... | collective-permute-start | bytes 1327112 | tf_op jit(solution)/shard_map/ppermute | solution.py:409
  155.1 12.2 %collective-permute-start.39 = (bf16[288,768]{1,0:T(8,128)(2,1)S(1)}, bf16[288,768]{1,0:T(8,128)(2,1)S(1)}, u32[]{:S(2)}, u32[]{:S(2)}) collective-permute-start(bf16[288,768]{1,0:T(8,128)(2,1)S(1)} %fusion.7), channel_id=1, source_target_pairs={{0,1},{1,2},{2,3},{3,0},{4,5},{5,6},{6,7},{7,4},{8,9},{9,10},{10,1... | collective-permute-start | bytes 1327112 | tf_op jit(solution)/shard_map/ppermute | solution.py:425
  155.4 23.1 %collective-permute-start.42 = (bf16[2,288,768]{2,1,0:T(8,128)(2,1)S(1)}, bf16[2,288,768]{2,1,0:T(8,128)(2,1)S(1)}, u32[]{:S(2)}, u32[]{:S(2)}) collective-permute-start(bf16[2,288,768]{2,1,0:T(8,128)(2,1)S(1)} %add.618), channel_id=1, source_target_pairs={{0,8},{4,20},{8,0},{12,28},{16,24},{20,4},{24,16},{28,12},{1,9},{5... | collective-permute-start | bytes 2654216 | tf_op jit(solution)/shard_map/ppermute | solution.py:409
  170.1 11.3 %collective-permute-start.43 = (bf16[288,768]{1,0:T(8,128)(2,1)S(1)}, bf16[288,768]{1,0:T(8,128)(2,1)S(1)}, u32[]{:S(2)}, u32[]{:S(2)}) collective-permute-start(bf16[288,768]{1,0:T(8,128)(2,1)S(1)} %fusion.6), channel_id=1, source_target_pairs={{0,1},{1,2},{2,3},{3,0},{4,5},{5,6},{6,7},{7,4},{8,9},{9,10},{10,1... | collective-permute-start | bytes 1327112 | tf_op jit(solution)/shard_map/ppermute | solution.py:425
  184.0 12.3 %collective-permute-start.46 = (bf16[288,768]{1,0:T(8,128)(2,1)S(1)}, bf16[288,768]{1,0:T(8,128)(2,1)S(1)}, u32[]{:S(2)}, u32[]{:S(2)}) collective-permute-start(bf16[288,768]{1,0:T(8,128)(2,1)S(1)} %fusion.2), channel_id=1, source_target_pairs={{0,1},{1,2},{2,3},{3,0},{4,5},{5,6},{6,7},{7,4},{8,9},{9,10},{10,1... | collective-permute-start | bytes 1327112 | tf_op jit(solution)/shard_map/ppermute | solution.py:425
  196.3 12.3 %collective-permute-start.49 = (bf16[288,768]{1,0:T(8,128)(2,1)S(1)}, bf16[288,768]{1,0:T(8,128)(2,1)S(1)}, u32[]{:S(2)}, u32[]{:S(2)}) collective-permute-start(bf16[288,768]{1,0:T(8,128)(2,1)S(1)} %fusion.4.refs_0_), channel_id=1, source_target_pairs={{0,16},{4,12},{8,24},{12,4},{16,0},{20,28},{24,8},{28,20},{1,17},{... | collective-permute-start | bytes 1327112 | tf_op jit(solution)/shard_map/ppermute | solution.py:409
  197.1 11.5 %collective-permute-start.48 = (bf16[288,768]{1,0:T(8,128)(2,1)S(1)}, bf16[288,768]{1,0:T(8,128)(2,1)S(1)}, u32[]{:S(2)}, u32[]{:S(2)}) collective-permute-start(bf16[288,768]{1,0:T(8,128)(2,1)S(1)} %fusion.4.refs_0_), channel_id=1, source_target_pairs={{0,8},{4,20},{8,0},{12,28},{16,24},{20,4},{24,16},{28,12},{1,9},{5... | collective-permute-start | bytes 1327112 | tf_op jit(solution)/shard_map/ppermute | solution.py:409
  203.8 15.4 %collective-permute-start.58 = (bf16[2,1760,128]{2,1,0:T(8,128)(2,1)}, bf16[2,1760,128]{2,1,0:T(8,128)(2,1)}, u32[]{:S(2)}, u32[]{:S(2)}) collective-permute-start(bf16[2,1760,128]{2,1,0:T(8,128)(2,1)} %collective-permute-done.22.refs_10_), channel_id=1, source_target_pairs={{0,4},{4,0},{8,12},{12,8},{16,20},{20,16},{24,28},{28,24},{1,5},{5... | collective-permute-start | bytes 2703368 | tf_op jit(solution)/shard_map/ppermute | solution.py:409
  (70 other events, 636.7 us)

commit v11 on v10

--- a/solution.py
+++ b/solution.py
@@ -1054,14 +1054,11 @@
 fence = lax.optimization_barrier
 
 
-def gather_matrices(params, shard, rep, early, moment_one, moment_two):
+def gather_matrices(params, shard, rep, early):
     piece = pack_pieces(params, shard, [rep], False)[0][0]
     own, vec = pack_pieces(params, shard, [rep * 0 + turn for turn in range(REPS)], True)
     one = ring_step(piece)
-    _, moment_one, moment_two = fence((piece, moment_one, moment_two))
-    moments = align_moments(moment_one, moment_two, rep)
-    first_moments = first_cross(moments)
-    one, own, vec, first_moments = fence((one, own, vec, first_moments))
+    one, own, vec = fence((one, own, vec))
     two, first_one, second_one = ring_step(one), first_cross(one), second_cross(one)
     vec_one = ring_step(vec)
     two, first_one, second_one, vec_one, early = fence(
@@ -1094,7 +1091,7 @@
         owner = (shard + SHARDS - hop) % SHARDS
         ids += [owner * REPS + which for which in spread_ids(rep)]
     hops = [vec, vec_one, vec_two, vec_three]
-    return blocks, own.reshape(REPS * PIECE, D), ids, hops, early, [moments, first_moments]
+    return blocks, own.reshape(REPS * PIECE, D), ids, hops, early
 
 
 def slots_by_piece(shard, rep):
@@ -1148,15 +1145,20 @@
         kept = pair[0]
         final = second_cross(pair[1])
         met = plane_permute(vectors, ((1, 1), (2, 2), (4, 4))[turn - 1])
-        if turn < SHARDS - 1:
+        if turn == 1:
             crossed = first_cross(far[turn + 1])
-            final, crossed, carried, met, moments = fence(
-                (final, crossed, carried, met, moments)
+            final, crossed, carried, met = fence((final, crossed, carried, met))
+        elif turn == 2:
+            crossed = first_cross(far[turn + 1])
+            first_other = core_cross(moments[1])
+            final, crossed, carried, met, moments, first_other = fence(
+                (final, crossed, carried, met, moments, first_other)
             )
         else:
-            final, carried, met = fence((final, carried, met))
-        if turn > 1:
-            moments.append(core_cross(moments[turn]))
+            both_moments, second_other = second_cross(moments[1]), core_cross(moments[2])
+            final, carried, met, both_moments, second_other = fence(
+                (final, carried, met, both_moments, second_other)
+            )
         vectors = vectors + met
     total = kept + final + carried
 
@@ -1167,22 +1169,21 @@
     both = second_cross(first)
     mine = [total, first, second]
     spread = [core_cross(value) for value in mine]
+    both_other = core_cross(both_moments)
     both, spread = fence((both, spread))
     spread.append(core_cross(both))
+    moments = moments[:3] + [both_moments, moments[3], first_other, second_other, both_other]
     return mine + [both] + spread, moments, output, grad_input, vectors
 
 
 def on_device_rows(tokens, segment_ids, cotangent, params, moment_one, moment_two):
     shard = lax.axis_index("z")
     rep = lax.axis_index(PLANE)
-    early = prepare(tokens, cotangent, segment_ids)
-    blocks, own, ids, hops, early, moments = gather_matrices(
-        params, shard, rep, early, moment_one, moment_two
-    )
-    normed, inv_std, grad_y, tables = early
+    early = (prepare(tokens, cotangent, segment_ids), align_moments(moment_one, moment_two, rep))
+    blocks, own, ids, hops, early = gather_matrices(params, shard, rep, early)
+    (normed, inv_std, grad_y, tables), moments = early
     moments, blocks = fence((moments, blocks))
-    moments += [second_cross(value) for value in moments]
-    moments += [core_cross(value) for value in moments[:2]]
+    moments = [moments, first_cross(moments), second_cross(moments), core_cross(moments)]
     scalars = jnp.stack([shard] + ids + slots_by_piece(shard, rep))
     made = layer_gradients(scalars, blocks, own, (normed, grad_y, tables, *hops))
     made, moments = fence((made, moments))

time: 239 us -> 239 us (level)
    ppermute x48, waiting for transfers between devices: 66.1 us -> 76 us  [plane_permute(): lax.ppermute(value, PLANE, [(i, i ^ flips[i % 2]) for i in range(REPS)])]
    ppermute x3, waiting for transfers between devices: 9.9 us -> 4.44 us  [ring_shift(): lax.ppermute(value, 'z', [(i, (i + hop) % SHARDS) for i in range(SHARDS)])]
    ppermute x9, waiting for transfers between devices: 37.7 us -> 32.7 us  [ring_step(): lax.ppermute(value, 'z', [(i, (i + 1) % SHARDS) for i in range(SHARDS)])]
    ppermute x48, starting transfers between devices: 31.3 us -> 28.5 us  [plane_permute(): lax.ppermute(value, PLANE, [(i, i ^ flips[i % 2]) for i in range(REPS)])]
    unnamed x84 -> x92, local copies, waits for them, and re-layouts: 6.59 us -> 7.21 us
  transfers between devices with their start and end apart: 60 -> 60, of which waited for: 31 -> 29; matrix products, arithmetic and copies ran while one was open for 4% -> 5% of each run, Pallas kernels for 19% -> 19%
where the time goes in v11:
time: 239 us; the launch traced here: 238 us
  waiting for transfers between devices  113 us (47%)
  Pallas kernels  64.1 us (27%)
  starting transfers between devices  35 us (15%)
  other arithmetic  14.8 us (6%)
  local copies, waits for them, and re-layouts  9.88 us (4%)
    ppermute x48, waiting for transfers between devices, plane_permute(): lax.ppermute(value, PLANE, [(i, i ^ flips[i % 2]) for i in range(REPS)])  76 us
    ppermute x9, waiting for transfers between devices, ring_step(): lax.ppermute(value, 'z', [(i, (i + 1) % SHARDS) for i in range(SHARDS)])  32.7 us
    ppermute x48, starting transfers between devices, plane_permute(): lax.ppermute(value, PLANE, [(i, i ^ flips[i % 2]) for i in range(REPS)])  28.5 us
    pallas_call x1, Pallas kernels, layer_gradients(): pl.pallas_call(layer_kernel, grid_spec=pltpu.PrefetchScalarGridSpec(num_s...  24.5 us
    pallas_call x1, Pallas kernels, update_shard(): pl.pallas_call(functools.partial(update_kernel, factor), grid_spec=pltpu....  15.3 us
    pallas_call x1, Pallas kernels, layer_results(): pl.pallas_call(result_kernel, grid_spec=pltpu.PrefetchScalarGridSpec(num_...  11.9 us
    pallas_call x2, Pallas kernels, pack_pieces(): pl.pallas_call(pack_kernel, grid_spec=pltpu.PrefetchScalarGridSpec(num_sc...  11.7 us
    unnamed x92, local copies, waits for them, and re-layouts  7.21 us
  transfers between devices with their start and end apart: 60, of which 29 were waited for; matrix products, arithmetic and copies ran while one was open for 5% of the time, Pallas kernels for 19%

profile of v11, /device:TPU:0, one launch (start us, length us, event | category | flops | bytes accessed | tf_op | source)
XLA Modules:
  0.0 238.2 jit_solution(5304391608295397172)
XLA Ops:
  1.2 2.8 %shard_map.109 = bf16[1,288,768]{2,1,0:T(8,128)(2,1)} custom-call(s32[2]{0:T(128)} %pad_add_fusion.where, f32[13848,128]{1,0:T(8,128)} %bitcast.132), custom_call_target="tpu_custom_call" | custom-call | bytes 3145728 | tf_op jit(solution)/shard_map/pallas_call | solution.py:522
  4.0 3.1 %collective-permute-start = (bf16[288,768]{1,0:T(8,128)(2,1)}, bf16[288,768]{1,0:T(8,128)(2,1)S(1)}, u32[]{:S(2)}, u32[]{:S(2)}) collective-permute-start(bf16[288,768]{1,0:T(8,128)(2,1)} %bitcast.153), channel_id=1, source_target_pairs={{0,1},{1,2},{2,3},{3,0},{4,5},{5,6},{6,7},{7,4},{8,9},{9,10},{10,1... | collective-permute-start | bytes 1327112 | tf_op jit(solution)/shard_map/ppermute | solution.py:425
  7.7 8.9 %shard_map.110 = (bf16[8,288,768]{2,1,0:T(8,128)(2,1)}, f32[8,768]{1,0:T(8,128)}) custom-call(s32[9]{0:T(128)} %stack.302.where, f32[13848,128]{1,0:T(8,128)} %bitcast.133), custom_call_target="tpu_custom_call" | custom-call | bytes 25165824 | tf_op jit(solution)/shard_map/pallas_call | solution.py:522
  16.7 2.8 %collective-permute-done = bf16[288,768]{1,0:T(8,128)(2,1)S(1)} collective-permute-done((bf16[288,768]{1,0:T(8,128)(2,1)}, bf16[288,768]{1,0:T(8,128)(2,1)S(1)}, u32[]{:S(2)}, u32[]{:S(2)}) %collective-permute-start) | collective-permute-done | bytes 442400 | tf_op jit(solution)/shard_map/ppermute | solution.py:425
  19.5 1.5 collective-permute-start.3
  27.3 8.1 %collective-permute-done.4.refs_17_ = f32[8,768]{1,0:T(8,128)S(1)} collective-permute-done((f32[8,768]{1,0:T(8,128)}, f32[8,768]{1,0:T(8,128)S(1)}, u32[]{:S(2)}, u32[]{:S(2)}) %collective-permute-start.4) | collective-permute-done | bytes 24608 | tf_op jit(solution)/shard_map/ppermute | solution.py:425
  38.0 11.1 %collective-permute-done.9.refs_18_ = f32[8,768]{1,0:T(8,128)S(1)} collective-permute-done((f32[8,768]{1,0:T(8,128)S(1)}, f32[8,768]{1,0:T(8,128)S(1)}, u32[]{:S(2)}, u32[]{:S(2)}) %collective-permute-start.9) | collective-permute-done | bytes 24608 | tf_op jit(solution)/shard_map/ppermute | solution.py:425
  49.1 2.2 collective-permute-done.7
  53.4 1.5 collective-permute-start.11
  55.4 5.6 %collective-permute-done.14.refs_19_ = f32[8,768]{1,0:T(8,128)S(1)} collective-permute-done((f32[8,768]{1,0:T(8,128)S(1)}, f32[8,768]{1,0:T(8,128)S(1)}, u32[]{:S(2)}, u32[]{:S(2)}) %collective-permute-start.14) | collective-permute-done | bytes 24608 | tf_op jit(solution)/shard_map/ppermute | solution.py:425
  61.1 3.9 %collective-permute-done.12 = bf16[288,768]{1,0:T(8,128)(2,1)S(1)} collective-permute-done((bf16[288,768]{1,0:T(8,128)(2,1)S(1)}, bf16[288,768]{1,0:T(8,128)(2,1)S(1)}, u32[]{:S(2)}, u32[]{:S(2)}) %collective-permute-start.12) | collective-permute-done | bytes 442400 | tf_op jit(solution)/shard_map/ppermute | solution.py:409
  65.0 5.7 %collective-permute-done.11.refs_6_ = bf16[288,768]{1,0:T(8,128)(2,1)S(1)} collective-permute-done((bf16[288,768]{1,0:T(8,128)(2,1)S(1)}, bf16[288,768]{1,0:T(8,128)(2,1)S(1)}, u32[]{:S(2)}, u32[]{:S(2)}) %collective-permute-start.11) | collective-permute-done | bytes 442400 | tf_op jit(solution)/shard_map/ppermute | solution.py:409
  74.4 2.1 collective-permute-done.15.refs_8_
  77.2 5.1 %collective-permute-done.18.refs_7_ = bf16[288,768]{1,0:T(8,128)(2,1)} collective-permute-done((bf16[288,768]{1,0:T(8,128)(2,1)S(1)}, bf16[288,768]{1,0:T(8,128)(2,1)}, u32[]{:S(2)}, u32[]{:S(2)}) %collective-permute-start.18) | collective-permute-done | bytes 442400 | tf_op jit(solution)/shard_map/ppermute | solution.py:409
  88.0 24.5 %shard_map.113 = (bf16[576,768]{1,0:T(8,128)(2,1)}, bf16[576,768]{1,0:T(8,128)(2,1)}, bf16[576,768]{1,0:T(8,128)(2,1)}, bf16[576,768]{1,0:T(8,128)(2,1)}, bf16[5...) custom-call(s32[57]{0:T(128)} %stack.299.where, ...), custom_call_target="tpu_custom_call" | custom-call | flops 20000000000 | bytes 83886080 | tf_op jit(solution)/shard_map/pallas_call | solution.py:795
  113.9 1.5 collective-permute-done.24
  123.1 9.5 %collective-permute-done.27 = bf16[2,288,768]{2,1,0:T(8,128)(2,1)S(1)} collective-permute-done((bf16[2,288,768]{2,1,0:T(8,128)(2,1)S(1)}, bf16[2,288,768]{2,1,0:T(8,128)(2,1)S(1)}, u32[]{:S(2)}, u32[]{:S(2)}) %collective-permute-start.27) | collective-permute-done | bytes 884768 | tf_op jit(solution)/shard_map/ppermute | solution.py:409
  136.5 11.9 %shard_map.114 = (f32[128,768]{1,0:T(8,128)}, f32[128,768]{1,0:T(8,128)}, f32[16,768]{1,0:T(8,128)}) custom-call(s32[57]{0:T(128)} %stack.299.where, bf16[4,288,768]{2,1,0:T(8,128)(2,1)} %copy-done.10, bf16[4,288,768]{2,1,0:T(8,128)(2,1)} %copy-done.12, bf16[4,288,768]{2,1,0:T(8,128)(2,1)} %copy-done.11, bf16[4,288,768]{2,1,0:T(8,128)(2,1)} %copy-done.13, ...), custom_call_target="tpu_custom_call" | custom-call | flops 4000000000 | bytes 31457280 | tf_op jit(solution)/shard_map/pallas_call | solution.py:878
  148.5 1.7 add_add_fusion
  154.3 5.4 %collective-permute-done.36 = bf16[2,288,768]{2,1,0:T(8,128)(2,1)} collective-permute-done((bf16[2,288,768]{2,1,0:T(8,128)(2,1)}, bf16[2,288,768]{2,1,0:T(8,128)(2,1)}, u32[]{:S(2)}, u32[]{:S(2)}) %collective-permute-start.36) | collective-permute-done | bytes 884768 | tf_op jit(solution)/shard_map/ppermute | solution.py:409
  159.7 4.1 %collective-permute-done.35 = bf16[288,768]{1,0:T(8,128)(2,1)S(1)} collective-permute-done((bf16[288,768]{1,0:T(8,128)(2,1)S(1)}, bf16[288,768]{1,0:T(8,128)(2,1)S(1)}, u32[]{:S(2)}, u32[]{:S(2)}) %collective-permute-start.35) | collective-permute-done | bytes 442400 | tf_op jit(solution)/shard_map/ppermute | solution.py:409
  168.2 5.8 %collective-permute-done.40 = bf16[2,288,768]{2,1,0:T(8,128)(2,1)S(1)} collective-permute-done((bf16[2,288,768]{2,1,0:T(8,128)(2,1)S(1)}, bf16[2,288,768]{2,1,0:T(8,128)(2,1)S(1)}, u32[]{:S(2)}, u32[]{:S(2)}) %collective-permute-start.40) | collective-permute-done | bytes 884768 | tf_op jit(solution)/shard_map/ppermute | solution.py:409
  175.1 3.9 %collective-permute-done.41 = bf16[288,768]{1,0:T(8,128)(2,1)S(1)} collective-permute-done((bf16[288,768]{1,0:T(8,128)(2,1)S(1)}, bf16[288,768]{1,0:T(8,128)(2,1)S(1)}, u32[]{:S(2)}, u32[]{:S(2)}) %collective-permute-start.41) | collective-permute-done | bytes 442400 | tf_op jit(solution)/shard_map/ppermute | solution.py:425
  180.8 1.6 collective-permute-start.44
  183.1 15.1 %collective-permute-done.46 = f32[16,768]{1,0:T(8,128)S(1)} collective-permute-done((f32[16,768]{1,0:T(8,128)S(1)}, f32[16,768]{1,0:T(8,128)S(1)}, u32[]{:S(2)}, u32[]{:S(2)}) %collective-permute-start.46) | collective-permute-done | bytes 49184 | tf_op jit(solution)/shard_map/ppermute | solution.py:409
  199.9 1.9 collective-permute-start.51
  201.8 3.1 %collective-permute-done.53 = f32[16,768]{1,0:T(8,128)S(1)} collective-permute-done((f32[16,768]{1,0:T(8,128)S(1)}, f32[16,768]{1,0:T(8,128)S(1)}, u32[]{:S(2)}, u32[]{:S(2)}) %collective-permute-start.53) | collective-permute-done | bytes 49184 | tf_op jit(solution)/shard_map/ppermute | solution.py:1051
  206.8 2.2 collective-permute-done.50.refs_2_
  209.5 1.7 collective-permute-start.54
  211.4 6.5 %collective-permute-done.54.refs_3_ = bf16[288,768]{1,0:T(8,128)(2,1)} collective-permute-done((bf16[288,768]{1,0:T(8,128)(2,1)S(1)}, bf16[288,768]{1,0:T(8,128)(2,1)}, u32[]{:S(2)}, u32[]{:S(2)}) %collective-permute-start.54) | collective-permute-done | bytes 442400 | tf_op jit(solution)/shard_map/ppermute | solution.py:409
  220.2 15.3 %shard_map.115 = (f32[13848,128]{1,0:T(8,128)}, f32[13848,128]{1,0:T(8,128)}) custom-call(s32[9]{0:T(128)} %stack.320.where, bf16[288,768]{1,0:T(8,128)(2,1)} %copy-done.14, bf16[288,768]{1,0:T(8,128)(2,1)} %copy-done.38, bf16[288,768]{1,0:T(8,128)(2,1)} %copy-done.37, bf16[288,768]{1,0:T(8,128)(2,1)} %collective-permute-done.54.refs_3_, ...), custom_call_target="tpu_custom_call" | custom-call | tf_op jit(solution)/shard_map/pallas_call | solution.py:1029
  235.4 2.8 %fusion = (f32[221568]{0:T(1024)}, f32[221568]{0:T(1024)}) fusion(f32[221568]{0:T(1024)S(1)} %copy-done.2, f32[1772544]{0:T(1024)} %bitcast.154, s32[]{:T(128)S(6)} %select_n.334, f32[221568]{0:T(1024)S(1)} %copy-done.1), kind=kLoop, calls=%fused_computation.3 | loop fusion | flops 1550976 | bytes 4431364 | tf_op jit(solution)/shard_map/add | solution.py:352
  (217 shorter events, 53.8 us)
Async XLA Ops:
  4.0 15.5 %collective-permute-start = (bf16[288,768]{1,0:T(8,128)(2,1)}, bf16[288,768]{1,0:T(8,128)(2,1)S(1)}, u32[]{:S(2)}, u32[]{:S(2)}) collective-permute-start(bf16[288,768]{1,0:T(8,128)(2,1)} %bitcast.153), channel_id=1, source_target_pairs={{0,1},{1,2},{2,3},{3,0},{4,5},{5,6},{6,7},{7,4},{8,9},{9,10},{10,1... | collective-permute-start | bytes 1327112 | tf_op jit(solution)/shard_map/ppermute | solution.py:425
  19.5 15.9 %collective-permute-start.3 = (bf16[288,768]{1,0:T(8,128)(2,1)S(1)}, bf16[288,768]{1,0:T(8,128)(2,1)S(1)}, u32[]{:S(2)}, u32[]{:S(2)}) collective-permute-start(bf16[288,768]{1,0:T(8,128)(2,1)S(1)} %collective-permute-done), channel_id=1, source_target_pairs={{0,16},{4,12},{8,24},{12,4},{16,0},{20,28},{24,8},{28,20},{1,17},{... | collective-permute-start | bytes 1327112 | tf_op jit(solution)/shard_map/ppermute | solution.py:409
  21.0 14.4 %collective-permute-start.2 = (bf16[288,768]{1,0:T(8,128)(2,1)S(1)}, bf16[288,768]{1,0:T(8,128)(2,1)S(1)}, u32[]{:S(2)}, u32[]{:S(2)}) collective-permute-start(bf16[288,768]{1,0:T(8,128)(2,1)S(1)} %collective-permute-done), channel_id=1, source_target_pairs={{0,8},{4,20},{8,0},{12,28},{16,24},{20,4},{24,16},{28,12},{1,9},{5... | collective-permute-start | bytes 1327112 | tf_op jit(solution)/shard_map/ppermute | solution.py:409
  22.5 12.9 %collective-permute-start.1 = (bf16[288,768]{1,0:T(8,128)(2,1)S(1)}, bf16[288,768]{1,0:T(8,128)(2,1)S(1)}, u32[]{:S(2)}, u32[]{:S(2)}) collective-permute-start(bf16[288,768]{1,0:T(8,128)(2,1)S(1)} %collective-permute-done), channel_id=1, source_target_pairs={{0,1},{1,2},{2,3},{3,0},{4,5},{5,6},{6,7},{7,4},{8,9},{9,10},{10,1... | collective-permute-start | bytes 1327112 | tf_op jit(solution)/shard_map/ppermute | solution.py:425
  22.5 12.9 %collective-permute-start.4 = (f32[8,768]{1,0:T(8,128)}, f32[8,768]{1,0:T(8,128)S(1)}, u32[]{:S(2)}, u32[]{:S(2)}) collective-permute-start(f32[8,768]{1,0:T(8,128)} %get-tuple-element.160.refs_16_), channel_id=1, source_target_pairs={{0,1},{1,2},{2,3},{3,0},{4,5},{5,6},{6,7},{7,4},{8,9},{9,10},{10,1... | collective-permute-start | bytes 73736 | tf_op jit(solution)/shard_map/ppermute | solution.py:425
  35.4 13.7 %collective-permute-start.8 = (bf16[288,768]{1,0:T(8,128)(2,1)S(1)}, bf16[288,768]{1,0:T(8,128)(2,1)S(1)}, u32[]{:S(2)}, u32[]{:S(2)}) collective-permute-start(bf16[288,768]{1,0:T(8,128)(2,1)S(1)} %collective-permute-done.2), channel_id=1, source_target_pairs={{0,16},{4,12},{8,24},{12,4},{16,0},{20,28},{24,8},{28,20},{1,17},{... | collective-permute-start | bytes 1327112 | tf_op jit(solution)/shard_map/ppermute | solution.py:409
  36.0 15.3 %collective-permute-start.7 = (bf16[288,768]{1,0:T(8,128)(2,1)S(1)}, bf16[288,768]{1,0:T(8,128)(2,1)S(1)}, u32[]{:S(2)}, u32[]{:S(2)}) collective-permute-start(bf16[288,768]{1,0:T(8,128)(2,1)S(1)} %collective-permute-done.1), channel_id=1, source_target_pairs={{0,16},{4,12},{8,24},{12,4},{16,0},{20,28},{24,8},{28,20},{1,17},{... | collective-permute-start | bytes 1327112 | tf_op jit(solution)/shard_map/ppermute | solution.py:409
  37.5 13.8 %collective-permute-start.6 = (bf16[288,768]{1,0:T(8,128)(2,1)S(1)}, bf16[288,768]{1,0:T(8,128)(2,1)S(1)}, u32[]{:S(2)}, u32[]{:S(2)}) collective-permute-start(bf16[288,768]{1,0:T(8,128)(2,1)S(1)} %collective-permute-done.1), channel_id=1, source_target_pairs={{0,8},{4,20},{8,0},{12,28},{16,24},{20,4},{24,16},{28,12},{1,9},{5... | collective-permute-start | bytes 1327112 | tf_op jit(solution)/shard_map/ppermute | solution.py:409
  38.0 13.3 %collective-permute-start.5 = (bf16[288,768]{1,0:T(8,128)(2,1)S(1)}, bf16[288,768]{1,0:T(8,128)(2,1)S(1)}, u32[]{:S(2)}, u32[]{:S(2)}) collective-permute-start(bf16[288,768]{1,0:T(8,128)(2,1)S(1)} %collective-permute-done.1), channel_id=1, source_target_pairs={{0,1},{1,2},{2,3},{3,0},{4,5},{5,6},{6,7},{7,4},{8,9},{9,10},{10,1... | collective-permute-start | bytes 1327112 | tf_op jit(solution)/shard_map/ppermute | solution.py:425
  52.7 17.9 %collective-permute-start.13 = (bf16[4,288,768]{2,1,0:T(8,128)(2,1)S(1)}, bf16[4,288,768]{2,1,0:T(8,128)(2,1)S(1)}, u32[]{:S(2)}, u32[]{:S(2)}) collective-permute-start(bf16[4,288,768]{2,1,0:T(8,128)(2,1)S(1)} %pad_maximum_fusion.refs_0_), channel_id=1, source_target_pairs={{0,4},{4,0},{8,12},{12,8},{16,20},{20,16},{24,28},{28,24},{1,5},{5... | collective-permute-start | bytes 5308424 | tf_op jit(solution)/shard_map/ppermute | solution.py:409
  52.8 12.2 %collective-permute-start.12 = (bf16[288,768]{1,0:T(8,128)(2,1)S(1)}, bf16[288,768]{1,0:T(8,128)(2,1)S(1)}, u32[]{:S(2)}, u32[]{:S(2)}) collective-permute-start(bf16[288,768]{1,0:T(8,128)(2,1)S(1)} %collective-permute-done.6), channel_id=1, source_target_pairs={{0,16},{4,12},{8,24},{12,4},{16,0},{20,28},{24,8},{28,20},{1,17},{... | collective-permute-start | bytes 1327112 | tf_op jit(solution)/shard_map/ppermute | solution.py:409
  53.4 17.3 %collective-permute-start.11 = (bf16[288,768]{1,0:T(8,128)(2,1)S(1)}, bf16[288,768]{1,0:T(8,128)(2,1)S(1)}, u32[]{:S(2)}, u32[]{:S(2)}) collective-permute-start(bf16[288,768]{1,0:T(8,128)(2,1)S(1)} %collective-permute-done.5.refs_4_), channel_id=1, source_target_pairs={{0,16},{4,12},{8,24},{12,4},{16,0},{20,28},{24,8},{28,20},{1,17},{... | collective-permute-start | bytes 1327112 | tf_op jit(solution)/shard_map/ppermute | solution.py:409
  54.9 15.7 %collective-permute-start.10 = (bf16[288,768]{1,0:T(8,128)(2,1)S(1)}, bf16[288,768]{1,0:T(8,128)(2,1)S(1)}, u32[]{:S(2)}, u32[]{:S(2)}) collective-permute-start(bf16[288,768]{1,0:T(8,128)(2,1)S(1)} %collective-permute-done.5.refs_4_), channel_id=1, source_target_pairs={{0,8},{4,20},{8,0},{12,28},{16,24},{20,4},{24,16},{28,12},{1,9},{5... | collective-permute-start | bytes 1327112 | tf_op jit(solution)/shard_map/ppermute | solution.py:409
  86.3 26.2 %collective-permute-start.23 = (bf16[2,1760,128]{2,1,0:T(8,128)(2,1)S(1)}, bf16[2,1760,128]{2,1,0:T(8,128)(2,1)}, u32[]{:S(2)}, u32[]{:S(2)}) collective-permute-start(bf16[2,1760,128]{2,1,0:T(8,128)(2,1)S(1)} %shard_map.112.refs_8_), channel_id=1, source_target_pairs={{0,4},{4,0},{8,12},{12,8},{16,20},{20,16},{24,28},{28,24},{1,5},{5... | collective-permute-start | bytes 2703368 | tf_op jit(solution)/shard_map/ppermute | solution.py:409
  86.5 26.1 %collective-permute-start.22 = (bf16[2,1760,128]{2,1,0:T(8,128)(2,1)S(1)}, bf16[2,1760,128]{2,1,0:T(8,128)(2,1)}, u32[]{:S(2)}, u32[]{:S(2)}) collective-permute-start(bf16[2,1760,128]{2,1,0:T(8,128)(2,1)S(1)} %shard_map.112.refs_8_), channel_id=1, source_target_pairs={{0,16},{4,12},{8,24},{12,4},{16,0},{20,28},{24,8},{28,20},{1,17},{... | collective-permute-start | bytes 2703368 | tf_op jit(solution)/shard_map/ppermute | solution.py:409
  87.0 25.6 %collective-permute-start.21 = (bf16[2,1760,128]{2,1,0:T(8,128)(2,1)S(1)}, bf16[2,1760,128]{2,1,0:T(8,128)(2,1)}, u32[]{:S(2)}, u32[]{:S(2)}) collective-permute-start(bf16[2,1760,128]{2,1,0:T(8,128)(2,1)S(1)} %shard_map.112.refs_8_), channel_id=1, source_target_pairs={{0,8},{4,20},{8,0},{12,28},{16,24},{20,4},{24,16},{28,12},{1,9},{5... | collective-permute-start | bytes 2703368 | tf_op jit(solution)/shard_map/ppermute | solution.py:409
  119.4 13.1 %collective-permute-start.27 = (bf16[2,288,768]{2,1,0:T(8,128)(2,1)S(1)}, bf16[2,288,768]{2,1,0:T(8,128)(2,1)S(1)}, u32[]{:S(2)}, u32[]{:S(2)}) collective-permute-start(bf16[2,288,768]{2,1,0:T(8,128)(2,1)S(1)} %add.607), channel_id=1, source_target_pairs={{0,8},{4,20},{8,0},{12,28},{16,24},{20,4},{24,16},{28,12},{1,9},{5... | collective-permute-start | bytes 2654216 | tf_op jit(solution)/shard_map/ppermute | solution.py:409
  121.6 26.8 %collective-permute-start.34 = (bf16[2,288,768]{2,1,0:T(8,128)(2,1)}, bf16[2,288,768]{2,1,0:T(8,128)(2,1)}, u32[]{:S(2)}, u32[]{:S(2)}) collective-permute-start(bf16[2,288,768]{2,1,0:T(8,128)(2,1)} %bitcast.91), channel_id=1, source_target_pairs={{0,4},{4,0},{8,12},{12,8},{16,20},{20,16},{24,28},{28,24},{1,5},{5... | collective-permute-start | bytes 2654216 | tf_op jit(solution)/shard_map/ppermute | solution.py:409
  121.7 26.8 %collective-permute-start.33 = (bf16[2,288,768]{2,1,0:T(8,128)(2,1)}, bf16[2,288,768]{2,1,0:T(8,128)(2,1)}, u32[]{:S(2)}, u32[]{:S(2)}) collective-permute-start(bf16[2,288,768]{2,1,0:T(8,128)(2,1)} %add.610), channel_id=1, source_target_pairs={{0,8},{4,20},{8,0},{12,28},{16,24},{20,4},{24,16},{28,12},{1,9},{5... | collective-permute-start | bytes 2654216 | tf_op jit(solution)/shard_map/ppermute | solution.py:409
  132.7 15.7 %collective-permute-start.32 = (bf16[288,768]{1,0:T(8,128)(2,1)S(1)}, bf16[288,768]{1,0:T(8,128)(2,1)}, u32[]{:S(2)}, u32[]{:S(2)}) collective-permute-start(bf16[288,768]{1,0:T(8,128)(2,1)S(1)} %slice_bitcast_fusion.7), channel_id=1, source_target_pairs={{0,16},{4,12},{8,24},{12,4},{16,0},{20,28},{24,8},{28,20},{1,17},{... | collective-permute-start | bytes 1327112 | tf_op jit(solution)/shard_map/ppermute | solution.py:409
  135.0 24.7 %collective-permute-start.36 = (bf16[2,288,768]{2,1,0:T(8,128)(2,1)}, bf16[2,288,768]{2,1,0:T(8,128)(2,1)}, u32[]{:S(2)}, u32[]{:S(2)}) collective-permute-start(bf16[2,288,768]{2,1,0:T(8,128)(2,1)} %add.615), channel_id=1, source_target_pairs={{0,8},{4,20},{8,0},{12,28},{16,24},{20,4},{24,16},{28,12},{1,9},{5... | collective-permute-start | bytes 2654216 | tf_op jit(solution)/shard_map/ppermute | solution.py:409
  151.5 12.3 %collective-permute-start.35 = (bf16[288,768]{1,0:T(8,128)(2,1)S(1)}, bf16[288,768]{1,0:T(8,128)(2,1)S(1)}, u32[]{:S(2)}, u32[]{:S(2)}) collective-permute-start(bf16[288,768]{1,0:T(8,128)(2,1)S(1)} %slice_bitcast_fusion.6), channel_id=1, source_target_pairs={{0,16},{4,12},{8,24},{12,4},{16,0},{20,28},{24,8},{28,20},{1,17},{... | collective-permute-start | bytes 1327112 | tf_op jit(solution)/shard_map/ppermute | solution.py:409
  152.4 12.6 %collective-permute-start.37 = (bf16[288,768]{1,0:T(8,128)(2,1)S(1)}, bf16[288,768]{1,0:T(8,128)(2,1)S(1)}, u32[]{:S(2)}, u32[]{:S(2)}) collective-permute-start(bf16[288,768]{1,0:T(8,128)(2,1)S(1)} %fusion.7), channel_id=1, source_target_pairs={{0,1},{1,2},{2,3},{3,0},{4,5},{5,6},{6,7},{7,4},{8,9},{9,10},{10,1... | collective-permute-start | bytes 1327112 | tf_op jit(solution)/shard_map/ppermute | solution.py:425
  152.5 15.7 %collective-permute-start.43 = (bf16[2,1760,128]{2,1,0:T(8,128)(2,1)}, bf16[2,1760,128]{2,1,0:T(8,128)(2,1)S(1)}, u32[]{:S(2)}, u32[]{:S(2)}) collective-permute-start(bf16[2,1760,128]{2,1,0:T(8,128)(2,1)} %collective-permute-done.21.refs_9_), channel_id=1, source_target_pairs={{0,4},{4,0},{8,12},{12,8},{16,20},{20,16},{24,28},{28,24},{1,5},{5... | collective-permute-start | bytes 2703368 | tf_op jit(solution)/shard_map/ppermute | solution.py:409
  153.7 20.3 %collective-permute-start.40 = (bf16[2,288,768]{2,1,0:T(8,128)(2,1)S(1)}, bf16[2,288,768]{2,1,0:T(8,128)(2,1)S(1)}, u32[]{:S(2)}, u32[]{:S(2)}) collective-permute-start(bf16[2,288,768]{2,1,0:T(8,128)(2,1)S(1)} %add.618), channel_id=1, source_target_pairs={{0,8},{4,20},{8,0},{12,28},{16,24},{20,4},{24,16},{28,12},{1,9},{5... | collective-permute-start | bytes 2654216 | tf_op jit(solution)/shard_map/ppermute | solution.py:409
  167.1 11.9 %collective-permute-start.41 = (bf16[288,768]{1,0:T(8,128)(2,1)S(1)}, bf16[288,768]{1,0:T(8,128)(2,1)S(1)}, u32[]{:S(2)}, u32[]{:S(2)}) collective-permute-start(bf16[288,768]{1,0:T(8,128)(2,1)S(1)} %fusion.6), channel_id=1, source_target_pairs={{0,1},{1,2},{2,3},{3,0},{4,5},{5,6},{6,7},{7,4},{8,9},{9,10},{10,1... | collective-permute-start | bytes 1327112 | tf_op jit(solution)/shard_map/ppermute | solution.py:425
  179.0 19.2 %collective-permute-start.47 = (bf16[2,1760,128]{2,1,0:T(8,128)(2,1)}, bf16[2,1760,128]{2,1,0:T(8,128)(2,1)}, u32[]{:S(2)}, u32[]{:S(2)}) collective-permute-start(bf16[2,1760,128]{2,1,0:T(8,128)(2,1)} %collective-permute-done.21.refs_9_), channel_id=1, source_target_pairs={{0,16},{4,12},{8,24},{12,4},{16,0},{20,28},{24,8},{28,20},{1,17},{... | collective-permute-start | bytes 2703368 | tf_op jit(solution)/shard_map/ppermute | solution.py:409
  179.5 18.8 %collective-permute-start.48 = (bf16[2,1760,128]{2,1,0:T(8,128)(2,1)}, bf16[2,1760,128]{2,1,0:T(8,128)(2,1)S(1)}, u32[]{:S(2)}, u32[]{:S(2)}) collective-permute-start(bf16[2,1760,128]{2,1,0:T(8,128)(2,1)} %collective-permute-done.22.refs_10_), channel_id=1, source_target_pairs={{0,4},{4,0},{8,12},{12,8},{16,20},{20,16},{24,28},{28,24},{1,5},{5... | collective-permute-start | bytes 2703368 | tf_op jit(solution)/shard_map/ppermute | solution.py:409
  180.8 17.4 %collective-permute-start.44 = (bf16[288,768]{1,0:T(8,128)(2,1)S(1)}, bf16[288,768]{1,0:T(8,128)(2,1)S(1)}, u32[]{:S(2)}, u32[]{:S(2)}) collective-permute-start(bf16[288,768]{1,0:T(8,128)(2,1)S(1)} %slice_bitcast_fusion.1), channel_id=1, source_target_pairs={{0,16},{4,12},{8,24},{12,4},{16,0},{20,28},{24,8},{28,20},{1,17},{... | collective-permute-start | bytes 1327112 | tf_op jit(solution)/shard_map/ppermute | solution.py:409
  182.5 15.7 %collective-permute-start.45 = (bf16[288,768]{1,0:T(8,128)(2,1)S(1)}, bf16[288,768]{1,0:T(8,128)(2,1)S(1)}, u32[]{:S(2)}, u32[]{:S(2)}) collective-permute-start(bf16[288,768]{1,0:T(8,128)(2,1)S(1)} %fusion.2), channel_id=1, source_target_pairs={{0,1},{1,2},{2,3},{3,0},{4,5},{5,6},{6,7},{7,4},{8,9},{9,10},{10,1... | collective-permute-start | bytes 1327112 | tf_op jit(solution)/shard_map/ppermute | solution.py:425
  182.6 15.6 %collective-permute-start.46 = (f32[16,768]{1,0:T(8,128)S(1)}, f32[16,768]{1,0:T(8,128)S(1)}, u32[]{:S(2)}, u32[]{:S(2)}) collective-permute-start(f32[16,768]{1,0:T(8,128)S(1)} %add.625), channel_id=1, source_target_pairs={{0,16},{4,20},{8,24},{12,28},{16,0},{20,4},{24,8},{28,12},{1,17},{... | collective-permute-start | bytes 147464 | tf_op jit(solution)/shard_map/ppermute | solution.py:409
  204.9 14.4 %collective-permute-start.59 = (bf16[2,1760,128]{2,1,0:T(8,128)(2,1)}, bf16[2,1760,128]{2,1,0:T(8,128)(2,1)}, u32[]{:S(2)}, u32[]{:S(2)}) collective-permute-start(bf16[2,1760,128]{2,1,0:T(8,128)(2,1)} %collective-permute-done.47.refs_11_), channel_id=1, source_target_pairs={{0,4},{4,0},{8,12},{12,8},{16,20},{20,16},{24,28},{28,24},{1,5},{5... | collective-permute-start | bytes 2703368 | tf_op jit(solution)/shard_map/ppermute | solution.py:409
  (74 other events, 646.4 us)

commit v12 on v10

--- a/solution.py
+++ b/solution.py
@@ -1054,14 +1054,11 @@
 fence = lax.optimization_barrier
 
 
-def gather_matrices(params, shard, rep, early, moment_one, moment_two):
+def gather_matrices(params, shard, rep, early):
     piece = pack_pieces(params, shard, [rep], False)[0][0]
     own, vec = pack_pieces(params, shard, [rep * 0 + turn for turn in range(REPS)], True)
     one = ring_step(piece)
-    _, moment_one, moment_two = fence((piece, moment_one, moment_two))
-    moments = align_moments(moment_one, moment_two, rep)
-    first_moments = first_cross(moments)
-    one, own, vec, first_moments = fence((one, own, vec, first_moments))
+    one, own, vec = fence((one, own, vec))
     two, first_one, second_one = ring_step(one), first_cross(one), second_cross(one)
     vec_one = ring_step(vec)
     two, first_one, second_one, vec_one, early = fence(
@@ -1078,14 +1075,17 @@
     mine_one = jnp.stack([one, first_one, second_one, both_one])
     other_one = core_cross(mine_one)
     vec_three = ring_step(vec_two)
-    first_three, second_three, both_two, other_one, vec_three = fence(
-        (first_three, second_three, both_two, other_one, vec_three)
-    )
+    first_three, second_three, both_two, other_one, vec_three, moments = fence(
+        (first_three, second_three, both_two, other_one, vec_three, early[1])
+    )
+    first_moments = first_cross(moments)
     both_three = second_cross(first_three)
     mine_two = jnp.stack([two, first_two, second_two, both_two])
     other_two = core_cross(mine_two)
     others = [core_cross(value) for value in (three, first_three, second_three)]
-    others, both_three, other_two = fence((others, both_three, other_two))
+    others, both_three, other_two, first_moments = fence(
+        (others, both_three, other_two, first_moments)
+    )
     others.append(core_cross(both_three))
     threes = [three, first_three, second_three, both_three]
     blocks = [mine_one, other_one, mine_two, other_two] + threes + others
@@ -1094,7 +1094,7 @@
         owner = (shard + SHARDS - hop) % SHARDS
         ids += [owner * REPS + which for which in spread_ids(rep)]
     hops = [vec, vec_one, vec_two, vec_three]
-    return blocks, own.reshape(REPS * PIECE, D), ids, hops, early, [moments, first_moments]
+    return blocks, own.reshape(REPS * PIECE, D), ids, hops, early[0], [moments, first_moments]
 
 
 def slots_by_piece(shard, rep):
@@ -1175,10 +1175,8 @@
 def on_device_rows(tokens, segment_ids, cotangent, params, moment_one, moment_two):
     shard = lax.axis_index("z")
     rep = lax.axis_index(PLANE)
-    early = prepare(tokens, cotangent, segment_ids)
-    blocks, own, ids, hops, early, moments = gather_matrices(
-        params, shard, rep, early, moment_one, moment_two
-    )
+    early = (prepare(tokens, cotangent, segment_ids), align_moments(moment_one, moment_two, rep))
+    blocks, own, ids, hops, early, moments = gather_matrices(params, shard, rep, early)
     normed, inv_std, grad_y, tables = early
     moments, blocks = fence((moments, blocks))
     moments += [second_cross(value) for value in moments]

time: 239 us -> 242 us (1.013)
  waiting for transfers between devices: 114 us -> 118 us
    ppermute x48, waiting for transfers between devices: 66.1 us -> 72.3 us  [plane_permute(): lax.ppermute(value, PLANE, [(i, i ^ flips[i % 2]) for i in range(REPS)])]
    ppermute x48, starting transfers between devices: 31.3 us -> 28.6 us  [plane_permute(): lax.ppermute(value, PLANE, [(i, i ^ flips[i % 2]) for i in range(REPS)])]
    unnamed x84 -> x92, local copies, waits for them, and re-layouts: 6.59 us -> 8.43 us
  transfers between devices with their start and end apart: 60 -> 60, of which waited for: 31 -> 32; matrix products, arithmetic and copies ran while one was open for 4% -> 5% of each run, Pallas kernels for 19% -> 19%
where the time goes in v12:
time: 242 us; the launch traced here: 241 us
  waiting for transfers between devices  118 us (49%)
  Pallas kernels  64.1 us (26%)
  starting transfers between devices  33.2 us (14%)
  other arithmetic  13.8 us (6%)
  local copies, waits for them, and re-layouts  11.2 us (5%)
    ppermute x48, waiting for transfers between devices, plane_permute(): lax.ppermute(value, PLANE, [(i, i ^ flips[i % 2]) for i in range(REPS)])  72.3 us
    ppermute x9, waiting for transfers between devices, ring_step(): lax.ppermute(value, 'z', [(i, (i + 1) % SHARDS) for i in range(SHARDS)])  35.6 us
    ppermute x48, starting transfers between devices, plane_permute(): lax.ppermute(value, PLANE, [(i, i ^ flips[i % 2]) for i in range(REPS)])  28.6 us
    pallas_call x1, Pallas kernels, layer_gradients(): pl.pallas_call(layer_kernel, grid_spec=pltpu.PrefetchScalarGridSpec(num_s...  24.5 us
    pallas_call x1, Pallas kernels, update_shard(): pl.pallas_call(functools.partial(update_kernel, factor), grid_spec=pltpu....  15.3 us
    pallas_call x1, Pallas kernels, layer_results(): pl.pallas_call(result_kernel, grid_spec=pltpu.PrefetchScalarGridSpec(num_...  11.9 us
    pallas_call x2, Pallas kernels, pack_pieces(): pl.pallas_call(pack_kernel, grid_spec=pltpu.PrefetchScalarGridSpec(num_sc...  11.7 us
    ppermute x3, waiting for transfers between devices, ring_shift(): lax.ppermute(value, 'z', [(i, (i + hop) % SHARDS) for i in range(SHARDS)])  9.9 us
  transfers between devices with their start and end apart: 60, of which 32 were waited for; matrix products, arithmetic and copies ran while one was open for 5% of the time, Pallas kernels for 19%

profile of v12, /device:TPU:0, one launch (start us, length us, event | category | flops | bytes accessed | tf_op | source)
XLA Modules:
  0.0 241.3 jit_solution(18256740698646140247)
XLA Ops:
  1.2 2.8 %shard_map.109 = bf16[1,288,768]{2,1,0:T(8,128)(2,1)} custom-call(s32[2]{0:T(128)} %pad_add_fusion.where, f32[13848,128]{1,0:T(8,128)} %bitcast.132), custom_call_target="tpu_custom_call" | custom-call | bytes 3145728 | tf_op jit(solution)/shard_map/pallas_call | solution.py:522
  4.0 3.1 %collective-permute-start = (bf16[288,768]{1,0:T(8,128)(2,1)}, bf16[288,768]{1,0:T(8,128)(2,1)S(1)}, u32[]{:S(2)}, u32[]{:S(2)}) collective-permute-start(bf16[288,768]{1,0:T(8,128)(2,1)} %bitcast.153), channel_id=1, source_target_pairs={{0,1},{1,2},{2,3},{3,0},{4,5},{5,6},{6,7},{7,4},{8,9},{9,10},{10,1... | collective-permute-start | bytes 1327112 | tf_op jit(solution)/shard_map/ppermute | solution.py:425
  7.7 8.9 %shard_map.110 = (bf16[8,288,768]{2,1,0:T(8,128)(2,1)}, f32[8,768]{1,0:T(8,128)}) custom-call(s32[9]{0:T(128)} %stack.302.where, f32[13848,128]{1,0:T(8,128)} %bitcast.133), custom_call_target="tpu_custom_call" | custom-call | bytes 25165824 | tf_op jit(solution)/shard_map/pallas_call | solution.py:522
  16.7 2.8 %collective-permute-done = bf16[288,768]{1,0:T(8,128)(2,1)S(1)} collective-permute-done((bf16[288,768]{1,0:T(8,128)(2,1)}, bf16[288,768]{1,0:T(8,128)(2,1)S(1)}, u32[]{:S(2)}, u32[]{:S(2)}) %collective-permute-start) | collective-permute-done | bytes 442400 | tf_op jit(solution)/shard_map/ppermute | solution.py:425
  19.5 1.5 collective-permute-start.3
  27.3 8.1 %collective-permute-done.4.refs_17_ = f32[8,768]{1,0:T(8,128)S(1)} collective-permute-done((f32[8,768]{1,0:T(8,128)}, f32[8,768]{1,0:T(8,128)S(1)}, u32[]{:S(2)}, u32[]{:S(2)}) %collective-permute-start.4) | collective-permute-done | bytes 24608 | tf_op jit(solution)/shard_map/ppermute | solution.py:425
  36.0 1.5 collective-permute-start.7
  38.0 11.1 %collective-permute-done.9.refs_18_ = f32[8,768]{1,0:T(8,128)S(1)} collective-permute-done((f32[8,768]{1,0:T(8,128)S(1)}, f32[8,768]{1,0:T(8,128)S(1)}, u32[]{:S(2)}, u32[]{:S(2)}) %collective-permute-start.9) | collective-permute-done | bytes 24608 | tf_op jit(solution)/shard_map/ppermute | solution.py:425
  49.1 2.2 collective-permute-done.7
  53.4 1.5 collective-permute-start.11
  55.4 5.6 %collective-permute-done.14.refs_19_ = f32[8,768]{1,0:T(8,128)S(1)} collective-permute-done((f32[8,768]{1,0:T(8,128)S(1)}, f32[8,768]{1,0:T(8,128)S(1)}, u32[]{:S(2)}, u32[]{:S(2)}) %collective-permute-start.14) | collective-permute-done | bytes 24608 | tf_op jit(solution)/shard_map/ppermute | solution.py:425
  61.1 3.9 %collective-permute-done.12 = bf16[288,768]{1,0:T(8,128)(2,1)S(1)} collective-permute-done((bf16[288,768]{1,0:T(8,128)(2,1)S(1)}, bf16[288,768]{1,0:T(8,128)(2,1)S(1)}, u32[]{:S(2)}, u32[]{:S(2)}) %collective-permute-start.12) | collective-permute-done | bytes 442400 | tf_op jit(solution)/shard_map/ppermute | solution.py:409
  65.0 5.7 %collective-permute-done.11.refs_6_ = bf16[288,768]{1,0:T(8,128)(2,1)S(1)} collective-permute-done((bf16[288,768]{1,0:T(8,128)(2,1)S(1)}, bf16[288,768]{1,0:T(8,128)(2,1)S(1)}, u32[]{:S(2)}, u32[]{:S(2)}) %collective-permute-start.11) | collective-permute-done | bytes 442400 | tf_op jit(solution)/shard_map/ppermute | solution.py:409
  74.5 2.1 collective-permute-done.15.refs_8_
  77.2 9.4 %collective-permute-done.18.refs_7_ = bf16[288,768]{1,0:T(8,128)(2,1)} collective-permute-done((bf16[288,768]{1,0:T(8,128)(2,1)S(1)}, bf16[288,768]{1,0:T(8,128)(2,1)}, u32[]{:S(2)}, u32[]{:S(2)}) %collective-permute-start.18) | collective-permute-done | bytes 442400 | tf_op jit(solution)/shard_map/ppermute | solution.py:409
  86.6 3.7 %collective-permute-done.20.refs_9_ = bf16[2,1760,128]{2,1,0:T(8,128)(2,1)S(1)} collective-permute-done((bf16[2,1760,128]{2,1,0:T(8,128)(2,1)S(1)}, bf16[2,1760,128]{2,1,0:T(8,128)(2,1)S(1)}, u32[]{:S(2)}, u32[]{:S(2)}) %collective-permute-start.20) | collective-permute-done | bytes 901152 | tf_op jit(solution)/shard_map/ppermute | solution.py:409
  96.8 24.5 %shard_map.113 = (bf16[576,768]{1,0:T(8,128)(2,1)}, bf16[576,768]{1,0:T(8,128)(2,1)}, bf16[576,768]{1,0:T(8,128)(2,1)}, bf16[576,768]{1,0:T(8,128)(2,1)}, bf16[5...) custom-call(s32[57]{0:T(128)} %stack.299.where, ...), custom_call_target="tpu_custom_call" | custom-call | flops 20000000000 | bytes 83886080 | tf_op jit(solution)/shard_map/pallas_call | solution.py:795
  122.6 1.5 collective-permute-done.26
  132.2 8.9 %collective-permute-done.29 = bf16[2,288,768]{2,1,0:T(8,128)(2,1)S(1)} collective-permute-done((bf16[2,288,768]{2,1,0:T(8,128)(2,1)S(1)}, bf16[2,288,768]{2,1,0:T(8,128)(2,1)S(1)}, u32[]{:S(2)}, u32[]{:S(2)}) %collective-permute-start.29) | collective-permute-done | bytes 884768 | tf_op jit(solution)/shard_map/ppermute | solution.py:409
  144.7 11.9 %shard_map.114 = (f32[128,768]{1,0:T(8,128)}, f32[128,768]{1,0:T(8,128)}, f32[16,768]{1,0:T(8,128)}) custom-call(s32[57]{0:T(128)} %stack.299.where, bf16[4,288,768]{2,1,0:T(8,128)(2,1)} %copy-done.10, bf16[4,288,768]{2,1,0:T(8,128)(2,1)} %copy-done.12, bf16[4,288,768]{2,1,0:T(8,128)(2,1)} %copy-done.11, bf16[4,288,768]{2,1,0:T(8,128)(2,1)} %copy-done.13, ...), custom_call_target="tpu_custom_call" | custom-call | flops 4000000000 | bytes 31457280 | tf_op jit(solution)/shard_map/pallas_call | solution.py:878
  157.6 1.8 add_add_fusion
  163.0 4.7 %collective-permute-done.38 = bf16[2,288,768]{2,1,0:T(8,128)(2,1)} collective-permute-done((bf16[2,288,768]{2,1,0:T(8,128)(2,1)}, bf16[2,288,768]{2,1,0:T(8,128)(2,1)}, u32[]{:S(2)}, u32[]{:S(2)}) %collective-permute-start.38) | collective-permute-done | bytes 884768 | tf_op jit(solution)/shard_map/ppermute | solution.py:409
  167.7 5.4 %collective-permute-done.37 = bf16[288,768]{1,0:T(8,128)(2,1)S(1)} collective-permute-done((bf16[288,768]{1,0:T(8,128)(2,1)S(1)}, bf16[288,768]{1,0:T(8,128)(2,1)S(1)}, u32[]{:S(2)}, u32[]{:S(2)}) %collective-permute-start.37) | collective-permute-done | bytes 442400 | tf_op jit(solution)/shard_map/ppermute | solution.py:409
  177.9 4.2 %collective-permute-done.42 = bf16[2,288,768]{2,1,0:T(8,128)(2,1)S(1)} collective-permute-done((bf16[2,288,768]{2,1,0:T(8,128)(2,1)S(1)}, bf16[2,288,768]{2,1,0:T(8,128)(2,1)S(1)}, u32[]{:S(2)}, u32[]{:S(2)}) %collective-permute-start.42) | collective-permute-done | bytes 884768 | tf_op jit(solution)/shard_map/ppermute | solution.py:409
  184.0 4.1 %collective-permute-done.43 = bf16[288,768]{1,0:T(8,128)(2,1)S(1)} collective-permute-done((bf16[288,768]{1,0:T(8,128)(2,1)S(1)}, bf16[288,768]{1,0:T(8,128)(2,1)S(1)}, u32[]{:S(2)}, u32[]{:S(2)}) %collective-permute-start.43) | collective-permute-done | bytes 442400 | tf_op jit(solution)/shard_map/ppermute | solution.py:425
  190.6 6.6 %collective-permute-done.47 = f32[16,768]{1,0:T(8,128)S(1)} collective-permute-done((f32[16,768]{1,0:T(8,128)S(1)}, f32[16,768]{1,0:T(8,128)S(1)}, u32[]{:S(2)}, u32[]{:S(2)}) %collective-permute-start.47) | collective-permute-done | bytes 49184 | tf_op jit(solution)/shard_map/ppermute | solution.py:409
  197.2 2.7 %collective-permute-done.46 = bf16[288,768]{1,0:T(8,128)(2,1)S(1)} collective-permute-done((bf16[288,768]{1,0:T(8,128)(2,1)S(1)}, bf16[288,768]{1,0:T(8,128)(2,1)S(1)}, u32[]{:S(2)}, u32[]{:S(2)}) %collective-permute-start.46) | collective-permute-done | bytes 442400 | tf_op jit(solution)/shard_map/ppermute | solution.py:425
  202.1 4.0 %collective-permute-done.52 = f32[16,768]{1,0:T(8,128)S(1)} collective-permute-done((f32[16,768]{1,0:T(8,128)S(1)}, f32[16,768]{1,0:T(8,128)S(1)}, u32[]{:S(2)}, u32[]{:S(2)}) %collective-permute-start.52) | collective-permute-done | bytes 49184 | tf_op jit(solution)/shard_map/ppermute | solution.py:1051
  207.1 4.8 %collective-permute-done.50 = f32[16,768]{1,0:T(8,128)S(1)} collective-permute-done((f32[16,768]{1,0:T(8,128)S(1)}, f32[16,768]{1,0:T(8,128)S(1)}, u32[]{:S(2)}, u32[]{:S(2)}) %collective-permute-start.50) | collective-permute-done | bytes 49184 | tf_op jit(solution)/shard_map/ppermute | solution.py:1051
  215.7 5.4 %collective-permute-done.53.refs_3_ = bf16[288,768]{1,0:T(8,128)(2,1)} collective-permute-done((bf16[288,768]{1,0:T(8,128)(2,1)S(1)}, bf16[288,768]{1,0:T(8,128)(2,1)}, u32[]{:S(2)}, u32[]{:S(2)}) %collective-permute-start.53) | collective-permute-done | bytes 442400 | tf_op jit(solution)/shard_map/ppermute | solution.py:409
  223.3 15.3 %shard_map.115 = (f32[13848,128]{1,0:T(8,128)}, f32[13848,128]{1,0:T(8,128)}) custom-call(s32[9]{0:T(128)} %stack.320.where, bf16[288,768]{1,0:T(8,128)(2,1)} %copy-done.14, bf16[288,768]{1,0:T(8,128)(2,1)} %copy-done.38, bf16[288,768]{1,0:T(8,128)(2,1)} %copy-done.37, bf16[288,768]{1,0:T(8,128)(2,1)} %collective-permute-done.53.refs_3_, ...), custom_call_target="tpu_custom_call" | custom-call | tf_op jit(solution)/shard_map/pallas_call | solution.py:1029
  238.6 2.8 %fusion = (f32[221568]{0:T(1024)}, f32[221568]{0:T(1024)}) fusion(f32[221568]{0:T(1024)S(1)} %copy-done.2, f32[1772544]{0:T(1024)} %bitcast.154, s32[]{:T(128)S(6)} %select_n.334, f32[221568]{0:T(1024)S(1)} %copy-done.1), kind=kLoop, calls=%fused_computation.3 | loop fusion | flops 1550976 | bytes 4431364 | tf_op jit(solution)/shard_map/add | solution.py:352
  (217 shorter events, 57.5 us)
Async XLA Ops:
  4.0 15.5 %collective-permute-start = (bf16[288,768]{1,0:T(8,128)(2,1)}, bf16[288,768]{1,0:T(8,128)(2,1)S(1)}, u32[]{:S(2)}, u32[]{:S(2)}) collective-permute-start(bf16[288,768]{1,0:T(8,128)(2,1)} %bitcast.153), channel_id=1, source_target_pairs={{0,1},{1,2},{2,3},{3,0},{4,5},{5,6},{6,7},{7,4},{8,9},{9,10},{10,1... | collective-permute-start | bytes 1327112 | tf_op jit(solution)/shard_map/ppermute | solution.py:425
  19.5 15.9 %collective-permute-start.3 = (bf16[288,768]{1,0:T(8,128)(2,1)S(1)}, bf16[288,768]{1,0:T(8,128)(2,1)S(1)}, u32[]{:S(2)}, u32[]{:S(2)}) collective-permute-start(bf16[288,768]{1,0:T(8,128)(2,1)S(1)} %collective-permute-done), channel_id=1, source_target_pairs={{0,16},{4,12},{8,24},{12,4},{16,0},{20,28},{24,8},{28,20},{1,17},{... | collective-permute-start | bytes 1327112 | tf_op jit(solution)/shard_map/ppermute | solution.py:409
  21.0 14.4 %collective-permute-start.2 = (bf16[288,768]{1,0:T(8,128)(2,1)S(1)}, bf16[288,768]{1,0:T(8,128)(2,1)S(1)}, u32[]{:S(2)}, u32[]{:S(2)}) collective-permute-start(bf16[288,768]{1,0:T(8,128)(2,1)S(1)} %collective-permute-done), channel_id=1, source_target_pairs={{0,8},{4,20},{8,0},{12,28},{16,24},{20,4},{24,16},{28,12},{1,9},{5... | collective-permute-start | bytes 1327112 | tf_op jit(solution)/shard_map/ppermute | solution.py:409
  22.5 12.9 %collective-permute-start.1 = (bf16[288,768]{1,0:T(8,128)(2,1)S(1)}, bf16[288,768]{1,0:T(8,128)(2,1)S(1)}, u32[]{:S(2)}, u32[]{:S(2)}) collective-permute-start(bf16[288,768]{1,0:T(8,128)(2,1)S(1)} %collective-permute-done), channel_id=1, source_target_pairs={{0,1},{1,2},{2,3},{3,0},{4,5},{5,6},{6,7},{7,4},{8,9},{9,10},{10,1... | collective-permute-start | bytes 1327112 | tf_op jit(solution)/shard_map/ppermute | solution.py:425
  22.5 12.9 %collective-permute-start.4 = (f32[8,768]{1,0:T(8,128)}, f32[8,768]{1,0:T(8,128)S(1)}, u32[]{:S(2)}, u32[]{:S(2)}) collective-permute-start(f32[8,768]{1,0:T(8,128)} %get-tuple-element.170.refs_16_), channel_id=1, source_target_pairs={{0,1},{1,2},{2,3},{3,0},{4,5},{5,6},{6,7},{7,4},{8,9},{9,10},{10,1... | collective-permute-start | bytes 73736 | tf_op jit(solution)/shard_map/ppermute | solution.py:425
  35.4 13.7 %collective-permute-start.8 = (bf16[288,768]{1,0:T(8,128)(2,1)S(1)}, bf16[288,768]{1,0:T(8,128)(2,1)S(1)}, u32[]{:S(2)}, u32[]{:S(2)}) collective-permute-start(bf16[288,768]{1,0:T(8,128)(2,1)S(1)} %collective-permute-done.2), channel_id=1, source_target_pairs={{0,16},{4,12},{8,24},{12,4},{16,0},{20,28},{24,8},{28,20},{1,17},{... | collective-permute-start | bytes 1327112 | tf_op jit(solution)/shard_map/ppermute | solution.py:409
  36.0 15.3 %collective-permute-start.7 = (bf16[288,768]{1,0:T(8,128)(2,1)S(1)}, bf16[288,768]{1,0:T(8,128)(2,1)S(1)}, u32[]{:S(2)}, u32[]{:S(2)}) collective-permute-start(bf16[288,768]{1,0:T(8,128)(2,1)S(1)} %collective-permute-done.1), channel_id=1, source_target_pairs={{0,16},{4,12},{8,24},{12,4},{16,0},{20,28},{24,8},{28,20},{1,17},{... | collective-permute-start | bytes 1327112 | tf_op jit(solution)/shard_map/ppermute | solution.py:409
  37.5 13.8 %collective-permute-start.6 = (bf16[288,768]{1,0:T(8,128)(2,1)S(1)}, bf16[288,768]{1,0:T(8,128)(2,1)S(1)}, u32[]{:S(2)}, u32[]{:S(2)}) collective-permute-start(bf16[288,768]{1,0:T(8,128)(2,1)S(1)} %collective-permute-done.1), channel_id=1, source_target_pairs={{0,8},{4,20},{8,0},{12,28},{16,24},{20,4},{24,16},{28,12},{1,9},{5... | collective-permute-start | bytes 1327112 | tf_op jit(solution)/shard_map/ppermute | solution.py:409
  38.0 13.3 %collective-permute-start.5 = (bf16[288,768]{1,0:T(8,128)(2,1)S(1)}, bf16[288,768]{1,0:T(8,128)(2,1)S(1)}, u32[]{:S(2)}, u32[]{:S(2)}) collective-permute-start(bf16[288,768]{1,0:T(8,128)(2,1)S(1)} %collective-permute-done.1), channel_id=1, source_target_pairs={{0,1},{1,2},{2,3},{3,0},{4,5},{5,6},{6,7},{7,4},{8,9},{9,10},{10,1... | collective-permute-start | bytes 1327112 | tf_op jit(solution)/shard_map/ppermute | solution.py:425
  38.0 11.1 %collective-permute-start.9 = (f32[8,768]{1,0:T(8,128)S(1)}, f32[8,768]{1,0:T(8,128)S(1)}, u32[]{:S(2)}, u32[]{:S(2)}) collective-permute-start(f32[8,768]{1,0:T(8,128)S(1)} %collective-permute-done.4.refs_17_), channel_id=1, source_target_pairs={{0,1},{1,2},{2,3},{3,0},{4,5},{5,6},{6,7},{7,4},{8,9},{9,10},{10,1... | collective-permute-start | bytes 73736 | tf_op jit(solution)/shard_map/ppermute | solution.py:425
  52.7 17.9 %collective-permute-start.13 = (bf16[4,288,768]{2,1,0:T(8,128)(2,1)S(1)}, bf16[4,288,768]{2,1,0:T(8,128)(2,1)S(1)}, u32[]{:S(2)}, u32[]{:S(2)}) collective-permute-start(bf16[4,288,768]{2,1,0:T(8,128)(2,1)S(1)} %pad_maximum_fusion.refs_0_), channel_id=1, source_target_pairs={{0,4},{4,0},{8,12},{12,8},{16,20},{20,16},{24,28},{28,24},{1,5},{5... | collective-permute-start | bytes 5308424 | tf_op jit(solution)/shard_map/ppermute | solution.py:409
  52.8 12.2 %collective-permute-start.12 = (bf16[288,768]{1,0:T(8,128)(2,1)S(1)}, bf16[288,768]{1,0:T(8,128)(2,1)S(1)}, u32[]{:S(2)}, u32[]{:S(2)}) collective-permute-start(bf16[288,768]{1,0:T(8,128)(2,1)S(1)} %collective-permute-done.6), channel_id=1, source_target_pairs={{0,16},{4,12},{8,24},{12,4},{16,0},{20,28},{24,8},{28,20},{1,17},{... | collective-permute-start | bytes 1327112 | tf_op jit(solution)/shard_map/ppermute | solution.py:409
  53.4 17.3 %collective-permute-start.11 = (bf16[288,768]{1,0:T(8,128)(2,1)S(1)}, bf16[288,768]{1,0:T(8,128)(2,1)S(1)}, u32[]{:S(2)}, u32[]{:S(2)}) collective-permute-start(bf16[288,768]{1,0:T(8,128)(2,1)S(1)} %collective-permute-done.5.refs_4_), channel_id=1, source_target_pairs={{0,16},{4,12},{8,24},{12,4},{16,0},{20,28},{24,8},{28,20},{1,17},{... | collective-permute-start | bytes 1327112 | tf_op jit(solution)/shard_map/ppermute | solution.py:409
  54.9 15.7 %collective-permute-start.10 = (bf16[288,768]{1,0:T(8,128)(2,1)S(1)}, bf16[288,768]{1,0:T(8,128)(2,1)S(1)}, u32[]{:S(2)}, u32[]{:S(2)}) collective-permute-start(bf16[288,768]{1,0:T(8,128)(2,1)S(1)} %collective-permute-done.5.refs_4_), channel_id=1, source_target_pairs={{0,8},{4,20},{8,0},{12,28},{16,24},{20,4},{24,16},{28,12},{1,9},{5... | collective-permute-start | bytes 1327112 | tf_op jit(solution)/shard_map/ppermute | solution.py:409
  72.1 18.1 %collective-permute-start.19 = (bf16[4,288,768]{2,1,0:T(8,128)(2,1)S(1)}, bf16[4,288,768]{2,1,0:T(8,128)(2,1)S(1)}, u32[]{:S(2)}, u32[]{:S(2)}) collective-permute-start(bf16[4,288,768]{2,1,0:T(8,128)(2,1)S(1)} %pad_maximum_fusion.1.refs_2_), channel_id=1, source_target_pairs={{0,4},{4,0},{8,12},{12,8},{16,20},{20,16},{24,28},{28,24},{1,5},{5... | collective-permute-start | bytes 5308424 | tf_op jit(solution)/shard_map/ppermute | solution.py:409
  72.2 18.0 %collective-permute-start.20 = (bf16[2,1760,128]{2,1,0:T(8,128)(2,1)S(1)}, bf16[2,1760,128]{2,1,0:T(8,128)(2,1)S(1)}, u32[]{:S(2)}, u32[]{:S(2)}) collective-permute-start(bf16[2,1760,128]{2,1,0:T(8,128)(2,1)S(1)} %shard_map.112.refs_8_), channel_id=1, source_target_pairs={{0,8},{4,20},{8,0},{12,28},{16,24},{20,4},{24,16},{28,12},{1,9},{5... | collective-permute-start | bytes 2703368 | tf_op jit(solution)/shard_map/ppermute | solution.py:409
  73.3 13.2 %collective-permute-start.18 = (bf16[288,768]{1,0:T(8,128)(2,1)S(1)}, bf16[288,768]{1,0:T(8,128)(2,1)}, u32[]{:S(2)}, u32[]{:S(2)}) collective-permute-start(bf16[288,768]{1,0:T(8,128)(2,1)S(1)} %collective-permute-done.10.refs_5_), channel_id=1, source_target_pairs={{0,16},{4,12},{8,24},{12,4},{16,0},{20,28},{24,8},{28,20},{1,17},{... | collective-permute-start | bytes 1327112 | tf_op jit(solution)/shard_map/ppermute | solution.py:409
  94.7 26.7 %collective-permute-start.24 = (bf16[2,1760,128]{2,1,0:T(8,128)(2,1)S(1)}, bf16[2,1760,128]{2,1,0:T(8,128)(2,1)S(1)}, u32[]{:S(2)}, u32[]{:S(2)}) collective-permute-start(bf16[2,1760,128]{2,1,0:T(8,128)(2,1)S(1)} %shard_map.112.refs_8_), channel_id=1, source_target_pairs={{0,4},{4,0},{8,12},{12,8},{16,20},{20,16},{24,28},{28,24},{1,5},{5... | collective-permute-start | bytes 2703368 | tf_op jit(solution)/shard_map/ppermute | solution.py:409
  94.8 26.6 %collective-permute-start.22 = (bf16[2,1760,128]{2,1,0:T(8,128)(2,1)S(1)}, bf16[2,1760,128]{2,1,0:T(8,128)(2,1)}, u32[]{:S(2)}, u32[]{:S(2)}) collective-permute-start(bf16[2,1760,128]{2,1,0:T(8,128)(2,1)S(1)} %shard_map.112.refs_8_), channel_id=1, source_target_pairs={{0,16},{4,12},{8,24},{12,4},{16,0},{20,28},{24,8},{28,20},{1,17},{... | collective-permute-start | bytes 2703368 | tf_op jit(solution)/shard_map/ppermute | solution.py:409
  95.3 26.1 %collective-permute-start.25 = (bf16[2,1760,128]{2,1,0:T(8,128)(2,1)}, bf16[2,1760,128]{2,1,0:T(8,128)(2,1)}, u32[]{:S(2)}, u32[]{:S(2)}) collective-permute-start(bf16[2,1760,128]{2,1,0:T(8,128)(2,1)} %copy-done.15), channel_id=1, source_target_pairs={{0,4},{4,0},{8,12},{12,8},{16,20},{20,16},{24,28},{28,24},{1,5},{5... | collective-permute-start | bytes 2703368 | tf_op jit(solution)/shard_map/ppermute | solution.py:409
  95.4 26.0 %collective-permute-start.23 = (bf16[2,1760,128]{2,1,0:T(8,128)(2,1)}, bf16[2,1760,128]{2,1,0:T(8,128)(2,1)}, u32[]{:S(2)}, u32[]{:S(2)}) collective-permute-start(bf16[2,1760,128]{2,1,0:T(8,128)(2,1)} %copy-done.15), channel_id=1, source_target_pairs={{0,16},{4,12},{8,24},{12,4},{16,0},{20,28},{24,8},{28,20},{1,17},{... | collective-permute-start | bytes 2703368 | tf_op jit(solution)/shard_map/ppermute | solution.py:409
  128.1 13.1 %collective-permute-start.29 = (bf16[2,288,768]{2,1,0:T(8,128)(2,1)S(1)}, bf16[2,288,768]{2,1,0:T(8,128)(2,1)S(1)}, u32[]{:S(2)}, u32[]{:S(2)}) collective-permute-start(bf16[2,288,768]{2,1,0:T(8,128)(2,1)S(1)} %add.607), channel_id=1, source_target_pairs={{0,8},{4,20},{8,0},{12,28},{16,24},{20,4},{24,16},{28,12},{1,9},{5... | collective-permute-start | bytes 2654216 | tf_op jit(solution)/shard_map/ppermute | solution.py:409
  130.8 25.8 %collective-permute-start.36 = (bf16[2,288,768]{2,1,0:T(8,128)(2,1)}, bf16[2,288,768]{2,1,0:T(8,128)(2,1)S(1)}, u32[]{:S(2)}, u32[]{:S(2)}) collective-permute-start(bf16[2,288,768]{2,1,0:T(8,128)(2,1)} %bitcast.91), channel_id=1, source_target_pairs={{0,4},{4,0},{8,12},{12,8},{16,20},{20,16},{24,28},{28,24},{1,5},{5... | collective-permute-start | bytes 2654216 | tf_op jit(solution)/shard_map/ppermute | solution.py:409
  130.8 25.9 %collective-permute-start.35 = (bf16[2,288,768]{2,1,0:T(8,128)(2,1)}, bf16[2,288,768]{2,1,0:T(8,128)(2,1)}, u32[]{:S(2)}, u32[]{:S(2)}) collective-permute-start(bf16[2,288,768]{2,1,0:T(8,128)(2,1)} %add.610), channel_id=1, source_target_pairs={{0,8},{4,20},{8,0},{12,28},{16,24},{20,4},{24,16},{28,12},{1,9},{5... | collective-permute-start | bytes 2654216 | tf_op jit(solution)/shard_map/ppermute | solution.py:409
  141.4 15.3 %collective-permute-start.34 = (bf16[288,768]{1,0:T(8,128)(2,1)S(1)}, bf16[288,768]{1,0:T(8,128)(2,1)}, u32[]{:S(2)}, u32[]{:S(2)}) collective-permute-start(bf16[288,768]{1,0:T(8,128)(2,1)S(1)} %slice_bitcast_fusion.7), channel_id=1, source_target_pairs={{0,16},{4,12},{8,24},{12,4},{16,0},{20,28},{24,8},{28,20},{1,17},{... | collective-permute-start | bytes 1327112 | tf_op jit(solution)/shard_map/ppermute | solution.py:409
  143.5 24.2 %collective-permute-start.38 = (bf16[2,288,768]{2,1,0:T(8,128)(2,1)}, bf16[2,288,768]{2,1,0:T(8,128)(2,1)}, u32[]{:S(2)}, u32[]{:S(2)}) collective-permute-start(bf16[2,288,768]{2,1,0:T(8,128)(2,1)} %add.615), channel_id=1, source_target_pairs={{0,8},{4,20},{8,0},{12,28},{16,24},{20,4},{24,16},{28,12},{1,9},{5... | collective-permute-start | bytes 2654216 | tf_op jit(solution)/shard_map/ppermute | solution.py:409
  160.7 12.4 %collective-permute-start.37 = (bf16[288,768]{1,0:T(8,128)(2,1)S(1)}, bf16[288,768]{1,0:T(8,128)(2,1)S(1)}, u32[]{:S(2)}, u32[]{:S(2)}) collective-permute-start(bf16[288,768]{1,0:T(8,128)(2,1)S(1)} %slice_bitcast_fusion.6), channel_id=1, source_target_pairs={{0,16},{4,12},{8,24},{12,4},{16,0},{20,28},{24,8},{28,20},{1,17},{... | collective-permute-start | bytes 1327112 | tf_op jit(solution)/shard_map/ppermute | solution.py:409
  161.7 12.6 %collective-permute-start.39 = (bf16[288,768]{1,0:T(8,128)(2,1)S(1)}, bf16[288,768]{1,0:T(8,128)(2,1)S(1)}, u32[]{:S(2)}, u32[]{:S(2)}) collective-permute-start(bf16[288,768]{1,0:T(8,128)(2,1)S(1)} %fusion.7), channel_id=1, source_target_pairs={{0,1},{1,2},{2,3},{3,0},{4,5},{5,6},{6,7},{7,4},{8,9},{9,10},{10,1... | collective-permute-start | bytes 1327112 | tf_op jit(solution)/shard_map/ppermute | solution.py:425
  162.0 20.1 %collective-permute-start.42 = (bf16[2,288,768]{2,1,0:T(8,128)(2,1)S(1)}, bf16[2,288,768]{2,1,0:T(8,128)(2,1)S(1)}, u32[]{:S(2)}, u32[]{:S(2)}) collective-permute-start(bf16[2,288,768]{2,1,0:T(8,128)(2,1)S(1)} %add.618), channel_id=1, source_target_pairs={{0,8},{4,20},{8,0},{12,28},{16,24},{20,4},{24,16},{28,12},{1,9},{5... | collective-permute-start | bytes 2654216 | tf_op jit(solution)/shard_map/ppermute | solution.py:409
  176.5 11.6 %collective-permute-start.43 = (bf16[288,768]{1,0:T(8,128)(2,1)S(1)}, bf16[288,768]{1,0:T(8,128)(2,1)S(1)}, u32[]{:S(2)}, u32[]{:S(2)}) collective-permute-start(bf16[288,768]{1,0:T(8,128)(2,1)S(1)} %fusion.6), channel_id=1, source_target_pairs={{0,1},{1,2},{2,3},{3,0},{4,5},{5,6},{6,7},{7,4},{8,9},{9,10},{10,1... | collective-permute-start | bytes 1327112 | tf_op jit(solution)/shard_map/ppermute | solution.py:425
  200.0 12.0 %collective-permute-start.49 = (bf16[288,768]{1,0:T(8,128)(2,1)S(1)}, bf16[288,768]{1,0:T(8,128)(2,1)S(1)}, u32[]{:S(2)}, u32[]{:S(2)}) collective-permute-start(bf16[288,768]{1,0:T(8,128)(2,1)S(1)} %fusion.4.refs_0_), channel_id=1, source_target_pairs={{0,16},{4,12},{8,24},{12,4},{16,0},{20,28},{24,8},{28,20},{1,17},{... | collective-permute-start | bytes 1327112 | tf_op jit(solution)/shard_map/ppermute | solution.py:409
  207.1 15.3 %collective-permute-start.58 = (bf16[2,1760,128]{2,1,0:T(8,128)(2,1)}, bf16[2,1760,128]{2,1,0:T(8,128)(2,1)}, u32[]{:S(2)}, u32[]{:S(2)}) collective-permute-start(bf16[2,1760,128]{2,1,0:T(8,128)(2,1)} %collective-permute-done.22.refs_10_), channel_id=1, source_target_pairs={{0,4},{4,0},{8,12},{12,8},{16,20},{20,16},{24,28},{28,24},{1,5},{5... | collective-permute-start | bytes 2703368 | tf_op jit(solution)/shard_map/ppermute | solution.py:409
  (74 other events, 696.6 us)
